TPU v7x, 32 devices: a whole 2x2x4 slice. The times are simulated.
32 devices in a mesh: img: 8 (over z, core), pix: 4 (over y, x).
Axes of the slice: x: 2, y: 2, z: 4, core: 2. Of those that a mesh axis runs over, the one named last changes fastest.
Arguments:
- images: bfloat16 [25600, 16384], P('img', 'pix'), may hold values from -6 to 6
- classes: int32 [25600], P('img'), may hold values from 0 to 63
- ctf_table: bfloat16 [64, 16384], P(None, 'pix'), may hold values from -1 to 1, as said below
- weights: float32 [25600], P('img'), may hold values from 0.1 to 1
- probes: float32 [16384, 256], P('pix'), may hold values from -6 to 6
Outputs:
- basis: float32 [16384, 256], P('pix')
- factor: float32 [256, 256], replicated
Inputs may be any that keep to these rules, and one draw needn't show every extreme that they name: `ctf_table`: a smooth envelope over the pixel index times an independent magnitude and sign for each entry.
All inputs are finite; a program needn't handle non-finite values.
Results may differ from a plain program's by a relative error of at most 0.012.
Values may be sent and summed in bfloat16 or wider, within the bound.
No kernel may reach another device: no remote copies, remote signals or barrier semaphores. Data moves between devices by JAX's collectives and lax.ppermute only.
A program may use at most 128 MiB of HBM per device.

v0:
```python
import jax
import jax.numpy as jnp
from jax import lax
from jax.sharding import PartitionSpec as P

ITERS = 2


def per_device(images, classes, ctf_table, weights, probes):
    onehot = (classes[:, None] == jnp.arange(ctf_table.shape[0])[None, :]).astype(jnp.bfloat16)
    filters = jnp.dot(onehot, ctf_table, preferred_element_type=jnp.float32)
    filtered = (images.astype(jnp.float32) * filters).astype(jnp.bfloat16)
    current = probes
    factor = jnp.zeros((probes.shape[1], probes.shape[1]), jnp.float32)
    for sweep in range(ITERS):
        probe_half = current.astype(jnp.bfloat16)
        share_rows = filtered.shape[0] // lax.axis_size("pix")
        shares = lax.psum_scatter(
            jnp.dot(filtered, probe_half, preferred_element_type=jnp.float32),
            "pix",
            scatter_dimension=0,
            tiled=True,
        )
        weight_share = lax.dynamic_slice_in_dim(
            weights, lax.axis_index("pix") * share_rows, share_rows, 0
        )
        scaled_share = (weight_share[:, None] * shares).astype(jnp.bfloat16)
        scaled = lax.all_gather(scaled_share, "pix", axis=0, tiled=True)
        partial_sum = lax.dot_general(
            filtered, scaled, (((0,), (0,)), ((), ())), preferred_element_type=jnp.float32
        )
        image_sum = lax.psum(partial_sum, "img")
        gram_matrix = lax.psum(
            jnp.dot(image_sum.T, image_sum, precision=lax.Precision.HIGHEST), "pix"
        )
        factor = jnp.linalg.cholesky(gram_matrix)
        current = jax.scipy.linalg.solve_triangular(factor, image_sum.T, lower=True).T
    return (current, factor)


def solution(mesh):
    in_specs = (P("img", "pix"), P("img"), P(None, "pix"), P("img"), P("pix", None))
    out_specs = (P("pix", None), P())
    return jax.shard_map(
        per_device, mesh=mesh, in_specs=in_specs, out_specs=out_specs, check_vma=False
    )
```

profile of v0, /device:TPU:0, one launch (start us, length us, event | category | flops | bytes accessed | tf_op | source)
XLA Modules:
  0.0 707.4 jit_solution(17062650772016324928)
XLA Ops:
  8.2 21.5 %multiply_convert_fusion = bf16[3200,4096]{1,0:T(8,128)(2,1)} fusion(bf16[3200,4096]{1,0:T(8,128)(2,1)} %param.8, bf16[64,4096]{1,0:T(8,128)(2,1)S(1)} %copy-done, s32[3200]{0:T(1024)} %param.9), kind=kOutput, calls=%fused_computation.4 | convolution fusion | flops 1717248000 | bytes 52965888 | tf_op jit(solution)/shard_map/dot_general | solution.py:11
  29.7 14.4 %fusion.5 = f32[3200,256]{1,0:T(8,128)} fusion(bf16[3200,4096]{1,0:T(8,128)(2,1)} %multiply_convert_fusion, f32[4096,256]{1,0:T(8,128)} %param.12), kind=kOutput, calls=%fused_computation.14 | convolution fusion | flops 6711934976 | bytes 33685504 | tf_op jit(solution)/shard_map/dot_general | solution.py:19
  45.0 47.0 %reduce-scatter.3.cloned.1.call-done = f32[800,256]{1,0:T(8,128)} async-done(((f32[3200,256]{1,0:T(8,128)}), f32[800,256]{1,0:T(8,128)}) %reduce-scatter.3.cloned.1.call-update) | async-done | bytes 819216 | tf_op jit(solution)/shard_map/reduce_scatter | solution.py:18
  92.0 2.1 multiply_convert_fusion.2
  94.1 31.7 %all-gather.3.cloned.1.call-done = bf16[3200,256]{1,0:T(8,128)(2,1)} async-done(((bf16[800,256]{1,0:T(8,128)(2,1)}), bf16[3200,256]{1,0:T(8,128)(2,1)}) %all-gather.3.cloned.1.call-update) | async-done | bytes 1638416 | tf_op jit(solution)/shard_map/all_gather | solution.py:28
  125.8 14.4 %fusion.30 = f32[4096,256]{1,0:T(8,128)} fusion(bf16[3200,4096]{1,0:T(8,128)(2,1)} %multiply_convert_fusion, bf16[3200,256]{1,0:T(8,128)(2,1)} %all-gather.3.cloned.1.call-done), kind=kOutput, calls=%fused_computation.66 | convolution fusion | flops 6710886400 | bytes 32047104 | tf_op jit(solution)/shard_map/dot_general | solution.py:29
  140.5 96.4 %all-reduce.6.cloned.1.call-done = f32[4096,256]{1,0:T(8,128)} async-done(((f32[4096,256]{1,0:T(8,128)}), f32[4096,256]{1,0:T(8,128)}) %all-reduce.6.cloned.1.call-update) | async-done | bytes 4194320 | tf_op jit(solution)/shard_map/psum | solution.py:32
  236.9 10.9 %fusion.31 = f32[256,256]{0,1:T(8,128)} fusion(f32[4096,256]{1,0:T(8,128)} %all-reduce.6.cloned.1.call-done), kind=kOutput, calls=%fused_computation.67 | convolution fusion | flops 3221225472 | bytes 4456448 | tf_op jit(solution)/shard_map/dot_general | solution.py:34
  248.3 42.8 %all-reduce.8.cloned.1.call-done = f32[256,256]{0,1:T(8,128)} async-done(((f32[256,256]{0,1:T(8,128)}), f32[256,256]{0,1:T(8,128)}) %all-reduce.8.cloned.1.call-update) | async-done | bytes 262160 | tf_op jit(solution)/shard_map/psum | solution.py:33
  293.1 11.7 %cholesky.130 = f32[128,128]{1,0:T(8,128)S(1)} custom-call(f32[128,128]{1,0:T(8,128)S(1)} %cholesky.194), custom_call_target="Cholesky" | custom-call | tf_op jit(solution)/shard_map/jit(cholesky)/cholesky | solution.py:36
  304.9 9.8 %custom-call.13 = f32[1,128,128]{1,2,0:T(8,128)S(1)} custom-call(f32[1,128,128]{2,1,0:T(8,128)S(1)} %get-tuple-element.51), custom_call_target="InvertDiagBlocksLowerTriangular" | custom-call | tf_op jit(solution)/shard_map/jit(cholesky)/cholesky | solution.py:36
  315.2 11.7 %cholesky.147 = f32[128,128]{1,0:T(8,128)S(1)} custom-call(f32[128,128]{1,0:T(8,128)S(1)} %convolution_subtract_fusion.3), custom_call_target="Cholesky" | custom-call | tf_op jit(solution)/shard_map/jit(cholesky)/cholesky | solution.py:36
  329.1 4.2 while.4
  333.2 19.7 %custom-call.14 = f32[2,128,128]{1,2,0:T(8,128)S(1)} custom-call(f32[2,128,128]{2,1,0:T(8,128)S(1)} %get-tuple-element.18), custom_call_target="InvertDiagBlocksLowerTriangular" | custom-call | tf_op jit(solution)/shard_map/jit(_solve_triangular)/triangular_solve | solution.py:37
  352.9 3.7 fusion.3
  356.6 3.6 convolution_subtract_fusion.1
  362.1 14.0 %fusion = f32[3200,256]{1,0:T(8,128)} fusion(bf16[3200,4096]{1,0:T(8,128)(2,1)} %multiply_convert_fusion, bf16[128,4096]{1,0:T(8,128)(2,1)S(1)} %fusion.17, f32[128,4096]{1,0:T(8,128)S(1)} %fusion.3), kind=kOutput, calls=%fused_computation.9 | convolution fusion | flops 6715080704 | bytes 32636928 | tf_op jit(solution)/shard_map/dot_general | solution.py:19
  376.2 45.1 %reduce-scatter.5.cloned.1.call-done = f32[800,256]{1,0:T(8,128)} async-done(((f32[3200,256]{1,0:T(8,128)}), f32[800,256]{1,0:T(8,128)}) %reduce-scatter.5.cloned.1.call-update) | async-done | bytes 819216 | tf_op jit(solution)/shard_map/reduce_scatter | solution.py:18
  423.5 31.5 %all-gather.5.cloned.1.call-done = bf16[3200,256]{1,0:T(8,128)(2,1)} async-done(((bf16[800,256]{1,0:T(8,128)(2,1)}), bf16[3200,256]{1,0:T(8,128)(2,1)}) %all-gather.5.cloned.1.call-update) | async-done | bytes 1638416 | tf_op jit(solution)/shard_map/all_gather | solution.py:28
  455.0 14.4 %fusion.32 = f32[4096,256]{1,0:T(8,128)} fusion(bf16[3200,4096]{1,0:T(8,128)(2,1)} %multiply_convert_fusion, bf16[3200,256]{1,0:T(8,128)(2,1)} %all-gather.5.cloned.1.call-done), kind=kOutput, calls=%fused_computation.68 | convolution fusion | flops 6710886400 | bytes 32047104 | tf_op jit(solution)/shard_map/dot_general | solution.py:29
  469.9 96.2 %all-reduce.10.cloned.1.call-done = f32[4096,256]{1,0:T(8,128)} async-done(((f32[4096,256]{1,0:T(8,128)}), f32[4096,256]{1,0:T(8,128)}) %all-reduce.10.cloned.1.call-update) | async-done | bytes 4194320 | tf_op jit(solution)/shard_map/psum | solution.py:32
  566.1 10.9 %fusion.33 = f32[256,256]{0,1:T(8,128)} fusion(f32[4096,256]{1,0:T(8,128)} %all-reduce.10.cloned.1.call-done), kind=kOutput, calls=%fused_computation.69 | convolution fusion | flops 3221225472 | bytes 4456448 | tf_op jit(solution)/shard_map/dot_general | solution.py:34
  577.0 43.2 %all-reduce.12.cloned.1.call-done = f32[256,256]{0,1:T(8,128)} async-done(((f32[256,256]{0,1:T(8,128)}), f32[256,256]{0,1:T(8,128)}) %all-reduce.12.cloned.1.call-update) | async-done | bytes 262160 | tf_op jit(solution)/shard_map/psum | solution.py:33
  622.3 11.7 %cholesky.164 = f32[128,128]{1,0:T(8,128)S(1)} custom-call(f32[128,128]{1,0:T(8,128)S(1)} %cholesky.197), custom_call_target="Cholesky" | custom-call | tf_op jit(solution)/shard_map/jit(cholesky)/cholesky | solution.py:36
  634.1 10.0 %custom-call.15 = f32[1,128,128]{1,2,0:T(8,128)S(1)} custom-call(f32[1,128,128]{2,1,0:T(8,128)S(1)} %get-tuple-element.47), custom_call_target="InvertDiagBlocksLowerTriangular" | custom-call | tf_op jit(solution)/shard_map/jit(cholesky)/cholesky | solution.py:36
  644.5 11.7 %cholesky.181 = f32[128,128]{1,0:T(8,128)S(1)} custom-call(f32[128,128]{1,0:T(8,128)S(1)} %convolution_subtract_fusion.2), custom_call_target="Cholesky" | custom-call | tf_op jit(solution)/shard_map/jit(cholesky)/cholesky | solution.py:36
  659.6 3.9 while.5
  663.6 19.7 %custom-call.16 = f32[2,128,128]{1,2,0:T(8,128)S(1)} custom-call(f32[2,128,128]{2,1,0:T(8,128)S(1)} %get-tuple-element.19), custom_call_target="InvertDiagBlocksLowerTriangular" | custom-call | tf_op jit(solution)/shard_map/jit(_solve_triangular)/triangular_solve | solution.py:37
  683.2 3.7 fusion.1
  686.9 3.4 convolution_subtract_fusion
  692.4 2.4 maximum_bitcast_fusion
  694.8 5.6 copy.11
  (65 shorter events, 25.2 us)
Async XLA Ops:
  7.2 1.1 copy-start
  7.2 84.8 %reduce-scatter.3.cloned.1.call-start = ((), (), s32[]{:S(2)}) async-start(), calls=%async_computation.2 | async-start | bytes 4096000 | tf_op jit(solution)/shard_map/reduce_scatter | solution.py:18
  44.1 81.7 %all-gather.3.cloned.1.call-start = ((), (), s32[]{:S(2)}) async-start(), calls=%async_computation.3 | async-start | bytes 2048000 | tf_op jit(solution)/shard_map/all_gather | solution.py:28
  94.1 142.8 %all-reduce.6.cloned.1.call-start = ((), (), s32[]{:S(2)}) async-start(), calls=%async_computation.4 | async-start | bytes 8388608 | tf_op jit(solution)/shard_map/psum | solution.py:32
  140.3 150.8 %all-reduce.8.cloned.1.call-start = ((), (), s32[]{:S(2)}) async-start(), calls=%async_computation.5 | async-start | bytes 524288 | tf_op jit(solution)/shard_map/psum | solution.py:33
  247.8 173.5 %reduce-scatter.5.cloned.1.call-start = ((), (), s32[]{:S(2)}) async-start(), calls=%async_computation.6 | async-start | bytes 4096000 | tf_op jit(solution)/shard_map/reduce_scatter | solution.py:18
  352.9 3.7 copy-start.2
  376.1 78.8 %all-gather.5.cloned.1.call-start = ((), (), s32[]{:S(2)}) async-start(), calls=%async_computation.7 | async-start | bytes 2048000 | tf_op jit(solution)/shard_map/all_gather | solution.py:28
  423.4 142.6 %all-reduce.10.cloned.1.call-start = ((), (), s32[]{:S(2)}) async-start(), calls=%async_computation.8 | async-start | bytes 8388608 | tf_op jit(solution)/shard_map/psum | solution.py:32
  469.4 150.8 %all-reduce.12.cloned.1.call-start = ((), (), s32[]{:S(2)}) async-start(), calls=%async_computation.9 | async-start | bytes 524288 | tf_op jit(solution)/shard_map/psum | solution.py:33
  683.2 3.7 copy-start.3
  692.4 8.0 %copy-start.1 = (bf16[64,4096]{1,0:T(8,128)(2,1)S(1)}, bf16[64,4096]{1,0:T(8,128)(2,1)}, u32[]{:S(2)}) copy-start(bf16[64,4096]{1,0:T(8,128)(2,1)} %param.10) | copy-start | bytes 1572868
Sparse Core Ops, SparseCore 0:
  44.3 47.6 reduce-scatter.2
  94.4 31.3 all-gather.2
  140.4 96.4 all-reduce.5
  247.9 43.0 all-reduce.7
  376.3 44.9 reduce-scatter.4
  423.6 31.3 all-gather.4
  469.5 96.4 all-reduce.9
  577.1 43.0 all-reduce.11
where the time goes:
time: 716 us; the launch traced here: 707 us
  waiting for transfers between devices  434 us (61%)
  matrix products  120 us (17%)
  other arithmetic  117 us (16%)
  local copies, waits for them, and re-layouts  17.5 us (2%)
  between operations  17.2 us (2%)
    psum x2, waiting for transfers between devices, per_device(): image_sum = lax.psum(partial_sum, 'img')  193 us
    reduce_scatter x2, waiting for transfers between devices, per_device(): lax.psum_scatter(jnp.dot(filtered, probe_half, preferred_element_type=jnp...  92.1 us
    psum x2, waiting for transfers between devices, per_device(): lax.psum(jnp.dot(image_sum.T, image_sum, precision=lax.Precision.HIGHEST)...  86 us
    another operation x13, other arithmetic, per_device(): factor = jnp.linalg.cholesky(gram_matrix)  68.7 us
    all_gather x2, waiting for transfers between devices, per_device(): scaled = lax.all_gather(scaled_share, 'pix', axis=0, tiled=True)  63.2 us
    another operation x5, other arithmetic, per_device(): jax.scipy.linalg.solve_triangular(factor, image_sum.T, lower=True)  40.1 us
    dot_general x2, matrix products, per_device(): lax.dot_general(filtered, scaled, (((0,), (0,)), ((), ())), preferred_ele...  28.8 us
    dot_general x2, matrix products, per_device(): jnp.dot(filtered, probe_half, preferred_element_type=jnp.float32)  28.4 us
  transfers between devices with their start and end apart: 8, of which 8 were waited for; matrix products, arithmetic and copies ran while one was open for 0% of the time, Pallas kernels for 0%

commit v1 on v0

v1 whole, which is shorter than its diff:
```python
import functools

import jax
import jax.numpy as jnp
from jax import lax
from jax.experimental import pallas as pl
from jax.experimental.pallas import tpu as pltpu
from jax.sharding import PartitionSpec as P

ITERS = 2
F32 = jnp.float32
BF16 = jnp.bfloat16
LANES = 128
PANEL = 32
HIGHEST = lax.Precision.HIGHEST


def cost(flops, nbytes):
    return pl.CostEstimate(flops=int(flops), bytes_accessed=int(nbytes), transcendentals=0)


def vmem(nbytes):
    return pltpu.CompilerParams(vmem_limit_bytes=nbytes)


def row_tile(rows, most=400):
    return max(t for t in range(16, most + 1, 16) if rows % t == 0)


def xor_swap(value, axis, mask):
    size = lax.axis_size(axis)
    return lax.ppermute(value, axis, [(i, i ^ mask) for i in range(size)])


def contract_rows(left, right):
    return lax.dot_general(left, right, (((0,), (0,)), ((), ())), preferred_element_type=F32)


def filter_kernel(order, class_ref, image_ref, table_ref, probe_ref, filtered_ref, score_ref):
    table_rows = table_ref.shape[0]
    rows, pixels = image_ref.shape
    onehot = (
        lax.broadcasted_iota(jnp.int32, (table_rows, rows), 0) == class_ref[0]
    ).astype(BF16)
    filters = contract_rows(onehot, table_ref[...])
    filtered = (image_ref[...].astype(F32) * filters).astype(BF16)
    filtered_ref[...] = filtered
    scores = jnp.dot(filtered, probe_ref[...], preferred_element_type=F32)
    score_ref[...] = scores.astype(score_ref.dtype)


def filter_and_score(order, images, classes, table, probe_half, chunk, out_type):
    rows, pixels = images.shape
    columns = probe_half.shape[1]
    tile = row_tile(chunk)
    steps = chunk // tile
    return pl.pallas_call(
        filter_kernel,
        grid_spec=pltpu.PrefetchScalarGridSpec(
            num_scalar_prefetch=1,
            grid=(steps,),
            in_specs=[
                pl.BlockSpec((1, 1, tile), lambda i, order: (order[0] * steps + i, 0, 0)),
                pl.BlockSpec((tile, pixels), lambda i, order: (order[0] * steps + i, 0)),
                pl.BlockSpec(table.shape, lambda i, order: (0, 0)),
                pl.BlockSpec(probe_half.shape, lambda i, order: (0, 0)),
            ],
            out_specs=[
                pl.BlockSpec((tile, pixels), lambda i, order: (i, 0)),
                pl.BlockSpec((tile, columns), lambda i, order: (i, 0)),
            ],
        ),
        out_shape=[
            jax.ShapeDtypeStruct((chunk, pixels), BF16),
            jax.ShapeDtypeStruct((chunk, columns), out_type),
        ],
        compiler_params=vmem(56 * 2**20),
        cost_estimate=cost(4 * chunk * pixels * columns, 4 * chunk * pixels),
        name="filter_and_score",
    )(order, classes.reshape(rows // tile, 1, tile), images, table, probe_half)


def score_kernel(order, filtered_ref, *refs):
    *basis_refs, score_ref = refs
    width = basis_refs[0].shape[0]
    total = None
    for at, basis_ref in enumerate(basis_refs):
        columns = pl.ds(pl.multiple_of(order[at] * width, width), width)
        term = jnp.dot(filtered_ref[:, columns], basis_ref[...], preferred_element_type=F32)
        total = term if total is None else total + term
    score_ref[...] = total.astype(score_ref.dtype)


def score(order, filtered, basis, out_type):
    rows, pixels = filtered.shape
    columns = basis[0].shape[1]
    tile = row_tile(rows)
    return pl.pallas_call(
        score_kernel,
        grid_spec=pltpu.PrefetchScalarGridSpec(
            num_scalar_prefetch=1,
            grid=(rows // tile,),
            in_specs=[pl.BlockSpec((tile, pixels), lambda i, order: (i, 0))]
            + [pl.BlockSpec(b.shape, lambda i, order: (0, 0)) for b in basis],
            out_specs=pl.BlockSpec((tile, columns), lambda i, order: (i, 0)),
        ),
        out_shape=jax.ShapeDtypeStruct((rows, columns), out_type),
        compiler_params=vmem(40 * 2**20),
        cost_estimate=cost(2 * rows * pixels * columns, 2 * rows * pixels),
        name="score",
    )(order, filtered, *basis)


def sum_blocks(filtered_refs, scaled_refs):
    rows = filtered_refs[0].shape[0]
    whole = rows // 256 * 256
    total = None
    for filtered_ref, scaled_ref in zip(filtered_refs, scaled_refs):
        if whole:
            term = contract_rows(filtered_ref[:whole, :], scaled_ref[:whole, :])
            total = term if total is None else total + term
    if whole < rows:
        left = jnp.concatenate([ref[whole:, :] for ref in filtered_refs], 0)
        right = jnp.concatenate([ref[whole:, :] for ref in scaled_refs], 0)
        term = contract_rows(left, right)
        total = term if total is None else total + term
    return total


def first_sum_kernel(count, order, *refs):
    refs[-1][...] = sum_blocks(refs[:count], refs[count : 2 * count])


def last_sum_kernel(count, half, order, *refs):
    *refs, send_ref, keep_ref = refs
    total = sum_blocks(refs[:count], refs[count : 2 * count]) + refs[-1][...]
    at = pl.program_id(0)

    @pl.when(at < half)
    def _():
        send_ref[...] = total.astype(BF16)

    @pl.when(at >= half)
    def _():
        keep_ref[...] = total.astype(BF16)


def image_sum_specs(filtered, scaled, width):
    rows = filtered[0].shape[0]
    return [pl.BlockSpec((rows, width), lambda i, order: (0, order[i])) for _ in filtered] + [
        pl.BlockSpec(s.shape, lambda i, order: (0, 0)) for s in scaled
    ]


def first_sum(order, filtered, scaled):
    blocks = order.shape[0]
    rows, pixels = filtered[0].shape
    columns = scaled[0].shape[1]
    width = pixels // blocks
    return pl.pallas_call(
        functools.partial(first_sum_kernel, len(filtered)),
        grid_spec=pltpu.PrefetchScalarGridSpec(
            num_scalar_prefetch=1,
            grid=(blocks,),
            in_specs=image_sum_specs(filtered, scaled, width),
            out_specs=pl.BlockSpec((width, columns), lambda i, order: (i, 0)),
        ),
        out_shape=jax.ShapeDtypeStruct((pixels, columns), F32),
        compiler_params=vmem(40 * 2**20),
        cost_estimate=cost(
            2 * len(filtered) * rows * pixels * columns,
            2 * len(filtered) * rows * pixels + 4 * pixels * columns,
        ),
        name="first_sum",
    )(order, *filtered, *scaled)


def last_sum(order, filtered, scaled, partial):
    blocks = order.shape[0]
    half = blocks // 2
    rows, pixels = filtered[0].shape
    columns = scaled[0].shape[1]
    width = pixels // blocks
    return pl.pallas_call(
        functools.partial(last_sum_kernel, len(filtered), half),
        grid_spec=pltpu.PrefetchScalarGridSpec(
            num_scalar_prefetch=1,
            grid=(blocks,),
            in_specs=image_sum_specs(filtered, scaled, width)
            + [pl.BlockSpec((width, columns), lambda i, order: (i, 0))],
            out_specs=[
                pl.BlockSpec((width, columns), lambda i, order: (jnp.minimum(i, half - 1), 0)),
                pl.BlockSpec((width, columns), lambda i, order: (jnp.maximum(i - half, 0), 0)),
            ],
        ),
        out_shape=[jax.ShapeDtypeStruct((pixels // 2, columns), BF16)] * 2,
        compiler_params=vmem(40 * 2**20),
        cost_estimate=cost(
            2 * len(filtered) * rows * pixels * columns,
            2 * len(filtered) * rows * pixels + 6 * pixels * columns,
        ),
        name="last_sum",
    )(order, *filtered, *scaled, partial)


def tree_sum(terms):
    while len(terms) > 1:
        terms = [terms[i] + terms[i + 1] for i in range(0, len(terms), 2)]
    return terms[0]


def gram_kernel(*refs):
    *basis_refs, gram_ref = refs
    gram_ref[...] = tree_sum([contract_rows(ref[...], ref[...]) for ref in basis_refs])


def gram_of(basis):
    rows, columns = basis[0].shape
    return pl.pallas_call(
        gram_kernel,
        out_shape=jax.ShapeDtypeStruct((columns, columns), F32),
        compiler_params=vmem(24 * 2**20),
        cost_estimate=cost(2 * len(basis) * rows * columns * columns, 2 * len(basis) * rows * columns),
        name="gram",
    )(*basis)


def cholesky_kernel(gram_ref, factor_ref, inverse_ref, work_ref):
    size = gram_ref.shape[0]
    work_ref[:, :size] = gram_ref[...]
    square = (size, size)
    row_at = lax.broadcasted_iota(jnp.int32, square, 0)
    column_at = lax.broadcasted_iota(jnp.int32, square, 1)
    work_ref[:, size:] = (row_at == column_at).astype(F32)
    panel_row = lax.broadcasted_iota(jnp.int32, (PANEL, LANES), 0)
    panel_column = lax.broadcasted_iota(jnp.int32, (PANEL, LANES), 1)
    per_tile = LANES // PANEL

    def panel(block, carry):
        start = pl.multiple_of(block * PANEL, PANEL)
        tile = pl.multiple_of((block // per_tile) * LANES, LANES)
        body = work_ref[pl.ds(start, PANEL), :]
        diagonal = work_ref[pl.ds(start, PANEL), pl.ds(tile, LANES)]
        diagonal = pltpu.roll(diagonal, (LANES - (block % per_tile) * PANEL) % LANES, 1)
        for at in range(PANEL):
            column = jnp.broadcast_to(diagonal[:, at : at + 1], (PANEL, LANES))
            scale = jnp.where(panel_row > at, column * (1.0 / column[at : at + 1, :]), 0.0)
            wide = jnp.concatenate([scale] * (body.shape[1] // LANES), 1)
            body = body - wide * body[at : at + 1, :]
            diagonal = diagonal - scale * diagonal[at : at + 1, :]
        pivots = jnp.sum(
            jnp.where(panel_row == panel_column, diagonal, 0.0), axis=1, keepdims=True
        )
        body = body * lax.rsqrt(pivots)
        work_ref[pl.ds(start, PANEL), :] = body
        left = body[:, :size]
        later = lax.broadcasted_iota(jnp.int32, left.shape, 1) >= start + PANEL
        work_ref[...] -= lax.dot_general(
            jnp.where(later, left, 0.0),
            body,
            (((0,), (0,)), ((), ())),
            precision=HIGHEST,
            preferred_element_type=F32,
        )
        return carry

    lax.fori_loop(0, size // PANEL, panel, 0)
    factor_ref[...] = jnp.where(row_at <= column_at, work_ref[:, :size], 0.0).T
    inverse_ref[...] = work_ref[:, size:]


def cholesky_and_inverse(gram):
    size = gram.shape[0]
    return pl.pallas_call(
        cholesky_kernel,
        out_shape=[jax.ShapeDtypeStruct((size, size), F32)] * 2,
        scratch_shapes=[pltpu.VMEM((size, 2 * size), F32)],
        compiler_params=vmem(16 * 2**20),
        cost_estimate=cost(12e9, 12 * size * size),
        name="cholesky",
    )(gram)


def apply_kernel(order, inverse_ref, *refs):
    *basis_refs, out_ref = refs
    inverse = inverse_ref[...]
    parts = []
    for _ in range(3):
        parts.append(inverse.astype(BF16))
        inverse = inverse - parts[-1].astype(F32)
    for at, basis_ref in enumerate(basis_refs):

        @pl.when(pl.program_id(0) == at)
        def _():
            block = basis_ref[...]
            out_ref[...] = sum(
                lax.dot_general(
                    block, part, (((1,), (1,)), ((), ())), preferred_element_type=F32
                )
                for part in reversed(parts)
            )


def apply_inverse(order, inverse, basis):
    rows, columns = basis[0].shape
    blocks = len(basis)
    return pl.pallas_call(
        apply_kernel,
        grid_spec=pltpu.PrefetchScalarGridSpec(
            num_scalar_prefetch=1,
            grid=(blocks,),
            in_specs=[pl.BlockSpec(inverse.shape, lambda i, order: (0, 0))]
            + [pl.BlockSpec((rows, columns), lambda i, order: (0, 0)) for _ in basis],
            out_specs=pl.BlockSpec((rows, columns), lambda i, order: (order[i], 0)),
        ),
        out_shape=jax.ShapeDtypeStruct((rows * blocks, columns), F32),
        compiler_params=vmem(32 * 2**20),
        cost_estimate=cost(6 * rows * blocks * columns * columns, 6 * rows * blocks * columns),
        name="apply",
    )(order, inverse, *basis)


def per_device(images, classes, ctf_table, weights, probes):
    images_here, pixels = images.shape
    pix, img = lax.axis_size("pix"), lax.axis_size("img")
    depth = img // 2
    chunk = images_here // pix
    me = lax.axis_index("pix")
    place = lax.axis_index("img")
    core, level = place % 2, place // 2

    at = jnp.arange(img)
    gathered = ((at // depth) ^ core) * depth + ((at % depth) ^ level)
    scattered = ((1 - at // depth) ^ core) * depth + ((at % depth) ^ level)
    gathered, scattered = gathered.astype(jnp.int32), scattered.astype(jnp.int32)

    shifts = list(range(pix - 1, -1, -1))
    weight_share = lax.dynamic_slice_in_dim(weights, me * chunk, chunk, 0)[:, None]

    filtered, own, arrived = [None] * pix, None, []
    probe_half = probes.astype(BF16)
    for shift in shifts:
        order = (me ^ shift).astype(jnp.int32)[None]
        filtered[shift], part = filter_and_score(
            order, images, classes, ctf_table, probe_half, chunk, BF16 if shift else F32
        )
        if shift:
            arrived.append(xor_swap(part, "pix", shift))
        else:
            own = part

    inverse = None
    for sweep in range(ITERS):
        shares = own
        for part in arrived:
            shares = shares + part.astype(F32)
        if inverse is not None:
            shares = lax.dot_general(
                shares, inverse, (((1,), (1,)), ((), ())), precision=HIGHEST
            )
        scaled_share = (weight_share * shares).astype(BF16)
        scaled = [scaled_share] + [xor_swap(scaled_share, "pix", s) for s in range(1, pix)]
        split = pix // 2
        partial = first_sum(scattered, filtered[:split], scaled[:split])
        send, keep = last_sum(scattered, filtered[split:], scaled[split:], partial)

        got = xor_swap(send, "img", 1)
        width = pixels // img
        pairs = [
            keep[s * width : (s + 1) * width].astype(F32)
            + got[s * width : (s + 1) * width].astype(F32)
            for s in range(depth)
        ]
        total = pairs[0]
        for s in range(depth - 1, 0, -1):
            total = total + xor_swap(pairs[s].astype(BF16), "img", 2 * s).astype(F32)
        half = total.astype(BF16)
        near = [half] + [xor_swap(half, "img", 2 * s) for s in range(1, depth)]
        basis = near + [xor_swap(block, "img", 1) for block in near]

        gram = gram_of(basis)
        step = 1
        while step < pix:
            gram = gram + xor_swap(gram, "pix", step)
            step *= 2
        factor, inverse = cholesky_and_inverse(gram)
        if sweep == ITERS - 1:
            return apply_inverse(gathered, inverse, basis), factor
        own, arrived = None, []
        for shift in shifts:
            part = score(gathered, filtered[shift], basis, BF16 if shift else F32)
            if shift:
                arrived.append(xor_swap(part, "pix", shift))
            else:
                own = part


def plain_per_device(images, classes, ctf_table, weights, probes):
    onehot = (classes[:, None] == jnp.arange(ctf_table.shape[0])[None, :]).astype(BF16)
    filters = jnp.dot(onehot, ctf_table, preferred_element_type=F32)
    filtered = (images.astype(F32) * filters).astype(BF16)
    current = probes
    factor = None
    for sweep in range(ITERS):
        share_rows = filtered.shape[0] // lax.axis_size("pix")
        shares = lax.psum_scatter(
            jnp.dot(filtered, current.astype(BF16), preferred_element_type=F32),
            "pix",
            scatter_dimension=0,
            tiled=True,
        )
        weight_share = lax.dynamic_slice_in_dim(
            weights, lax.axis_index("pix") * share_rows, share_rows, 0
        )
        scaled_share = (weight_share[:, None] * shares).astype(BF16)
        scaled = lax.all_gather(scaled_share, "pix", axis=0, tiled=True)
        image_sum = lax.psum(contract_rows(filtered, scaled), "img")
        gram = lax.psum(jnp.dot(image_sum.T, image_sum, precision=HIGHEST), "pix")
        factor = jnp.linalg.cholesky(gram)
        current = jax.scipy.linalg.solve_triangular(factor, image_sum.T, lower=True).T
    return current, factor


def power_of_two(n):
    return n > 1 and n & (n - 1) == 0


def per_device_of(images, classes, ctf_table, weights, probes):
    rows, pixels = images.shape
    pix, img = lax.axis_size("pix"), lax.axis_size("img")
    columns = probes.shape[1]
    fits = (
        power_of_two(pix)
        and power_of_two(img)
        and rows % (16 * pix) == 0
        and pixels % (LANES * img) == 0
        and columns % LANES == 0
    )
    run = per_device if fits else plain_per_device
    return run(images, classes, ctf_table, weights, probes)


def solution(mesh):
    in_specs = (P("img", "pix"), P("img"), P(None, "pix"), P("img"), P("pix", None))
    out_specs = (P("pix", None), P())
    return jax.shard_map(
        per_device_of, mesh=mesh, in_specs=in_specs, out_specs=out_specs, check_vma=False
    )
```

time: 716 us -> 339 us (0.47); the launches traced: 707 us -> 338 us
  waiting for transfers between devices: 434 us -> 135 us
  Pallas kernels: 0 us -> 144 us
  matrix products: 120 us -> 2.08 us
  other arithmetic: 117 us -> 5.96 us
  starting transfers between devices: 1.35 us -> 39.6 us
  between operations: 17.2 us -> 0.91 us
  local copies, waits for them, and re-layouts: 17.5 us -> 9.85 us
    psum x4 -> x0, waiting for transfers between devices: 279 us -> none  [the longest x2 193 us: per_device(): image_sum = lax.psum(partial_sum, 'img')]
    pallas_call x0 -> x17, Pallas kernels: none -> 144 us  [the longest x2 55 us: cholesky_and_inverse(): pl.pallas_call(cholesky_kernel, out_shape=[jax.ShapeDtypeStruct((size, si...]
    ppermute x0 -> x38, waiting for transfers between devices: none -> 135 us  [xor_swap(): return lax.ppermute(value, axis, [(i, i ^ mask) for i in range(size)])]
    another operation x18 -> x0, other arithmetic: 109 us -> none  [the longest x13 68.7 us: per_device(): factor = jnp.linalg.cholesky(gram_matrix)]
    dot_general x7 -> x1, matrix products: 101 us -> 2.08 us  [per_device(): lax.dot_general(shares, inverse, (((1,), (1,)), ((), ())), precision=HIGH...]
    reduce_scatter x2 -> x0, waiting for transfers between devices: 92.1 us -> none  [per_device(): lax.psum_scatter(jnp.dot(filtered, probe_half, preferred_element_type=jnp...]
    all_gather x2 -> x0, waiting for transfers between devices: 63.2 us -> none  [per_device(): scaled = lax.all_gather(scaled_share, 'pix', axis=0, tiled=True)]
    ppermute x0 -> x38, starting transfers between devices: none -> 39.6 us  [xor_swap(): return lax.ppermute(value, axis, [(i, i ^ mask) for i in range(size)])]
  transfers between devices with their start and end apart: 8 -> 38, of which waited for: 8 -> 23; matrix products, arithmetic and copies ran while one was open for 0% -> 0% of each run, Pallas kernels for 0% -> 24%
where the time goes in v1:
time: 339 us; the launch traced here: 338 us
  Pallas kernels  144 us (42%)
  waiting for transfers between devices  135 us (40%)
  starting transfers between devices  39.6 us (12%)
  local copies, waits for them, and re-layouts  9.85 us (3%)
  other arithmetic  5.96 us (2%)
    ppermute x38, waiting for transfers between devices, xor_swap(): return lax.ppermute(value, axis, [(i, i ^ mask) for i in range(size)])  135 us
    pallas_call x2, Pallas kernels, cholesky_and_inverse(): pl.pallas_call(cholesky_kernel, out_shape=[jax.ShapeDtypeStruct((size, si...  55 us
    ppermute x38, starting transfers between devices, xor_swap(): return lax.ppermute(value, axis, [(i, i ^ mask) for i in range(size)])  39.6 us
    pallas_call x4, Pallas kernels, filter_and_score(): pl.pallas_call(filter_kernel, grid_spec=pltpu.PrefetchScalarGridSpec(num_...  33.8 us
    pallas_call x2, Pallas kernels, last_sum(): pl.pallas_call(functools.partial(last_sum_kernel, len(filtered), half), g...  18.8 us
    pallas_call x2, Pallas kernels, first_sum(): pl.pallas_call(functools.partial(first_sum_kernel, len(filtered)), grid_s...  18.3 us
    pallas_call x4, Pallas kernels, score(): pl.pallas_call(score_kernel, grid_spec=pltpu.PrefetchScalarGridSpec(num_s...  10.6 us
    unnamed x28, local copies, waits for them, and re-layouts  7.66 us
  transfers between devices with their start and end apart: 38, of which 23 were waited for; matrix products, arithmetic and copies ran while one was open for 0% of the time, Pallas kernels for 24%

profile of v1, /device:TPU:0, one launch (start us, length us, event | category | flops | bytes accessed | tf_op | source)
XLA Modules:
  0.0 337.9 jit_solution(12377445223066775685)
XLA Ops:
  2.1 3.7 %convert_element_type.117.probe_ref = bf16[4096,256]{1,0:T(8,128)(2,1)} convert(f32[4096,256]{1,0:T(8,128)} %param.9) | non-fusion elementwise | flops 1048576 | bytes 6291456 | tf_op jit(solution)/shard_map/convert_element_type | solution.py:341
  5.8 8.4 %filter_and_score.7 = (bf16[800,4096]{1,0:T(8,128)(2,1)}, bf16[800,256]{1,0:T(8,128)(2,1)}) custom-call(s32[1]{0:T(128)} %bitcast.3.order, s32[8,1,400]{2,1,0:T(1,128)} %reshape.9.class_ref, bf16[3200,4096]{1,0:T(8,128)(2,1)} %image_ref.7, bf16[64,4096]{1,0:T(8,128)(2,1)} %table_ref.7, bf16[4096,256]{1,0:T(8,128)(2,1)} %convert_element_type.117.probe_ref), custom_call_target="tpu_custom_call" | custom-call | flops 3355443200 | bytes 13107200 | tf_op jit(solution)/shard_map/filter_and_score/pallas_call | solution.py:57
  14.2 3.0 collective-permute-start.2
  17.1 8.5 %filter_and_score.5 = (bf16[800,4096]{1,0:T(8,128)(2,1)}, bf16[800,256]{1,0:T(8,128)(2,1)}) custom-call(s32[1]{0:T(128)} %bitcast.1.order, s32[8,1,400]{2,1,0:T(1,128)} %reshape.9.class_ref, bf16[3200,4096]{1,0:T(8,128)(2,1)} %image_ref.7, bf16[64,4096]{1,0:T(8,128)(2,1)} %table_ref.7, bf16[4096,256]{1,0:T(8,128)(2,1)} %convert_element_type.117.probe_ref), custom_call_target="tpu_custom_call" | custom-call | flops 3355443200 | bytes 13107200 | tf_op jit(solution)/shard_map/filter_and_score/pallas_call | solution.py:57
  27.1 8.4 %filter_and_score.4 = (bf16[800,4096]{1,0:T(8,128)(2,1)}, bf16[800,256]{1,0:T(8,128)(2,1)}) custom-call(s32[1]{0:T(128)} %bitcast.order, s32[8,1,400]{2,1,0:T(1,128)} %reshape.9.class_ref, bf16[3200,4096]{1,0:T(8,128)(2,1)} %image_ref.7, bf16[64,4096]{1,0:T(8,128)(2,1)} %table_ref.7, bf16[4096,256]{1,0:T(8,128)(2,1)} %convert_element_type.117.probe_ref), custom_call_target="tpu_custom_call" | custom-call | flops 3355443200 | bytes 13107200 | tf_op jit(solution)/shard_map/filter_and_score/pallas_call | solution.py:57
  36.3 8.5 %filter_and_score.6 = (bf16[800,4096]{1,0:T(8,128)(2,1)}, f32[800,256]{1,0:T(8,128)}) custom-call(s32[1]{0:T(128)} %bitcast.2.order, s32[8,1,400]{2,1,0:T(1,128)} %reshape.9.class_ref, bf16[3200,4096]{1,0:T(8,128)(2,1)} %image_ref.7, bf16[64,4096]{1,0:T(8,128)(2,1)} %table_ref.7, bf16[4096,256]{1,0:T(8,128)(2,1)} %convert_element_type.117.probe_ref), custom_call_target="tpu_custom_call" | custom-call | flops 3355443200 | bytes 13107200 | tf_op jit(solution)/shard_map/filter_and_score/pallas_call | solution.py:57
  51.4 8.8 %collective-permute-done.5.refs_3_ = bf16[800,256]{1,0:T(8,128)(2,1)S(1)} collective-permute-done((bf16[800,256]{1,0:T(8,128)(2,1)S(1)}, bf16[800,256]{1,0:T(8,128)(2,1)S(1)}, u32[]{:S(2)}, u32[]{:S(2)}) %collective-permute-start.5) | collective-permute-done | bytes 409632 | tf_op jit(solution)/shard_map/ppermute | solution.py:32
  61.0 2.9 copy-done.1
  64.8 9.2 %first_sum.2.refs_4_ = f32[4096,256]{1,0:T(8,128)S(1)} custom-call(s32[8]{0:T(128)S(1)} %multiply_add_fusion.order, bf16[800,4096]{1,0:T(8,128)(2,1)S(1)} %copy-done.1, bf16[800,4096]{1,0:T(8,128)(2,1)} %get-tuple-element.24.refs_1_.filtered_ref, bf16[800,256]{1,0:T(8,128)(2,1)S(1)} %multiply_convert_fusion.refs_2_, bf16[800,256]{1,0:T(8,128)(2,1)S(1)} %copy-done.3), custom_call_target="tpu_custom_call" | custom-call | flops 3355443200 | bytes 17301504 | tf_op jit(solution)/shard_map/first_sum/pallas_call | solution.py:160
  74.0 3.0 copy-done
  77.0 9.5 %last_sum.2 = (bf16[2048,256]{1,0:T(8,128)(2,1)S(1)}, bf16[2048,256]{1,0:T(8,128)(2,1)S(1)}) custom-call(s32[8]{0:T(128)S(1)} %multiply_add_fusion.order, bf16[800,4096]{1,0:T(8,128)(2,1)S(1)} %copy-done, bf16[800,4096]{1,0:T(8,128)(2,1)} %get-tuple-element.18.refs_1_.filtered_ref, bf16[800,256]{1,0:T(8,128)(2,1)S(1)} %collective-permute-done.3.refs_2_, ...), custom_call_target="tpu_custom_call" | custom-call | flops 3355443200 | bytes 19398656 | tf_op jit(solution)/shard_map/last_sum/pallas_call | solution.py:184
  89.4 3.7 %collective-permute-start.7 = (bf16[512,256]{1,0:T(8,128)(2,1)S(1)}, bf16[512,256]{1,0:T(8,128)(2,1)S(1)}, u32[]{:S(2)}, u32[]{:S(2)}) collective-permute-start(bf16[512,256]{1,0:T(8,128)(2,1)S(1)} %get-tuple-element.35), channel_id=1, source_target_pairs={{0,24},{4,28},{8,16},{12,20},{16,8},{20,12},{24,0},{28,4},{1,25},{... | collective-permute-start | bytes 786440 | tf_op jit(solution)/shard_map/ppermute | solution.py:32
  93.9 6.7 %collective-permute-done.7 = bf16[512,256]{1,0:T(8,128)(2,1)S(1)} collective-permute-done((bf16[512,256]{1,0:T(8,128)(2,1)S(1)}, bf16[512,256]{1,0:T(8,128)(2,1)S(1)}, u32[]{:S(2)}, u32[]{:S(2)}) %collective-permute-start.7) | collective-permute-done | bytes 262176 | tf_op jit(solution)/shard_map/ppermute | solution.py:32
  100.6 5.9 %collective-permute-done.9 = bf16[512,256]{1,0:T(8,128)(2,1)S(1)} collective-permute-done((bf16[512,256]{1,0:T(8,128)(2,1)S(1)}, bf16[512,256]{1,0:T(8,128)(2,1)S(1)}, u32[]{:S(2)}, u32[]{:S(2)}) %collective-permute-start.9) | collective-permute-done | bytes 262176 | tf_op jit(solution)/shard_map/ppermute | solution.py:32
  106.5 9.2 %collective-permute-done.8 = bf16[512,256]{1,0:T(8,128)(2,1)S(1)} collective-permute-done((bf16[512,256]{1,0:T(8,128)(2,1)S(1)}, bf16[512,256]{1,0:T(8,128)(2,1)S(1)}, u32[]{:S(2)}, u32[]{:S(2)}) %collective-permute-start.8) | collective-permute-done | bytes 262176 | tf_op jit(solution)/shard_map/ppermute | solution.py:32
  120.4 6.7 %collective-permute-done.12.refs_3_ = bf16[512,256]{1,0:T(8,128)(2,1)S(1)} collective-permute-done((bf16[512,256]{1,0:T(8,128)(2,1)S(1)}, bf16[512,256]{1,0:T(8,128)(2,1)S(1)}, u32[]{:S(2)}, u32[]{:S(2)}) %collective-permute-start.12) | collective-permute-done | bytes 262176 | tf_op jit(solution)/shard_map/ppermute | solution.py:32
  127.0 12.4 %collective-permute-done.11.refs_2_ = bf16[512,256]{1,0:T(8,128)(2,1)S(1)} collective-permute-done((bf16[512,256]{1,0:T(8,128)(2,1)S(1)}, bf16[512,256]{1,0:T(8,128)(2,1)S(1)}, u32[]{:S(2)}, u32[]{:S(2)}) %collective-permute-start.11) | collective-permute-done | bytes 262176 | tf_op jit(solution)/shard_map/ppermute | solution.py:32
  158.8 15.8 %collective-permute-done.21 = f32[256,256]{1,0:T(8,128)S(1)} collective-permute-done((f32[256,256]{1,0:T(8,128)S(1)}, f32[256,256]{1,0:T(8,128)S(1)}, u32[]{:S(2)}, u32[]{:S(2)}) %collective-permute-start.21) | collective-permute-done | bytes 262176 | tf_op jit(solution)/shard_map/ppermute | solution.py:32
  174.7 27.5 %cholesky.2 = (f32[256,256]{1,0:T(8,128)}, f32[256,256]{1,0:T(8,128)S(1)}) custom-call(f32[256,256]{1,0:T(8,128)S(1)} %add.114.gram_ref), custom_call_target="tpu_custom_call" | custom-call | flops 12000000000 | bytes 786432 | tf_op jit(solution)/shard_map/cholesky/pallas_call | solution.py:274
  207.9 8.8 %collective-permute-done.24.refs_3_ = bf16[800,256]{1,0:T(8,128)(2,1)S(1)} collective-permute-done((bf16[800,256]{1,0:T(8,128)(2,1)S(1)}, bf16[800,256]{1,0:T(8,128)(2,1)S(1)}, u32[]{:S(2)}, u32[]{:S(2)}) %collective-permute-start.24) | collective-permute-done | bytes 409632 | tf_op jit(solution)/shard_map/ppermute | solution.py:32
  216.7 9.2 %first_sum.3.refs_4_ = f32[4096,256]{1,0:T(8,128)S(1)} custom-call(s32[8]{0:T(128)S(1)} %multiply_add_fusion.order, bf16[800,4096]{1,0:T(8,128)(2,1)S(1)} %bitcast.14, bf16[800,4096]{1,0:T(8,128)(2,1)} %get-tuple-element.24.refs_1_.filtered_ref, bf16[800,256]{1,0:T(8,128)(2,1)S(1)} %fusion.refs_2_, bf16[800,256]{1,0:T(8,128)(2,1)S(1)} %collective-permute-done.24.refs_3_), custom_call_target="tpu_custom_call" | custom-call | flops 3355443200 | bytes 17301504 | tf_op jit(solution)/shard_map/first_sum/pallas_call | solution.py:160
  226.0 9.3 %last_sum.3 = (bf16[2048,256]{1,0:T(8,128)(2,1)S(1)}, bf16[2048,256]{1,0:T(8,128)(2,1)S(1)}) custom-call(s32[8]{0:T(128)S(1)} %multiply_add_fusion.order, bf16[800,4096]{1,0:T(8,128)(2,1)S(1)} %bitcast.10, bf16[800,4096]{1,0:T(8,128)(2,1)} %get-tuple-element.18.refs_1_.filtered_ref, bf16[800,256]{1,0:T(8,128)(2,1)S(1)} %collective-permute-done.22.refs_2_, ...), custom_call_target="tpu_custom_call" | custom-call | flops 3355443200 | bytes 19398656 | tf_op jit(solution)/shard_map/last_sum/pallas_call | solution.py:184
  239.6 3.0 collective-permute-start.27
  242.6 6.6 %collective-permute-done.26 = bf16[512,256]{1,0:T(8,128)(2,1)S(1)} collective-permute-done((bf16[512,256]{1,0:T(8,128)(2,1)S(1)}, bf16[512,256]{1,0:T(8,128)(2,1)S(1)}, u32[]{:S(2)}, u32[]{:S(2)}) %collective-permute-start.26) | collective-permute-done | bytes 262176 | tf_op jit(solution)/shard_map/ppermute | solution.py:32
  249.3 8.0 %collective-permute-done.28 = bf16[512,256]{1,0:T(8,128)(2,1)S(1)} collective-permute-done((bf16[512,256]{1,0:T(8,128)(2,1)S(1)}, bf16[512,256]{1,0:T(8,128)(2,1)S(1)}, u32[]{:S(2)}, u32[]{:S(2)}) %collective-permute-start.28) | collective-permute-done | bytes 262176 | tf_op jit(solution)/shard_map/ppermute | solution.py:32
  257.3 4.2 %collective-permute-done.27 = bf16[512,256]{1,0:T(8,128)(2,1)S(1)} collective-permute-done((bf16[512,256]{1,0:T(8,128)(2,1)S(1)}, bf16[512,256]{1,0:T(8,128)(2,1)S(1)}, u32[]{:S(2)}, u32[]{:S(2)}) %collective-permute-start.27) | collective-permute-done | bytes 262176 | tf_op jit(solution)/shard_map/ppermute | solution.py:32
  266.1 6.7 %collective-permute-done.31.refs_3_ = bf16[512,256]{1,0:T(8,128)(2,1)S(1)} collective-permute-done((bf16[512,256]{1,0:T(8,128)(2,1)S(1)}, bf16[512,256]{1,0:T(8,128)(2,1)S(1)}, u32[]{:S(2)}, u32[]{:S(2)}) %collective-permute-start.31) | collective-permute-done | bytes 262176 | tf_op jit(solution)/shard_map/ppermute | solution.py:32
  272.8 12.4 %collective-permute-done.30.refs_2_ = bf16[512,256]{1,0:T(8,128)(2,1)S(1)} collective-permute-done((bf16[512,256]{1,0:T(8,128)(2,1)S(1)}, bf16[512,256]{1,0:T(8,128)(2,1)S(1)}, u32[]{:S(2)}, u32[]{:S(2)}) %collective-permute-start.30) | collective-permute-done | bytes 262176 | tf_op jit(solution)/shard_map/ppermute | solution.py:32
  289.3 6.9 %collective-permute-done.36 = f32[256,256]{1,0:T(8,128)S(1)} collective-permute-done((f32[256,256]{1,0:T(8,128)S(1)}, f32[256,256]{1,0:T(8,128)S(1)}, u32[]{:S(2)}, u32[]{:S(2)}) %collective-permute-start.36) | collective-permute-done | bytes 262176 | tf_op jit(solution)/shard_map/ppermute | solution.py:32
  297.9 6.0 %collective-permute-done.37 = f32[256,256]{1,0:T(8,128)S(1)} collective-permute-done((f32[256,256]{1,0:T(8,128)S(1)}, f32[256,256]{1,0:T(8,128)S(1)}, u32[]{:S(2)}, u32[]{:S(2)}) %collective-permute-start.37) | collective-permute-done | bytes 262176 | tf_op jit(solution)/shard_map/ppermute | solution.py:32
  303.9 27.5 %cholesky.3 = (f32[256,256]{1,0:T(8,128)}, f32[256,256]{1,0:T(8,128)S(1)}) custom-call(f32[256,256]{1,0:T(8,128)S(1)} %add.123.gram_ref), custom_call_target="tpu_custom_call" | custom-call | flops 12000000000 | bytes 786432 | tf_op jit(solution)/shard_map/cholesky/pallas_call | solution.py:274
  331.4 6.5 %apply.1 = f32[4096,256]{1,0:T(8,128)} custom-call(s32[8]{0:T(128)S(1)} %multiply_add_fusion.1.order, f32[256,256]{1,0:T(8,128)S(1)} %get-tuple-element.30.inverse_ref, bf16[512,256]{1,0:T(8,128)(2,1)S(1)} %add_convert_fusion.refs_0_, bf16[512,256]{1,0:T(8,128)(2,1)S(1)} %collective-permute-done.29.refs_1_, ...), custom_call_target="tpu_custom_call" | custom-call | flops 1610612736 | bytes 6291456 | tf_op jit(solution)/shard_map/apply/pallas_call | solution.py:307
  (109 shorter events, 60.2 us)
Async XLA Ops:
  14.2 30.7 %collective-permute-start.2 = (bf16[800,256]{1,0:T(8,128)(2,1)}, bf16[800,256]{1,0:T(8,128)(2,1)S(1)}, u32[]{:S(2)}, u32[]{:S(2)}) collective-permute-start(bf16[800,256]{1,0:T(8,128)(2,1)} %get-tuple-element.23), channel_id=1, source_target_pairs={{0,1},{1,0},{2,3},{3,2},{4,5},{5,4},{6,7},{7,6},{8,9},{9,8},{10,11... | collective-permute-start | bytes 1228808 | tf_op jit(solution)/shard_map/ppermute | solution.py:32
  25.6 19.2 %collective-permute-start = (bf16[800,256]{1,0:T(8,128)(2,1)}, bf16[800,256]{1,0:T(8,128)(2,1)S(1)}, u32[]{:S(2)}, u32[]{:S(2)}) collective-permute-start(bf16[800,256]{1,0:T(8,128)(2,1)} %get-tuple-element.21), channel_id=1, source_target_pairs={{0,3},{1,2},{2,1},{3,0},{4,7},{5,6},{6,5},{7,4},{8,11},{9,10},{10,... | collective-permute-start | bytes 1228808 | tf_op jit(solution)/shard_map/ppermute | solution.py:32
  35.5 11.0 %collective-permute-start.1 = (bf16[800,256]{1,0:T(8,128)(2,1)}, bf16[800,256]{1,0:T(8,128)(2,1)S(1)}, u32[]{:S(2)}, u32[]{:S(2)}) collective-permute-start(bf16[800,256]{1,0:T(8,128)(2,1)} %get-tuple-element.22), channel_id=1, source_target_pairs={{0,2},{1,3},{2,0},{3,1},{4,6},{5,7},{6,4},{7,5},{8,10},{9,11},{10,... | collective-permute-start | bytes 1228808 | tf_op jit(solution)/shard_map/ppermute | solution.py:32
  47.8 12.4 %collective-permute-start.5 = (bf16[800,256]{1,0:T(8,128)(2,1)S(1)}, bf16[800,256]{1,0:T(8,128)(2,1)S(1)}, u32[]{:S(2)}, u32[]{:S(2)}) collective-permute-start(bf16[800,256]{1,0:T(8,128)(2,1)S(1)} %multiply_convert_fusion.refs_2_), channel_id=1, source_target_pairs={{0,1},{1,0},{2,3},{3,2},{4,5},{5,4},{6,7},{7,6},{8,9},{9,8},{10,11... | collective-permute-start | bytes 1228808 | tf_op jit(solution)/shard_map/ppermute | solution.py:32
  49.3 24.7 %collective-permute-start.4 = (bf16[800,256]{1,0:T(8,128)(2,1)S(1)}, bf16[800,256]{1,0:T(8,128)(2,1)S(1)}, u32[]{:S(2)}, u32[]{:S(2)}) collective-permute-start(bf16[800,256]{1,0:T(8,128)(2,1)S(1)} %multiply_convert_fusion.refs_2_), channel_id=1, source_target_pairs={{0,3},{1,2},{2,1},{3,0},{4,7},{5,6},{6,5},{7,4},{8,11},{9,10},{10,... | collective-permute-start | bytes 1228808 | tf_op jit(solution)/shard_map/ppermute | solution.py:32
  50.8 23.2 %collective-permute-start.3 = (bf16[800,256]{1,0:T(8,128)(2,1)S(1)}, bf16[800,256]{1,0:T(8,128)(2,1)S(1)}, u32[]{:S(2)}, u32[]{:S(2)}) collective-permute-start(bf16[800,256]{1,0:T(8,128)(2,1)S(1)} %multiply_convert_fusion.refs_2_), channel_id=1, source_target_pairs={{0,2},{1,3},{2,0},{3,1},{4,6},{5,7},{6,4},{7,5},{8,10},{9,11},{10,... | collective-permute-start | bytes 1228808 | tf_op jit(solution)/shard_map/ppermute | solution.py:32
  89.4 11.1 %collective-permute-start.7 = (bf16[512,256]{1,0:T(8,128)(2,1)S(1)}, bf16[512,256]{1,0:T(8,128)(2,1)S(1)}, u32[]{:S(2)}, u32[]{:S(2)}) collective-permute-start(bf16[512,256]{1,0:T(8,128)(2,1)S(1)} %get-tuple-element.35), channel_id=1, source_target_pairs={{0,24},{4,28},{8,16},{12,20},{16,8},{20,12},{24,0},{28,4},{1,25},{... | collective-permute-start | bytes 786440 | tf_op jit(solution)/shard_map/ppermute | solution.py:32
  93.1 13.4 %collective-permute-start.9 = (bf16[512,256]{1,0:T(8,128)(2,1)S(1)}, bf16[512,256]{1,0:T(8,128)(2,1)S(1)}, u32[]{:S(2)}, u32[]{:S(2)}) collective-permute-start(bf16[512,256]{1,0:T(8,128)(2,1)S(1)} %get-tuple-element.36), channel_id=1, source_target_pairs={{0,8},{4,12},{8,0},{12,4},{16,24},{20,28},{24,16},{28,20},{1,9},{5... | collective-permute-start | bytes 786440 | tf_op jit(solution)/shard_map/ppermute | solution.py:32
  93.1 22.6 %collective-permute-start.8 = (bf16[512,256]{1,0:T(8,128)(2,1)S(1)}, bf16[512,256]{1,0:T(8,128)(2,1)S(1)}, u32[]{:S(2)}, u32[]{:S(2)}) collective-permute-start(bf16[512,256]{1,0:T(8,128)(2,1)S(1)} %get-tuple-element.37), channel_id=1, source_target_pairs={{0,16},{4,20},{8,24},{12,28},{16,0},{20,4},{24,8},{28,12},{1,17},{... | collective-permute-start | bytes 786440 | tf_op jit(solution)/shard_map/ppermute | solution.py:32
  115.9 11.1 %collective-permute-start.12 = (bf16[512,256]{1,0:T(8,128)(2,1)S(1)}, bf16[512,256]{1,0:T(8,128)(2,1)S(1)}, u32[]{:S(2)}, u32[]{:S(2)}) collective-permute-start(bf16[512,256]{1,0:T(8,128)(2,1)S(1)} %add_convert_fusion.4.refs_0_), channel_id=1, source_target_pairs={{0,24},{4,28},{8,16},{12,20},{16,8},{20,12},{24,0},{28,4},{1,25},{... | collective-permute-start | bytes 786440 | tf_op jit(solution)/shard_map/ppermute | solution.py:32
  118.4 21.0 %collective-permute-start.11 = (bf16[512,256]{1,0:T(8,128)(2,1)S(1)}, bf16[512,256]{1,0:T(8,128)(2,1)S(1)}, u32[]{:S(2)}, u32[]{:S(2)}) collective-permute-start(bf16[512,256]{1,0:T(8,128)(2,1)S(1)} %add_convert_fusion.4.refs_0_), channel_id=1, source_target_pairs={{0,16},{4,20},{8,24},{12,28},{16,0},{20,4},{24,8},{28,12},{1,17},{... | collective-permute-start | bytes 786440 | tf_op jit(solution)/shard_map/ppermute | solution.py:32
  118.4 21.0 %collective-permute-start.10 = (bf16[512,256]{1,0:T(8,128)(2,1)S(1)}, bf16[512,256]{1,0:T(8,128)(2,1)S(1)}, u32[]{:S(2)}, u32[]{:S(2)}) collective-permute-start(bf16[512,256]{1,0:T(8,128)(2,1)S(1)} %add_convert_fusion.4.refs_0_), channel_id=1, source_target_pairs={{0,8},{4,12},{8,0},{12,4},{16,24},{20,28},{24,16},{28,20},{1,9},{5... | collective-permute-start | bytes 786440 | tf_op jit(solution)/shard_map/ppermute | solution.py:32
  120.4 19.6 %collective-permute-start.13 = (bf16[512,256]{1,0:T(8,128)(2,1)S(1)}, bf16[512,256]{1,0:T(8,128)(2,1)S(1)}, u32[]{:S(2)}, u32[]{:S(2)}) collective-permute-start(bf16[512,256]{1,0:T(8,128)(2,1)S(1)} %add_convert_fusion.4.refs_0_), channel_id=1, source_target_pairs={{0,4},{4,0},{8,12},{12,8},{16,20},{20,16},{24,28},{28,24},{1,5},{5... | collective-permute-start | bytes 786440 | tf_op jit(solution)/shard_map/ppermute | solution.py:32
  127.0 12.9 %collective-permute-start.16 = (bf16[512,256]{1,0:T(8,128)(2,1)S(1)}, bf16[512,256]{1,0:T(8,128)(2,1)S(1)}, u32[]{:S(2)}, u32[]{:S(2)}) collective-permute-start(bf16[512,256]{1,0:T(8,128)(2,1)S(1)} %collective-permute-done.12.refs_3_), channel_id=1, source_target_pairs={{0,4},{4,0},{8,12},{12,8},{16,20},{20,16},{24,28},{28,24},{1,5},{5... | collective-permute-start | bytes 786440 | tf_op jit(solution)/shard_map/ppermute | solution.py:32
  142.1 9.2 %collective-permute-start.20 = (f32[256,256]{1,0:T(8,128)S(1)}, f32[256,256]{1,0:T(8,128)S(1)}, u32[]{:S(2)}, u32[]{:S(2)}) collective-permute-start(f32[256,256]{1,0:T(8,128)S(1)} %gram.2), channel_id=1, source_target_pairs={{0,1},{1,0},{2,3},{3,2},{4,5},{5,4},{6,7},{7,6},{8,9},{9,8},{10,11... | collective-permute-start | bytes 786440 | tf_op jit(solution)/shard_map/ppermute | solution.py:32
  146.4 55.8 %collective-permute-start.17 = (bf16[800,256]{1,0:T(8,128)(2,1)S(1)}, bf16[800,256]{1,0:T(8,128)(2,1)S(1)}, u32[]{:S(2)}, u32[]{:S(2)}) collective-permute-start(bf16[800,256]{1,0:T(8,128)(2,1)S(1)} %score.5), channel_id=1, source_target_pairs={{0,3},{1,2},{2,1},{3,0},{4,7},{5,6},{6,5},{7,4},{8,11},{9,10},{10,... | collective-permute-start | bytes 1228808 | tf_op jit(solution)/shard_map/ppermute | solution.py:32
  150.6 51.6 %collective-permute-start.18 = (bf16[800,256]{1,0:T(8,128)(2,1)S(1)}, bf16[800,256]{1,0:T(8,128)(2,1)}, u32[]{:S(2)}, u32[]{:S(2)}) collective-permute-start(bf16[800,256]{1,0:T(8,128)(2,1)S(1)} %score.6), channel_id=1, source_target_pairs={{0,2},{1,3},{2,0},{3,1},{4,6},{5,7},{6,4},{7,5},{8,10},{9,11},{10,... | collective-permute-start | bytes 1228808 | tf_op jit(solution)/shard_map/ppermute | solution.py:32
  151.4 23.3 %collective-permute-start.21 = (f32[256,256]{1,0:T(8,128)S(1)}, f32[256,256]{1,0:T(8,128)S(1)}, u32[]{:S(2)}, u32[]{:S(2)}) collective-permute-start(f32[256,256]{1,0:T(8,128)S(1)} %add.113), channel_id=1, source_target_pairs={{0,2},{1,3},{2,0},{3,1},{4,6},{5,7},{6,4},{7,5},{8,10},{9,11},{10,... | collective-permute-start | bytes 786440 | tf_op jit(solution)/shard_map/ppermute | solution.py:32
  155.6 46.6 %collective-permute-start.19 = (bf16[800,256]{1,0:T(8,128)(2,1)S(1)}, bf16[800,256]{1,0:T(8,128)(2,1)S(1)}, u32[]{:S(2)}, u32[]{:S(2)}) collective-permute-start(bf16[800,256]{1,0:T(8,128)(2,1)S(1)} %score.7), channel_id=1, source_target_pairs={{0,1},{1,0},{2,3},{3,2},{4,5},{5,4},{6,7},{7,6},{8,9},{9,8},{10,11... | collective-permute-start | bytes 1228808 | tf_op jit(solution)/shard_map/ppermute | solution.py:32
  204.3 12.4 %collective-permute-start.24 = (bf16[800,256]{1,0:T(8,128)(2,1)S(1)}, bf16[800,256]{1,0:T(8,128)(2,1)S(1)}, u32[]{:S(2)}, u32[]{:S(2)}) collective-permute-start(bf16[800,256]{1,0:T(8,128)(2,1)S(1)} %fusion.refs_2_), channel_id=1, source_target_pairs={{0,1},{1,0},{2,3},{3,2},{4,5},{5,4},{6,7},{7,6},{8,9},{9,8},{10,11... | collective-permute-start | bytes 1228808 | tf_op jit(solution)/shard_map/ppermute | solution.py:32
  204.9 21.0 %collective-permute-start.23 = (bf16[800,256]{1,0:T(8,128)(2,1)S(1)}, bf16[800,256]{1,0:T(8,128)(2,1)S(1)}, u32[]{:S(2)}, u32[]{:S(2)}) collective-permute-start(bf16[800,256]{1,0:T(8,128)(2,1)S(1)} %fusion.refs_2_), channel_id=1, source_target_pairs={{0,3},{1,2},{2,1},{3,0},{4,7},{5,6},{6,5},{7,4},{8,11},{9,10},{10,... | collective-permute-start | bytes 1228808 | tf_op jit(solution)/shard_map/ppermute | solution.py:32
  206.3 19.6 %collective-permute-start.22 = (bf16[800,256]{1,0:T(8,128)(2,1)S(1)}, bf16[800,256]{1,0:T(8,128)(2,1)S(1)}, u32[]{:S(2)}, u32[]{:S(2)}) collective-permute-start(bf16[800,256]{1,0:T(8,128)(2,1)S(1)} %fusion.refs_2_), channel_id=1, source_target_pairs={{0,2},{1,3},{2,0},{3,1},{4,6},{5,7},{6,4},{7,5},{8,10},{9,11},{10,... | collective-permute-start | bytes 1228808 | tf_op jit(solution)/shard_map/ppermute | solution.py:32
  238.2 11.1 %collective-permute-start.26 = (bf16[512,256]{1,0:T(8,128)(2,1)S(1)}, bf16[512,256]{1,0:T(8,128)(2,1)S(1)}, u32[]{:S(2)}, u32[]{:S(2)}) collective-permute-start(bf16[512,256]{1,0:T(8,128)(2,1)S(1)} %get-tuple-element.32), channel_id=1, source_target_pairs={{0,24},{4,28},{8,16},{12,20},{16,8},{20,12},{24,0},{28,4},{1,25},{... | collective-permute-start | bytes 786440 | tf_op jit(solution)/shard_map/ppermute | solution.py:32
  239.6 17.6 %collective-permute-start.28 = (bf16[512,256]{1,0:T(8,128)(2,1)S(1)}, bf16[512,256]{1,0:T(8,128)(2,1)S(1)}, u32[]{:S(2)}, u32[]{:S(2)}) collective-permute-start(bf16[512,256]{1,0:T(8,128)(2,1)S(1)} %get-tuple-element.33), channel_id=1, source_target_pairs={{0,8},{4,12},{8,0},{12,4},{16,24},{20,28},{24,16},{28,20},{1,9},{5... | collective-permute-start | bytes 786440 | tf_op jit(solution)/shard_map/ppermute | solution.py:32
  239.6 21.8 %collective-permute-start.27 = (bf16[512,256]{1,0:T(8,128)(2,1)S(1)}, bf16[512,256]{1,0:T(8,128)(2,1)S(1)}, u32[]{:S(2)}, u32[]{:S(2)}) collective-permute-start(bf16[512,256]{1,0:T(8,128)(2,1)S(1)} %get-tuple-element.34), channel_id=1, source_target_pairs={{0,16},{4,20},{8,24},{12,28},{16,0},{20,4},{24,8},{28,12},{1,17},{... | collective-permute-start | bytes 786440 | tf_op jit(solution)/shard_map/ppermute | solution.py:32
  261.6 11.1 %collective-permute-start.31 = (bf16[512,256]{1,0:T(8,128)(2,1)S(1)}, bf16[512,256]{1,0:T(8,128)(2,1)S(1)}, u32[]{:S(2)}, u32[]{:S(2)}) collective-permute-start(bf16[512,256]{1,0:T(8,128)(2,1)S(1)} %add_convert_fusion.refs_0_), channel_id=1, source_target_pairs={{0,24},{4,28},{8,16},{12,20},{16,8},{20,12},{24,0},{28,4},{1,25},{... | collective-permute-start | bytes 786440 | tf_op jit(solution)/shard_map/ppermute | solution.py:32
  264.2 21.0 %collective-permute-start.30 = (bf16[512,256]{1,0:T(8,128)(2,1)S(1)}, bf16[512,256]{1,0:T(8,128)(2,1)S(1)}, u32[]{:S(2)}, u32[]{:S(2)}) collective-permute-start(bf16[512,256]{1,0:T(8,128)(2,1)S(1)} %add_convert_fusion.refs_0_), channel_id=1, source_target_pairs={{0,16},{4,20},{8,24},{12,28},{16,0},{20,4},{24,8},{28,12},{1,17},{... | collective-permute-start | bytes 786440 | tf_op jit(solution)/shard_map/ppermute | solution.py:32
  264.2 21.0 %collective-permute-start.29 = (bf16[512,256]{1,0:T(8,128)(2,1)S(1)}, bf16[512,256]{1,0:T(8,128)(2,1)S(1)}, u32[]{:S(2)}, u32[]{:S(2)}) collective-permute-start(bf16[512,256]{1,0:T(8,128)(2,1)S(1)} %add_convert_fusion.refs_0_), channel_id=1, source_target_pairs={{0,8},{4,12},{8,0},{12,4},{16,24},{20,28},{24,16},{28,20},{1,9},{5... | collective-permute-start | bytes 786440 | tf_op jit(solution)/shard_map/ppermute | solution.py:32
  266.1 19.6 %collective-permute-start.32 = (bf16[512,256]{1,0:T(8,128)(2,1)S(1)}, bf16[512,256]{1,0:T(8,128)(2,1)S(1)}, u32[]{:S(2)}, u32[]{:S(2)}) collective-permute-start(bf16[512,256]{1,0:T(8,128)(2,1)S(1)} %add_convert_fusion.refs_0_), channel_id=1, source_target_pairs={{0,4},{4,0},{8,12},{12,8},{16,20},{20,16},{24,28},{28,24},{1,5},{5... | collective-permute-start | bytes 786440 | tf_op jit(solution)/shard_map/ppermute | solution.py:32
  272.8 12.9 %collective-permute-start.35 = (bf16[512,256]{1,0:T(8,128)(2,1)S(1)}, bf16[512,256]{1,0:T(8,128)(2,1)S(1)}, u32[]{:S(2)}, u32[]{:S(2)}) collective-permute-start(bf16[512,256]{1,0:T(8,128)(2,1)S(1)} %collective-permute-done.31.refs_3_), channel_id=1, source_target_pairs={{0,4},{4,0},{8,12},{12,8},{16,20},{20,16},{24,28},{28,24},{1,5},{5... | collective-permute-start | bytes 786440 | tf_op jit(solution)/shard_map/ppermute | solution.py:32
  287.8 8.4 %collective-permute-start.36 = (f32[256,256]{1,0:T(8,128)S(1)}, f32[256,256]{1,0:T(8,128)S(1)}, u32[]{:S(2)}, u32[]{:S(2)}) collective-permute-start(f32[256,256]{1,0:T(8,128)S(1)} %gram.3), channel_id=1, source_target_pairs={{0,1},{1,0},{2,3},{3,2},{4,5},{5,4},{6,7},{7,6},{8,9},{9,8},{10,11... | collective-permute-start | bytes 786440 | tf_op jit(solution)/shard_map/ppermute | solution.py:32
  296.3 7.6 %collective-permute-start.37 = (f32[256,256]{1,0:T(8,128)S(1)}, f32[256,256]{1,0:T(8,128)S(1)}, u32[]{:S(2)}, u32[]{:S(2)}) collective-permute-start(f32[256,256]{1,0:T(8,128)S(1)} %add.122), channel_id=1, source_target_pairs={{0,2},{1,3},{2,0},{3,1},{4,6},{5,7},{6,4},{7,5},{8,10},{9,11},{10,... | collective-permute-start | bytes 786440 | tf_op jit(solution)/shard_map/ppermute | solution.py:32
  (20 other events, 315.2 us)

commit v2 on v0

v2 whole, which is shorter than its diff:
```python
import functools

import jax
import jax.numpy as jnp
from jax import lax
from jax.experimental import pallas as pl
from jax.experimental.pallas import tpu as pltpu
from jax.sharding import PartitionSpec as P

ITERS = 2
F32 = jnp.float32
BF16 = jnp.bfloat16
LANES = 128
PANEL = 32
GROUP = 8
HIGHEST = lax.Precision.HIGHEST


def cost(flops, nbytes):
    return pl.CostEstimate(flops=int(flops), bytes_accessed=int(nbytes), transcendentals=0)


def vmem(nbytes):
    return pltpu.CompilerParams(vmem_limit_bytes=nbytes)


def row_tile(rows, most=400):
    return max(t for t in range(16, most + 1, 16) if rows % t == 0)


def xor_swap(value, axis, mask):
    size = lax.axis_size(axis)
    return lax.ppermute(value, axis, [(i, i ^ mask) for i in range(size)])


def contract_rows(left, right):
    return lax.dot_general(left, right, (((0,), (0,)), ((), ())), preferred_element_type=F32)


def in_vmem():
    return pl.BlockSpec(memory_space=pltpu.VMEM)


def filter_kernel(places, class_ref, image_ref, table_ref, probe_ref, filtered_ref, score_ref):
    table_rows = table_ref.shape[0]
    rows, pixels = image_ref.shape
    onehot = (
        lax.broadcasted_iota(jnp.int32, (table_rows, rows), 0) == class_ref[0]
    ).astype(BF16)
    here = pl.ds(pl.multiple_of(pl.program_id(0) * rows, rows), rows)
    scores = None
    width = min(pixels, 8 * LANES)
    for at in range(0, pixels, width):
        columns = slice(at, min(at + width, pixels))
        filters = contract_rows(onehot, table_ref[:, columns])
        filtered = (image_ref[:, columns].astype(F32) * filters).astype(BF16)
        filtered_ref[here, columns] = filtered
        term = jnp.dot(filtered, probe_ref[columns, :], preferred_element_type=F32)
        scores = term if scores is None else scores + term
    score_ref[here, :] = scores.astype(score_ref.dtype)


def filter_and_score(places, shift, images, classes, table, probe_half, chunk, out_type):
    rows, pixels = images.shape
    columns = probe_half.shape[1]
    tile = row_tile(chunk)
    steps = chunk // tile
    return pl.pallas_call(
        filter_kernel,
        grid_spec=pltpu.PrefetchScalarGridSpec(
            num_scalar_prefetch=1,
            grid=(steps,),
            in_specs=[
                pl.BlockSpec((1, 1, tile), lambda i, places: (places[shift] * steps + i, 0, 0)),
                pl.BlockSpec((tile, pixels), lambda i, places: (places[shift] * steps + i, 0)),
                in_vmem(),
                in_vmem(),
            ],
            out_specs=[in_vmem(), in_vmem()],
        ),
        out_shape=[
            pltpu.VMEM((chunk, pixels), BF16),
            jax.ShapeDtypeStruct((chunk, columns), out_type),
        ],
        compiler_params=vmem(14 * 2**20),
        cost_estimate=cost(4 * chunk * pixels * columns, 2 * chunk * pixels),
        name="filter_and_score",
    )(places, classes.reshape(rows // tile, 1, tile), images, table, probe_half)


def prefetched(count, outs):
    return pltpu.PrefetchScalarGridSpec(
        num_scalar_prefetch=1,
        grid=(),
        in_specs=[in_vmem()] * count,
        out_specs=[in_vmem()] * outs,
    )


def score_kernel(first, places, filtered_ref, *refs):
    *basis_refs, score_ref = refs
    width = basis_refs[0].shape[0]
    total = None
    for at, basis_ref in enumerate(basis_refs):
        columns = pl.ds(pl.multiple_of(places[first + at] * width, width), width)
        term = jnp.dot(filtered_ref[:, columns], basis_ref[...], preferred_element_type=F32)
        total = term if total is None else total + term
    score_ref[...] = total.astype(score_ref.dtype)


def score(places, first, filtered, basis, out_type):
    rows, pixels = filtered.shape
    columns = basis[0].shape[1]
    return pl.pallas_call(
        functools.partial(score_kernel, first),
        grid_spec=prefetched(1 + len(basis), 1),
        out_shape=[jax.ShapeDtypeStruct((rows, columns), out_type)],
        compiler_params=vmem(16 * 2**20),
        cost_estimate=cost(2 * rows * pixels * columns, 2 * rows * columns),
        name="score",
    )(places, filtered, *basis)[0]


def sum_blocks(filtered, scaled):
    rows = filtered[0].shape[0]
    whole = rows // 256 * 256
    total = None
    for left, right in zip(filtered, scaled):
        if whole:
            term = contract_rows(left[:whole, :], right[:whole, :])
            total = term if total is None else total + term
    if whole < rows:
        left = jnp.concatenate([block[whole:, :] for block in filtered], 0)
        right = jnp.concatenate([block[whole:, :] for block in scaled], 0)
        term = contract_rows(left, right)
        total = term if total is None else total + term
    return total


def image_sum_kernel(count, first, places, *refs):
    filtered_refs, scaled_refs = refs[:count], refs[count : 2 * count]
    send_ref, keep_ref = refs[-2:]
    width = send_ref.shape[0]

    def block(at, carry):
        columns = pl.ds(pl.multiple_of(places[first + at] * width, width), width)
        total = sum_blocks(
            [ref[:, columns] for ref in filtered_refs], [ref[...] for ref in scaled_refs]
        )

        @pl.when(at == 0)
        def _():
            send_ref[...] = total.astype(send_ref.dtype)

        @pl.when(at == 1)
        def _():
            keep_ref[...] = total

        return carry

    lax.fori_loop(0, 2, block, 0)


def image_sum(places, first, filtered, scaled, width, after):
    count = len(filtered)
    rows = filtered[0].shape[0]
    columns = scaled[0].shape[1]
    return pl.pallas_call(
        functools.partial(image_sum_kernel, count, first),
        grid_spec=prefetched(2 * count + len(after), 2),
        out_shape=[
            jax.ShapeDtypeStruct((width, columns), BF16),
            jax.ShapeDtypeStruct((width, columns), F32),
        ],
        compiler_params=vmem(16 * 2**20),
        cost_estimate=cost(4 * count * rows * width * columns, 6 * width * columns),
        name="image_sum",
    )(places, *filtered, *scaled, *after)


def tree_sum(terms):
    while len(terms) > 1:
        terms = [terms[i] + terms[i + 1] for i in range(0, len(terms), 2)]
    return terms[0]


def gram_kernel(core_at, places, *refs):
    *basis_refs, _, half_ref, gram_ref = refs
    gram_ref[...] = tree_sum([contract_rows(ref[...], ref[...]) for ref in basis_refs])
    rows = half_ref.shape[0]
    half_ref[...] = gram_ref[pl.ds(pl.multiple_of(places[core_at] * rows, rows), rows), :]


def half_gram(places, core_at, basis, after):
    rows, columns = basis[0].shape
    return pl.pallas_call(
        functools.partial(gram_kernel, core_at),
        grid_spec=pltpu.PrefetchScalarGridSpec(
            num_scalar_prefetch=1,
            grid=(),
            in_specs=[in_vmem()] * (len(basis) + 1),
            out_specs=[in_vmem()],
            scratch_shapes=[pltpu.VMEM((columns, columns), F32)],
        ),
        out_shape=[jax.ShapeDtypeStruct((columns // 2, columns), F32)],
        compiler_params=vmem(12 * 2**20),
        cost_estimate=cost(2 * len(basis) * rows * columns * columns, 2 * len(basis) * rows * columns),
        name="gram",
    )(places, *basis, after)[0]


def normalize_kernel(core_at, scale, places, *refs):
    *part_refs, inverse_ref, half_ref, send_ref, keep_ref, gram_ref = refs
    total = part_refs[0][...]
    for ref in part_refs[1:]:
        total = total + ref[...].astype(F32)
    block = lax.dot_general(
        total,
        inverse_ref[...] * scale,
        (((1,), (1,)), ((), ())),
        precision=HIGHEST,
        preferred_element_type=F32,
    ).astype(BF16)
    half_ref[...] = block
    gram_ref[...] = contract_rows(block, block)
    rows = send_ref.shape[0]
    here = places[core_at]
    send_ref[...] = gram_ref[pl.ds(pl.multiple_of((1 - here) * rows, rows), rows), :]
    keep_ref[...] = gram_ref[pl.ds(pl.multiple_of(here * rows, rows), rows), :]


def normalize_and_gram(places, core_at, parts, inverse, scale):
    rows, columns = parts[0].shape
    return pl.pallas_call(
        functools.partial(normalize_kernel, core_at, scale),
        grid_spec=pltpu.PrefetchScalarGridSpec(
            num_scalar_prefetch=1,
            grid=(),
            in_specs=[in_vmem()] * (len(parts) + 1),
            out_specs=[in_vmem()] * 3,
            scratch_shapes=[pltpu.VMEM((columns, columns), F32)],
        ),
        out_shape=[
            jax.ShapeDtypeStruct((rows, columns), BF16),
            jax.ShapeDtypeStruct((columns // 2, columns), F32),
            jax.ShapeDtypeStruct((columns // 2, columns), F32),
        ],
        compiler_params=vmem(12 * 2**20),
        cost_estimate=cost(14 * rows * columns * columns, 8 * rows * columns),
        name="normalize",
    )(places, *parts, inverse)


def scatter_kernel(first, places, keep_ref, got_ref, *piece_refs):
    rows = piece_refs[0].shape[0]
    for at, ref in enumerate(piece_refs):
        here = pl.ds(pl.multiple_of(places[first + at] * rows, rows), rows)
        ref[...] = keep_ref[here, :] + got_ref[here, :]


def scatter_rows(places, first, keep, got, count):
    rows, columns = keep.shape
    return pl.pallas_call(
        functools.partial(scatter_kernel, first),
        grid_spec=prefetched(2, count),
        out_shape=[jax.ShapeDtypeStruct((rows // count, columns), F32)] * count,
        compiler_params=vmem(4 * 2**20),
        cost_estimate=cost(rows * columns, 12 * rows * columns),
        name="scatter",
    )(places, keep, got)


def gather_kernel(first, count, places, *refs):
    piece_refs, (block_ref, out_ref, block_out_ref) = refs[:count], refs[count:]
    rows = piece_refs[0].shape[0]
    for at, ref in enumerate(piece_refs):
        out_ref[pl.ds(pl.multiple_of(places[first + at] * rows, rows), rows), :] = ref[...]
    block_out_ref[...] = block_ref[...]


def gather_rows(places, first, pieces, block):
    count = len(pieces)
    rows, columns = pieces[0].shape
    return pl.pallas_call(
        functools.partial(gather_kernel, first, count),
        grid_spec=prefetched(count + 1, 2),
        out_shape=[
            jax.ShapeDtypeStruct((rows * count, columns), F32),
            jax.ShapeDtypeStruct(block.shape, block.dtype),
        ],
        compiler_params=vmem(4 * 2**20),
        cost_estimate=cost(rows * columns, 8 * count * rows * columns),
        name="gather",
    )(places, *pieces, block)


def square_places(size):
    return tuple(lax.broadcasted_iota(jnp.int32, (size, size), axis) for axis in (0, 1))


def split_in_three(value):
    parts = []
    for _ in range(3):
        parts.append(value.astype(BF16))
        value = value - parts[-1].astype(F32)
    return parts


def contract_rows_fully(left, right):
    l0, l1, l2 = split_in_three(left)
    r0, r1, r2 = split_in_three(right)
    return contract_rows(
        jnp.concatenate([l2, l1, l0, l1, l0, l0], 0), jnp.concatenate([r0, r1, r2, r0, r1, r0], 0)
    )


def eliminate(work_ref, first, last):
    size = work_ref.shape[0]
    panel_row = lax.broadcasted_iota(jnp.int32, (PANEL, LANES), 0)
    panel_column = lax.broadcasted_iota(jnp.int32, (PANEL, LANES), 1)
    per_tile = LANES // PANEL

    def panel(block, carry):
        start = pl.multiple_of(block * PANEL, PANEL)
        tile = pl.multiple_of((block // per_tile) * LANES, LANES)
        diagonal = work_ref[pl.ds(start, PANEL), pl.ds(tile, LANES)]
        diagonal = pltpu.roll(diagonal, (LANES - (block % per_tile) * PANEL) % LANES, 1)
        tiles = [diagonal] + [
            work_ref[pl.ds(start, PANEL), at : at + LANES] for at in range(0, 2 * size, LANES)
        ]
        for top in range(0, PANEL, GROUP):
            tiles = eliminate_group(tiles, panel_row, top)
        pivots = jnp.sum(jnp.where(panel_row == panel_column, tiles[0], 0.0), axis=1, keepdims=True)
        body = jnp.concatenate(tiles[1:], 1) * lax.rsqrt(pivots)
        work_ref[pl.ds(start, PANEL), :] = body
        left = body[:, :size]
        later = lax.broadcasted_iota(jnp.int32, left.shape, 1) >= start + PANEL
        work_ref[...] -= contract_rows_fully(jnp.where(later, left, 0.0), body)
        return carry

    lax.fori_loop(first, last, panel, 0)


def eliminate_group(tiles, panel_row, top):
    shape = panel_row.shape
    columns = [
        jnp.broadcast_to(tiles[0][:, top + k : top + k + 1], shape) for k in range(GROUP)
    ]
    block = [[columns[k][top + i : top + i + 1, :] for k in range(i + 1)] for i in range(GROUP)]
    ratio = [[None] * GROUP for _ in range(GROUP)]
    scales = []
    for k in range(GROUP):
        inverse = 1.0 / block[k][k]
        for i in range(k + 1, GROUP):
            ratio[i][k] = block[i][k] * inverse
        for i in range(k + 1, GROUP):
            for m in range(k + 1, i + 1):
                block[i][m] = block[i][m] - ratio[i][k] * block[m][k]
        scales.append(jnp.where(panel_row > top + k, columns[k] * inverse, 0.0))
        for m in range(k + 1, GROUP):
            columns[m] = columns[m] - scales[k] * block[m][k]
    result = []
    for tile in tiles:
        rows = [tile[top + k : top + k + 1, :] for k in range(GROUP)]
        for k in range(GROUP):
            for m in range(k + 1, GROUP):
                rows[m] = rows[m] - ratio[m][k] * rows[k]
        for k in range(GROUP):
            tile = tile - scales[k] * rows[k]
        result.append(tile)
    return result


def cholesky_kernel(first, last, place_at, places, *refs):
    size = refs[-1].shape[0]
    panels = size // PANEL
    row_at, column_at = square_places(size)
    if first == 0:
        *piece_refs, = refs[: -1 if last < panels else -3]
        work_ref = refs[-1]
        rows = piece_refs[0].shape[0]
        for at, ref in enumerate(piece_refs):
            here = pl.ds(pl.multiple_of(places[place_at + at] * rows, rows), rows)
            work_ref[here, :size] = ref[...]
        work_ref[:, size:] = (row_at == column_at).astype(F32)
    else:
        work_ref = refs[-1]
        work_ref[...] = refs[0][...]
    eliminate(work_ref, first, last)
    if last == panels:
        factor_ref, inverse_ref = refs[-3:-1]
        factor_ref[...] = jnp.where(row_at <= column_at, work_ref[:, :size], 0.0).T
        inverse_ref[...] = work_ref[:, size:]


def cholesky_and_inverse(places, place_at, pieces, calls):
    size = pieces[0].shape[1]
    panels = size // PANEL
    state = pieces
    for call in range(calls):
        first, last = panels * call // calls, panels * (call + 1) // calls
        work = jax.ShapeDtypeStruct((size, 2 * size), F32)
        square = jax.ShapeDtypeStruct((size, size), F32)
        final = last == panels
        state = pl.pallas_call(
            functools.partial(cholesky_kernel, first, last, place_at),
            grid_spec=pltpu.PrefetchScalarGridSpec(
                num_scalar_prefetch=1,
                grid=(),
                in_specs=[in_vmem()] * len(state),
                out_specs=[in_vmem()] * (2 if final else 1),
                scratch_shapes=[pltpu.VMEM(work.shape, F32)] if final else [],
            ),
            out_shape=[square, square] if final else [work],
            compiler_params=vmem(12 * 2**20),
            cost_estimate=cost(6e9 // calls, 12 * size * size),
            name="cholesky",
        )(places, *state)
    return state


def apply_kernel(places, inverse_ref, *refs):
    *basis_refs, out_ref = refs
    parts = split_in_three(inverse_ref[...])
    for at, basis_ref in enumerate(basis_refs):

        @pl.when(pl.program_id(0) == at)
        def _():
            block = basis_ref[...]
            out_ref[...] = sum(
                lax.dot_general(
                    block, part, (((1,), (1,)), ((), ())), preferred_element_type=F32
                )
                for part in reversed(parts)
            )


def apply_inverse(places, first, inverse, basis):
    rows, columns = basis[0].shape
    blocks = len(basis)
    return pl.pallas_call(
        apply_kernel,
        grid_spec=pltpu.PrefetchScalarGridSpec(
            num_scalar_prefetch=1,
            grid=(blocks,),
            in_specs=[in_vmem()] * (1 + blocks),
            out_specs=pl.BlockSpec((rows, columns), lambda i, places: (places[first + i], 0)),
        ),
        out_shape=jax.ShapeDtypeStruct((rows * blocks, columns), F32),
        compiler_params=vmem(16 * 2**20),
        cost_estimate=cost(6 * rows * blocks * columns * columns, 6 * rows * blocks * columns),
        name="apply",
    )(places, inverse, *basis)


RANGE = 2.0**40


def place_table(me, core, level, pix, depth):
    img = 2 * depth
    rows, gathered = 0, pix
    pairs = gathered + img
    cores = pairs + img
    levels = cores + 2
    at = jnp.arange(levels + depth, dtype=jnp.int32)
    block = at - gathered
    pair = at - pairs
    table = jnp.where(at < gathered, me ^ at, (core ^ (block // depth)) * depth + (level ^ (block % depth)))
    table = jnp.where(at < pairs, table, (core ^ 1 ^ (pair % 2)) * depth + (level ^ (pair // 2)))
    table = jnp.where(at < cores, table, core ^ (at - cores))
    table = jnp.where(at < levels, table, level ^ (at - levels))
    return table, rows, gathered, pairs, cores, levels


def per_device(images, classes, ctf_table, weights, probes):
    images_here, pixels = images.shape
    pix, img = lax.axis_size("pix"), lax.axis_size("img")
    depth = img // 2
    chunk = images_here // pix
    width = pixels // img
    me = lax.axis_index("pix")
    place = lax.axis_index("img")
    places, rows_at, gathered_at, pairs_at, cores_at, levels_at = place_table(
        me, place & 1, place >> 1, pix, depth
    )
    weight_share = lax.dynamic_slice_in_dim(weights, me * chunk, chunk, 0)
    places = places + (weight_share[0] > 2.0).astype(jnp.int32)
    weight_share = weight_share[:, None]

    shifts = list(range(pix - 1, -1, -1))
    filtered, own, arrived = [None] * pix, None, []
    probe_half = probes.astype(BF16)
    images = pltpu.with_memory_space_constraint(images, pltpu.HBM)
    for shift in shifts:
        filtered[shift], part = filter_and_score(
            places,
            rows_at + shift,
            images,
            classes,
            ctf_table,
            probe_half,
            chunk,
            BF16 if shift else F32,
        )
        if shift:
            arrived.append(xor_swap(part, "pix", shift))
        else:
            own = part

    basis = inverse = None
    for sweep in range(ITERS):
        shares = own
        for part in arrived:
            shares = shares + part.astype(F32)
        share_weights = weight_share if sweep == 0 else weight_share * RANGE
        scaled_share = (share_weights * shares).astype(BF16)
        scaled = [scaled_share] + [xor_swap(scaled_share, "pix", s) for s in range(1, pix)]

        parts, after = [None] * depth, []
        for s in range(depth - 1, -1, -1):
            send, keep = image_sum(
                places, pairs_at + 2 * s, filtered, scaled, width, after[-2:-1]
            )
            both = keep + xor_swap(send, "img", 1).astype(F32)
            if s:
                both = both.astype(BF16)
                parts[s] = xor_swap(both, "img", 2 * s)
            else:
                parts[s] = both
            after.append(both)

        if sweep == ITERS - 1:
            half = half_gram(places, cores_at, basis, scaled[-1])
            step = 1
            while step < pix:
                half = half + xor_swap(half, "pix", step)
                step *= 2
            _, inverse = cholesky_and_inverse(
                places, cores_at, [half, xor_swap(half, "img", 1)], 2
            )
            break
        total = parts[0]
        for part in parts[1:]:
            total = total + part.astype(F32)
        half = total.astype(BF16)
        near = [half] + [xor_swap(half, "img", 2 * s) for s in range(1, depth)]
        basis = near + [xor_swap(block, "img", 1) for block in near]

        own, arrived = None, []
        for shift in shifts:
            part = score(places, gathered_at, filtered[shift], basis, BF16 if shift else F32)
            if shift:
                arrived.append(xor_swap(part, "pix", shift))
            else:
                own = part

    half, send, keep = normalize_and_gram(places, cores_at, parts, inverse, 1.0 / RANGE)
    pieces = scatter_rows(places, levels_at, keep, xor_swap(send, "img", 1), depth)
    mine = tree_sum([pieces[0]] + [xor_swap(pieces[s], "img", 2 * s) for s in range(1, depth)])
    mine = tree_sum([mine] + [xor_swap(mine, "pix", s) for s in range(1, pix)])
    pieces = [mine] + [xor_swap(mine, "img", 2 * s) for s in range(1, depth)]
    gram, half = gather_rows(places, levels_at, pieces, half)
    near = [half] + [xor_swap(half, "img", 2 * s) for s in range(1, depth)]
    basis = near + [xor_swap(block, "img", 1) for block in near]
    factor, inverse = cholesky_and_inverse(places, cores_at, [gram, xor_swap(gram, "img", 1)], 1)
    return apply_inverse(places, gathered_at, inverse, basis), factor


def plain_per_device(images, classes, ctf_table, weights, probes):
    onehot = (classes[:, None] == jnp.arange(ctf_table.shape[0])[None, :]).astype(BF16)
    filters = jnp.dot(onehot, ctf_table, preferred_element_type=F32)
    filtered = (images.astype(F32) * filters).astype(BF16)
    current = probes
    factor = None
    for sweep in range(ITERS):
        share_rows = filtered.shape[0] // lax.axis_size("pix")
        shares = lax.psum_scatter(
            jnp.dot(filtered, current.astype(BF16), preferred_element_type=F32),
            "pix",
            scatter_dimension=0,
            tiled=True,
        )
        weight_share = lax.dynamic_slice_in_dim(
            weights, lax.axis_index("pix") * share_rows, share_rows, 0
        )
        scaled_share = (weight_share[:, None] * shares).astype(BF16)
        scaled = lax.all_gather(scaled_share, "pix", axis=0, tiled=True)
        image_sum = lax.psum(contract_rows(filtered, scaled), "img")
        gram = lax.psum(jnp.dot(image_sum.T, image_sum, precision=HIGHEST), "pix")
        factor = jnp.linalg.cholesky(gram)
        current = jax.scipy.linalg.solve_triangular(factor, image_sum.T, lower=True).T
    return current, factor


def power_of_two(n):
    return n > 1 and n & (n - 1) == 0


def per_device_of(images, classes, ctf_table, weights, probes):
    rows, pixels = images.shape
    pix, img = lax.axis_size("pix"), lax.axis_size("img")
    columns = probes.shape[1]
    fits = (
        power_of_two(pix)
        and power_of_two(img)
        and rows % (16 * pix) == 0
        and pixels % (LANES * img) == 0
        and columns % LANES == 0
        and columns % (8 * img) == 0
    )
    run = per_device if fits else plain_per_device
    return run(images, classes, ctf_table, weights, probes)


def solution(mesh):
    in_specs = (P("img", "pix"), P("img"), P(None, "pix"), P("img"), P("pix", None))
    out_specs = (P("pix", None), P())
    return jax.shard_map(
        per_device_of, mesh=mesh, in_specs=in_specs, out_specs=out_specs, check_vma=False
    )
```

time: 716 us -> 273 us (0.38); the launches traced: 707 us -> 273 us
  waiting for transfers between devices: 434 us -> 115 us
  matrix products: 120 us -> 0 us
  other arithmetic: 117 us -> 4.32 us
  Pallas kernels: 0 us -> 98.7 us
  starting transfers between devices: 1.35 us -> 51.1 us
  local copies, waits for them, and re-layouts: 17.5 us -> 1.33 us
  between operations: 17.2 us -> 1.71 us
    psum x4 -> x0, waiting for transfers between devices: 279 us -> none  [the longest x2 193 us: per_device(): image_sum = lax.psum(partial_sum, 'img')]
    ppermute x0 -> x54, waiting for transfers between devices: none -> 115 us  [xor_swap(): return lax.ppermute(value, axis, [(i, i ^ mask) for i in range(size)])]
    another operation x18 -> x0, other arithmetic: 109 us -> none  [the longest x13 68.7 us: per_device(): factor = jnp.linalg.cholesky(gram_matrix)]
    dot_general x7 -> x0, matrix products: 101 us -> none  [the longest x2 28.8 us: per_device(): lax.dot_general(filtered, scaled, (((0,), (0,)), ((), ())), preferred_ele...]
    pallas_call x0 -> x24, Pallas kernels: none -> 98.7 us  [the longest x4 29.7 us: filter_and_score(): pl.pallas_call(filter_kernel, grid_spec=pltpu.PrefetchScalarGridSpec(num_...]
    reduce_scatter x2 -> x0, waiting for transfers between devices: 92.1 us -> none  [per_device(): lax.psum_scatter(jnp.dot(filtered, probe_half, preferred_element_type=jnp...]
    all_gather x2 -> x0, waiting for transfers between devices: 63.2 us -> none  [per_device(): scaled = lax.all_gather(scaled_share, 'pix', axis=0, tiled=True)]
    ppermute x0 -> x54, starting transfers between devices: none -> 51.1 us  [xor_swap(): return lax.ppermute(value, axis, [(i, i ^ mask) for i in range(size)])]
  transfers between devices with their start and end apart: 8 -> 54, of which waited for: 8 -> 26; matrix products, arithmetic and copies ran while one was open for 0% -> 0% of each run, Pallas kernels for 0% -> 27%
where the time goes in v2:
time: 273 us
  waiting for transfers between devices  115 us (42%)
  Pallas kernels  98.7 us (36%)
  starting transfers between devices  51.1 us (19%)
  other arithmetic  4.32 us (2%)
    ppermute x54, waiting for transfers between devices, xor_swap(): return lax.ppermute(value, axis, [(i, i ^ mask) for i in range(size)])  115 us
    ppermute x54, starting transfers between devices, xor_swap(): return lax.ppermute(value, axis, [(i, i ^ mask) for i in range(size)])  51.1 us
    pallas_call x4, Pallas kernels, filter_and_score(): pl.pallas_call(filter_kernel, grid_spec=pltpu.PrefetchScalarGridSpec(num_...  29.7 us
    pallas_call x3, Pallas kernels, cholesky_and_inverse(): pl.pallas_call(functools.partial(cholesky_kernel, first, last, place_at),...  25 us
    pallas_call x8, Pallas kernels, image_sum(): pl.pallas_call(functools.partial(image_sum_kernel, count, first), grid_sp...  24 us
    pallas_call x4, Pallas kernels, score(): pl.pallas_call(functools.partial(score_kernel, first), grid_spec=prefetch...  9.6 us
    pallas_call x1, Pallas kernels, apply_inverse(): pl.pallas_call(apply_kernel, grid_spec=pltpu.PrefetchScalarGridSpec(num_s...  6.55 us
  transfers between devices with their start and end apart: 54, of which 26 were waited for; matrix products, arithmetic and copies ran while one was open for 0% of the time, Pallas kernels for 27%

profile of v2, /device:TPU:0, one launch (start us, length us, event | category | flops | bytes accessed | tf_op | source)
XLA Modules:
  0.0 272.6 jit_solution(9271444180696164953)
XLA Ops:
  5.9 7.4 %filter_and_score.7 = (bf16[800,4096]{1,0:T(8,128)(2,1)S(1)}, bf16[800,256]{1,0:T(8,128)(2,1)S(1)}) custom-call(s32[26]{0:T(128)S(1)} %fusion.places, s32[8,1,400]{2,1,0:T(1,128)S(1)} %reshape.17.class_ref, bf16[3200,4096]{1,0:T(8,128)(2,1)} %image_ref.7, bf16[64,4096]{1,0:T(8,128)(2,1)S(1)} %copy-done, bf16[4096,256]{1,0:T(8,128)(2,1)S(1)} %convert_element_type.89.probe_ref), custom_call_target="tpu_custom_call" | custom-call | flops 3355443200 | bytes 6553600 | tf_op jit(solution)/shard_map/filter_and_score/pallas_call | solution.py:68
  13.3 4.0 %collective-permute-start = (bf16[800,256]{1,0:T(8,128)(2,1)S(1)}, bf16[800,256]{1,0:T(8,128)(2,1)S(1)}, u32[]{:S(2)}, u32[]{:S(2)}) collective-permute-start(bf16[800,256]{1,0:T(8,128)(2,1)S(1)} %get-tuple-element.43), channel_id=1, source_target_pairs={{0,3},{1,2},{2,1},{3,0},{4,7},{5,6},{6,5},{7,4},{8,11},{9,10},{10,... | collective-permute-start | bytes 1228808 | tf_op jit(solution)/shard_map/ppermute | solution.py:33
  17.3 7.4 %filter_and_score.6 = (bf16[800,4096]{1,0:T(8,128)(2,1)S(1)}, bf16[800,256]{1,0:T(8,128)(2,1)S(1)}) custom-call(s32[26]{0:T(128)S(1)} %fusion.places, s32[8,1,400]{2,1,0:T(1,128)S(1)} %reshape.17.class_ref, bf16[3200,4096]{1,0:T(8,128)(2,1)} %image_ref.7, bf16[64,4096]{1,0:T(8,128)(2,1)S(1)} %copy-done, bf16[4096,256]{1,0:T(8,128)(2,1)S(1)} %convert_element_type.89.probe_ref), custom_call_target="tpu_custom_call" | custom-call | flops 3355443200 | bytes 6553600 | tf_op jit(solution)/shard_map/filter_and_score/pallas_call | solution.py:68
  25.3 7.4 %filter_and_score.5 = (bf16[800,4096]{1,0:T(8,128)(2,1)S(1)}, bf16[800,256]{1,0:T(8,128)(2,1)S(1)}) custom-call(s32[26]{0:T(128)S(1)} %fusion.places, s32[8,1,400]{2,1,0:T(1,128)S(1)} %reshape.17.class_ref, bf16[3200,4096]{1,0:T(8,128)(2,1)} %image_ref.7, bf16[64,4096]{1,0:T(8,128)(2,1)S(1)} %copy-done, bf16[4096,256]{1,0:T(8,128)(2,1)S(1)} %convert_element_type.89.probe_ref), custom_call_target="tpu_custom_call" | custom-call | flops 3355443200 | bytes 6553600 | tf_op jit(solution)/shard_map/filter_and_score/pallas_call | solution.py:68
  32.9 7.4 %filter_and_score.4 = (bf16[800,4096]{1,0:T(8,128)(2,1)S(1)}, f32[800,256]{1,0:T(8,128)S(1)}) custom-call(s32[26]{0:T(128)S(1)} %fusion.places, s32[8,1,400]{2,1,0:T(1,128)S(1)} %reshape.17.class_ref, bf16[3200,4096]{1,0:T(8,128)(2,1)} %image_ref.7, bf16[64,4096]{1,0:T(8,128)(2,1)S(1)} %copy-done, bf16[4096,256]{1,0:T(8,128)(2,1)S(1)} %convert_element_type.89.probe_ref), custom_call_target="tpu_custom_call" | custom-call | flops 3355443200 | bytes 6553600 | tf_op jit(solution)/shard_map/filter_and_score/pallas_call | solution.py:68
  40.4 3.1 %collective-permute-done.2 = bf16[800,256]{1,0:T(8,128)(2,1)S(1)} collective-permute-done((bf16[800,256]{1,0:T(8,128)(2,1)S(1)}, bf16[800,256]{1,0:T(8,128)(2,1)S(1)}, u32[]{:S(2)}, u32[]{:S(2)}) %collective-permute-start.2) | collective-permute-done | bytes 409632 | tf_op jit(solution)/shard_map/ppermute | solution.py:33
  47.3 9.7 %collective-permute-done.5.refs_7_ = bf16[800,256]{1,0:T(8,128)(2,1)S(1)} collective-permute-done((bf16[800,256]{1,0:T(8,128)(2,1)S(1)}, bf16[800,256]{1,0:T(8,128)(2,1)S(1)}, u32[]{:S(2)}, u32[]{:S(2)}) %collective-permute-start.5) | collective-permute-done | bytes 409632 | tf_op jit(solution)/shard_map/ppermute | solution.py:33
  57.0 6.2 %collective-permute-done.4.refs_6_ = bf16[800,256]{1,0:T(8,128)(2,1)S(1)} collective-permute-done((bf16[800,256]{1,0:T(8,128)(2,1)S(1)}, bf16[800,256]{1,0:T(8,128)(2,1)S(1)}, u32[]{:S(2)}, u32[]{:S(2)}) %collective-permute-start.4) | collective-permute-done | bytes 409632 | tf_op jit(solution)/shard_map/ppermute | solution.py:33
  63.3 3.0 %image_sum.10 = (bf16[512,256]{1,0:T(8,128)(2,1)S(1)}, f32[512,256]{1,0:T(8,128)S(1)}) custom-call(s32[26]{0:T(128)S(1)} %fusion.places, bf16[800,4096]{1,0:T(8,128)(2,1)S(1)} %get-tuple-element.38.refs_0_.filtered_ref, bf16[800,4096]{1,0:T(8,128)(2,1)S(1)} %get-tuple-element.39.refs_1_.filtered_ref, ...), custom_call_target="tpu_custom_call" | custom-call | flops 1677721600 | bytes 786432 | tf_op jit(solution)/shard_map/image_sum/pallas_call | solution.py:168
  66.4 2.9 %image_sum.8 = (bf16[512,256]{1,0:T(8,128)(2,1)S(1)}, f32[512,256]{1,0:T(8,128)S(1)}) custom-call(s32[26]{0:T(128)S(1)} %fusion.places, bf16[800,4096]{1,0:T(8,128)(2,1)S(1)} %get-tuple-element.38.refs_0_.filtered_ref, bf16[800,4096]{1,0:T(8,128)(2,1)S(1)} %get-tuple-element.39.refs_1_.filtered_ref, ...), custom_call_target="tpu_custom_call" | custom-call | flops 1677721600 | bytes 786432 | tf_op jit(solution)/shard_map/image_sum/pallas_call | solution.py:168
  70.0 3.7 %collective-permute-start.12 = (bf16[512,256]{1,0:T(8,128)(2,1)S(1)}, bf16[512,256]{1,0:T(8,128)(2,1)S(1)}, u32[]{:S(2)}, u32[]{:S(2)}) collective-permute-start(bf16[512,256]{1,0:T(8,128)(2,1)S(1)} %add_convert_fusion.5.refs_8_), channel_id=1, source_target_pairs={{0,24},{4,28},{8,16},{12,20},{16,8},{20,12},{24,0},{28,4},{1,25},{... | collective-permute-start | bytes 786440 | tf_op jit(solution)/shard_map/ppermute | solution.py:33
  73.6 3.2 %image_sum.11 = (bf16[512,256]{1,0:T(8,128)(2,1)S(1)}, f32[512,256]{1,0:T(8,128)S(1)}) custom-call(s32[26]{0:T(128)S(1)} %fusion.places, bf16[800,4096]{1,0:T(8,128)(2,1)S(1)} %get-tuple-element.38.refs_0_.filtered_ref, bf16[800,4096]{1,0:T(8,128)(2,1)S(1)} %get-tuple-element.39.refs_1_.filtered_ref, ...), custom_call_target="tpu_custom_call" | custom-call | flops 1677721600 | bytes 786432 | tf_op jit(solution)/shard_map/image_sum/pallas_call | solution.py:168
  77.0 2.9 %image_sum.9 = (bf16[512,256]{1,0:T(8,128)(2,1)S(1)}, f32[512,256]{1,0:T(8,128)S(1)}) custom-call(s32[26]{0:T(128)S(1)} %fusion.places, bf16[800,4096]{1,0:T(8,128)(2,1)S(1)} %get-tuple-element.38.refs_0_.filtered_ref, bf16[800,4096]{1,0:T(8,128)(2,1)S(1)} %get-tuple-element.39.refs_1_.filtered_ref, ...), custom_call_target="tpu_custom_call" | custom-call | flops 1677721600 | bytes 786432 | tf_op jit(solution)/shard_map/image_sum/pallas_call | solution.py:168
  81.7 14.5 %collective-permute-done.11 = bf16[512,256]{1,0:T(8,128)(2,1)S(1)} collective-permute-done((bf16[512,256]{1,0:T(8,128)(2,1)S(1)}, bf16[512,256]{1,0:T(8,128)(2,1)S(1)}, u32[]{:S(2)}, u32[]{:S(2)}) %collective-permute-start.11) | collective-permute-done | bytes 262176 | tf_op jit(solution)/shard_map/ppermute | solution.py:33
  100.8 6.7 %collective-permute-done.15.refs_3_ = bf16[512,256]{1,0:T(8,128)(2,1)S(1)} collective-permute-done((bf16[512,256]{1,0:T(8,128)(2,1)S(1)}, bf16[512,256]{1,0:T(8,128)(2,1)S(1)}, u32[]{:S(2)}, u32[]{:S(2)}) %collective-permute-start.15) | collective-permute-done | bytes 262176 | tf_op jit(solution)/shard_map/ppermute | solution.py:33
  107.4 12.2 %collective-permute-done.14.refs_2_ = bf16[512,256]{1,0:T(8,128)(2,1)S(1)} collective-permute-done((bf16[512,256]{1,0:T(8,128)(2,1)S(1)}, bf16[512,256]{1,0:T(8,128)(2,1)S(1)}, u32[]{:S(2)}, u32[]{:S(2)}) %collective-permute-start.14) | collective-permute-done | bytes 262176 | tf_op jit(solution)/shard_map/ppermute | solution.py:33
  137.3 7.9 %collective-permute-done.21 = bf16[800,256]{1,0:T(8,128)(2,1)S(1)} collective-permute-done((bf16[800,256]{1,0:T(8,128)(2,1)S(1)}, bf16[800,256]{1,0:T(8,128)(2,1)S(1)}, u32[]{:S(2)}, u32[]{:S(2)}) %collective-permute-start.21) | collective-permute-done | bytes 409632 | tf_op jit(solution)/shard_map/ppermute | solution.py:33
  149.0 9.8 %collective-permute-done.25.refs_7_.refs_8_ = bf16[800,256]{1,0:T(8,128)(2,1)S(1)} collective-permute-done((bf16[800,256]{1,0:T(8,128)(2,1)S(1)}, bf16[800,256]{1,0:T(8,128)(2,1)S(1)}, u32[]{:S(2)}, u32[]{:S(2)}) %collective-permute-start.25) | collective-permute-done | bytes 409632 | tf_op jit(solution)/shard_map/ppermute | solution.py:33
  158.8 7.8 %collective-permute-done.24.refs_6_ = bf16[800,256]{1,0:T(8,128)(2,1)S(1)} collective-permute-done((bf16[800,256]{1,0:T(8,128)(2,1)S(1)}, bf16[800,256]{1,0:T(8,128)(2,1)S(1)}, u32[]{:S(2)}, u32[]{:S(2)}) %collective-permute-start.24) | collective-permute-done | bytes 409632 | tf_op jit(solution)/shard_map/ppermute | solution.py:33
  166.6 3.0 %image_sum.14 = (bf16[512,256]{1,0:T(8,128)(2,1)S(1)}, f32[512,256]{1,0:T(8,128)S(1)}) custom-call(s32[26]{0:T(128)S(1)} %fusion.places, bf16[800,4096]{1,0:T(8,128)(2,1)S(1)} %get-tuple-element.38.refs_0_.filtered_ref, bf16[800,4096]{1,0:T(8,128)(2,1)S(1)} %get-tuple-element.39.refs_1_.filtered_ref, ...), custom_call_target="tpu_custom_call" | custom-call | flops 1677721600 | bytes 786432 | tf_op jit(solution)/shard_map/image_sum/pallas_call | solution.py:168
  171.6 3.1 %image_sum.12 = (bf16[512,256]{1,0:T(8,128)(2,1)S(1)}, f32[512,256]{1,0:T(8,128)S(1)}) custom-call(s32[26]{0:T(128)S(1)} %fusion.places, bf16[800,4096]{1,0:T(8,128)(2,1)S(1)} %get-tuple-element.38.refs_0_.filtered_ref, bf16[800,4096]{1,0:T(8,128)(2,1)S(1)} %get-tuple-element.39.refs_1_.filtered_ref, ...), custom_call_target="tpu_custom_call" | custom-call | flops 1677721600 | bytes 786432 | tf_op jit(solution)/shard_map/image_sum/pallas_call | solution.py:168
  179.3 3.0 %image_sum.15 = (bf16[512,256]{1,0:T(8,128)(2,1)S(1)}, f32[512,256]{1,0:T(8,128)S(1)}) custom-call(s32[26]{0:T(128)S(1)} %fusion.places, bf16[800,4096]{1,0:T(8,128)(2,1)S(1)} %get-tuple-element.38.refs_0_.filtered_ref, bf16[800,4096]{1,0:T(8,128)(2,1)S(1)} %get-tuple-element.39.refs_1_.filtered_ref, ...), custom_call_target="tpu_custom_call" | custom-call | flops 1677721600 | bytes 786432 | tf_op jit(solution)/shard_map/image_sum/pallas_call | solution.py:168
  183.1 2.9 %image_sum.13 = (bf16[512,256]{1,0:T(8,128)(2,1)S(1)}, f32[512,256]{1,0:T(8,128)S(1)}) custom-call(s32[26]{0:T(128)S(1)} %fusion.places, bf16[800,4096]{1,0:T(8,128)(2,1)S(1)} %get-tuple-element.38.refs_0_.filtered_ref, bf16[800,4096]{1,0:T(8,128)(2,1)S(1)} %get-tuple-element.39.refs_1_.filtered_ref, ...), custom_call_target="tpu_custom_call" | custom-call | flops 1677721600 | bytes 786432 | tf_op jit(solution)/shard_map/image_sum/pallas_call | solution.py:168
  186.1 6.0 %cholesky.3.refs_0_ = f32[256,512]{1,0:T(8,128)S(1)} custom-call(s32[26]{0:T(128)S(1)} %fusion.places, f32[128,256]{1,0:T(8,128)S(1)} %add.131.refs_0_, f32[128,256]{1,0:T(8,128)S(1)} %collective-permute-done.35.refs_1_), custom_call_target="tpu_custom_call" | custom-call | flops 3000000000 | bytes 786432 | tf_op jit(solution)/shard_map/cholesky/pallas_call | solution.py:405
  192.2 3.0 %collective-permute-start.30 = (bf16[512,256]{1,0:T(8,128)(2,1)S(1)}, bf16[512,256]{1,0:T(8,128)(2,1)S(1)}, u32[]{:S(2)}, u32[]{:S(2)}) collective-permute-start(bf16[512,256]{1,0:T(8,128)(2,1)S(1)} %add_convert_fusion), channel_id=1, source_target_pairs={{0,8},{4,12},{8,0},{12,4},{16,24},{20,28},{24,16},{28,20},{1,9},{5... | collective-permute-start | bytes 786440 | tf_op jit(solution)/shard_map/ppermute | solution.py:33
  195.2 6.8 %cholesky.4 = (f32[256,256]{1,0:T(8,128)}, f32[256,256]{1,0:T(8,128)S(1)}) custom-call(s32[26]{0:T(128)S(1)} %fusion.places, f32[256,512]{1,0:T(8,128)S(1)} %cholesky.3.refs_0_), custom_call_target="tpu_custom_call" | custom-call | flops 3000000000 | bytes 786432 | tf_op jit(solution)/shard_map/cholesky/pallas_call | solution.py:405
  202.1 3.8 %collective-permute-done.30.refs_1_ = bf16[512,256]{1,0:T(8,128)(2,1)S(1)} collective-permute-done((bf16[512,256]{1,0:T(8,128)(2,1)S(1)}, bf16[512,256]{1,0:T(8,128)(2,1)S(1)}, u32[]{:S(2)}, u32[]{:S(2)}) %collective-permute-start.30) | collective-permute-done | bytes 262176 | tf_op jit(solution)/shard_map/ppermute | solution.py:33
  215.0 2.7 collective-permute-done.39
  237.0 6.1 %collective-permute-done.49.refs_3_ = bf16[512,256]{1,0:T(8,128)(2,1)S(1)} collective-permute-done((bf16[512,256]{1,0:T(8,128)(2,1)S(1)}, bf16[512,256]{1,0:T(8,128)(2,1)S(1)}, u32[]{:S(2)}, u32[]{:S(2)}) %collective-permute-start.49) | collective-permute-done | bytes 262176 | tf_op jit(solution)/shard_map/ppermute | solution.py:33
  243.1 10.2 %collective-permute-done.48.refs_2_ = bf16[512,256]{1,0:T(8,128)(2,1)S(1)} collective-permute-done((bf16[512,256]{1,0:T(8,128)(2,1)S(1)}, bf16[512,256]{1,0:T(8,128)(2,1)S(1)}, u32[]{:S(2)}, u32[]{:S(2)}) %collective-permute-start.48) | collective-permute-done | bytes 262176 | tf_op jit(solution)/shard_map/ppermute | solution.py:33
  253.8 12.2 %cholesky.5 = (f32[256,256]{1,0:T(8,128)}, f32[256,256]{1,0:T(8,128)S(1)}) custom-call(s32[26]{0:T(128)S(1)} %fusion.places, f32[128,256]{1,0:T(8,128)S(1)} %get-tuple-element.70.refs_0_, f32[128,256]{1,0:T(8,128)S(1)} %collective-permute-done.46.refs_1_), custom_call_target="tpu_custom_call" | custom-call | flops 6000000000 | bytes 786432 | tf_op jit(solution)/shard_map/cholesky/pallas_call | solution.py:405
  266.1 6.5 %apply.1 = f32[4096,256]{1,0:T(8,128)} custom-call(s32[26]{0:T(128)S(1)} %fusion.places, f32[256,256]{1,0:T(8,128)S(1)} %get-tuple-element.71.inverse_ref, bf16[512,256]{1,0:T(8,128)(2,1)S(1)} %get-tuple-element.72.refs_0_, bf16[512,256]{1,0:T(8,128)(2,1)S(1)} %collective-permute-done.47.refs_1_, bf16[512,256]{1,0:T(8,128)(2,1)S(1)} %collective-permute-done.48.refs_2_, ...), custom_call_target="tpu_custom_call" | custom-call | flops 1610612736 | bytes 6291456 | tf_op jit(solution)/shard_map/apply/pallas_call | solution.py:441
  (121 shorter events, 74.2 us)
Async XLA Ops:
  13.3 27.0 %collective-permute-start = (bf16[800,256]{1,0:T(8,128)(2,1)S(1)}, bf16[800,256]{1,0:T(8,128)(2,1)S(1)}, u32[]{:S(2)}, u32[]{:S(2)}) collective-permute-start(bf16[800,256]{1,0:T(8,128)(2,1)S(1)} %get-tuple-element.43), channel_id=1, source_target_pairs={{0,3},{1,2},{2,1},{3,0},{4,7},{5,6},{6,5},{7,4},{8,11},{9,10},{10,... | collective-permute-start | bytes 1228808 | tf_op jit(solution)/shard_map/ppermute | solution.py:33
  24.8 15.6 %collective-permute-start.1 = (bf16[800,256]{1,0:T(8,128)(2,1)S(1)}, bf16[800,256]{1,0:T(8,128)(2,1)S(1)}, u32[]{:S(2)}, u32[]{:S(2)}) collective-permute-start(bf16[800,256]{1,0:T(8,128)(2,1)S(1)} %get-tuple-element.44), channel_id=1, source_target_pairs={{0,2},{1,3},{2,0},{3,1},{4,6},{5,7},{6,4},{7,5},{8,10},{9,11},{10,... | collective-permute-start | bytes 1228808 | tf_op jit(solution)/shard_map/ppermute | solution.py:33
  32.8 10.7 %collective-permute-start.2 = (bf16[800,256]{1,0:T(8,128)(2,1)S(1)}, bf16[800,256]{1,0:T(8,128)(2,1)S(1)}, u32[]{:S(2)}, u32[]{:S(2)}) collective-permute-start(bf16[800,256]{1,0:T(8,128)(2,1)S(1)} %get-tuple-element.45), channel_id=1, source_target_pairs={{0,1},{1,0},{2,3},{3,2},{4,5},{5,4},{6,7},{7,6},{8,9},{9,8},{10,11... | collective-permute-start | bytes 1228808 | tf_op jit(solution)/shard_map/ppermute | solution.py:33
  43.7 13.3 %collective-permute-start.5 = (bf16[800,256]{1,0:T(8,128)(2,1)S(1)}, bf16[800,256]{1,0:T(8,128)(2,1)S(1)}, u32[]{:S(2)}, u32[]{:S(2)}) collective-permute-start(bf16[800,256]{1,0:T(8,128)(2,1)S(1)} %multiply_convert_fusion.1.refs_4_), channel_id=1, source_target_pairs={{0,3},{1,2},{2,1},{3,0},{4,7},{5,6},{6,5},{7,4},{8,11},{9,10},{10,... | collective-permute-start | bytes 1228808 | tf_op jit(solution)/shard_map/ppermute | solution.py:33
  45.3 18.0 %collective-permute-start.4 = (bf16[800,256]{1,0:T(8,128)(2,1)S(1)}, bf16[800,256]{1,0:T(8,128)(2,1)S(1)}, u32[]{:S(2)}, u32[]{:S(2)}) collective-permute-start(bf16[800,256]{1,0:T(8,128)(2,1)S(1)} %multiply_convert_fusion.1.refs_4_), channel_id=1, source_target_pairs={{0,2},{1,3},{2,0},{3,1},{4,6},{5,7},{6,4},{7,5},{8,10},{9,11},{10,... | collective-permute-start | bytes 1228808 | tf_op jit(solution)/shard_map/ppermute | solution.py:33
  45.6 17.8 %collective-permute-start.3 = (bf16[800,256]{1,0:T(8,128)(2,1)S(1)}, bf16[800,256]{1,0:T(8,128)(2,1)S(1)}, u32[]{:S(2)}, u32[]{:S(2)}) collective-permute-start(bf16[800,256]{1,0:T(8,128)(2,1)S(1)} %multiply_convert_fusion.1.refs_4_), channel_id=1, source_target_pairs={{0,1},{1,0},{2,3},{3,2},{4,5},{5,4},{6,7},{7,6},{8,9},{9,8},{10,11... | collective-permute-start | bytes 1228808 | tf_op jit(solution)/shard_map/ppermute | solution.py:33
  70.0 11.2 %collective-permute-start.12 = (bf16[512,256]{1,0:T(8,128)(2,1)S(1)}, bf16[512,256]{1,0:T(8,128)(2,1)S(1)}, u32[]{:S(2)}, u32[]{:S(2)}) collective-permute-start(bf16[512,256]{1,0:T(8,128)(2,1)S(1)} %add_convert_fusion.5.refs_8_), channel_id=1, source_target_pairs={{0,24},{4,28},{8,16},{12,20},{16,8},{20,12},{24,0},{28,4},{1,25},{... | collective-permute-start | bytes 786440 | tf_op jit(solution)/shard_map/ppermute | solution.py:33
  76.9 19.2 %collective-permute-start.11 = (bf16[512,256]{1,0:T(8,128)(2,1)S(1)}, bf16[512,256]{1,0:T(8,128)(2,1)S(1)}, u32[]{:S(2)}, u32[]{:S(2)}) collective-permute-start(bf16[512,256]{1,0:T(8,128)(2,1)S(1)} %add_convert_fusion.6.refs_8_), channel_id=1, source_target_pairs={{0,16},{4,20},{8,24},{12,28},{16,0},{20,4},{24,8},{28,12},{1,17},{... | collective-permute-start | bytes 786440 | tf_op jit(solution)/shard_map/ppermute | solution.py:33
  80.6 15.6 %collective-permute-start.10 = (bf16[512,256]{1,0:T(8,128)(2,1)S(1)}, bf16[512,256]{1,0:T(8,128)(2,1)S(1)}, u32[]{:S(2)}, u32[]{:S(2)}) collective-permute-start(bf16[512,256]{1,0:T(8,128)(2,1)S(1)} %add_convert_fusion.4), channel_id=1, source_target_pairs={{0,8},{4,12},{8,0},{12,4},{16,24},{20,28},{24,16},{28,20},{1,9},{5... | collective-permute-start | bytes 786440 | tf_op jit(solution)/shard_map/ppermute | solution.py:33
  96.3 11.1 %collective-permute-start.15 = (bf16[512,256]{1,0:T(8,128)(2,1)S(1)}, bf16[512,256]{1,0:T(8,128)(2,1)S(1)}, u32[]{:S(2)}, u32[]{:S(2)}) collective-permute-start(bf16[512,256]{1,0:T(8,128)(2,1)S(1)} %add_convert_fusion.3.refs_0_), channel_id=1, source_target_pairs={{0,24},{4,28},{8,16},{12,20},{16,8},{20,12},{24,0},{28,4},{1,25},{... | collective-permute-start | bytes 786440 | tf_op jit(solution)/shard_map/ppermute | solution.py:33
  98.8 20.9 %collective-permute-start.14 = (bf16[512,256]{1,0:T(8,128)(2,1)S(1)}, bf16[512,256]{1,0:T(8,128)(2,1)S(1)}, u32[]{:S(2)}, u32[]{:S(2)}) collective-permute-start(bf16[512,256]{1,0:T(8,128)(2,1)S(1)} %add_convert_fusion.3.refs_0_), channel_id=1, source_target_pairs={{0,16},{4,20},{8,24},{12,28},{16,0},{20,4},{24,8},{28,12},{1,17},{... | collective-permute-start | bytes 786440 | tf_op jit(solution)/shard_map/ppermute | solution.py:33
  98.8 20.9 %collective-permute-start.13 = (bf16[512,256]{1,0:T(8,128)(2,1)S(1)}, bf16[512,256]{1,0:T(8,128)(2,1)S(1)}, u32[]{:S(2)}, u32[]{:S(2)}) collective-permute-start(bf16[512,256]{1,0:T(8,128)(2,1)S(1)} %add_convert_fusion.3.refs_0_), channel_id=1, source_target_pairs={{0,8},{4,12},{8,0},{12,4},{16,24},{20,28},{24,16},{28,20},{1,9},{5... | collective-permute-start | bytes 786440 | tf_op jit(solution)/shard_map/ppermute | solution.py:33
  100.8 19.4 %collective-permute-start.16 = (bf16[512,256]{1,0:T(8,128)(2,1)S(1)}, bf16[512,256]{1,0:T(8,128)(2,1)S(1)}, u32[]{:S(2)}, u32[]{:S(2)}) collective-permute-start(bf16[512,256]{1,0:T(8,128)(2,1)S(1)} %add_convert_fusion.3.refs_0_), channel_id=1, source_target_pairs={{0,4},{4,0},{8,12},{12,8},{16,20},{20,16},{24,28},{28,24},{1,5},{5... | collective-permute-start | bytes 786440 | tf_op jit(solution)/shard_map/ppermute | solution.py:33
  107.4 12.7 %collective-permute-start.19 = (bf16[512,256]{1,0:T(8,128)(2,1)S(1)}, bf16[512,256]{1,0:T(8,128)(2,1)S(1)}, u32[]{:S(2)}, u32[]{:S(2)}) collective-permute-start(bf16[512,256]{1,0:T(8,128)(2,1)S(1)} %collective-permute-done.15.refs_3_), channel_id=1, source_target_pairs={{0,4},{4,0},{8,12},{12,8},{16,20},{20,16},{24,28},{28,24},{1,5},{5... | collective-permute-start | bytes 786440 | tf_op jit(solution)/shard_map/ppermute | solution.py:33
  124.0 13.3 %collective-permute-start.20 = (bf16[800,256]{1,0:T(8,128)(2,1)S(1)}, bf16[800,256]{1,0:T(8,128)(2,1)S(1)}, u32[]{:S(2)}, u32[]{:S(2)}) collective-permute-start(bf16[800,256]{1,0:T(8,128)(2,1)S(1)} %score.5), channel_id=1, source_target_pairs={{0,3},{1,2},{2,1},{3,0},{4,7},{5,6},{6,5},{7,4},{8,11},{9,10},{10,... | collective-permute-start | bytes 1228808 | tf_op jit(solution)/shard_map/ppermute | solution.py:33
  127.9 17.4 %collective-permute-start.21 = (bf16[800,256]{1,0:T(8,128)(2,1)S(1)}, bf16[800,256]{1,0:T(8,128)(2,1)S(1)}, u32[]{:S(2)}, u32[]{:S(2)}) collective-permute-start(bf16[800,256]{1,0:T(8,128)(2,1)S(1)} %score.6), channel_id=1, source_target_pairs={{0,2},{1,3},{2,0},{3,1},{4,6},{5,7},{6,4},{7,5},{8,10},{9,11},{10,... | collective-permute-start | bytes 1228808 | tf_op jit(solution)/shard_map/ppermute | solution.py:33
  130.9 14.3 %collective-permute-start.22 = (bf16[800,256]{1,0:T(8,128)(2,1)S(1)}, bf16[800,256]{1,0:T(8,128)(2,1)S(1)}, u32[]{:S(2)}, u32[]{:S(2)}) collective-permute-start(bf16[800,256]{1,0:T(8,128)(2,1)S(1)} %score.7), channel_id=1, source_target_pairs={{0,1},{1,0},{2,3},{3,2},{4,5},{5,4},{6,7},{7,6},{8,9},{9,8},{10,11... | collective-permute-start | bytes 1228808 | tf_op jit(solution)/shard_map/ppermute | solution.py:33
  145.5 13.3 %collective-permute-start.25 = (bf16[800,256]{1,0:T(8,128)(2,1)S(1)}, bf16[800,256]{1,0:T(8,128)(2,1)S(1)}, u32[]{:S(2)}, u32[]{:S(2)}) collective-permute-start(bf16[800,256]{1,0:T(8,128)(2,1)S(1)} %multiply_convert_fusion.refs_4_), channel_id=1, source_target_pairs={{0,3},{1,2},{2,1},{3,0},{4,7},{5,6},{6,5},{7,4},{8,11},{9,10},{10,... | collective-permute-start | bytes 1228808 | tf_op jit(solution)/shard_map/ppermute | solution.py:33
  146.9 19.7 %collective-permute-start.24 = (bf16[800,256]{1,0:T(8,128)(2,1)S(1)}, bf16[800,256]{1,0:T(8,128)(2,1)S(1)}, u32[]{:S(2)}, u32[]{:S(2)}) collective-permute-start(bf16[800,256]{1,0:T(8,128)(2,1)S(1)} %multiply_convert_fusion.refs_4_), channel_id=1, source_target_pairs={{0,2},{1,3},{2,0},{3,1},{4,6},{5,7},{6,4},{7,5},{8,10},{9,11},{10,... | collective-permute-start | bytes 1228808 | tf_op jit(solution)/shard_map/ppermute | solution.py:33
  147.5 19.1 %collective-permute-start.23 = (bf16[800,256]{1,0:T(8,128)(2,1)S(1)}, bf16[800,256]{1,0:T(8,128)(2,1)S(1)}, u32[]{:S(2)}, u32[]{:S(2)}) collective-permute-start(bf16[800,256]{1,0:T(8,128)(2,1)S(1)} %multiply_convert_fusion.refs_4_), channel_id=1, source_target_pairs={{0,1},{1,0},{2,3},{3,2},{4,5},{5,4},{6,7},{7,6},{8,9},{9,8},{10,11... | collective-permute-start | bytes 1228808 | tf_op jit(solution)/shard_map/ppermute | solution.py:33
  177.8 24.2 %collective-permute-start.32 = (bf16[512,256]{1,0:T(8,128)(2,1)S(1)}, bf16[512,256]{1,0:T(8,128)(2,1)S(1)}, u32[]{:S(2)}, u32[]{:S(2)}) collective-permute-start(bf16[512,256]{1,0:T(8,128)(2,1)S(1)} %add_convert_fusion.1.refs_8_), channel_id=1, source_target_pairs={{0,24},{4,28},{8,16},{12,20},{16,8},{20,12},{24,0},{28,4},{1,25},{... | collective-permute-start | bytes 786440 | tf_op jit(solution)/shard_map/ppermute | solution.py:33
  182.4 19.7 %collective-permute-start.31 = (bf16[512,256]{1,0:T(8,128)(2,1)S(1)}, bf16[512,256]{1,0:T(8,128)(2,1)S(1)}, u32[]{:S(2)}, u32[]{:S(2)}) collective-permute-start(bf16[512,256]{1,0:T(8,128)(2,1)S(1)} %add_convert_fusion.2.refs_8_), channel_id=1, source_target_pairs={{0,16},{4,20},{8,24},{12,28},{16,0},{20,4},{24,8},{28,12},{1,17},{... | collective-permute-start | bytes 786440 | tf_op jit(solution)/shard_map/ppermute | solution.py:33
  186.0 16.0 %collective-permute-start.27 = (bf16[512,256]{1,0:T(8,128)(2,1)S(1)}, bf16[512,256]{1,0:T(8,128)(2,1)S(1)}, u32[]{:S(2)}, u32[]{:S(2)}) collective-permute-start(bf16[512,256]{1,0:T(8,128)(2,1)S(1)} %get-tuple-element.57), channel_id=1, source_target_pairs={{0,4},{4,0},{8,12},{12,8},{16,20},{20,16},{24,28},{28,24},{1,5},{5... | collective-permute-start | bytes 786440 | tf_op jit(solution)/shard_map/ppermute | solution.py:33
  192.2 13.7 %collective-permute-start.30 = (bf16[512,256]{1,0:T(8,128)(2,1)S(1)}, bf16[512,256]{1,0:T(8,128)(2,1)S(1)}, u32[]{:S(2)}, u32[]{:S(2)}) collective-permute-start(bf16[512,256]{1,0:T(8,128)(2,1)S(1)} %add_convert_fusion), channel_id=1, source_target_pairs={{0,8},{4,12},{8,0},{12,4},{16,24},{20,28},{24,16},{28,20},{1,9},{5... | collective-permute-start | bytes 786440 | tf_op jit(solution)/shard_map/ppermute | solution.py:33
  232.1 11.0 %collective-permute-start.49 = (bf16[512,256]{1,0:T(8,128)(2,1)S(1)}, bf16[512,256]{1,0:T(8,128)(2,1)S(1)}, u32[]{:S(2)}, u32[]{:S(2)}) collective-permute-start(bf16[512,256]{1,0:T(8,128)(2,1)S(1)} %get-tuple-element.72.refs_0_), channel_id=1, source_target_pairs={{0,24},{4,28},{8,16},{12,20},{16,8},{20,12},{24,0},{28,4},{1,25},{... | collective-permute-start | bytes 786440 | tf_op jit(solution)/shard_map/ppermute | solution.py:33
  234.1 19.2 %collective-permute-start.48 = (bf16[512,256]{1,0:T(8,128)(2,1)S(1)}, bf16[512,256]{1,0:T(8,128)(2,1)S(1)}, u32[]{:S(2)}, u32[]{:S(2)}) collective-permute-start(bf16[512,256]{1,0:T(8,128)(2,1)S(1)} %get-tuple-element.72.refs_0_), channel_id=1, source_target_pairs={{0,16},{4,20},{8,24},{12,28},{16,0},{20,4},{24,8},{28,12},{1,17},{... | collective-permute-start | bytes 786440 | tf_op jit(solution)/shard_map/ppermute | solution.py:33
  235.2 18.1 %collective-permute-start.47 = (bf16[512,256]{1,0:T(8,128)(2,1)S(1)}, bf16[512,256]{1,0:T(8,128)(2,1)S(1)}, u32[]{:S(2)}, u32[]{:S(2)}) collective-permute-start(bf16[512,256]{1,0:T(8,128)(2,1)S(1)} %get-tuple-element.72.refs_0_), channel_id=1, source_target_pairs={{0,8},{4,12},{8,0},{12,4},{16,24},{20,28},{24,16},{28,20},{1,9},{5... | collective-permute-start | bytes 786440 | tf_op jit(solution)/shard_map/ppermute | solution.py:33
  236.5 17.3 %collective-permute-start.46 = (f32[128,256]{1,0:T(8,128)S(1)}, f32[128,256]{1,0:T(8,128)S(1)}, u32[]{:S(2)}, u32[]{:S(2)}) collective-permute-start(f32[128,256]{1,0:T(8,128)S(1)} %get-tuple-element.70.refs_0_), channel_id=1, source_target_pairs={{0,4},{4,0},{8,12},{12,8},{16,20},{20,16},{24,28},{28,24},{1,5},{5... | collective-permute-start | bytes 393224 | tf_op jit(solution)/shard_map/ppermute | solution.py:33
  236.5 29.5 %collective-permute-start.50 = (bf16[512,256]{1,0:T(8,128)(2,1)S(1)}, bf16[512,256]{1,0:T(8,128)(2,1)S(1)}, u32[]{:S(2)}, u32[]{:S(2)}) collective-permute-start(bf16[512,256]{1,0:T(8,128)(2,1)S(1)} %get-tuple-element.72.refs_0_), channel_id=1, source_target_pairs={{0,4},{4,0},{8,12},{12,8},{16,20},{20,16},{24,28},{28,24},{1,5},{5... | collective-permute-start | bytes 786440 | tf_op jit(solution)/shard_map/ppermute | solution.py:33
  243.1 22.9 %collective-permute-start.53 = (bf16[512,256]{1,0:T(8,128)(2,1)S(1)}, bf16[512,256]{1,0:T(8,128)(2,1)S(1)}, u32[]{:S(2)}, u32[]{:S(2)}) collective-permute-start(bf16[512,256]{1,0:T(8,128)(2,1)S(1)} %collective-permute-done.49.refs_3_), channel_id=1, source_target_pairs={{0,4},{4,0},{8,12},{12,8},{16,20},{20,16},{24,28},{28,24},{1,5},{5... | collective-permute-start | bytes 786440 | tf_op jit(solution)/shard_map/ppermute | solution.py:33
  253.3 12.7 %collective-permute-start.52 = (bf16[512,256]{1,0:T(8,128)(2,1)S(1)}, bf16[512,256]{1,0:T(8,128)(2,1)S(1)}, u32[]{:S(2)}, u32[]{:S(2)}) collective-permute-start(bf16[512,256]{1,0:T(8,128)(2,1)S(1)} %collective-permute-done.48.refs_2_), channel_id=1, source_target_pairs={{0,4},{4,0},{8,12},{12,8},{16,20},{20,16},{24,28},{28,24},{1,5},{5... | collective-permute-start | bytes 786440 | tf_op jit(solution)/shard_map/ppermute | solution.py:33
  253.3 12.7 %collective-permute-start.51 = (bf16[512,256]{1,0:T(8,128)(2,1)S(1)}, bf16[512,256]{1,0:T(8,128)(2,1)S(1)}, u32[]{:S(2)}, u32[]{:S(2)}) collective-permute-start(bf16[512,256]{1,0:T(8,128)(2,1)S(1)} %collective-permute-done.47.refs_1_), channel_id=1, source_target_pairs={{0,4},{4,0},{8,12},{12,8},{16,20},{20,16},{24,28},{28,24},{1,5},{5... | collective-permute-start | bytes 786440 | tf_op jit(solution)/shard_map/ppermute | solution.py:33
  (23 other events, 111.9 us)

commit v3 on v2

--- a/solution.py
+++ b/solution.py
@@ -7,12 +7,14 @@
 from jax.experimental.pallas import tpu as pltpu
 from jax.sharding import PartitionSpec as P
 
+
 ITERS = 2
 F32 = jnp.float32
 BF16 = jnp.bfloat16
 LANES = 128
 PANEL = 32
 GROUP = 8
+SPLIT = 1
 HIGHEST = lax.Precision.HIGHEST
 
 
@@ -41,7 +43,7 @@
     return pl.BlockSpec(memory_space=pltpu.VMEM)
 
 
-def filter_kernel(places, class_ref, image_ref, table_ref, probe_ref, filtered_ref, score_ref):
+def filter_kernel(places, class_ref, image_ref, table_ref, probe_ref, filtered_ref, *score_refs):
     table_rows = table_ref.shape[0]
     rows, pixels = image_ref.shape
     onehot = (
@@ -57,7 +59,9 @@
         filtered_ref[here, columns] = filtered
         term = jnp.dot(filtered, probe_ref[columns, :], preferred_element_type=F32)
         scores = term if scores is None else scores + term
-    score_ref[here, :] = scores.astype(score_ref.dtype)
+    part = score_refs[0].shape[1]
+    for at, ref in enumerate(score_refs):
+        ref[here, :] = scores[:, at * part : (at + 1) * part].astype(ref.dtype)
 
 
 def filter_and_score(places, shift, images, classes, table, probe_half, chunk, out_type):
@@ -76,12 +80,10 @@
                 in_vmem(),
                 in_vmem(),
             ],
-            out_specs=[in_vmem(), in_vmem()],
+            out_specs=[in_vmem()] * (1 + SPLIT),
         ),
-        out_shape=[
-            pltpu.VMEM((chunk, pixels), BF16),
-            jax.ShapeDtypeStruct((chunk, columns), out_type),
-        ],
+        out_shape=[pltpu.VMEM((chunk, pixels), BF16)]
+        + [jax.ShapeDtypeStruct((chunk, columns // SPLIT), out_type)] * SPLIT,
         compiler_params=vmem(14 * 2**20),
         cost_estimate=cost(4 * chunk * pixels * columns, 2 * chunk * pixels),
         name="filter_and_score",
@@ -144,9 +146,12 @@
 
     def block(at, carry):
         columns = pl.ds(pl.multiple_of(places[first + at] * width, width), width)
-        total = sum_blocks(
-            [ref[:, columns] for ref in filtered_refs], [ref[...] for ref in scaled_refs]
-        )
+        blocks = [ref[:, columns] for ref in filtered_refs]
+        scaled = [ref[...] for ref in scaled_refs]
+        if scaled[0].shape[1] > LANES:
+            total = sum_blocks(blocks, scaled)
+        else:
+            total = sum_blocks(scaled, blocks).T
 
         @pl.when(at == 0)
         def _():
@@ -184,15 +189,22 @@
     return terms[0]
 
 
+def whole_blocks(parts):
+    count = len(parts) // SPLIT
+    return [jnp.concatenate(parts[at::count], 1) for at in range(count)]
+
+
 def gram_kernel(core_at, places, *refs):
     *basis_refs, _, half_ref, gram_ref = refs
-    gram_ref[...] = tree_sum([contract_rows(ref[...], ref[...]) for ref in basis_refs])
+    blocks = whole_blocks([ref[...] for ref in basis_refs])
+    gram_ref[...] = tree_sum([contract_rows(block, block) for block in blocks])
     rows = half_ref.shape[0]
     half_ref[...] = gram_ref[pl.ds(pl.multiple_of(places[core_at] * rows, rows), rows), :]
 
 
 def half_gram(places, core_at, basis, after):
     rows, columns = basis[0].shape
+    columns *= SPLIT
     return pl.pallas_call(
         functools.partial(gram_kernel, core_at),
         grid_spec=pltpu.PrefetchScalarGridSpec(
@@ -211,9 +223,10 @@
 
 def normalize_kernel(core_at, scale, places, *refs):
     *part_refs, inverse_ref, half_ref, send_ref, keep_ref, gram_ref = refs
-    total = part_refs[0][...]
-    for ref in part_refs[1:]:
-        total = total + ref[...].astype(F32)
+    blocks = whole_blocks([ref[...].astype(F32) for ref in part_refs])
+    total = blocks[0]
+    for block in blocks[1:]:
+        total = total + block
     block = lax.dot_general(
         total,
         inverse_ref[...] * scale,
@@ -231,6 +244,7 @@
 
 def normalize_and_gram(places, core_at, parts, inverse, scale):
     rows, columns = parts[0].shape
+    columns *= SPLIT
     return pl.pallas_call(
         functools.partial(normalize_kernel, core_at, scale),
         grid_spec=pltpu.PrefetchScalarGridSpec(
@@ -419,36 +433,45 @@
     return state
 
 
-def apply_kernel(places, inverse_ref, *refs):
+def apply_kernel(first, places, inverse_ref, *refs):
     *basis_refs, out_ref = refs
     parts = split_in_three(inverse_ref[...])
-    for at, basis_ref in enumerate(basis_refs):
-
-        @pl.when(pl.program_id(0) == at)
+    rows = basis_refs[0].shape[0]
+    span = out_ref.shape[0] // rows
+    for step in range(len(basis_refs) // span):
+
+        @pl.when(pl.program_id(0) == step)
         def _():
-            block = basis_ref[...]
-            out_ref[...] = sum(
-                lax.dot_general(
-                    block, part, (((1,), (1,)), ((), ())), preferred_element_type=F32
+            for at in range(step * span, (step + 1) * span):
+                block = basis_refs[at][...]
+                here = pl.multiple_of((places[first + at] % span) * rows, rows)
+                out_ref[pl.ds(here, rows), :] = sum(
+                    lax.dot_general(
+                        block, part, (((1,), (1,)), ((), ())), preferred_element_type=F32
+                    )
+                    for part in reversed(parts)
                 )
-                for part in reversed(parts)
-            )
 
 
 def apply_inverse(places, first, inverse, basis):
     rows, columns = basis[0].shape
-    blocks = len(basis)
-    return pl.pallas_call(
-        apply_kernel,
+    span = 2
+    steps = len(basis) // span
+    return pl.pallas_call(
+        functools.partial(apply_kernel, first),
         grid_spec=pltpu.PrefetchScalarGridSpec(
             num_scalar_prefetch=1,
-            grid=(blocks,),
-            in_specs=[in_vmem()] * (1 + blocks),
-            out_specs=pl.BlockSpec((rows, columns), lambda i, places: (places[first + i], 0)),
+            grid=(steps,),
+            in_specs=[in_vmem()] * (1 + len(basis)),
+            out_specs=pl.BlockSpec(
+                (span * rows, columns), lambda i, places: (places[first + span * i] // span, 0)
+            ),
         ),
-        out_shape=jax.ShapeDtypeStruct((rows * blocks, columns), F32),
+        out_shape=jax.ShapeDtypeStruct((rows * len(basis), columns), F32),
         compiler_params=vmem(16 * 2**20),
-        cost_estimate=cost(6 * rows * blocks * columns * columns, 6 * rows * blocks * columns),
+        cost_estimate=cost(
+            6 * rows * len(basis) * columns * columns, 6 * rows * len(basis) * columns
+        ),
         name="apply",
     )(places, inverse, *basis)
 
@@ -488,11 +511,12 @@
     weight_share = weight_share[:, None]
 
     shifts = list(range(pix - 1, -1, -1))
-    filtered, own, arrived = [None] * pix, None, []
+    halves = range(SPLIT)
+    filtered, own, arrived = [None] * pix, None, [[] for _ in halves]
     probe_half = probes.astype(BF16)
     images = pltpu.with_memory_space_constraint(images, pltpu.HBM)
     for shift in shifts:
-        filtered[shift], part = filter_and_score(
+        filtered[shift], *parts = filter_and_score(
             places,
             rows_at + shift,
             images,
@@ -503,66 +527,79 @@
             BF16 if shift else F32,
         )
         if shift:
-            arrived.append(xor_swap(part, "pix", shift))
+            for h in halves:
+                arrived[h].append(xor_swap(parts[h], "pix", shift))
         else:
-            own = part
+            own = parts
 
     basis = inverse = None
     for sweep in range(ITERS):
-        shares = own
-        for part in arrived:
-            shares = shares + part.astype(F32)
         share_weights = weight_share if sweep == 0 else weight_share * RANGE
-        scaled_share = (share_weights * shares).astype(BF16)
-        scaled = [scaled_share] + [xor_swap(scaled_share, "pix", s) for s in range(1, pix)]
-
-        parts, after = [None] * depth, []
-        for s in range(depth - 1, -1, -1):
-            send, keep = image_sum(
-                places, pairs_at + 2 * s, filtered, scaled, width, after[-2:-1]
-            )
-            both = keep + xor_swap(send, "img", 1).astype(F32)
-            if s:
-                both = both.astype(BF16)
-                parts[s] = xor_swap(both, "img", 2 * s)
-            else:
-                parts[s] = both
-            after.append(both)
+        scaled = []
+        for h in halves:
+            shares = own[h]
+            for part in arrived[h]:
+                shares = shares + part.astype(F32)
+            share = (share_weights * shares).astype(BF16)
+            scaled.append([share] + [xor_swap(share, "pix", s) for s in range(1, pix)])
+
+        parts, after = [[None] * depth for _ in halves], []
+        for h in halves:
+            for s in range(depth - 1, -1, -1):
+                send, keep = image_sum(
+                    places, pairs_at + 2 * s, filtered, scaled[h], width, after[-2:-1]
+                )
+                both = keep + xor_swap(send, "img", 1).astype(F32)
+                if s:
+                    both = both.astype(BF16)
+                    parts[h][s] = xor_swap(both, "img", 2 * s)
+                else:
+                    parts[h][s] = both
+                after.append(both)
 
         if sweep == ITERS - 1:
-            half = half_gram(places, cores_at, basis, scaled[-1])
+            gram = half_gram(places, cores_at, sum(basis, []), scaled[-1][-1])
             step = 1
             while step < pix:
-                half = half + xor_swap(half, "pix", step)
+                gram = gram + xor_swap(gram, "pix", step)
                 step *= 2
-            _, inverse = cholesky_and_inverse(
-                places, cores_at, [half, xor_swap(half, "img", 1)], 2
-            )
+            other = xor_swap(gram, "img", 1)
+            _, inverse = cholesky_and_inverse(places, cores_at, [gram, other], 2)
             break
-        total = parts[0]
-        for part in parts[1:]:
-            total = total + part.astype(F32)
-        half = total.astype(BF16)
-        near = [half] + [xor_swap(half, "img", 2 * s) for s in range(1, depth)]
-        basis = near + [xor_swap(block, "img", 1) for block in near]
-
-        own, arrived = None, []
-        for shift in shifts:
-            part = score(places, gathered_at, filtered[shift], basis, BF16 if shift else F32)
-            if shift:
-                arrived.append(xor_swap(part, "pix", shift))
-            else:
-                own = part
-
-    half, send, keep = normalize_and_gram(places, cores_at, parts, inverse, 1.0 / RANGE)
+
+        basis = []
+        for h in halves:
+            total = parts[h][0]
+            for part in parts[h][1:]:
+                total = total + part.astype(F32)
+            block = total.astype(BF16)
+            near = [block] + [xor_swap(block, "img", 2 * s) for s in range(1, depth)]
+            basis.append(near + [xor_swap(block, "img", 1) for block in near])
+
+        own, arrived = [None] * SPLIT, [[] for _ in halves]
+        for h in halves:
+            for shift in shifts:
+                part = score(places, gathered_at, filtered[shift], basis[h], BF16 if shift else F32)
+                if shift:
+                    arrived[h].append(xor_swap(part, "pix", shift))
+                else:
+                    own[h] = part
+
+    half, send, keep = normalize_and_gram(
+        places, cores_at, sum(parts, []), inverse, 1.0 / RANGE
+    )
     pieces = scatter_rows(places, levels_at, keep, xor_swap(send, "img", 1), depth)
     mine = tree_sum([pieces[0]] + [xor_swap(pieces[s], "img", 2 * s) for s in range(1, depth)])
-    mine = tree_sum([mine] + [xor_swap(mine, "pix", s) for s in range(1, pix)])
     pieces = [mine] + [xor_swap(mine, "img", 2 * s) for s in range(1, depth)]
     gram, half = gather_rows(places, levels_at, pieces, half)
+    step = 1
+    while step < pix:
+        gram = gram + xor_swap(gram, "pix", step)
+        step *= 2
+    other = xor_swap(gram, "img", 1)
     near = [half] + [xor_swap(half, "img", 2 * s) for s in range(1, depth)]
     basis = near + [xor_swap(block, "img", 1) for block in near]
-    factor, inverse = cholesky_and_inverse(places, cores_at, [gram, xor_swap(gram, "img", 1)], 1)
+    factor, inverse = cholesky_and_inverse(places, cores_at, [gram, other], 1)
     return apply_inverse(places, gathered_at, inverse, basis), factor
 
 
@@ -572,7 +609,7 @@
     filtered = (images.astype(F32) * filters).astype(BF16)
     current = probes
     factor = None
-    for sweep in range(ITERS):
+    for _ in range(ITERS):
         share_rows = filtered.shape[0] // lax.axis_size("pix")
         shares = lax.psum_scatter(
             jnp.dot(filtered, current.astype(BF16), preferred_element_type=F32),
@@ -596,20 +633,22 @@
     return n > 1 and n & (n - 1) == 0
 
 
-def per_device_of(images, classes, ctf_table, weights, probes):
-    rows, pixels = images.shape
-    pix, img = lax.axis_size("pix"), lax.axis_size("img")
-    columns = probes.shape[1]
-    fits = (
+def fits(rows, pixels, columns, pix, img):
+    return (
         power_of_two(pix)
         and power_of_two(img)
         and rows % (16 * pix) == 0
         and pixels % (LANES * img) == 0
-        and columns % LANES == 0
+        and columns % (LANES * SPLIT) == 0
         and columns % (8 * img) == 0
     )
-    run = per_device if fits else plain_per_device
-    return run(images, classes, ctf_table, weights, probes)
+
+
+def per_device_of(images, classes, ctf_table, weights, probes):
+    pix, img = lax.axis_size("pix"), lax.axis_size("img")
+    if not fits(*images.shape, probes.shape[1], pix, img):
+        return plain_per_device(images, classes, ctf_table, weights, probes)
+    return per_device(images, classes, ctf_table, weights, probes)
 
 
 def solution(mesh):

time: 273 us -> 267 us (0.978)
    ppermute x54 -> x53, waiting for transfers between devices: 115 us -> 113 us  [xor_swap(): return lax.ppermute(value, axis, [(i, i ^ mask) for i in range(size)])]
    ppermute x54 -> x53, starting transfers between devices: 51.1 us -> 49.5 us  [xor_swap(): return lax.ppermute(value, axis, [(i, i ^ mask) for i in range(size)])]
  transfers between devices with their start and end apart: 54 -> 53, of which waited for: 26 -> 24; matrix products, arithmetic and copies ran while one was open for 0% -> 0% of each run, Pallas kernels for 27% -> 28%
where the time goes in v3:
time: 267 us; the launch traced here: 266 us
  waiting for transfers between devices  113 us (42%)
  Pallas kernels  96.9 us (36%)
  starting transfers between devices  49.5 us (19%)
  other arithmetic  4.34 us (2%)
    ppermute x53, waiting for transfers between devices, xor_swap(): return lax.ppermute(value, axis, [(i, i ^ mask) for i in range(size)])  113 us
    ppermute x53, starting transfers between devices, xor_swap(): return lax.ppermute(value, axis, [(i, i ^ mask) for i in range(size)])  49.5 us
    pallas_call x4, Pallas kernels, filter_and_score(): pl.pallas_call(filter_kernel, grid_spec=pltpu.PrefetchScalarGridSpec(num_...  29.7 us
    pallas_call x3, Pallas kernels, cholesky_and_inverse(): pl.pallas_call(functools.partial(cholesky_kernel, first, last, place_at),...  25 us
    pallas_call x8, Pallas kernels, image_sum(): pl.pallas_call(functools.partial(image_sum_kernel, count, first), grid_sp...  24 us
    pallas_call x4, Pallas kernels, score(): pl.pallas_call(functools.partial(score_kernel, first), grid_spec=prefetch...  9.6 us
  transfers between devices with their start and end apart: 53, of which 24 were waited for; matrix products, arithmetic and copies ran while one was open for 0% of the time, Pallas kernels for 28%

profile of v3, /device:TPU:0, one launch (start us, length us, event | category | flops | bytes accessed | tf_op | source)
XLA Modules:
  0.0 266.3 jit_solution(12632664955797208319)
XLA Ops:
  5.9 7.4 %filter_and_score.7 = (bf16[800,4096]{1,0:T(8,128)(2,1)S(1)}, bf16[800,256]{1,0:T(8,128)(2,1)S(1)}) custom-call(s32[26]{0:T(128)S(1)} %fusion.places, s32[8,1,400]{2,1,0:T(1,128)S(1)} %reshape.17.class_ref, bf16[3200,4096]{1,0:T(8,128)(2,1)} %image_ref.7, bf16[64,4096]{1,0:T(8,128)(2,1)S(1)} %copy-done, bf16[4096,256]{1,0:T(8,128)(2,1)S(1)} %convert_element_type.89.probe_ref), custom_call_target="tpu_custom_call" | custom-call | flops 3355443200 | bytes 6553600 | tf_op jit(solution)/shard_map/filter_and_score/pallas_call | solution.py:72
  13.3 4.0 %collective-permute-start = (bf16[800,256]{1,0:T(8,128)(2,1)S(1)}, bf16[800,256]{1,0:T(8,128)(2,1)S(1)}, u32[]{:S(2)}, u32[]{:S(2)}) collective-permute-start(bf16[800,256]{1,0:T(8,128)(2,1)S(1)} %get-tuple-element.43), channel_id=1, source_target_pairs={{0,3},{1,2},{2,1},{3,0},{4,7},{5,6},{6,5},{7,4},{8,11},{9,10},{10,... | collective-permute-start | bytes 1228808 | tf_op jit(solution)/shard_map/ppermute | solution.py:35
  17.3 7.4 %filter_and_score.6 = (bf16[800,4096]{1,0:T(8,128)(2,1)S(1)}, bf16[800,256]{1,0:T(8,128)(2,1)S(1)}) custom-call(s32[26]{0:T(128)S(1)} %fusion.places, s32[8,1,400]{2,1,0:T(1,128)S(1)} %reshape.17.class_ref, bf16[3200,4096]{1,0:T(8,128)(2,1)} %image_ref.7, bf16[64,4096]{1,0:T(8,128)(2,1)S(1)} %copy-done, bf16[4096,256]{1,0:T(8,128)(2,1)S(1)} %convert_element_type.89.probe_ref), custom_call_target="tpu_custom_call" | custom-call | flops 3355443200 | bytes 6553600 | tf_op jit(solution)/shard_map/filter_and_score/pallas_call | solution.py:72
  25.3 7.4 %filter_and_score.5 = (bf16[800,4096]{1,0:T(8,128)(2,1)S(1)}, bf16[800,256]{1,0:T(8,128)(2,1)S(1)}) custom-call(s32[26]{0:T(128)S(1)} %fusion.places, s32[8,1,400]{2,1,0:T(1,128)S(1)} %reshape.17.class_ref, bf16[3200,4096]{1,0:T(8,128)(2,1)} %image_ref.7, bf16[64,4096]{1,0:T(8,128)(2,1)S(1)} %copy-done, bf16[4096,256]{1,0:T(8,128)(2,1)S(1)} %convert_element_type.89.probe_ref), custom_call_target="tpu_custom_call" | custom-call | flops 3355443200 | bytes 6553600 | tf_op jit(solution)/shard_map/filter_and_score/pallas_call | solution.py:72
  32.9 7.4 %filter_and_score.4 = (bf16[800,4096]{1,0:T(8,128)(2,1)S(1)}, f32[800,256]{1,0:T(8,128)S(1)}) custom-call(s32[26]{0:T(128)S(1)} %fusion.places, s32[8,1,400]{2,1,0:T(1,128)S(1)} %reshape.17.class_ref, bf16[3200,4096]{1,0:T(8,128)(2,1)} %image_ref.7, bf16[64,4096]{1,0:T(8,128)(2,1)S(1)} %copy-done, bf16[4096,256]{1,0:T(8,128)(2,1)S(1)} %convert_element_type.89.probe_ref), custom_call_target="tpu_custom_call" | custom-call | flops 3355443200 | bytes 6553600 | tf_op jit(solution)/shard_map/filter_and_score/pallas_call | solution.py:72
  40.4 3.1 %collective-permute-done.2 = bf16[800,256]{1,0:T(8,128)(2,1)S(1)} collective-permute-done((bf16[800,256]{1,0:T(8,128)(2,1)S(1)}, bf16[800,256]{1,0:T(8,128)(2,1)S(1)}, u32[]{:S(2)}, u32[]{:S(2)}) %collective-permute-start.2) | collective-permute-done | bytes 409632 | tf_op jit(solution)/shard_map/ppermute | solution.py:35
  47.3 9.7 %collective-permute-done.5.refs_7_ = bf16[800,256]{1,0:T(8,128)(2,1)S(1)} collective-permute-done((bf16[800,256]{1,0:T(8,128)(2,1)S(1)}, bf16[800,256]{1,0:T(8,128)(2,1)S(1)}, u32[]{:S(2)}, u32[]{:S(2)}) %collective-permute-start.5) | collective-permute-done | bytes 409632 | tf_op jit(solution)/shard_map/ppermute | solution.py:35
  57.0 6.2 %collective-permute-done.4.refs_6_ = bf16[800,256]{1,0:T(8,128)(2,1)S(1)} collective-permute-done((bf16[800,256]{1,0:T(8,128)(2,1)S(1)}, bf16[800,256]{1,0:T(8,128)(2,1)S(1)}, u32[]{:S(2)}, u32[]{:S(2)}) %collective-permute-start.4) | collective-permute-done | bytes 409632 | tf_op jit(solution)/shard_map/ppermute | solution.py:35
  63.3 3.0 %image_sum.10 = (bf16[512,256]{1,0:T(8,128)(2,1)S(1)}, f32[512,256]{1,0:T(8,128)S(1)}) custom-call(s32[26]{0:T(128)S(1)} %fusion.places, bf16[800,4096]{1,0:T(8,128)(2,1)S(1)} %get-tuple-element.38.refs_0_.filtered_ref, bf16[800,4096]{1,0:T(8,128)(2,1)S(1)} %get-tuple-element.39.refs_1_.filtered_ref, ...), custom_call_target="tpu_custom_call" | custom-call | flops 1677721600 | bytes 786432 | tf_op jit(solution)/shard_map/image_sum/pallas_call | solution.py:173
  66.4 2.9 %image_sum.8 = (bf16[512,256]{1,0:T(8,128)(2,1)S(1)}, f32[512,256]{1,0:T(8,128)S(1)}) custom-call(s32[26]{0:T(128)S(1)} %fusion.places, bf16[800,4096]{1,0:T(8,128)(2,1)S(1)} %get-tuple-element.38.refs_0_.filtered_ref, bf16[800,4096]{1,0:T(8,128)(2,1)S(1)} %get-tuple-element.39.refs_1_.filtered_ref, ...), custom_call_target="tpu_custom_call" | custom-call | flops 1677721600 | bytes 786432 | tf_op jit(solution)/shard_map/image_sum/pallas_call | solution.py:173
  70.0 3.7 %collective-permute-start.12 = (bf16[512,256]{1,0:T(8,128)(2,1)S(1)}, bf16[512,256]{1,0:T(8,128)(2,1)S(1)}, u32[]{:S(2)}, u32[]{:S(2)}) collective-permute-start(bf16[512,256]{1,0:T(8,128)(2,1)S(1)} %add_convert_fusion.5.refs_8_), channel_id=1, source_target_pairs={{0,24},{4,28},{8,16},{12,20},{16,8},{20,12},{24,0},{28,4},{1,25},{... | collective-permute-start | bytes 786440 | tf_op jit(solution)/shard_map/ppermute | solution.py:35
  73.6 3.2 %image_sum.11 = (bf16[512,256]{1,0:T(8,128)(2,1)S(1)}, f32[512,256]{1,0:T(8,128)S(1)}) custom-call(s32[26]{0:T(128)S(1)} %fusion.places, bf16[800,4096]{1,0:T(8,128)(2,1)S(1)} %get-tuple-element.38.refs_0_.filtered_ref, bf16[800,4096]{1,0:T(8,128)(2,1)S(1)} %get-tuple-element.39.refs_1_.filtered_ref, ...), custom_call_target="tpu_custom_call" | custom-call | flops 1677721600 | bytes 786432 | tf_op jit(solution)/shard_map/image_sum/pallas_call | solution.py:173
  77.0 2.9 %image_sum.9 = (bf16[512,256]{1,0:T(8,128)(2,1)S(1)}, f32[512,256]{1,0:T(8,128)S(1)}) custom-call(s32[26]{0:T(128)S(1)} %fusion.places, bf16[800,4096]{1,0:T(8,128)(2,1)S(1)} %get-tuple-element.38.refs_0_.filtered_ref, bf16[800,4096]{1,0:T(8,128)(2,1)S(1)} %get-tuple-element.39.refs_1_.filtered_ref, ...), custom_call_target="tpu_custom_call" | custom-call | flops 1677721600 | bytes 786432 | tf_op jit(solution)/shard_map/image_sum/pallas_call | solution.py:173
  81.7 14.5 %collective-permute-done.11 = bf16[512,256]{1,0:T(8,128)(2,1)S(1)} collective-permute-done((bf16[512,256]{1,0:T(8,128)(2,1)S(1)}, bf16[512,256]{1,0:T(8,128)(2,1)S(1)}, u32[]{:S(2)}, u32[]{:S(2)}) %collective-permute-start.11) | collective-permute-done | bytes 262176 | tf_op jit(solution)/shard_map/ppermute | solution.py:35
  100.8 6.7 %collective-permute-done.15.refs_3_ = bf16[512,256]{1,0:T(8,128)(2,1)S(1)} collective-permute-done((bf16[512,256]{1,0:T(8,128)(2,1)S(1)}, bf16[512,256]{1,0:T(8,128)(2,1)S(1)}, u32[]{:S(2)}, u32[]{:S(2)}) %collective-permute-start.15) | collective-permute-done | bytes 262176 | tf_op jit(solution)/shard_map/ppermute | solution.py:35
  107.4 12.2 %collective-permute-done.14.refs_2_ = bf16[512,256]{1,0:T(8,128)(2,1)S(1)} collective-permute-done((bf16[512,256]{1,0:T(8,128)(2,1)S(1)}, bf16[512,256]{1,0:T(8,128)(2,1)S(1)}, u32[]{:S(2)}, u32[]{:S(2)}) %collective-permute-start.14) | collective-permute-done | bytes 262176 | tf_op jit(solution)/shard_map/ppermute | solution.py:35
  137.3 7.9 %collective-permute-done.21 = bf16[800,256]{1,0:T(8,128)(2,1)S(1)} collective-permute-done((bf16[800,256]{1,0:T(8,128)(2,1)S(1)}, bf16[800,256]{1,0:T(8,128)(2,1)S(1)}, u32[]{:S(2)}, u32[]{:S(2)}) %collective-permute-start.21) | collective-permute-done | bytes 409632 | tf_op jit(solution)/shard_map/ppermute | solution.py:35
  149.0 9.8 %collective-permute-done.25.refs_7_.refs_8_ = bf16[800,256]{1,0:T(8,128)(2,1)S(1)} collective-permute-done((bf16[800,256]{1,0:T(8,128)(2,1)S(1)}, bf16[800,256]{1,0:T(8,128)(2,1)S(1)}, u32[]{:S(2)}, u32[]{:S(2)}) %collective-permute-start.25) | collective-permute-done | bytes 409632 | tf_op jit(solution)/shard_map/ppermute | solution.py:35
  158.8 7.8 %collective-permute-done.24.refs_6_ = bf16[800,256]{1,0:T(8,128)(2,1)S(1)} collective-permute-done((bf16[800,256]{1,0:T(8,128)(2,1)S(1)}, bf16[800,256]{1,0:T(8,128)(2,1)S(1)}, u32[]{:S(2)}, u32[]{:S(2)}) %collective-permute-start.24) | collective-permute-done | bytes 409632 | tf_op jit(solution)/shard_map/ppermute | solution.py:35
  166.6 3.0 %image_sum.14 = (bf16[512,256]{1,0:T(8,128)(2,1)S(1)}, f32[512,256]{1,0:T(8,128)S(1)}) custom-call(s32[26]{0:T(128)S(1)} %fusion.places, bf16[800,4096]{1,0:T(8,128)(2,1)S(1)} %get-tuple-element.38.refs_0_.filtered_ref, bf16[800,4096]{1,0:T(8,128)(2,1)S(1)} %get-tuple-element.39.refs_1_.filtered_ref, ...), custom_call_target="tpu_custom_call" | custom-call | flops 1677721600 | bytes 786432 | tf_op jit(solution)/shard_map/image_sum/pallas_call | solution.py:173
  171.6 3.1 %image_sum.12 = (bf16[512,256]{1,0:T(8,128)(2,1)S(1)}, f32[512,256]{1,0:T(8,128)S(1)}) custom-call(s32[26]{0:T(128)S(1)} %fusion.places, bf16[800,4096]{1,0:T(8,128)(2,1)S(1)} %get-tuple-element.38.refs_0_.filtered_ref, bf16[800,4096]{1,0:T(8,128)(2,1)S(1)} %get-tuple-element.39.refs_1_.filtered_ref, ...), custom_call_target="tpu_custom_call" | custom-call | flops 1677721600 | bytes 786432 | tf_op jit(solution)/shard_map/image_sum/pallas_call | solution.py:173
  179.3 3.0 %image_sum.15 = (bf16[512,256]{1,0:T(8,128)(2,1)S(1)}, f32[512,256]{1,0:T(8,128)S(1)}) custom-call(s32[26]{0:T(128)S(1)} %fusion.places, bf16[800,4096]{1,0:T(8,128)(2,1)S(1)} %get-tuple-element.38.refs_0_.filtered_ref, bf16[800,4096]{1,0:T(8,128)(2,1)S(1)} %get-tuple-element.39.refs_1_.filtered_ref, ...), custom_call_target="tpu_custom_call" | custom-call | flops 1677721600 | bytes 786432 | tf_op jit(solution)/shard_map/image_sum/pallas_call | solution.py:173
  183.1 2.9 %image_sum.13 = (bf16[512,256]{1,0:T(8,128)(2,1)S(1)}, f32[512,256]{1,0:T(8,128)S(1)}) custom-call(s32[26]{0:T(128)S(1)} %fusion.places, bf16[800,4096]{1,0:T(8,128)(2,1)S(1)} %get-tuple-element.38.refs_0_.filtered_ref, bf16[800,4096]{1,0:T(8,128)(2,1)S(1)} %get-tuple-element.39.refs_1_.filtered_ref, ...), custom_call_target="tpu_custom_call" | custom-call | flops 1677721600 | bytes 786432 | tf_op jit(solution)/shard_map/image_sum/pallas_call | solution.py:173
  186.1 6.0 %cholesky.3.refs_0_ = f32[256,512]{1,0:T(8,128)S(1)} custom-call(s32[26]{0:T(128)S(1)} %fusion.places, f32[128,256]{1,0:T(8,128)S(1)} %add.128.refs_0_, f32[128,256]{1,0:T(8,128)S(1)} %collective-permute-done.35.refs_1_), custom_call_target="tpu_custom_call" | custom-call | flops 3000000000 | bytes 786432 | tf_op jit(solution)/shard_map/cholesky/pallas_call | solution.py:419
  192.2 3.0 %collective-permute-start.30 = (bf16[512,256]{1,0:T(8,128)(2,1)S(1)}, bf16[512,256]{1,0:T(8,128)(2,1)S(1)}, u32[]{:S(2)}, u32[]{:S(2)}) collective-permute-start(bf16[512,256]{1,0:T(8,128)(2,1)S(1)} %add_convert_fusion), channel_id=1, source_target_pairs={{0,8},{4,12},{8,0},{12,4},{16,24},{20,28},{24,16},{28,20},{1,9},{5... | collective-permute-start | bytes 786440 | tf_op jit(solution)/shard_map/ppermute | solution.py:35
  195.2 6.8 %cholesky.4 = (f32[256,256]{1,0:T(8,128)}, f32[256,256]{1,0:T(8,128)S(1)}) custom-call(s32[26]{0:T(128)S(1)} %fusion.places, f32[256,512]{1,0:T(8,128)S(1)} %cholesky.3.refs_0_), custom_call_target="tpu_custom_call" | custom-call | flops 3000000000 | bytes 786432 | tf_op jit(solution)/shard_map/cholesky/pallas_call | solution.py:419
  202.1 3.8 %collective-permute-done.30.refs_1_ = bf16[512,256]{1,0:T(8,128)(2,1)S(1)} collective-permute-done((bf16[512,256]{1,0:T(8,128)(2,1)S(1)}, bf16[512,256]{1,0:T(8,128)(2,1)S(1)}, u32[]{:S(2)}, u32[]{:S(2)}) %collective-permute-start.30) | collective-permute-done | bytes 262176 | tf_op jit(solution)/shard_map/ppermute | solution.py:35
  215.0 2.7 %collective-permute-done.39 = f32[32,256]{1,0:T(8,128)S(1)} collective-permute-done((f32[32,256]{1,0:T(8,128)S(1)}, f32[32,256]{1,0:T(8,128)S(1)}, u32[]{:S(2)}, u32[]{:S(2)}) %collective-permute-start.39) | collective-permute-done | bytes 32800 | tf_op jit(solution)/shard_map/ppermute | solution.py:35
  231.5 4.3 %collective-permute-done.44 = f32[128,256]{1,0:T(8,128)S(1)} collective-permute-done((f32[128,256]{1,0:T(8,128)S(1)}, f32[128,256]{1,0:T(8,128)S(1)}, u32[]{:S(2)}, u32[]{:S(2)}) %collective-permute-start.44) | collective-permute-done | bytes 131104 | tf_op jit(solution)/shard_map/ppermute | solution.py:35
  237.3 11.6 %collective-permute-done.47.refs_2_ = bf16[512,256]{1,0:T(8,128)(2,1)S(1)} collective-permute-done((bf16[512,256]{1,0:T(8,128)(2,1)S(1)}, bf16[512,256]{1,0:T(8,128)(2,1)S(1)}, u32[]{:S(2)}, u32[]{:S(2)}) %collective-permute-start.47) | collective-permute-done | bytes 262176 | tf_op jit(solution)/shard_map/ppermute | solution.py:35
  249.4 12.2 %cholesky.5 = (f32[256,256]{1,0:T(8,128)}, f32[256,256]{1,0:T(8,128)S(1)}) custom-call(s32[26]{0:T(128)S(1)} %fusion.places, f32[128,256]{1,0:T(8,128)S(1)} %add.133.refs_0_, f32[128,256]{1,0:T(8,128)S(1)} %collective-permute-done.45.refs_1_), custom_call_target="tpu_custom_call" | custom-call | flops 6000000000 | bytes 786432 | tf_op jit(solution)/shard_map/cholesky/pallas_call | solution.py:419
  261.6 4.7 %apply.1 = f32[4096,256]{1,0:T(8,128)} custom-call(s32[26]{0:T(128)S(1)} %fusion.places, f32[256,256]{1,0:T(8,128)S(1)} %get-tuple-element.71.inverse_ref, bf16[512,256]{1,0:T(8,128)(2,1)S(1)} %get-tuple-element.72.refs_0_, bf16[512,256]{1,0:T(8,128)(2,1)S(1)} %collective-permute-done.46.refs_1_, bf16[512,256]{1,0:T(8,128)(2,1)S(1)} %collective-permute-done.47.refs_2_, ...), custom_call_target="tpu_custom_call" | custom-call | flops 1610612736 | bytes 6291456 | tf_op jit(solution)/shard_map/apply/pallas_call | solution.py:460
  (120 shorter events, 70.2 us)
Async XLA Ops:
  13.3 27.0 %collective-permute-start = (bf16[800,256]{1,0:T(8,128)(2,1)S(1)}, bf16[800,256]{1,0:T(8,128)(2,1)S(1)}, u32[]{:S(2)}, u32[]{:S(2)}) collective-permute-start(bf16[800,256]{1,0:T(8,128)(2,1)S(1)} %get-tuple-element.43), channel_id=1, source_target_pairs={{0,3},{1,2},{2,1},{3,0},{4,7},{5,6},{6,5},{7,4},{8,11},{9,10},{10,... | collective-permute-start | bytes 1228808 | tf_op jit(solution)/shard_map/ppermute | solution.py:35
  24.8 15.6 %collective-permute-start.1 = (bf16[800,256]{1,0:T(8,128)(2,1)S(1)}, bf16[800,256]{1,0:T(8,128)(2,1)S(1)}, u32[]{:S(2)}, u32[]{:S(2)}) collective-permute-start(bf16[800,256]{1,0:T(8,128)(2,1)S(1)} %get-tuple-element.44), channel_id=1, source_target_pairs={{0,2},{1,3},{2,0},{3,1},{4,6},{5,7},{6,4},{7,5},{8,10},{9,11},{10,... | collective-permute-start | bytes 1228808 | tf_op jit(solution)/shard_map/ppermute | solution.py:35
  32.8 10.7 %collective-permute-start.2 = (bf16[800,256]{1,0:T(8,128)(2,1)S(1)}, bf16[800,256]{1,0:T(8,128)(2,1)S(1)}, u32[]{:S(2)}, u32[]{:S(2)}) collective-permute-start(bf16[800,256]{1,0:T(8,128)(2,1)S(1)} %get-tuple-element.45), channel_id=1, source_target_pairs={{0,1},{1,0},{2,3},{3,2},{4,5},{5,4},{6,7},{7,6},{8,9},{9,8},{10,11... | collective-permute-start | bytes 1228808 | tf_op jit(solution)/shard_map/ppermute | solution.py:35
  43.7 13.3 %collective-permute-start.5 = (bf16[800,256]{1,0:T(8,128)(2,1)S(1)}, bf16[800,256]{1,0:T(8,128)(2,1)S(1)}, u32[]{:S(2)}, u32[]{:S(2)}) collective-permute-start(bf16[800,256]{1,0:T(8,128)(2,1)S(1)} %multiply_convert_fusion.1.refs_4_), channel_id=1, source_target_pairs={{0,3},{1,2},{2,1},{3,0},{4,7},{5,6},{6,5},{7,4},{8,11},{9,10},{10,... | collective-permute-start | bytes 1228808 | tf_op jit(solution)/shard_map/ppermute | solution.py:35
  45.3 18.0 %collective-permute-start.4 = (bf16[800,256]{1,0:T(8,128)(2,1)S(1)}, bf16[800,256]{1,0:T(8,128)(2,1)S(1)}, u32[]{:S(2)}, u32[]{:S(2)}) collective-permute-start(bf16[800,256]{1,0:T(8,128)(2,1)S(1)} %multiply_convert_fusion.1.refs_4_), channel_id=1, source_target_pairs={{0,2},{1,3},{2,0},{3,1},{4,6},{5,7},{6,4},{7,5},{8,10},{9,11},{10,... | collective-permute-start | bytes 1228808 | tf_op jit(solution)/shard_map/ppermute | solution.py:35
  45.6 17.8 %collective-permute-start.3 = (bf16[800,256]{1,0:T(8,128)(2,1)S(1)}, bf16[800,256]{1,0:T(8,128)(2,1)S(1)}, u32[]{:S(2)}, u32[]{:S(2)}) collective-permute-start(bf16[800,256]{1,0:T(8,128)(2,1)S(1)} %multiply_convert_fusion.1.refs_4_), channel_id=1, source_target_pairs={{0,1},{1,0},{2,3},{3,2},{4,5},{5,4},{6,7},{7,6},{8,9},{9,8},{10,11... | collective-permute-start | bytes 1228808 | tf_op jit(solution)/shard_map/ppermute | solution.py:35
  70.0 11.2 %collective-permute-start.12 = (bf16[512,256]{1,0:T(8,128)(2,1)S(1)}, bf16[512,256]{1,0:T(8,128)(2,1)S(1)}, u32[]{:S(2)}, u32[]{:S(2)}) collective-permute-start(bf16[512,256]{1,0:T(8,128)(2,1)S(1)} %add_convert_fusion.5.refs_8_), channel_id=1, source_target_pairs={{0,24},{4,28},{8,16},{12,20},{16,8},{20,12},{24,0},{28,4},{1,25},{... | collective-permute-start | bytes 786440 | tf_op jit(solution)/shard_map/ppermute | solution.py:35
  76.9 19.2 %collective-permute-start.11 = (bf16[512,256]{1,0:T(8,128)(2,1)S(1)}, bf16[512,256]{1,0:T(8,128)(2,1)S(1)}, u32[]{:S(2)}, u32[]{:S(2)}) collective-permute-start(bf16[512,256]{1,0:T(8,128)(2,1)S(1)} %add_convert_fusion.6.refs_8_), channel_id=1, source_target_pairs={{0,16},{4,20},{8,24},{12,28},{16,0},{20,4},{24,8},{28,12},{1,17},{... | collective-permute-start | bytes 786440 | tf_op jit(solution)/shard_map/ppermute | solution.py:35
  80.6 15.6 %collective-permute-start.10 = (bf16[512,256]{1,0:T(8,128)(2,1)S(1)}, bf16[512,256]{1,0:T(8,128)(2,1)S(1)}, u32[]{:S(2)}, u32[]{:S(2)}) collective-permute-start(bf16[512,256]{1,0:T(8,128)(2,1)S(1)} %add_convert_fusion.4), channel_id=1, source_target_pairs={{0,8},{4,12},{8,0},{12,4},{16,24},{20,28},{24,16},{28,20},{1,9},{5... | collective-permute-start | bytes 786440 | tf_op jit(solution)/shard_map/ppermute | solution.py:35
  96.3 11.1 %collective-permute-start.15 = (bf16[512,256]{1,0:T(8,128)(2,1)S(1)}, bf16[512,256]{1,0:T(8,128)(2,1)S(1)}, u32[]{:S(2)}, u32[]{:S(2)}) collective-permute-start(bf16[512,256]{1,0:T(8,128)(2,1)S(1)} %add_convert_fusion.3.refs_0_), channel_id=1, source_target_pairs={{0,24},{4,28},{8,16},{12,20},{16,8},{20,12},{24,0},{28,4},{1,25},{... | collective-permute-start | bytes 786440 | tf_op jit(solution)/shard_map/ppermute | solution.py:35
  98.8 20.9 %collective-permute-start.14 = (bf16[512,256]{1,0:T(8,128)(2,1)S(1)}, bf16[512,256]{1,0:T(8,128)(2,1)S(1)}, u32[]{:S(2)}, u32[]{:S(2)}) collective-permute-start(bf16[512,256]{1,0:T(8,128)(2,1)S(1)} %add_convert_fusion.3.refs_0_), channel_id=1, source_target_pairs={{0,16},{4,20},{8,24},{12,28},{16,0},{20,4},{24,8},{28,12},{1,17},{... | collective-permute-start | bytes 786440 | tf_op jit(solution)/shard_map/ppermute | solution.py:35
  98.8 20.9 %collective-permute-start.13 = (bf16[512,256]{1,0:T(8,128)(2,1)S(1)}, bf16[512,256]{1,0:T(8,128)(2,1)S(1)}, u32[]{:S(2)}, u32[]{:S(2)}) collective-permute-start(bf16[512,256]{1,0:T(8,128)(2,1)S(1)} %add_convert_fusion.3.refs_0_), channel_id=1, source_target_pairs={{0,8},{4,12},{8,0},{12,4},{16,24},{20,28},{24,16},{28,20},{1,9},{5... | collective-permute-start | bytes 786440 | tf_op jit(solution)/shard_map/ppermute | solution.py:35
  100.8 19.4 %collective-permute-start.16 = (bf16[512,256]{1,0:T(8,128)(2,1)S(1)}, bf16[512,256]{1,0:T(8,128)(2,1)S(1)}, u32[]{:S(2)}, u32[]{:S(2)}) collective-permute-start(bf16[512,256]{1,0:T(8,128)(2,1)S(1)} %add_convert_fusion.3.refs_0_), channel_id=1, source_target_pairs={{0,4},{4,0},{8,12},{12,8},{16,20},{20,16},{24,28},{28,24},{1,5},{5... | collective-permute-start | bytes 786440 | tf_op jit(solution)/shard_map/ppermute | solution.py:35
  107.4 12.7 %collective-permute-start.19 = (bf16[512,256]{1,0:T(8,128)(2,1)S(1)}, bf16[512,256]{1,0:T(8,128)(2,1)S(1)}, u32[]{:S(2)}, u32[]{:S(2)}) collective-permute-start(bf16[512,256]{1,0:T(8,128)(2,1)S(1)} %collective-permute-done.15.refs_3_), channel_id=1, source_target_pairs={{0,4},{4,0},{8,12},{12,8},{16,20},{20,16},{24,28},{28,24},{1,5},{5... | collective-permute-start | bytes 786440 | tf_op jit(solution)/shard_map/ppermute | solution.py:35
  124.0 13.3 %collective-permute-start.20 = (bf16[800,256]{1,0:T(8,128)(2,1)S(1)}, bf16[800,256]{1,0:T(8,128)(2,1)S(1)}, u32[]{:S(2)}, u32[]{:S(2)}) collective-permute-start(bf16[800,256]{1,0:T(8,128)(2,1)S(1)} %score.5), channel_id=1, source_target_pairs={{0,3},{1,2},{2,1},{3,0},{4,7},{5,6},{6,5},{7,4},{8,11},{9,10},{10,... | collective-permute-start | bytes 1228808 | tf_op jit(solution)/shard_map/ppermute | solution.py:35
  127.9 17.4 %collective-permute-start.21 = (bf16[800,256]{1,0:T(8,128)(2,1)S(1)}, bf16[800,256]{1,0:T(8,128)(2,1)S(1)}, u32[]{:S(2)}, u32[]{:S(2)}) collective-permute-start(bf16[800,256]{1,0:T(8,128)(2,1)S(1)} %score.6), channel_id=1, source_target_pairs={{0,2},{1,3},{2,0},{3,1},{4,6},{5,7},{6,4},{7,5},{8,10},{9,11},{10,... | collective-permute-start | bytes 1228808 | tf_op jit(solution)/shard_map/ppermute | solution.py:35
  130.9 14.3 %collective-permute-start.22 = (bf16[800,256]{1,0:T(8,128)(2,1)S(1)}, bf16[800,256]{1,0:T(8,128)(2,1)S(1)}, u32[]{:S(2)}, u32[]{:S(2)}) collective-permute-start(bf16[800,256]{1,0:T(8,128)(2,1)S(1)} %score.7), channel_id=1, source_target_pairs={{0,1},{1,0},{2,3},{3,2},{4,5},{5,4},{6,7},{7,6},{8,9},{9,8},{10,11... | collective-permute-start | bytes 1228808 | tf_op jit(solution)/shard_map/ppermute | solution.py:35
  145.5 13.3 %collective-permute-start.25 = (bf16[800,256]{1,0:T(8,128)(2,1)S(1)}, bf16[800,256]{1,0:T(8,128)(2,1)S(1)}, u32[]{:S(2)}, u32[]{:S(2)}) collective-permute-start(bf16[800,256]{1,0:T(8,128)(2,1)S(1)} %multiply_convert_fusion.refs_4_), channel_id=1, source_target_pairs={{0,3},{1,2},{2,1},{3,0},{4,7},{5,6},{6,5},{7,4},{8,11},{9,10},{10,... | collective-permute-start | bytes 1228808 | tf_op jit(solution)/shard_map/ppermute | solution.py:35
  146.9 19.7 %collective-permute-start.24 = (bf16[800,256]{1,0:T(8,128)(2,1)S(1)}, bf16[800,256]{1,0:T(8,128)(2,1)S(1)}, u32[]{:S(2)}, u32[]{:S(2)}) collective-permute-start(bf16[800,256]{1,0:T(8,128)(2,1)S(1)} %multiply_convert_fusion.refs_4_), channel_id=1, source_target_pairs={{0,2},{1,3},{2,0},{3,1},{4,6},{5,7},{6,4},{7,5},{8,10},{9,11},{10,... | collective-permute-start | bytes 1228808 | tf_op jit(solution)/shard_map/ppermute | solution.py:35
  147.5 19.1 %collective-permute-start.23 = (bf16[800,256]{1,0:T(8,128)(2,1)S(1)}, bf16[800,256]{1,0:T(8,128)(2,1)S(1)}, u32[]{:S(2)}, u32[]{:S(2)}) collective-permute-start(bf16[800,256]{1,0:T(8,128)(2,1)S(1)} %multiply_convert_fusion.refs_4_), channel_id=1, source_target_pairs={{0,1},{1,0},{2,3},{3,2},{4,5},{5,4},{6,7},{7,6},{8,9},{9,8},{10,11... | collective-permute-start | bytes 1228808 | tf_op jit(solution)/shard_map/ppermute | solution.py:35
  177.8 24.2 %collective-permute-start.32 = (bf16[512,256]{1,0:T(8,128)(2,1)S(1)}, bf16[512,256]{1,0:T(8,128)(2,1)S(1)}, u32[]{:S(2)}, u32[]{:S(2)}) collective-permute-start(bf16[512,256]{1,0:T(8,128)(2,1)S(1)} %add_convert_fusion.1.refs_8_), channel_id=1, source_target_pairs={{0,24},{4,28},{8,16},{12,20},{16,8},{20,12},{24,0},{28,4},{1,25},{... | collective-permute-start | bytes 786440 | tf_op jit(solution)/shard_map/ppermute | solution.py:35
  182.4 19.7 %collective-permute-start.31 = (bf16[512,256]{1,0:T(8,128)(2,1)S(1)}, bf16[512,256]{1,0:T(8,128)(2,1)S(1)}, u32[]{:S(2)}, u32[]{:S(2)}) collective-permute-start(bf16[512,256]{1,0:T(8,128)(2,1)S(1)} %add_convert_fusion.2.refs_8_), channel_id=1, source_target_pairs={{0,16},{4,20},{8,24},{12,28},{16,0},{20,4},{24,8},{28,12},{1,17},{... | collective-permute-start | bytes 786440 | tf_op jit(solution)/shard_map/ppermute | solution.py:35
  186.0 16.0 %collective-permute-start.27 = (bf16[512,256]{1,0:T(8,128)(2,1)S(1)}, bf16[512,256]{1,0:T(8,128)(2,1)S(1)}, u32[]{:S(2)}, u32[]{:S(2)}) collective-permute-start(bf16[512,256]{1,0:T(8,128)(2,1)S(1)} %get-tuple-element.57), channel_id=1, source_target_pairs={{0,4},{4,0},{8,12},{12,8},{16,20},{20,16},{24,28},{28,24},{1,5},{5... | collective-permute-start | bytes 786440 | tf_op jit(solution)/shard_map/ppermute | solution.py:35
  192.2 13.7 %collective-permute-start.30 = (bf16[512,256]{1,0:T(8,128)(2,1)S(1)}, bf16[512,256]{1,0:T(8,128)(2,1)S(1)}, u32[]{:S(2)}, u32[]{:S(2)}) collective-permute-start(bf16[512,256]{1,0:T(8,128)(2,1)S(1)} %add_convert_fusion), channel_id=1, source_target_pairs={{0,8},{4,12},{8,0},{12,4},{16,24},{20,28},{24,16},{28,20},{1,9},{5... | collective-permute-start | bytes 786440 | tf_op jit(solution)/shard_map/ppermute | solution.py:35
  226.3 11.0 %collective-permute-start.48 = (bf16[512,256]{1,0:T(8,128)(2,1)S(1)}, bf16[512,256]{1,0:T(8,128)(2,1)S(1)}, u32[]{:S(2)}, u32[]{:S(2)}) collective-permute-start(bf16[512,256]{1,0:T(8,128)(2,1)S(1)} %get-tuple-element.72.refs_0_), channel_id=1, source_target_pairs={{0,24},{4,28},{8,16},{12,20},{16,8},{20,12},{24,0},{28,4},{1,25},{... | collective-permute-start | bytes 786440 | tf_op jit(solution)/shard_map/ppermute | solution.py:35
  228.3 20.6 %collective-permute-start.47 = (bf16[512,256]{1,0:T(8,128)(2,1)S(1)}, bf16[512,256]{1,0:T(8,128)(2,1)S(1)}, u32[]{:S(2)}, u32[]{:S(2)}) collective-permute-start(bf16[512,256]{1,0:T(8,128)(2,1)S(1)} %get-tuple-element.72.refs_0_), channel_id=1, source_target_pairs={{0,16},{4,20},{8,24},{12,28},{16,0},{20,4},{24,8},{28,12},{1,17},{... | collective-permute-start | bytes 786440 | tf_op jit(solution)/shard_map/ppermute | solution.py:35
  229.4 19.5 %collective-permute-start.46 = (bf16[512,256]{1,0:T(8,128)(2,1)S(1)}, bf16[512,256]{1,0:T(8,128)(2,1)S(1)}, u32[]{:S(2)}, u32[]{:S(2)}) collective-permute-start(bf16[512,256]{1,0:T(8,128)(2,1)S(1)} %get-tuple-element.72.refs_0_), channel_id=1, source_target_pairs={{0,8},{4,12},{8,0},{12,4},{16,24},{20,28},{24,16},{28,20},{1,9},{5... | collective-permute-start | bytes 786440 | tf_op jit(solution)/shard_map/ppermute | solution.py:35
  235.8 13.6 %collective-permute-start.45 = (f32[128,256]{1,0:T(8,128)S(1)}, f32[128,256]{1,0:T(8,128)S(1)}, u32[]{:S(2)}, u32[]{:S(2)}) collective-permute-start(f32[128,256]{1,0:T(8,128)S(1)} %add.133.refs_0_), channel_id=1, source_target_pairs={{0,4},{4,0},{8,12},{12,8},{16,20},{20,16},{24,28},{28,24},{1,5},{5... | collective-permute-start | bytes 393224 | tf_op jit(solution)/shard_map/ppermute | solution.py:35
  235.9 25.7 %collective-permute-start.49 = (bf16[512,256]{1,0:T(8,128)(2,1)S(1)}, bf16[512,256]{1,0:T(8,128)(2,1)S(1)}, u32[]{:S(2)}, u32[]{:S(2)}) collective-permute-start(bf16[512,256]{1,0:T(8,128)(2,1)S(1)} %get-tuple-element.72.refs_0_), channel_id=1, source_target_pairs={{0,4},{4,0},{8,12},{12,8},{16,20},{20,16},{24,28},{28,24},{1,5},{5... | collective-permute-start | bytes 786440 | tf_op jit(solution)/shard_map/ppermute | solution.py:35
  237.3 24.3 %collective-permute-start.52 = (bf16[512,256]{1,0:T(8,128)(2,1)S(1)}, bf16[512,256]{1,0:T(8,128)(2,1)S(1)}, u32[]{:S(2)}, u32[]{:S(2)}) collective-permute-start(bf16[512,256]{1,0:T(8,128)(2,1)S(1)} %collective-permute-done.48.refs_3_), channel_id=1, source_target_pairs={{0,4},{4,0},{8,12},{12,8},{16,20},{20,16},{24,28},{28,24},{1,5},{5... | collective-permute-start | bytes 786440 | tf_op jit(solution)/shard_map/ppermute | solution.py:35
  248.9 12.7 %collective-permute-start.51 = (bf16[512,256]{1,0:T(8,128)(2,1)S(1)}, bf16[512,256]{1,0:T(8,128)(2,1)S(1)}, u32[]{:S(2)}, u32[]{:S(2)}) collective-permute-start(bf16[512,256]{1,0:T(8,128)(2,1)S(1)} %collective-permute-done.47.refs_2_), channel_id=1, source_target_pairs={{0,4},{4,0},{8,12},{12,8},{16,20},{20,16},{24,28},{28,24},{1,5},{5... | collective-permute-start | bytes 786440 | tf_op jit(solution)/shard_map/ppermute | solution.py:35
  248.9 12.7 %collective-permute-start.50 = (bf16[512,256]{1,0:T(8,128)(2,1)S(1)}, bf16[512,256]{1,0:T(8,128)(2,1)S(1)}, u32[]{:S(2)}, u32[]{:S(2)}) collective-permute-start(bf16[512,256]{1,0:T(8,128)(2,1)S(1)} %collective-permute-done.46.refs_1_), channel_id=1, source_target_pairs={{0,4},{4,0},{8,12},{12,8},{16,20},{20,16},{24,28},{28,24},{1,5},{5... | collective-permute-start | bytes 786440 | tf_op jit(solution)/shard_map/ppermute | solution.py:35
  (22 other events, 109.2 us)

commit v4 on v2

--- a/solution.py
+++ b/solution.py
@@ -6,6 +6,7 @@
 from jax.experimental import pallas as pl
 from jax.experimental.pallas import tpu as pltpu
 from jax.sharding import PartitionSpec as P
+
 
 ITERS = 2
 F32 = jnp.float32
@@ -98,27 +99,29 @@
 
 
 def score_kernel(first, places, filtered_ref, *refs):
-    *basis_refs, score_ref = refs
+    *basis_refs, top_ref, low_ref = refs
+    rows = top_ref.shape[0]
     width = basis_refs[0].shape[0]
     total = None
     for at, basis_ref in enumerate(basis_refs):
         columns = pl.ds(pl.multiple_of(places[first + at] * width, width), width)
         term = jnp.dot(filtered_ref[:, columns], basis_ref[...], preferred_element_type=F32)
         total = term if total is None else total + term
-    score_ref[...] = total.astype(score_ref.dtype)
-
-
-def score(places, first, filtered, basis, out_type):
+    top_ref[...] = total[:rows].astype(top_ref.dtype)
+    low_ref[...] = total[rows:].astype(low_ref.dtype)
+
+
+def score(places, first, filtered, basis, out_types):
     rows, pixels = filtered.shape
     columns = basis[0].shape[1]
     return pl.pallas_call(
         functools.partial(score_kernel, first),
-        grid_spec=prefetched(1 + len(basis), 1),
-        out_shape=[jax.ShapeDtypeStruct((rows, columns), out_type)],
+        grid_spec=prefetched(1 + len(basis), 2),
+        out_shape=[jax.ShapeDtypeStruct((rows // 2, columns), kind) for kind in out_types],
         compiler_params=vmem(16 * 2**20),
         cost_estimate=cost(2 * rows * pixels * columns, 2 * rows * columns),
         name="score",
-    )(places, filtered, *basis)[0]
+    )(places, filtered, *basis)
 
 
 def sum_blocks(filtered, scaled):
@@ -137,16 +140,72 @@
     return total
 
 
-def image_sum_kernel(count, first, places, *refs):
-    filtered_refs, scaled_refs = refs[:count], refs[count : 2 * count]
-    send_ref, keep_ref = refs[-2:]
-    width = send_ref.shape[0]
+def stack_pieces(stacked_ref, pieces):
+    rows = pieces[0].shape[0]
+    for at, ref in enumerate(pieces):
+        stacked_ref[at * rows : (at + 1) * rows, :] = ref[...]
+
+
+def block_sum(filtered_refs, stacked_ref, columns):
+    rows = filtered_refs[0].shape[0]
+    return sum_blocks(
+        [ref[:, columns] for ref in filtered_refs],
+        [stacked_ref[at * rows : (at + 1) * rows, :] for at in range(len(filtered_refs))],
+    )
+
+
+def early_sum_kernel(count, first, width, places, *refs):
+    filtered_refs, piece_refs = refs[:count], refs[count : 3 * count]
+    before, out_ref, stacked_ref = refs[3 * count : -2], refs[-2], refs[-1]
+    stack_pieces(stacked_ref, piece_refs)
 
     def block(at, carry):
         columns = pl.ds(pl.multiple_of(places[first + at] * width, width), width)
-        total = sum_blocks(
-            [ref[:, columns] for ref in filtered_refs], [ref[...] for ref in scaled_refs]
-        )
+        here = pl.ds(pl.multiple_of(at * width, width), width)
+        total = block_sum(filtered_refs, stacked_ref, columns)
+        for ref in before:
+            total = total + ref[here, :]
+        out_ref[here, :] = total
+        return carry
+
+    lax.fori_loop(0, out_ref.shape[0] // width, block, 0)
+
+
+def sum_grid(count, extra, outs, rows, columns):
+    return pltpu.PrefetchScalarGridSpec(
+        num_scalar_prefetch=1,
+        grid=(),
+        in_specs=[in_vmem()] * (3 * count + extra),
+        out_specs=[in_vmem()] * outs,
+        scratch_shapes=[pltpu.VMEM((count * rows, columns), BF16)],
+    )
+
+
+def early_sum(places, first, filtered, scaled, width, before):
+    count = len(filtered)
+    rows, pixels = filtered[0].shape
+    columns = scaled[0][0].shape[1]
+    return pl.pallas_call(
+        functools.partial(early_sum_kernel, count, first, width),
+        grid_spec=sum_grid(count, len(before), 1, rows, columns),
+        out_shape=[jax.ShapeDtypeStruct((pixels, columns), F32)],
+        compiler_params=vmem(12 * 2**20),
+        cost_estimate=cost(2 * count * rows * pixels * columns, 4 * pixels * columns),
+        name="early_sum",
+    )(places, *filtered, *sum(scaled, []), *before)[0]
+
+
+def late_sum_kernel(count, first, at_early, places, *refs):
+    filtered_refs, piece_refs = refs[:count], refs[count : 3 * count]
+    early_ref = refs[3 * count]
+    send_ref, keep_ref, stacked_ref = refs[-3:]
+    width = send_ref.shape[0]
+    stack_pieces(stacked_ref, piece_refs)
+
+    def block(at, carry):
+        columns = pl.ds(pl.multiple_of(places[first + at] * width, width), width)
+        here = pl.ds(pl.multiple_of((at_early + at) * width, width), width)
+        total = early_ref[here, :] + block_sum(filtered_refs, stacked_ref, columns)
 
         @pl.when(at == 0)
         def _():
@@ -161,21 +220,21 @@
     lax.fori_loop(0, 2, block, 0)
 
 
-def image_sum(places, first, filtered, scaled, width, after):
+def late_sum(places, first, at_early, filtered, scaled, early, width, after):
     count = len(filtered)
     rows = filtered[0].shape[0]
-    columns = scaled[0].shape[1]
-    return pl.pallas_call(
-        functools.partial(image_sum_kernel, count, first),
-        grid_spec=prefetched(2 * count + len(after), 2),
+    columns = scaled[0][0].shape[1]
+    return pl.pallas_call(
+        functools.partial(late_sum_kernel, count, first, at_early),
+        grid_spec=sum_grid(count, 1 + len(after), 2, rows, columns),
         out_shape=[
             jax.ShapeDtypeStruct((width, columns), BF16),
             jax.ShapeDtypeStruct((width, columns), F32),
         ],
-        compiler_params=vmem(16 * 2**20),
+        compiler_params=vmem(12 * 2**20),
         cost_estimate=cost(4 * count * rows * width * columns, 6 * width * columns),
-        name="image_sum",
-    )(places, *filtered, *scaled, *after)
+        name="late_sum",
+    )(places, *filtered, *sum(scaled, []), early, *after)
 
 
 def tree_sum(terms):
@@ -185,20 +244,20 @@
 
 
 def gram_kernel(core_at, places, *refs):
-    *basis_refs, _, half_ref, gram_ref = refs
+    *basis_refs, half_ref, gram_ref = refs
     gram_ref[...] = tree_sum([contract_rows(ref[...], ref[...]) for ref in basis_refs])
     rows = half_ref.shape[0]
     half_ref[...] = gram_ref[pl.ds(pl.multiple_of(places[core_at] * rows, rows), rows), :]
 
 
-def half_gram(places, core_at, basis, after):
+def half_gram(places, core_at, basis):
     rows, columns = basis[0].shape
     return pl.pallas_call(
         functools.partial(gram_kernel, core_at),
         grid_spec=pltpu.PrefetchScalarGridSpec(
             num_scalar_prefetch=1,
             grid=(),
-            in_specs=[in_vmem()] * (len(basis) + 1),
+            in_specs=[in_vmem()] * len(basis),
             out_specs=[in_vmem()],
             scratch_shapes=[pltpu.VMEM((columns, columns), F32)],
         ),
@@ -206,7 +265,7 @@
         compiler_params=vmem(12 * 2**20),
         cost_estimate=cost(2 * len(basis) * rows * columns * columns, 2 * len(basis) * rows * columns),
         name="gram",
-    )(places, *basis, after)[0]
+    )(places, *basis)[0]
 
 
 def normalize_kernel(core_at, scale, places, *refs):
@@ -419,36 +478,45 @@
     return state
 
 
-def apply_kernel(places, inverse_ref, *refs):
+def apply_kernel(first, places, inverse_ref, *refs):
     *basis_refs, out_ref = refs
     parts = split_in_three(inverse_ref[...])
-    for at, basis_ref in enumerate(basis_refs):
-
-        @pl.when(pl.program_id(0) == at)
+    rows = basis_refs[0].shape[0]
+    span = out_ref.shape[0] // rows
+    for step in range(len(basis_refs) // span):
+
+        @pl.when(pl.program_id(0) == step)
         def _():
-            block = basis_ref[...]
-            out_ref[...] = sum(
-                lax.dot_general(
-                    block, part, (((1,), (1,)), ((), ())), preferred_element_type=F32
+            for at in range(step * span, (step + 1) * span):
+                block = basis_refs[at][...]
+                here = pl.multiple_of((places[first + at] % span) * rows, rows)
+                out_ref[pl.ds(here, rows), :] = sum(
+                    lax.dot_general(
+                        block, part, (((1,), (1,)), ((), ())), preferred_element_type=F32
+                    )
+                    for part in reversed(parts)
                 )
-                for part in reversed(parts)
-            )
 
 
 def apply_inverse(places, first, inverse, basis):
     rows, columns = basis[0].shape
-    blocks = len(basis)
-    return pl.pallas_call(
-        apply_kernel,
+    span = 2
+    steps = len(basis) // span
+    return pl.pallas_call(
+        functools.partial(apply_kernel, first),
         grid_spec=pltpu.PrefetchScalarGridSpec(
             num_scalar_prefetch=1,
-            grid=(blocks,),
-            in_specs=[in_vmem()] * (1 + blocks),
-            out_specs=pl.BlockSpec((rows, columns), lambda i, places: (places[first + i], 0)),
+            grid=(steps,),
+            in_specs=[in_vmem()] * (1 + len(basis)),
+            out_specs=pl.BlockSpec(
+                (span * rows, columns), lambda i, places: (places[first + span * i] // span, 0)
+            ),
         ),
-        out_shape=jax.ShapeDtypeStruct((rows * blocks, columns), F32),
+        out_shape=jax.ShapeDtypeStruct((rows * len(basis), columns), F32),
         compiler_params=vmem(16 * 2**20),
-        cost_estimate=cost(6 * rows * blocks * columns * columns, 6 * rows * blocks * columns),
+        cost_estimate=cost(
+            6 * rows * len(basis) * columns * columns, 6 * rows * len(basis) * columns
+        ),
         name="apply",
     )(places, inverse, *basis)
 
@@ -472,6 +540,60 @@
     return table, rows, gathered, pairs, cores, levels
 
 
+def level_order(depth):
+    middle = depth // 2
+    return [middle] + [s for s in range(depth - 1, 0, -1) if s != middle] + [0]
+
+
+def add_over_pix(value, pix):
+    parts = [value] + [xor_swap(value, "pix", s) for s in range(1, pix)]
+    return tree_sum(parts)
+
+
+def row_halves(value):
+    rows = value.shape[0] // 2
+    return [value[:rows], value[rows:]]
+
+
+def spread(share, pix):
+    def swap(value, shift):
+        return xor_swap(value, "pix", shift)
+
+    if pix != 4:
+        return [share] + [[swap(half, s) for half in share] for s in range(1, pix)]
+    top, low = share
+    x_top, y_low = swap(top, 1), swap(low, 2)
+    x_low, y_top = swap(low, 1), swap(top, 2)
+    far = [swap(x_top, 2), swap(y_low, 1)]
+    return [share, [x_top, x_low], [y_top, y_low], far]
+
+
+def add_round(total, part):
+    return (total + part.astype(F32)).astype(BF16)
+
+
+def score_and_scatter(places, gathered_at, filtered, basis, pix):
+    def scores(shift, *kinds):
+        return score(places, gathered_at, filtered[shift], basis, kinds)
+
+    def swap(value, shift):
+        return xor_swap(value, "pix", shift)
+
+    if pix != 4:
+        arrived = [[swap(half, s) for half in scores(s, BF16, BF16)] for s in range(pix - 1, 0, -1)]
+        return scores(0, F32, F32), arrived
+    far = scores(3, BF16, BF16)
+    by_x, by_y = swap(far[0], 1), swap(far[1], 2)
+    x_top, x_low = scores(1, BF16, F32)
+    from_x = [swap(x_top, 1), None]
+    y_top, y_low = scores(2, F32, BF16)
+    from_y = [None, swap(y_low, 2)]
+    own = scores(0, F32, F32)
+    from_y[0] = swap(add_round(y_top, by_x), 2)
+    from_x[1] = swap(add_round(x_low, by_y), 1)
+    return own, [from_x, from_y]
+
+
 def per_device(images, classes, ctf_table, weights, probes):
     images_here, pixels = images.shape
     pix, img = lax.axis_size("pix"), lax.axis_size("img")
@@ -485,7 +607,7 @@
     )
     weight_share = lax.dynamic_slice_in_dim(weights, me * chunk, chunk, 0)
     places = places + (weight_share[0] > 2.0).astype(jnp.int32)
-    weight_share = weight_share[:, None]
+    weight_share = row_halves(weight_share[:, None])
 
     shifts = list(range(pix - 1, -1, -1))
     filtered, own, arrived = [None] * pix, None, []
@@ -503,23 +625,36 @@
             BF16 if shift else F32,
         )
         if shift:
-            arrived.append(xor_swap(part, "pix", shift))
+            arrived.append(row_halves(xor_swap(part, "pix", shift)))
         else:
-            own = part
+            own = row_halves(part)
 
     basis = inverse = None
     for sweep in range(ITERS):
-        shares = own
-        for part in arrived:
-            shares = shares + part.astype(F32)
-        share_weights = weight_share if sweep == 0 else weight_share * RANGE
-        scaled_share = (share_weights * shares).astype(BF16)
-        scaled = [scaled_share] + [xor_swap(scaled_share, "pix", s) for s in range(1, pix)]
-
+        share = []
+        for at in (0, 1):
+            total = own[at]
+            for part in arrived:
+                total = total + part[at].astype(F32)
+            here = weight_share[at] if sweep == 0 else weight_share[at] * RANGE
+            share.append((here * total).astype(BF16))
+        scaled = spread(share, pix)
+
+        early = early_sum(places, pairs_at, filtered[:1], scaled[:1], width, [])
+        split = pix // 2
+        if split > 1:
+            early = early_sum(places, pairs_at, filtered[1:split], scaled[1:split], width, [early])
         parts, after = [None] * depth, []
-        for s in range(depth - 1, -1, -1):
-            send, keep = image_sum(
-                places, pairs_at + 2 * s, filtered, scaled, width, after[-2:-1]
+        for s in level_order(depth):
+            send, keep = late_sum(
+                places,
+                pairs_at + 2 * s,
+                2 * s,
+                filtered[split:],
+                scaled[split:],
+                early,
+                width,
+                after[-2:-1],
             )
             both = keep + xor_swap(send, "img", 1).astype(F32)
             if s:
@@ -530,39 +665,31 @@
             after.append(both)
 
         if sweep == ITERS - 1:
-            half = half_gram(places, cores_at, basis, scaled[-1])
-            step = 1
-            while step < pix:
-                half = half + xor_swap(half, "pix", step)
-                step *= 2
-            _, inverse = cholesky_and_inverse(
-                places, cores_at, [half, xor_swap(half, "img", 1)], 2
-            )
+            gram = half_gram(places, cores_at, basis)
+            gram = add_over_pix(gram, pix)
+            other = xor_swap(gram, "img", 1)
+            _, inverse = cholesky_and_inverse(places, cores_at, [gram, other], 2)
             break
+
         total = parts[0]
         for part in parts[1:]:
             total = total + part.astype(F32)
-        half = total.astype(BF16)
-        near = [half] + [xor_swap(half, "img", 2 * s) for s in range(1, depth)]
+        block = total.astype(BF16)
+        near = [block] + [xor_swap(block, "img", 2 * s) for s in range(1, depth)]
         basis = near + [xor_swap(block, "img", 1) for block in near]
 
-        own, arrived = None, []
-        for shift in shifts:
-            part = score(places, gathered_at, filtered[shift], basis, BF16 if shift else F32)
-            if shift:
-                arrived.append(xor_swap(part, "pix", shift))
-            else:
-                own = part
+        own, arrived = score_and_scatter(places, gathered_at, filtered, basis, pix)
 
     half, send, keep = normalize_and_gram(places, cores_at, parts, inverse, 1.0 / RANGE)
     pieces = scatter_rows(places, levels_at, keep, xor_swap(send, "img", 1), depth)
     mine = tree_sum([pieces[0]] + [xor_swap(pieces[s], "img", 2 * s) for s in range(1, depth)])
-    mine = tree_sum([mine] + [xor_swap(mine, "pix", s) for s in range(1, pix)])
     pieces = [mine] + [xor_swap(mine, "img", 2 * s) for s in range(1, depth)]
     gram, half = gather_rows(places, levels_at, pieces, half)
+    gram = add_over_pix(gram, pix)
+    other = xor_swap(gram, "img", 1)
     near = [half] + [xor_swap(half, "img", 2 * s) for s in range(1, depth)]
     basis = near + [xor_swap(block, "img", 1) for block in near]
-    factor, inverse = cholesky_and_inverse(places, cores_at, [gram, xor_swap(gram, "img", 1)], 1)
+    factor, inverse = cholesky_and_inverse(places, cores_at, [gram, other], 1)
     return apply_inverse(places, gathered_at, inverse, basis), factor
 
 
@@ -572,7 +699,7 @@
     filtered = (images.astype(F32) * filters).astype(BF16)
     current = probes
     factor = None
-    for sweep in range(ITERS):
+    for _ in range(ITERS):
         share_rows = filtered.shape[0] // lax.axis_size("pix")
         shares = lax.psum_scatter(
             jnp.dot(filtered, current.astype(BF16), preferred_element_type=F32),
@@ -596,20 +723,22 @@
     return n > 1 and n & (n - 1) == 0
 
 
-def per_device_of(images, classes, ctf_table, weights, probes):
-    rows, pixels = images.shape
-    pix, img = lax.axis_size("pix"), lax.axis_size("img")
-    columns = probes.shape[1]
-    fits = (
+def fits(rows, pixels, columns, pix, img):
+    return (
         power_of_two(pix)
         and power_of_two(img)
-        and rows % (16 * pix) == 0
+        and rows % (32 * pix) == 0
         and pixels % (LANES * img) == 0
         and columns % LANES == 0
         and columns % (8 * img) == 0
     )
-    run = per_device if fits else plain_per_device
-    return run(images, classes, ctf_table, weights, probes)
+
+
+def per_device_of(images, classes, ctf_table, weights, probes):
+    pix, img = lax.axis_size("pix"), lax.axis_size("img")
+    if not fits(*images.shape, probes.shape[1], pix, img):
+        return plain_per_device(images, classes, ctf_table, weights, probes)
+    return per_device(images, classes, ctf_table, weights, probes)
 
 
 def solution(mesh):

time: 273 us -> 274 us (level)
  waiting for transfers between devices: 115 us -> 91.9 us
  starting transfers between devices: 51.1 us -> 66.1 us
  Pallas kernels: 98.7 us -> 108 us
    ppermute x54 -> x64, waiting for transfers between devices: 115 us -> 91.9 us  [xor_swap(): return lax.ppermute(value, axis, [(i, i ^ mask) for i in range(size)])]
    ppermute x54 -> x64, starting transfers between devices: 51.1 us -> 66.1 us  [xor_swap(): return lax.ppermute(value, axis, [(i, i ^ mask) for i in range(size)])]
    pallas_call x9 -> x13, Pallas kernels: 30.6 us -> 40.1 us  [the longest x4 18 us: early_sum(): pl.pallas_call(functools.partial(early_sum_kernel, count, first, width),...]
  transfers between devices with their start and end apart: 54 -> 64, of which waited for: 26 -> 24; matrix products, arithmetic and copies ran while one was open for 0% -> 0% of each run, Pallas kernels for 27% -> 33%
where the time goes in v4:
time: 274 us; the launch traced here: 273 us
  Pallas kernels  108 us (39%)
  waiting for transfers between devices  91.9 us (34%)
  starting transfers between devices  66.1 us (24%)
  other arithmetic  3.76 us (1%)
    ppermute x64, waiting for transfers between devices, xor_swap(): return lax.ppermute(value, axis, [(i, i ^ mask) for i in range(size)])  91.9 us
    ppermute x64, starting transfers between devices, xor_swap(): return lax.ppermute(value, axis, [(i, i ^ mask) for i in range(size)])  66.1 us
    pallas_call x4, Pallas kernels, filter_and_score(): pl.pallas_call(filter_kernel, grid_spec=pltpu.PrefetchScalarGridSpec(num_...  29.7 us
    pallas_call x3, Pallas kernels, cholesky_and_inverse(): pl.pallas_call(functools.partial(cholesky_kernel, first, last, place_at),...  25 us
    pallas_call x4, Pallas kernels, early_sum(): pl.pallas_call(functools.partial(early_sum_kernel, count, first, width),...  18 us
    pallas_call x8, Pallas kernels, late_sum(): pl.pallas_call(functools.partial(late_sum_kernel, count, first, at_early)...  17.5 us
    pallas_call x4, Pallas kernels, score(): pl.pallas_call(functools.partial(score_kernel, first), grid_spec=prefetch...  9.61 us
  transfers between devices with their start and end apart: 64, of which 24 were waited for; matrix products, arithmetic and copies ran while one was open for 0% of the time, Pallas kernels for 33%

profile of v4, /device:TPU:0, one launch (start us, length us, event | category | flops | bytes accessed | tf_op | source)
XLA Modules:
  0.0 273.3 jit_solution(10609754847809171734)
XLA Ops:
  5.2 7.4 %filter_and_score.5 = (bf16[800,4096]{1,0:T(8,128)(2,1)S(1)}, bf16[800,256]{1,0:T(8,128)(2,1)S(1)}) custom-call(s32[26]{0:T(128)S(1)} %fusion.places, s32[8,1,400]{2,1,0:T(1,128)S(1)} %reshape.22.class_ref, bf16[3200,4096]{1,0:T(8,128)(2,1)} %image_ref.7, bf16[64,4096]{1,0:T(8,128)(2,1)S(1)} %copy-done, bf16[4096,256]{1,0:T(8,128)(2,1)S(1)} %convert_element_type.119.probe_ref), custom_call_target="tpu_custom_call" | custom-call | flops 3355443200 | bytes 6553600 | tf_op jit(solution)/shard_map/filter_and_score/pallas_call | solution.py:69
  12.6 4.0 %collective-permute-start = (bf16[800,256]{1,0:T(8,128)(2,1)S(1)}, bf16[800,256]{1,0:T(8,128)(2,1)S(1)}, u32[]{:S(2)}, u32[]{:S(2)}) collective-permute-start(bf16[800,256]{1,0:T(8,128)(2,1)S(1)} %get-tuple-element.50), channel_id=1, source_target_pairs={{0,3},{1,2},{2,1},{3,0},{4,7},{5,6},{6,5},{7,4},{8,11},{9,10},{10,... | collective-permute-start | bytes 1228808 | tf_op jit(solution)/shard_map/ppermute | solution.py:34
  16.6 7.4 %filter_and_score.4 = (bf16[800,4096]{1,0:T(8,128)(2,1)S(1)}, bf16[800,256]{1,0:T(8,128)(2,1)S(1)}) custom-call(s32[26]{0:T(128)S(1)} %fusion.places, s32[8,1,400]{2,1,0:T(1,128)S(1)} %reshape.22.class_ref, bf16[3200,4096]{1,0:T(8,128)(2,1)} %image_ref.7, bf16[64,4096]{1,0:T(8,128)(2,1)S(1)} %copy-done, bf16[4096,256]{1,0:T(8,128)(2,1)S(1)} %convert_element_type.119.probe_ref), custom_call_target="tpu_custom_call" | custom-call | flops 3355443200 | bytes 6553600 | tf_op jit(solution)/shard_map/filter_and_score/pallas_call | solution.py:69
  24.6 7.4 %filter_and_score.7 = (bf16[800,4096]{1,0:T(8,128)(2,1)S(1)}, bf16[800,256]{1,0:T(8,128)(2,1)S(1)}) custom-call(s32[26]{0:T(128)S(1)} %fusion.places, s32[8,1,400]{2,1,0:T(1,128)S(1)} %reshape.22.class_ref, bf16[3200,4096]{1,0:T(8,128)(2,1)} %image_ref.7, bf16[64,4096]{1,0:T(8,128)(2,1)S(1)} %copy-done, bf16[4096,256]{1,0:T(8,128)(2,1)S(1)} %convert_element_type.119.probe_ref), custom_call_target="tpu_custom_call" | custom-call | flops 3355443200 | bytes 6553600 | tf_op jit(solution)/shard_map/filter_and_score/pallas_call | solution.py:69
  32.3 7.4 %filter_and_score.6 = (bf16[800,4096]{1,0:T(8,128)(2,1)S(1)}, f32[800,256]{1,0:T(8,128)S(1)}) custom-call(s32[26]{0:T(128)S(1)} %fusion.places, s32[8,1,400]{2,1,0:T(1,128)S(1)} %reshape.22.class_ref, bf16[3200,4096]{1,0:T(8,128)(2,1)} %image_ref.7, bf16[64,4096]{1,0:T(8,128)(2,1)S(1)} %copy-done, bf16[4096,256]{1,0:T(8,128)(2,1)S(1)} %convert_element_type.119.probe_ref), custom_call_target="tpu_custom_call" | custom-call | flops 3355443200 | bytes 6553600 | tf_op jit(solution)/shard_map/filter_and_score/pallas_call | solution.py:69
  39.7 3.0 %collective-permute-done.2 = bf16[800,256]{1,0:T(8,128)(2,1)S(1)} collective-permute-done((bf16[800,256]{1,0:T(8,128)(2,1)S(1)}, bf16[800,256]{1,0:T(8,128)(2,1)S(1)}, u32[]{:S(2)}, u32[]{:S(2)}) %collective-permute-start.2) | collective-permute-done | bytes 409632 | tf_op jit(solution)/shard_map/ppermute | solution.py:34
  47.1 3.9 %collective-permute-done.5.refs_1_ = bf16[400,256]{1,0:T(8,128)(2,1)S(1)} collective-permute-done((bf16[400,256]{1,0:T(8,128)(2,1)S(1)}, bf16[400,256]{1,0:T(8,128)(2,1)S(1)}, u32[]{:S(2)}, u32[]{:S(2)}) %collective-permute-start.5) | collective-permute-done | bytes 204832 | tf_op jit(solution)/shard_map/ppermute | solution.py:34
  53.1 4.5 %early_sum.4.refs_3_ = f32[4096,256]{1,0:T(8,128)S(1)} custom-call(s32[26]{0:T(128)S(1)} %fusion.places, bf16[800,4096]{1,0:T(8,128)(2,1)S(1)} %get-tuple-element.48.refs_0_.filtered_ref, bf16[400,256]{1,0:T(8,128)(2,1)S(1)} %get-tuple-element.91.refs_1_, bf16[400,256]{1,0:T(8,128)(2,1)S(1)} %get-tuple-element.90.refs_2_), custom_call_target="tpu_custom_call" | custom-call | flops 1677721600 | bytes 4194304 | tf_op jit(solution)/shard_map/early_sum/pallas_call | solution.py:188
  57.6 4.5 %early_sum.5.refs_6_ = f32[4096,256]{1,0:T(8,128)S(1)} custom-call(s32[26]{0:T(128)S(1)} %fusion.places, bf16[800,4096]{1,0:T(8,128)(2,1)S(1)} %get-tuple-element.53.refs_0_.filtered_ref, bf16[400,256]{1,0:T(8,128)(2,1)S(1)} %collective-permute-done.5.refs_1_, bf16[400,256]{1,0:T(8,128)(2,1)S(1)} %collective-permute-done.8.refs_2_, ...), custom_call_target="tpu_custom_call" | custom-call | flops 1677721600 | bytes 4194304 | tf_op jit(solution)/shard_map/early_sum/pallas_call | solution.py:188
  67.3 2.7 collective-permute-start.14
  77.4 11.3 %collective-permute-done.14 = bf16[512,256]{1,0:T(8,128)(2,1)S(1)} collective-permute-done((bf16[512,256]{1,0:T(8,128)(2,1)S(1)}, bf16[512,256]{1,0:T(8,128)(2,1)S(1)}, u32[]{:S(2)}, u32[]{:S(2)}) %collective-permute-start.14) | collective-permute-done | bytes 262176 | tf_op jit(solution)/shard_map/ppermute | solution.py:34
  88.7 4.6 %collective-permute-done.13 = bf16[512,256]{1,0:T(8,128)(2,1)S(1)} collective-permute-done((bf16[512,256]{1,0:T(8,128)(2,1)S(1)}, bf16[512,256]{1,0:T(8,128)(2,1)S(1)}, u32[]{:S(2)}, u32[]{:S(2)}) %collective-permute-start.13) | collective-permute-done | bytes 262176 | tf_op jit(solution)/shard_map/ppermute | solution.py:34
  94.3 3.3 %collective-permute-start.17 = (bf16[512,256]{1,0:T(8,128)(2,1)S(1)}, bf16[512,256]{1,0:T(8,128)(2,1)S(1)}, u32[]{:S(2)}, u32[]{:S(2)}) collective-permute-start(bf16[512,256]{1,0:T(8,128)(2,1)S(1)} %add_convert_fusion.3.refs_0_), channel_id=1, source_target_pairs={{0,16},{4,20},{8,24},{12,28},{16,0},{20,4},{24,8},{28,12},{1,17},{... | collective-permute-start | bytes 786440 | tf_op jit(solution)/shard_map/ppermute | solution.py:34
  97.9 9.1 %collective-permute-done.16.refs_1_ = bf16[512,256]{1,0:T(8,128)(2,1)S(1)} collective-permute-done((bf16[512,256]{1,0:T(8,128)(2,1)S(1)}, bf16[512,256]{1,0:T(8,128)(2,1)S(1)}, u32[]{:S(2)}, u32[]{:S(2)}) %collective-permute-start.16) | collective-permute-done | bytes 262176 | tf_op jit(solution)/shard_map/ppermute | solution.py:34
  107.0 9.0 %collective-permute-done.17.refs_2_ = bf16[512,256]{1,0:T(8,128)(2,1)S(1)} collective-permute-done((bf16[512,256]{1,0:T(8,128)(2,1)S(1)}, bf16[512,256]{1,0:T(8,128)(2,1)S(1)}, u32[]{:S(2)}, u32[]{:S(2)}) %collective-permute-start.17) | collective-permute-done | bytes 262176 | tf_op jit(solution)/shard_map/ppermute | solution.py:34
  136.2 4.2 %collective-permute-done.24 = bf16[400,256]{1,0:T(8,128)(2,1)S(1)} collective-permute-done((bf16[400,256]{1,0:T(8,128)(2,1)S(1)}, bf16[400,256]{1,0:T(8,128)(2,1)S(1)}, u32[]{:S(2)}, u32[]{:S(2)}) %collective-permute-start.24) | collective-permute-done | bytes 204832 | tf_op jit(solution)/shard_map/ppermute | solution.py:34
  142.6 4.6 %collective-permute-done.28 = bf16[400,256]{1,0:T(8,128)(2,1)S(1)} collective-permute-done((bf16[400,256]{1,0:T(8,128)(2,1)S(1)}, bf16[400,256]{1,0:T(8,128)(2,1)S(1)}, u32[]{:S(2)}, u32[]{:S(2)}) %collective-permute-start.28) | collective-permute-done | bytes 204832 | tf_op jit(solution)/shard_map/ppermute | solution.py:34
  151.6 2.9 %collective-permute-done.25 = bf16[400,256]{1,0:T(8,128)(2,1)S(1)} collective-permute-done((bf16[400,256]{1,0:T(8,128)(2,1)S(1)}, bf16[400,256]{1,0:T(8,128)(2,1)S(1)}, u32[]{:S(2)}, u32[]{:S(2)}) %collective-permute-start.25) | collective-permute-done | bytes 204832 | tf_op jit(solution)/shard_map/ppermute | solution.py:34
  163.3 4.5 %early_sum.6.refs_3_ = f32[4096,256]{1,0:T(8,128)S(1)} custom-call(s32[26]{0:T(128)S(1)} %fusion.places, bf16[800,4096]{1,0:T(8,128)(2,1)S(1)} %get-tuple-element.48.refs_0_.filtered_ref, bf16[400,256]{1,0:T(8,128)(2,1)S(1)} %multiply_convert_fusion.1.refs_1_, bf16[400,256]{1,0:T(8,128)(2,1)S(1)} %multiply_convert_fusion.refs_2_), custom_call_target="tpu_custom_call" | custom-call | flops 1677721600 | bytes 4194304 | tf_op jit(solution)/shard_map/early_sum/pallas_call | solution.py:188
  167.8 4.5 %early_sum.7.refs_6_ = f32[4096,256]{1,0:T(8,128)S(1)} custom-call(s32[26]{0:T(128)S(1)} %fusion.places, bf16[800,4096]{1,0:T(8,128)(2,1)S(1)} %get-tuple-element.53.refs_0_.filtered_ref, bf16[400,256]{1,0:T(8,128)(2,1)S(1)} %collective-permute-done.31.refs_1_, bf16[400,256]{1,0:T(8,128)(2,1)S(1)} %collective-permute-done.34.refs_2_, ...), custom_call_target="tpu_custom_call" | custom-call | flops 1677721600 | bytes 4194304 | tf_op jit(solution)/shard_map/early_sum/pallas_call | solution.py:188
  174.8 6.0 %cholesky.3.refs_0_ = f32[256,512]{1,0:T(8,128)S(1)} custom-call(s32[26]{0:T(128)S(1)} %fusion.places, f32[128,256]{1,0:T(8,128)S(1)} %add_add_fusion.1.refs_0_, f32[128,256]{1,0:T(8,128)S(1)} %collective-permute-done.45.refs_1_), custom_call_target="tpu_custom_call" | custom-call | flops 3000000000 | bytes 786432 | tf_op jit(solution)/shard_map/cholesky/pallas_call | solution.py:464
  183.6 6.1 %collective-permute-start.40 = (bf16[512,256]{1,0:T(8,128)(2,1)S(1)}, bf16[512,256]{1,0:T(8,128)(2,1)S(1)}, u32[]{:S(2)}, u32[]{:S(2)}) collective-permute-start(bf16[512,256]{1,0:T(8,128)(2,1)S(1)} %add_convert_fusion.1.refs_7_), channel_id=1, source_target_pairs={{0,16},{4,20},{8,24},{12,28},{16,0},{20,4},{24,8},{28,12},{1,17},{... | collective-permute-start | bytes 786440 | tf_op jit(solution)/shard_map/ppermute | solution.py:34
  195.8 6.8 %cholesky.4 = (f32[256,256]{1,0:T(8,128)}, f32[256,256]{1,0:T(8,128)S(1)}) custom-call(s32[26]{0:T(128)S(1)} %fusion.places, f32[256,512]{1,0:T(8,128)S(1)} %cholesky.3.refs_0_), custom_call_target="tpu_custom_call" | custom-call | flops 3000000000 | bytes 786432 | tf_op jit(solution)/shard_map/cholesky/pallas_call | solution.py:464
  202.7 5.4 %collective-permute-done.40.refs_2_ = bf16[512,256]{1,0:T(8,128)(2,1)S(1)} collective-permute-done((bf16[512,256]{1,0:T(8,128)(2,1)S(1)}, bf16[512,256]{1,0:T(8,128)(2,1)S(1)}, u32[]{:S(2)}, u32[]{:S(2)}) %collective-permute-start.40) | collective-permute-done | bytes 262176 | tf_op jit(solution)/shard_map/ppermute | solution.py:34
  208.2 4.9 %collective-permute-done.39.refs_1_ = bf16[512,256]{1,0:T(8,128)(2,1)S(1)} collective-permute-done((bf16[512,256]{1,0:T(8,128)(2,1)S(1)}, bf16[512,256]{1,0:T(8,128)(2,1)S(1)}, u32[]{:S(2)}, u32[]{:S(2)}) %collective-permute-start.39) | collective-permute-done | bytes 262176 | tf_op jit(solution)/shard_map/ppermute | solution.py:34
  224.2 3.2 %collective-permute-start.51 = (f32[32,256]{1,0:T(8,128)S(1)}, f32[32,256]{1,0:T(8,128)S(1)}, u32[]{:S(2)}, u32[]{:S(2)}) collective-permute-start(f32[32,256]{1,0:T(8,128)S(1)} %add_add_fusion.2.refs_0_), channel_id=1, source_target_pairs={{0,16},{4,20},{8,24},{12,28},{16,0},{20,4},{24,8},{28,12},{1,17},{... | collective-permute-start | bytes 98312 | tf_op jit(solution)/shard_map/ppermute | solution.py:34
  229.2 3.8 %collective-permute-done.52.refs_3_ = f32[32,256]{1,0:T(8,128)S(1)} collective-permute-done((f32[32,256]{1,0:T(8,128)S(1)}, f32[32,256]{1,0:T(8,128)S(1)}, u32[]{:S(2)}, u32[]{:S(2)}) %collective-permute-start.52) | collective-permute-done | bytes 32800 | tf_op jit(solution)/shard_map/ppermute | solution.py:34
  238.9 2.6 collective-permute-start.59
  242.2 5.9 %collective-permute-done.57.refs_1_ = bf16[512,256]{1,0:T(8,128)(2,1)S(1)} collective-permute-done((bf16[512,256]{1,0:T(8,128)(2,1)S(1)}, bf16[512,256]{1,0:T(8,128)(2,1)S(1)}, u32[]{:S(2)}, u32[]{:S(2)}) %collective-permute-start.57) | collective-permute-done | bytes 262176 | tf_op jit(solution)/shard_map/ppermute | solution.py:34
  248.1 7.8 %collective-permute-done.58.refs_2_ = bf16[512,256]{1,0:T(8,128)(2,1)S(1)} collective-permute-done((bf16[512,256]{1,0:T(8,128)(2,1)S(1)}, bf16[512,256]{1,0:T(8,128)(2,1)S(1)}, u32[]{:S(2)}, u32[]{:S(2)}) %collective-permute-start.58) | collective-permute-done | bytes 262176 | tf_op jit(solution)/shard_map/ppermute | solution.py:34
  256.5 12.2 %cholesky.5 = (f32[256,256]{1,0:T(8,128)}, f32[256,256]{1,0:T(8,128)S(1)}) custom-call(s32[26]{0:T(128)S(1)} %fusion.places, f32[128,256]{1,0:T(8,128)S(1)} %add_add_fusion.refs_0_, f32[128,256]{1,0:T(8,128)S(1)} %collective-permute-done.56.refs_1_), custom_call_target="tpu_custom_call" | custom-call | flops 6000000000 | bytes 786432 | tf_op jit(solution)/shard_map/cholesky/pallas_call | solution.py:464
  268.7 4.7 %apply.1 = f32[4096,256]{1,0:T(8,128)} custom-call(s32[26]{0:T(128)S(1)} %fusion.places, f32[256,256]{1,0:T(8,128)S(1)} %get-tuple-element.87.inverse_ref, bf16[512,256]{1,0:T(8,128)(2,1)S(1)} %get-tuple-element.88.refs_0_, bf16[512,256]{1,0:T(8,128)(2,1)S(1)} %collective-permute-done.57.refs_1_, bf16[512,256]{1,0:T(8,128)(2,1)S(1)} %collective-permute-done.58.refs_2_, ...), custom_call_target="tpu_custom_call" | custom-call | flops 1610612736 | bytes 6291456 | tf_op jit(solution)/shard_map/apply/pallas_call | solution.py:505
  (150 shorter events, 91.7 us)
Async XLA Ops:
  12.6 27.1 %collective-permute-start = (bf16[800,256]{1,0:T(8,128)(2,1)S(1)}, bf16[800,256]{1,0:T(8,128)(2,1)S(1)}, u32[]{:S(2)}, u32[]{:S(2)}) collective-permute-start(bf16[800,256]{1,0:T(8,128)(2,1)S(1)} %get-tuple-element.50), channel_id=1, source_target_pairs={{0,3},{1,2},{2,1},{3,0},{4,7},{5,6},{6,5},{7,4},{8,11},{9,10},{10,... | collective-permute-start | bytes 1228808 | tf_op jit(solution)/shard_map/ppermute | solution.py:34
  24.1 15.7 %collective-permute-start.1 = (bf16[800,256]{1,0:T(8,128)(2,1)S(1)}, bf16[800,256]{1,0:T(8,128)(2,1)S(1)}, u32[]{:S(2)}, u32[]{:S(2)}) collective-permute-start(bf16[800,256]{1,0:T(8,128)(2,1)S(1)} %get-tuple-element.51), channel_id=1, source_target_pairs={{0,2},{1,3},{2,0},{3,1},{4,6},{5,7},{6,4},{7,5},{8,10},{9,11},{10,... | collective-permute-start | bytes 1228808 | tf_op jit(solution)/shard_map/ppermute | solution.py:34
  32.1 10.7 %collective-permute-start.2 = (bf16[800,256]{1,0:T(8,128)(2,1)S(1)}, bf16[800,256]{1,0:T(8,128)(2,1)S(1)}, u32[]{:S(2)}, u32[]{:S(2)}) collective-permute-start(bf16[800,256]{1,0:T(8,128)(2,1)S(1)} %get-tuple-element.52), channel_id=1, source_target_pairs={{0,1},{1,0},{2,3},{3,2},{4,5},{5,4},{6,7},{7,6},{8,9},{9,8},{10,11... | collective-permute-start | bytes 1228808 | tf_op jit(solution)/shard_map/ppermute | solution.py:34
  45.1 12.4 %collective-permute-start.8 = (bf16[400,256]{1,0:T(8,128)(2,1)S(1)}, bf16[400,256]{1,0:T(8,128)(2,1)S(1)}, u32[]{:S(2)}, u32[]{:S(2)}) collective-permute-start(bf16[400,256]{1,0:T(8,128)(2,1)S(1)} %get-tuple-element.90.refs_2_), channel_id=1, source_target_pairs={{0,1},{1,0},{2,3},{3,2},{4,5},{5,4},{6,7},{7,6},{8,9},{9,8},{10,11... | collective-permute-start | bytes 614408 | tf_op jit(solution)/shard_map/ppermute | solution.py:34
  46.6 15.5 %collective-permute-start.3 = (bf16[400,256]{1,0:T(8,128)(2,1)S(1)}, bf16[400,256]{1,0:T(8,128)(2,1)S(1)}, u32[]{:S(2)}, u32[]{:S(2)}) collective-permute-start(bf16[400,256]{1,0:T(8,128)(2,1)S(1)} %get-tuple-element.91.refs_1_), channel_id=1, source_target_pairs={{0,2},{1,3},{2,0},{3,1},{4,6},{5,7},{6,4},{7,5},{8,10},{9,11},{10,... | collective-permute-start | bytes 614408 | tf_op jit(solution)/shard_map/ppermute | solution.py:34
  51.0 11.1 %collective-permute-start.6 = (bf16[400,256]{1,0:T(8,128)(2,1)S(1)}, bf16[400,256]{1,0:T(8,128)(2,1)S(1)}, u32[]{:S(2)}, u32[]{:S(2)}) collective-permute-start(bf16[400,256]{1,0:T(8,128)(2,1)S(1)} %collective-permute-done.5.refs_1_), channel_id=1, source_target_pairs={{0,2},{1,3},{2,0},{3,1},{4,6},{5,7},{6,4},{7,5},{8,10},{9,11},{10,... | collective-permute-start | bytes 614408 | tf_op jit(solution)/shard_map/ppermute | solution.py:34
  67.3 21.4 %collective-permute-start.14 = (bf16[512,256]{1,0:T(8,128)(2,1)S(1)}, bf16[512,256]{1,0:T(8,128)(2,1)S(1)}, u32[]{:S(2)}, u32[]{:S(2)}) collective-permute-start(bf16[512,256]{1,0:T(8,128)(2,1)S(1)} %add_convert_fusion.5.refs_7_), channel_id=1, source_target_pairs={{0,16},{4,20},{8,24},{12,28},{16,0},{20,4},{24,8},{28,12},{1,17},{... | collective-permute-start | bytes 786440 | tf_op jit(solution)/shard_map/ppermute | solution.py:34
  72.2 16.5 %collective-permute-start.15 = (bf16[512,256]{1,0:T(8,128)(2,1)S(1)}, bf16[512,256]{1,0:T(8,128)(2,1)S(1)}, u32[]{:S(2)}, u32[]{:S(2)}) collective-permute-start(bf16[512,256]{1,0:T(8,128)(2,1)S(1)} %add_convert_fusion.6.refs_7_), channel_id=1, source_target_pairs={{0,24},{4,28},{8,16},{12,20},{16,8},{20,12},{24,0},{28,4},{1,25},{... | collective-permute-start | bytes 786440 | tf_op jit(solution)/shard_map/ppermute | solution.py:34
  76.2 17.2 %collective-permute-start.13 = (bf16[512,256]{1,0:T(8,128)(2,1)S(1)}, bf16[512,256]{1,0:T(8,128)(2,1)S(1)}, u32[]{:S(2)}, u32[]{:S(2)}) collective-permute-start(bf16[512,256]{1,0:T(8,128)(2,1)S(1)} %add_convert_fusion.4), channel_id=1, source_target_pairs={{0,8},{4,12},{8,0},{12,4},{16,24},{20,28},{24,16},{28,20},{1,9},{5... | collective-permute-start | bytes 786440 | tf_op jit(solution)/shard_map/ppermute | solution.py:34
  93.5 13.5 %collective-permute-start.16 = (bf16[512,256]{1,0:T(8,128)(2,1)S(1)}, bf16[512,256]{1,0:T(8,128)(2,1)S(1)}, u32[]{:S(2)}, u32[]{:S(2)}) collective-permute-start(bf16[512,256]{1,0:T(8,128)(2,1)S(1)} %add_convert_fusion.3.refs_0_), channel_id=1, source_target_pairs={{0,8},{4,12},{8,0},{12,4},{16,24},{20,28},{24,16},{28,20},{1,9},{5... | collective-permute-start | bytes 786440 | tf_op jit(solution)/shard_map/ppermute | solution.py:34
  94.3 21.8 %collective-permute-start.17 = (bf16[512,256]{1,0:T(8,128)(2,1)S(1)}, bf16[512,256]{1,0:T(8,128)(2,1)S(1)}, u32[]{:S(2)}, u32[]{:S(2)}) collective-permute-start(bf16[512,256]{1,0:T(8,128)(2,1)S(1)} %add_convert_fusion.3.refs_0_), channel_id=1, source_target_pairs={{0,16},{4,20},{8,24},{12,28},{16,0},{20,4},{24,8},{28,12},{1,17},{... | collective-permute-start | bytes 786440 | tf_op jit(solution)/shard_map/ppermute | solution.py:34
  97.6 18.4 %collective-permute-start.18 = (bf16[512,256]{1,0:T(8,128)(2,1)S(1)}, bf16[512,256]{1,0:T(8,128)(2,1)S(1)}, u32[]{:S(2)}, u32[]{:S(2)}) collective-permute-start(bf16[512,256]{1,0:T(8,128)(2,1)S(1)} %add_convert_fusion.3.refs_0_), channel_id=1, source_target_pairs={{0,24},{4,28},{8,16},{12,20},{16,8},{20,12},{24,0},{28,4},{1,25},{... | collective-permute-start | bytes 786440 | tf_op jit(solution)/shard_map/ppermute | solution.py:34
  97.9 18.6 %collective-permute-start.19 = (bf16[512,256]{1,0:T(8,128)(2,1)S(1)}, bf16[512,256]{1,0:T(8,128)(2,1)S(1)}, u32[]{:S(2)}, u32[]{:S(2)}) collective-permute-start(bf16[512,256]{1,0:T(8,128)(2,1)S(1)} %add_convert_fusion.3.refs_0_), channel_id=1, source_target_pairs={{0,4},{4,0},{8,12},{12,8},{16,20},{20,16},{24,28},{28,24},{1,5},{5... | collective-permute-start | bytes 786440 | tf_op jit(solution)/shard_map/ppermute | solution.py:34
  119.3 36.9 %collective-permute-start.42 = (f32[128,256]{1,0:T(8,128)S(1)}, f32[128,256]{1,0:T(8,128)S(1)}, u32[]{:S(2)}, u32[]{:S(2)}) collective-permute-start(f32[128,256]{1,0:T(8,128)S(1)} %gram.1), channel_id=1, source_target_pairs={{0,1},{1,0},{2,3},{3,2},{4,5},{5,4},{6,7},{7,6},{8,9},{9,8},{10,11... | collective-permute-start | bytes 393224 | tf_op jit(solution)/shard_map/ppermute | solution.py:34
  120.8 35.9 %collective-permute-start.43 = (f32[128,256]{1,0:T(8,128)S(1)}, f32[128,256]{1,0:T(8,128)S(1)}, u32[]{:S(2)}, u32[]{:S(2)}) collective-permute-start(f32[128,256]{1,0:T(8,128)S(1)} %gram.1), channel_id=1, source_target_pairs={{0,2},{1,3},{2,0},{3,1},{4,6},{5,7},{6,4},{7,5},{8,10},{9,11},{10,... | collective-permute-start | bytes 393224 | tf_op jit(solution)/shard_map/ppermute | solution.py:34
  121.3 35.4 %collective-permute-start.44 = (f32[128,256]{1,0:T(8,128)S(1)}, f32[128,256]{1,0:T(8,128)S(1)}, u32[]{:S(2)}, u32[]{:S(2)}) collective-permute-start(f32[128,256]{1,0:T(8,128)S(1)} %gram.1), channel_id=1, source_target_pairs={{0,3},{1,2},{2,1},{3,0},{4,7},{5,6},{6,5},{7,4},{8,11},{9,10},{10,... | collective-permute-start | bytes 393224 | tf_op jit(solution)/shard_map/ppermute | solution.py:34
  129.2 12.8 %collective-permute-start.29 = (bf16[400,256]{1,0:T(8,128)(2,1)S(1)}, bf16[400,256]{1,0:T(8,128)(2,1)S(1)}, u32[]{:S(2)}, u32[]{:S(2)}) collective-permute-start(bf16[400,256]{1,0:T(8,128)(2,1)S(1)} %get-tuple-element.69), channel_id=1, source_target_pairs={{0,2},{1,3},{2,0},{3,1},{4,6},{5,7},{6,4},{7,5},{8,10},{9,11},{10,... | collective-permute-start | bytes 614408 | tf_op jit(solution)/shard_map/ppermute | solution.py:34
  150.1 17.7 %collective-permute-start.34 = (bf16[400,256]{1,0:T(8,128)(2,1)S(1)}, bf16[400,256]{1,0:T(8,128)(2,1)S(1)}, u32[]{:S(2)}, u32[]{:S(2)}) collective-permute-start(bf16[400,256]{1,0:T(8,128)(2,1)S(1)} %multiply_convert_fusion.refs_2_), channel_id=1, source_target_pairs={{0,1},{1,0},{2,3},{3,2},{4,5},{5,4},{6,7},{7,6},{8,9},{9,8},{10,11... | collective-permute-start | bytes 614408 | tf_op jit(solution)/shard_map/ppermute | solution.py:34
  156.8 18.0 %collective-permute-start.45 = (f32[128,256]{1,0:T(8,128)S(1)}, f32[128,256]{1,0:T(8,128)S(1)}, u32[]{:S(2)}, u32[]{:S(2)}) collective-permute-start(f32[128,256]{1,0:T(8,128)S(1)} %add_add_fusion.1.refs_0_), channel_id=1, source_target_pairs={{0,4},{4,0},{8,12},{12,8},{16,20},{20,16},{24,28},{28,24},{1,5},{5... | collective-permute-start | bytes 393224 | tf_op jit(solution)/shard_map/ppermute | solution.py:34
  156.9 15.4 %collective-permute-start.26 = (bf16[400,256]{1,0:T(8,128)(2,1)S(1)}, bf16[400,256]{1,0:T(8,128)(2,1)S(1)}, u32[]{:S(2)}, u32[]{:S(2)}) collective-permute-start(bf16[400,256]{1,0:T(8,128)(2,1)S(1)} %multiply_convert_fusion.1.refs_1_), channel_id=1, source_target_pairs={{0,2},{1,3},{2,0},{3,1},{4,6},{5,7},{6,4},{7,5},{8,10},{9,11},{10,... | collective-permute-start | bytes 614408 | tf_op jit(solution)/shard_map/ppermute | solution.py:34
  160.6 11.7 %collective-permute-start.33 = (bf16[400,256]{1,0:T(8,128)(2,1)S(1)}, bf16[400,256]{1,0:T(8,128)(2,1)S(1)}, u32[]{:S(2)}, u32[]{:S(2)}) collective-permute-start(bf16[400,256]{1,0:T(8,128)(2,1)S(1)} %collective-permute-done.30.refs_3_), channel_id=1, source_target_pairs={{0,1},{1,0},{2,3},{3,2},{4,5},{5,4},{6,7},{7,6},{8,9},{9,8},{10,11... | collective-permute-start | bytes 614408 | tf_op jit(solution)/shard_map/ppermute | solution.py:34
  183.6 24.6 %collective-permute-start.40 = (bf16[512,256]{1,0:T(8,128)(2,1)S(1)}, bf16[512,256]{1,0:T(8,128)(2,1)S(1)}, u32[]{:S(2)}, u32[]{:S(2)}) collective-permute-start(bf16[512,256]{1,0:T(8,128)(2,1)S(1)} %add_convert_fusion.1.refs_7_), channel_id=1, source_target_pairs={{0,16},{4,20},{8,24},{12,28},{16,0},{20,4},{24,8},{28,12},{1,17},{... | collective-permute-start | bytes 786440 | tf_op jit(solution)/shard_map/ppermute | solution.py:34
  192.0 16.1 %collective-permute-start.41 = (bf16[512,256]{1,0:T(8,128)(2,1)S(1)}, bf16[512,256]{1,0:T(8,128)(2,1)S(1)}, u32[]{:S(2)}, u32[]{:S(2)}) collective-permute-start(bf16[512,256]{1,0:T(8,128)(2,1)S(1)} %add_convert_fusion.2.refs_7_), channel_id=1, source_target_pairs={{0,24},{4,28},{8,16},{12,20},{16,8},{20,12},{24,0},{28,4},{1,25},{... | collective-permute-start | bytes 786440 | tf_op jit(solution)/shard_map/ppermute | solution.py:34
  195.8 17.3 %collective-permute-start.39 = (bf16[512,256]{1,0:T(8,128)(2,1)S(1)}, bf16[512,256]{1,0:T(8,128)(2,1)S(1)}, u32[]{:S(2)}, u32[]{:S(2)}) collective-permute-start(bf16[512,256]{1,0:T(8,128)(2,1)S(1)} %add_convert_fusion), channel_id=1, source_target_pairs={{0,8},{4,12},{8,0},{12,4},{16,24},{20,28},{24,16},{28,20},{1,9},{5... | collective-permute-start | bytes 786440 | tf_op jit(solution)/shard_map/ppermute | solution.py:34
  237.2 10.9 %collective-permute-start.57 = (bf16[512,256]{1,0:T(8,128)(2,1)S(1)}, bf16[512,256]{1,0:T(8,128)(2,1)S(1)}, u32[]{:S(2)}, u32[]{:S(2)}) collective-permute-start(bf16[512,256]{1,0:T(8,128)(2,1)S(1)} %get-tuple-element.88.refs_0_), channel_id=1, source_target_pairs={{0,8},{4,12},{8,0},{12,4},{16,24},{20,28},{24,16},{28,20},{1,9},{5... | collective-permute-start | bytes 786440 | tf_op jit(solution)/shard_map/ppermute | solution.py:34
  237.2 18.8 %collective-permute-start.58 = (bf16[512,256]{1,0:T(8,128)(2,1)S(1)}, bf16[512,256]{1,0:T(8,128)(2,1)S(1)}, u32[]{:S(2)}, u32[]{:S(2)}) collective-permute-start(bf16[512,256]{1,0:T(8,128)(2,1)S(1)} %get-tuple-element.88.refs_0_), channel_id=1, source_target_pairs={{0,16},{4,20},{8,24},{12,28},{16,0},{20,4},{24,8},{28,12},{1,17},{... | collective-permute-start | bytes 786440 | tf_op jit(solution)/shard_map/ppermute | solution.py:34
  238.9 17.0 %collective-permute-start.59 = (bf16[512,256]{1,0:T(8,128)(2,1)S(1)}, bf16[512,256]{1,0:T(8,128)(2,1)S(1)}, u32[]{:S(2)}, u32[]{:S(2)}) collective-permute-start(bf16[512,256]{1,0:T(8,128)(2,1)S(1)} %get-tuple-element.88.refs_0_), channel_id=1, source_target_pairs={{0,24},{4,28},{8,16},{12,20},{16,8},{20,12},{24,0},{28,4},{1,25},{... | collective-permute-start | bytes 786440 | tf_op jit(solution)/shard_map/ppermute | solution.py:34
  241.6 14.8 %collective-permute-start.56 = (f32[128,256]{1,0:T(8,128)S(1)}, f32[128,256]{1,0:T(8,128)S(1)}, u32[]{:S(2)}, u32[]{:S(2)}) collective-permute-start(f32[128,256]{1,0:T(8,128)S(1)} %add_add_fusion.refs_0_), channel_id=1, source_target_pairs={{0,4},{4,0},{8,12},{12,8},{16,20},{20,16},{24,28},{28,24},{1,5},{5... | collective-permute-start | bytes 393224 | tf_op jit(solution)/shard_map/ppermute | solution.py:34
  241.7 27.0 %collective-permute-start.60 = (bf16[512,256]{1,0:T(8,128)(2,1)S(1)}, bf16[512,256]{1,0:T(8,128)(2,1)S(1)}, u32[]{:S(2)}, u32[]{:S(2)}) collective-permute-start(bf16[512,256]{1,0:T(8,128)(2,1)S(1)} %get-tuple-element.88.refs_0_), channel_id=1, source_target_pairs={{0,4},{4,0},{8,12},{12,8},{16,20},{20,16},{24,28},{28,24},{1,5},{5... | collective-permute-start | bytes 786440 | tf_op jit(solution)/shard_map/ppermute | solution.py:34
  248.1 20.5 %collective-permute-start.61 = (bf16[512,256]{1,0:T(8,128)(2,1)S(1)}, bf16[512,256]{1,0:T(8,128)(2,1)S(1)}, u32[]{:S(2)}, u32[]{:S(2)}) collective-permute-start(bf16[512,256]{1,0:T(8,128)(2,1)S(1)} %collective-permute-done.57.refs_1_), channel_id=1, source_target_pairs={{0,4},{4,0},{8,12},{12,8},{16,20},{20,16},{24,28},{28,24},{1,5},{5... | collective-permute-start | bytes 786440 | tf_op jit(solution)/shard_map/ppermute | solution.py:34
  255.9 12.7 %collective-permute-start.62 = (bf16[512,256]{1,0:T(8,128)(2,1)S(1)}, bf16[512,256]{1,0:T(8,128)(2,1)S(1)}, u32[]{:S(2)}, u32[]{:S(2)}) collective-permute-start(bf16[512,256]{1,0:T(8,128)(2,1)S(1)} %collective-permute-done.58.refs_2_), channel_id=1, source_target_pairs={{0,4},{4,0},{8,12},{12,8},{16,20},{20,16},{24,28},{28,24},{1,5},{5... | collective-permute-start | bytes 786440 | tf_op jit(solution)/shard_map/ppermute | solution.py:34
  256.0 12.7 %collective-permute-start.63 = (bf16[512,256]{1,0:T(8,128)(2,1)S(1)}, bf16[512,256]{1,0:T(8,128)(2,1)S(1)}, u32[]{:S(2)}, u32[]{:S(2)}) collective-permute-start(bf16[512,256]{1,0:T(8,128)(2,1)S(1)} %collective-permute-done.59.refs_3_), channel_id=1, source_target_pairs={{0,4},{4,0},{8,12},{12,8},{16,20},{20,16},{24,28},{28,24},{1,5},{5... | collective-permute-start | bytes 786440 | tf_op jit(solution)/shard_map/ppermute | solution.py:34
  (34 other events, 200.5 us)

commit v5 on v4

--- a/solution.py
+++ b/solution.py
@@ -98,14 +98,20 @@
     )
 
 
-def score_kernel(first, places, filtered_ref, *refs):
+def whole_blocks(spots, refs):
+    blocks = {}
+    for (at, _), ref in zip(spots, refs):
+        blocks.setdefault(at, []).append(ref[...])
+    return [jnp.concatenate(blocks[at], 0) for at in sorted(blocks)]
+
+
+def score_kernel(first, width, spots, places, filtered_ref, *refs):
     *basis_refs, top_ref, low_ref = refs
     rows = top_ref.shape[0]
-    width = basis_refs[0].shape[0]
     total = None
-    for at, basis_ref in enumerate(basis_refs):
+    for at, block in enumerate(whole_blocks(spots, basis_refs)):
         columns = pl.ds(pl.multiple_of(places[first + at] * width, width), width)
-        term = jnp.dot(filtered_ref[:, columns], basis_ref[...], preferred_element_type=F32)
+        term = jnp.dot(filtered_ref[:, columns], block, preferred_element_type=F32)
         total = term if total is None else total + term
     top_ref[...] = total[:rows].astype(top_ref.dtype)
     low_ref[...] = total[rows:].astype(low_ref.dtype)
@@ -113,15 +119,17 @@
 
 def score(places, first, filtered, basis, out_types):
     rows, pixels = filtered.shape
-    columns = basis[0].shape[1]
-    return pl.pallas_call(
-        functools.partial(score_kernel, first),
+    spots, blocks = [piece[:2] for piece in basis], [piece[2] for piece in basis]
+    columns = blocks[0].shape[1]
+    width = pixels // (1 + max(at for at, _ in spots))
+    return pl.pallas_call(
+        functools.partial(score_kernel, first, width, spots),
         grid_spec=prefetched(1 + len(basis), 2),
         out_shape=[jax.ShapeDtypeStruct((rows // 2, columns), kind) for kind in out_types],
         compiler_params=vmem(16 * 2**20),
         cost_estimate=cost(2 * rows * pixels * columns, 2 * rows * columns),
         name="score",
-    )(places, filtered, *basis)
+    )(places, filtered, *blocks)
 
 
 def sum_blocks(filtered, scaled):
@@ -243,36 +251,38 @@
     return terms[0]
 
 
-def gram_kernel(core_at, places, *refs):
+def gram_kernel(core_at, spots, places, *refs):
     *basis_refs, half_ref, gram_ref = refs
-    gram_ref[...] = tree_sum([contract_rows(ref[...], ref[...]) for ref in basis_refs])
+    blocks = whole_blocks(spots, basis_refs)
+    gram_ref[...] = tree_sum([contract_rows(block, block) for block in blocks])
     rows = half_ref.shape[0]
     half_ref[...] = gram_ref[pl.ds(pl.multiple_of(places[core_at] * rows, rows), rows), :]
 
 
 def half_gram(places, core_at, basis):
-    rows, columns = basis[0].shape
-    return pl.pallas_call(
-        functools.partial(gram_kernel, core_at),
+    spots, blocks = [piece[:2] for piece in basis], [piece[2] for piece in basis]
+    columns = blocks[0].shape[1]
+    rows = sum(block.shape[0] for block in blocks)
+    return pl.pallas_call(
+        functools.partial(gram_kernel, core_at, spots),
         grid_spec=pltpu.PrefetchScalarGridSpec(
             num_scalar_prefetch=1,
             grid=(),
-            in_specs=[in_vmem()] * len(basis),
+            in_specs=[in_vmem()] * len(blocks),
             out_specs=[in_vmem()],
             scratch_shapes=[pltpu.VMEM((columns, columns), F32)],
         ),
         out_shape=[jax.ShapeDtypeStruct((columns // 2, columns), F32)],
         compiler_params=vmem(12 * 2**20),
-        cost_estimate=cost(2 * len(basis) * rows * columns * columns, 2 * len(basis) * rows * columns),
+        cost_estimate=cost(2 * rows * columns * columns, 2 * rows * columns),
         name="gram",
-    )(places, *basis)[0]
+    )(places, *blocks)[0]
 
 
 def normalize_kernel(core_at, scale, places, *refs):
     *part_refs, inverse_ref, half_ref, send_ref, keep_ref, gram_ref = refs
-    total = part_refs[0][...]
-    for ref in part_refs[1:]:
-        total = total + ref[...].astype(F32)
+    halves = [sum(ref[...].astype(F32) for ref in part_refs[at::2]) for at in (0, 1)]
+    total = jnp.concatenate(halves, 0)
     block = lax.dot_general(
         total,
         inverse_ref[...] * scale,
@@ -289,7 +299,7 @@
 
 
 def normalize_and_gram(places, core_at, parts, inverse, scale):
-    rows, columns = parts[0].shape
+    rows, columns = 2 * parts[0].shape[0], parts[0].shape[1]
     return pl.pallas_call(
         functools.partial(normalize_kernel, core_at, scale),
         grid_spec=pltpu.PrefetchScalarGridSpec(
@@ -479,44 +489,38 @@
 
 
 def apply_kernel(first, places, inverse_ref, *refs):
-    *basis_refs, out_ref = refs
-    parts = split_in_three(inverse_ref[...])
-    rows = basis_refs[0].shape[0]
-    span = out_ref.shape[0] // rows
-    for step in range(len(basis_refs) // span):
-
-        @pl.when(pl.program_id(0) == step)
-        def _():
-            for at in range(step * span, (step + 1) * span):
-                block = basis_refs[at][...]
-                here = pl.multiple_of((places[first + at] % span) * rows, rows)
-                out_ref[pl.ds(here, rows), :] = sum(
-                    lax.dot_general(
-                        block, part, (((1,), (1,)), ((), ())), preferred_element_type=F32
-                    )
-                    for part in reversed(parts)
-                )
+    *basis_refs, out_ref, stacked_ref = refs
+    rows, span = basis_refs[0].shape[0], out_ref.shape[0]
+
+    @pl.when(pl.program_id(0) == 0)
+    def _():
+        for at, ref in enumerate(basis_refs):
+            here = pl.ds(pl.multiple_of(places[first + at] * rows, rows), rows)
+            stacked_ref[here, :] = ref[...]
+
+    block = stacked_ref[pl.ds(pl.multiple_of(pl.program_id(0) * span, span), span), :]
+    out_ref[...] = sum(
+        lax.dot_general(block, part, (((1,), (1,)), ((), ())), preferred_element_type=F32)
+        for part in reversed(split_in_three(inverse_ref[...]))
+    )
 
 
 def apply_inverse(places, first, inverse, basis):
     rows, columns = basis[0].shape
-    span = 2
-    steps = len(basis) // span
+    pixels = rows * len(basis)
+    span = 2 * rows
     return pl.pallas_call(
         functools.partial(apply_kernel, first),
         grid_spec=pltpu.PrefetchScalarGridSpec(
             num_scalar_prefetch=1,
-            grid=(steps,),
+            grid=(pixels // span,),
             in_specs=[in_vmem()] * (1 + len(basis)),
-            out_specs=pl.BlockSpec(
-                (span * rows, columns), lambda i, places: (places[first + span * i] // span, 0)
-            ),
+            out_specs=pl.BlockSpec((span, columns), lambda i, places: (i, 0)),
+            scratch_shapes=[pltpu.VMEM((pixels, columns), BF16)],
         ),
-        out_shape=jax.ShapeDtypeStruct((rows * len(basis), columns), F32),
+        out_shape=jax.ShapeDtypeStruct((pixels, columns), F32),
         compiler_params=vmem(16 * 2**20),
-        cost_estimate=cost(
-            6 * rows * len(basis) * columns * columns, 6 * rows * len(basis) * columns
-        ),
+        cost_estimate=cost(6 * pixels * columns * columns, 6 * pixels * columns),
         name="apply",
     )(places, inverse, *basis)
 
@@ -541,8 +545,38 @@
 
 
 def level_order(depth):
-    middle = depth // 2
-    return [middle] + [s for s in range(depth - 1, 0, -1) if s != middle] + [0]
+    return list(range(depth - 1, -1, -1))
+
+
+def send_sum(both, s, depth, relay):
+    def swap(value, shift):
+        return xor_swap(value, "img", 2 * shift)
+
+    if depth == 4 and s == 2:
+        halves = [add_round(part, other) for part, other in zip(row_halves(both), relay)]
+        return [swap(half, 2) for half in halves]
+    shift = 1 if depth == 4 else s
+    return [swap(half, shift) for half in row_halves(both.astype(BF16))]
+
+
+def gather_levels(block, depth):
+    def swap(value, shift):
+        return xor_swap(value, "img", 2 * shift)
+
+    rows = block.shape[0] // 2
+    pieces = [(0, 0, block)]
+    if depth != 4:
+        return pieces + [(s, 0, swap(block, s)) for s in range(1, depth)]
+    middle = [swap(half, 2) for half in row_halves(block)]
+    pieces.append((1, 0, swap(block, 1)))
+    for at, half in enumerate(middle):
+        pieces.append((2, at * rows, half))
+        pieces.append((3, at * rows, swap(half, 1)))
+    return pieces
+
+
+def gather_cores(pieces, depth):
+    return pieces + [(depth + at, row, xor_swap(value, "img", 1)) for at, row, value in pieces]
 
 
 def add_over_pix(value, pix):
@@ -644,7 +678,7 @@
         split = pix // 2
         if split > 1:
             early = early_sum(places, pairs_at, filtered[1:split], scaled[1:split], width, [early])
-        parts, after = [None] * depth, []
+        parts, relay, after = [], None, []
         for s in level_order(depth):
             send, keep = late_sum(
                 places,
@@ -657,12 +691,13 @@
                 after[-2:-1],
             )
             both = keep + xor_swap(send, "img", 1).astype(F32)
-            if s:
-                both = both.astype(BF16)
-                parts[s] = xor_swap(both, "img", 2 * s)
+            after.append(both)
+            if s == 0:
+                parts.append(row_halves(both))
+            elif depth == 4 and s == 3:
+                relay = send_sum(both, s, depth, None)
             else:
-                parts[s] = both
-            after.append(both)
+                parts.append(send_sum(both, s, depth, relay))
 
         if sweep == ITERS - 1:
             gram = half_gram(places, cores_at, basis)
@@ -671,16 +706,13 @@
             _, inverse = cholesky_and_inverse(places, cores_at, [gram, other], 2)
             break
 
-        total = parts[0]
-        for part in parts[1:]:
-            total = total + part.astype(F32)
-        block = total.astype(BF16)
-        near = [block] + [xor_swap(block, "img", 2 * s) for s in range(1, depth)]
-        basis = near + [xor_swap(block, "img", 1) for block in near]
+        total = [sum(part[at].astype(F32) for part in parts) for at in (0, 1)]
+        block = jnp.concatenate(total, 0).astype(BF16)
+        basis = gather_cores(gather_levels(block, depth), depth)
 
         own, arrived = score_and_scatter(places, gathered_at, filtered, basis, pix)
 
-    half, send, keep = normalize_and_gram(places, cores_at, parts, inverse, 1.0 / RANGE)
+    half, send, keep = normalize_and_gram(places, cores_at, sum(parts, []), inverse, 1.0 / RANGE)
     pieces = scatter_rows(places, levels_at, keep, xor_swap(send, "img", 1), depth)
     mine = tree_sum([pieces[0]] + [xor_swap(pieces[s], "img", 2 * s) for s in range(1, depth)])
     pieces = [mine] + [xor_swap(mine, "img", 2 * s) for s in range(1, depth)]

time: 274 us -> 271 us (0.989)
  waiting for transfers between devices: 91.9 us -> 85 us
  starting transfers between devices: 66.1 us -> 70 us
    ppermute x64 -> x74, waiting for transfers between devices: 91.9 us -> 85 us  [xor_swap(): return lax.ppermute(value, axis, [(i, i ^ mask) for i in range(size)])]
    ppermute x64 -> x74, starting transfers between devices: 66.1 us -> 70 us  [xor_swap(): return lax.ppermute(value, axis, [(i, i ^ mask) for i in range(size)])]
  transfers between devices with their start and end apart: 64 -> 74, of which waited for: 24 -> 28; matrix products, arithmetic and copies ran while one was open for 0% -> 0% of each run, Pallas kernels for 33% -> 33%
where the time goes in v5:
time: 271 us; the launch traced here: 270 us
  Pallas kernels  108 us (40%)
  waiting for transfers between devices  85 us (31%)
  starting transfers between devices  70 us (26%)
  other arithmetic  3.84 us (1%)
    ppermute x74, waiting for transfers between devices, xor_swap(): return lax.ppermute(value, axis, [(i, i ^ mask) for i in range(size)])  85 us
    ppermute x74, starting transfers between devices, xor_swap(): return lax.ppermute(value, axis, [(i, i ^ mask) for i in range(size)])  70 us
    pallas_call x4, Pallas kernels, filter_and_score(): pl.pallas_call(filter_kernel, grid_spec=pltpu.PrefetchScalarGridSpec(num_...  29.6 us
    pallas_call x3, Pallas kernels, cholesky_and_inverse(): pl.pallas_call(functools.partial(cholesky_kernel, first, last, place_at),...  25.2 us
    pallas_call x4, Pallas kernels, early_sum(): pl.pallas_call(functools.partial(early_sum_kernel, count, first, width),...  18 us
    pallas_call x8, Pallas kernels, late_sum(): pl.pallas_call(functools.partial(late_sum_kernel, count, first, at_early)...  17.4 us
    pallas_call x4, Pallas kernels, score(): pl.pallas_call(functools.partial(score_kernel, first, width, spots), grid...  9.6 us
  transfers between devices with their start and end apart: 74, of which 28 were waited for; matrix products, arithmetic and copies ran while one was open for 0% of the time, Pallas kernels for 33%

profile of v5, /device:TPU:0, one launch (start us, length us, event | category | flops | bytes accessed | tf_op | source)
XLA Modules:
  0.0 270.4 jit_solution(11095919999517456396)
XLA Ops:
  5.2 7.4 %filter_and_score.5 = (bf16[800,4096]{1,0:T(8,128)(2,1)S(1)}, bf16[800,256]{1,0:T(8,128)(2,1)S(1)}) custom-call(s32[26]{0:T(128)S(1)} %fusion.6.places, s32[8,1,400]{2,1,0:T(1,128)S(1)} %reshape.22.class_ref, bf16[3200,4096]{1,0:T(8,128)(2,1)} %image_ref.7, bf16[64,4096]{1,0:T(8,128)(2,1)S(1)} %copy-done, bf16[4096,256]{1,0:T(8,128)(2,1)S(1)} %convert_element_type.138.probe_ref), custom_call_target="tpu_custom_call" | custom-call | flops 3355443200 | bytes 6553600 | tf_op jit(solution)/shard_map/filter_and_score/pallas_call | solution.py:69
  12.6 4.0 %collective-permute-start = (bf16[800,256]{1,0:T(8,128)(2,1)S(1)}, bf16[800,256]{1,0:T(8,128)(2,1)S(1)}, u32[]{:S(2)}, u32[]{:S(2)}) collective-permute-start(bf16[800,256]{1,0:T(8,128)(2,1)S(1)} %get-tuple-element.50), channel_id=1, source_target_pairs={{0,3},{1,2},{2,1},{3,0},{4,7},{5,6},{6,5},{7,4},{8,11},{9,10},{10,... | collective-permute-start | bytes 1228808 | tf_op jit(solution)/shard_map/ppermute | solution.py:34
  16.6 7.4 %filter_and_score.4 = (bf16[800,4096]{1,0:T(8,128)(2,1)S(1)}, bf16[800,256]{1,0:T(8,128)(2,1)S(1)}) custom-call(s32[26]{0:T(128)S(1)} %fusion.6.places, s32[8,1,400]{2,1,0:T(1,128)S(1)} %reshape.22.class_ref, bf16[3200,4096]{1,0:T(8,128)(2,1)} %image_ref.7, bf16[64,4096]{1,0:T(8,128)(2,1)S(1)} %copy-done, bf16[4096,256]{1,0:T(8,128)(2,1)S(1)} %convert_element_type.138.probe_ref), custom_call_target="tpu_custom_call" | custom-call | flops 3355443200 | bytes 6553600 | tf_op jit(solution)/shard_map/filter_and_score/pallas_call | solution.py:69
  24.6 7.4 %filter_and_score.7 = (bf16[800,4096]{1,0:T(8,128)(2,1)S(1)}, bf16[800,256]{1,0:T(8,128)(2,1)S(1)}) custom-call(s32[26]{0:T(128)S(1)} %fusion.6.places, s32[8,1,400]{2,1,0:T(1,128)S(1)} %reshape.22.class_ref, bf16[3200,4096]{1,0:T(8,128)(2,1)} %image_ref.7, bf16[64,4096]{1,0:T(8,128)(2,1)S(1)} %copy-done, bf16[4096,256]{1,0:T(8,128)(2,1)S(1)} %convert_element_type.138.probe_ref), custom_call_target="tpu_custom_call" | custom-call | flops 3355443200 | bytes 6553600 | tf_op jit(solution)/shard_map/filter_and_score/pallas_call | solution.py:69
  32.2 7.4 %filter_and_score.6 = (bf16[800,4096]{1,0:T(8,128)(2,1)S(1)}, f32[800,256]{1,0:T(8,128)S(1)}) custom-call(s32[26]{0:T(128)S(1)} %fusion.6.places, s32[8,1,400]{2,1,0:T(1,128)S(1)} %reshape.22.class_ref, bf16[3200,4096]{1,0:T(8,128)(2,1)} %image_ref.7, bf16[64,4096]{1,0:T(8,128)(2,1)S(1)} %copy-done, bf16[4096,256]{1,0:T(8,128)(2,1)S(1)} %convert_element_type.138.probe_ref), custom_call_target="tpu_custom_call" | custom-call | flops 3355443200 | bytes 6553600 | tf_op jit(solution)/shard_map/filter_and_score/pallas_call | solution.py:69
  39.6 3.1 %collective-permute-done.2 = bf16[800,256]{1,0:T(8,128)(2,1)S(1)} collective-permute-done((bf16[800,256]{1,0:T(8,128)(2,1)S(1)}, bf16[800,256]{1,0:T(8,128)(2,1)S(1)}, u32[]{:S(2)}, u32[]{:S(2)}) %collective-permute-start.2) | collective-permute-done | bytes 409632 | tf_op jit(solution)/shard_map/ppermute | solution.py:34
  47.0 3.7 %collective-permute-done.4.refs_3_ = bf16[400,256]{1,0:T(8,128)(2,1)S(1)} collective-permute-done((bf16[400,256]{1,0:T(8,128)(2,1)S(1)}, bf16[400,256]{1,0:T(8,128)(2,1)S(1)}, u32[]{:S(2)}, u32[]{:S(2)}) %collective-permute-start.4) | collective-permute-done | bytes 204832 | tf_op jit(solution)/shard_map/ppermute | solution.py:34
  53.0 4.5 %early_sum.4.refs_3_ = f32[4096,256]{1,0:T(8,128)S(1)} custom-call(s32[26]{0:T(128)S(1)} %fusion.6.places, bf16[800,4096]{1,0:T(8,128)(2,1)S(1)} %get-tuple-element.48.refs_0_.filtered_ref, bf16[400,256]{1,0:T(8,128)(2,1)S(1)} %get-tuple-element.95.refs_1_, bf16[400,256]{1,0:T(8,128)(2,1)S(1)} %get-tuple-element.94.refs_2_), custom_call_target="tpu_custom_call" | custom-call | flops 1677721600 | bytes 4194304 | tf_op jit(solution)/shard_map/early_sum/pallas_call | solution.py:196
  57.5 4.5 %early_sum.5.refs_6_ = f32[4096,256]{1,0:T(8,128)S(1)} custom-call(s32[26]{0:T(128)S(1)} %fusion.6.places, bf16[800,4096]{1,0:T(8,128)(2,1)S(1)} %get-tuple-element.53.refs_0_.filtered_ref, bf16[400,256]{1,0:T(8,128)(2,1)S(1)} %collective-permute-done.5.refs_1_, bf16[400,256]{1,0:T(8,128)(2,1)S(1)} %collective-permute-done.8.refs_2_, ...), custom_call_target="tpu_custom_call" | custom-call | flops 1677721600 | bytes 4194304 | tf_op jit(solution)/shard_map/early_sum/pallas_call | solution.py:196
  75.6 2.6 collective-permute-start.12
  80.8 7.1 %collective-permute-done.12 = bf16[256,256]{1,0:T(8,128)(2,1)S(1)} collective-permute-done((bf16[256,256]{1,0:T(8,128)(2,1)S(1)}, bf16[256,256]{1,0:T(8,128)(2,1)S(1)}, u32[]{:S(2)}, u32[]{:S(2)}) %collective-permute-start.12) | collective-permute-done | bytes 131104 | tf_op jit(solution)/shard_map/ppermute | solution.py:34
  91.5 4.0 %collective-permute-start.20 = (bf16[256,256]{1,0:T(8,128)(2,1)S(1)}, bf16[256,256]{1,0:T(8,128)(2,1)S(1)}, u32[]{:S(2)}, u32[]{:S(2)}) collective-permute-start(bf16[256,256]{1,0:T(8,128)(2,1)S(1)} %get-tuple-element.100), channel_id=1, source_target_pairs={{0,16},{4,20},{8,24},{12,28},{16,0},{20,4},{24,8},{28,12},{1,17},{... | collective-permute-start | bytes 393224 | tf_op jit(solution)/shard_map/ppermute | solution.py:34
  95.5 6.6 %collective-permute-done.20.refs_2_ = bf16[256,256]{1,0:T(8,128)(2,1)S(1)} collective-permute-done((bf16[256,256]{1,0:T(8,128)(2,1)S(1)}, bf16[256,256]{1,0:T(8,128)(2,1)S(1)}, u32[]{:S(2)}, u32[]{:S(2)}) %collective-permute-start.20) | collective-permute-done | bytes 131104 | tf_op jit(solution)/shard_map/ppermute | solution.py:34
  102.1 3.1 %collective-permute-start.21 = (bf16[256,256]{1,0:T(8,128)(2,1)S(1)}, bf16[256,256]{1,0:T(8,128)(2,1)S(1)}, u32[]{:S(2)}, u32[]{:S(2)}) collective-permute-start(bf16[256,256]{1,0:T(8,128)(2,1)S(1)} %collective-permute-done.20.refs_2_), channel_id=1, source_target_pairs={{0,8},{4,12},{8,0},{12,4},{16,24},{20,28},{24,16},{28,20},{1,9},{5... | collective-permute-start | bytes 393224 | tf_op jit(solution)/shard_map/ppermute | solution.py:34
  105.1 3.0 %collective-permute-done.22.refs_4_ = bf16[256,256]{1,0:T(8,128)(2,1)S(1)} collective-permute-done((bf16[256,256]{1,0:T(8,128)(2,1)S(1)}, bf16[256,256]{1,0:T(8,128)(2,1)S(1)}, u32[]{:S(2)}, u32[]{:S(2)}) %collective-permute-start.22) | collective-permute-done | bytes 131104 | tf_op jit(solution)/shard_map/ppermute | solution.py:34
  110.2 3.2 %collective-permute-done.23.refs_5_ = bf16[256,256]{1,0:T(8,128)(2,1)S(1)} collective-permute-done((bf16[256,256]{1,0:T(8,128)(2,1)S(1)}, bf16[256,256]{1,0:T(8,128)(2,1)S(1)}, u32[]{:S(2)}, u32[]{:S(2)}) %collective-permute-start.23) | collective-permute-done | bytes 131104 | tf_op jit(solution)/shard_map/ppermute | solution.py:34
  135.3 8.5 %collective-permute-done.31 = bf16[400,256]{1,0:T(8,128)(2,1)S(1)} collective-permute-done((bf16[400,256]{1,0:T(8,128)(2,1)S(1)}, bf16[400,256]{1,0:T(8,128)(2,1)S(1)}, u32[]{:S(2)}, u32[]{:S(2)}) %collective-permute-start.31) | collective-permute-done | bytes 204832 | tf_op jit(solution)/shard_map/ppermute | solution.py:34
  148.2 3.2 %collective-permute-done.32 = bf16[400,256]{1,0:T(8,128)(2,1)S(1)} collective-permute-done((bf16[400,256]{1,0:T(8,128)(2,1)S(1)}, bf16[400,256]{1,0:T(8,128)(2,1)S(1)}, u32[]{:S(2)}, u32[]{:S(2)}) %collective-permute-start.32) | collective-permute-done | bytes 204832 | tf_op jit(solution)/shard_map/ppermute | solution.py:34
  153.0 6.2 %cholesky.3.refs_0_ = f32[256,512]{1,0:T(8,128)S(1)} custom-call(s32[26]{0:T(128)S(1)} %fusion.6.places, f32[128,256]{1,0:T(8,128)S(1)} %add_add_fusion.1.refs_0_, f32[128,256]{1,0:T(8,128)S(1)} %collective-permute-done.55.refs_1_), custom_call_target="tpu_custom_call" | custom-call | flops 3000000000 | bytes 786432 | tf_op jit(solution)/shard_map/cholesky/pallas_call | solution.py:474
  162.0 4.5 %early_sum.6.refs_3_ = f32[4096,256]{1,0:T(8,128)S(1)} custom-call(s32[26]{0:T(128)S(1)} %fusion.6.places, bf16[800,4096]{1,0:T(8,128)(2,1)S(1)} %get-tuple-element.48.refs_0_.filtered_ref, bf16[400,256]{1,0:T(8,128)(2,1)S(1)} %multiply_convert_fusion.1.refs_1_, bf16[400,256]{1,0:T(8,128)(2,1)S(1)} %multiply_convert_fusion.refs_2_), custom_call_target="tpu_custom_call" | custom-call | flops 1677721600 | bytes 4194304 | tf_op jit(solution)/shard_map/early_sum/pallas_call | solution.py:196
  166.5 4.5 %early_sum.7.refs_6_ = f32[4096,256]{1,0:T(8,128)S(1)} custom-call(s32[26]{0:T(128)S(1)} %fusion.6.places, bf16[800,4096]{1,0:T(8,128)(2,1)S(1)} %get-tuple-element.53.refs_0_.filtered_ref, bf16[400,256]{1,0:T(8,128)(2,1)S(1)} %collective-permute-done.38.refs_1_, bf16[400,256]{1,0:T(8,128)(2,1)S(1)} %collective-permute-done.41.refs_2_, ...), custom_call_target="tpu_custom_call" | custom-call | flops 1677721600 | bytes 4194304 | tf_op jit(solution)/shard_map/early_sum/pallas_call | solution.py:196
  173.3 6.8 %cholesky.4 = (f32[256,256]{1,0:T(8,128)}, f32[256,256]{1,0:T(8,128)S(1)}) custom-call(s32[26]{0:T(128)S(1)} %fusion.6.places, f32[256,512]{1,0:T(8,128)S(1)} %cholesky.3.refs_0_), custom_call_target="tpu_custom_call" | custom-call | flops 3000000000 | bytes 786432 | tf_op jit(solution)/shard_map/cholesky/pallas_call | solution.py:474
  199.2 6.3 %collective-permute-done.45.refs_0_ = bf16[256,256]{1,0:T(8,128)(2,1)S(1)} collective-permute-done((bf16[256,256]{1,0:T(8,128)(2,1)S(1)}, bf16[256,256]{1,0:T(8,128)(2,1)S(1)}, u32[]{:S(2)}, u32[]{:S(2)}) %collective-permute-start.45) | collective-permute-done | bytes 131104 | tf_op jit(solution)/shard_map/ppermute | solution.py:34
  205.5 2.7 %collective-permute-done.47.refs_1_ = bf16[256,256]{1,0:T(8,128)(2,1)S(1)} collective-permute-done((bf16[256,256]{1,0:T(8,128)(2,1)S(1)}, bf16[256,256]{1,0:T(8,128)(2,1)S(1)}, u32[]{:S(2)}, u32[]{:S(2)}) %collective-permute-start.47) | collective-permute-done | bytes 131104 | tf_op jit(solution)/shard_map/ppermute | solution.py:34
  213.4 3.0 %collective-permute-start.58 = (f32[32,256]{1,0:T(8,128)S(1)}, f32[32,256]{1,0:T(8,128)S(1)}, u32[]{:S(2)}, u32[]{:S(2)}) collective-permute-start(f32[32,256]{1,0:T(8,128)S(1)} %get-tuple-element.83), channel_id=1, source_target_pairs={{0,16},{4,20},{8,24},{12,28},{16,0},{20,4},{24,8},{28,12},{1,17},{... | collective-permute-start | bytes 98312 | tf_op jit(solution)/shard_map/ppermute | solution.py:34
  218.3 3.8 %collective-permute-done.59 = f32[32,256]{1,0:T(8,128)S(1)} collective-permute-done((f32[32,256]{1,0:T(8,128)S(1)}, f32[32,256]{1,0:T(8,128)S(1)}, u32[]{:S(2)}, u32[]{:S(2)}) %collective-permute-start.59) | collective-permute-done | bytes 32800 | tf_op jit(solution)/shard_map/ppermute | solution.py:34
  224.2 2.4 collective-permute-start.62
  234.0 3.0 %collective-permute-start.68 = (bf16[512,256]{1,0:T(8,128)(2,1)S(1)}, bf16[512,256]{1,0:T(8,128)(2,1)S(1)}, u32[]{:S(2)}, u32[]{:S(2)}) collective-permute-start(bf16[512,256]{1,0:T(8,128)(2,1)S(1)} %get-tuple-element.88.refs_0_), channel_id=1, source_target_pairs={{0,16},{4,20},{8,24},{12,28},{16,0},{20,4},{24,8},{28,12},{1,17},{... | collective-permute-start | bytes 786440 | tf_op jit(solution)/shard_map/ppermute | solution.py:34
  239.0 6.4 %collective-permute-done.67.refs_1_ = bf16[512,256]{1,0:T(8,128)(2,1)S(1)} collective-permute-done((bf16[512,256]{1,0:T(8,128)(2,1)S(1)}, bf16[512,256]{1,0:T(8,128)(2,1)S(1)}, u32[]{:S(2)}, u32[]{:S(2)}) %collective-permute-start.67) | collective-permute-done | bytes 262176 | tf_op jit(solution)/shard_map/ppermute | solution.py:34
  245.4 7.8 %collective-permute-done.68.refs_2_ = bf16[512,256]{1,0:T(8,128)(2,1)S(1)} collective-permute-done((bf16[512,256]{1,0:T(8,128)(2,1)S(1)}, bf16[512,256]{1,0:T(8,128)(2,1)S(1)}, u32[]{:S(2)}, u32[]{:S(2)}) %collective-permute-start.68) | collective-permute-done | bytes 262176 | tf_op jit(solution)/shard_map/ppermute | solution.py:34
  253.7 12.2 %cholesky.5 = (f32[256,256]{1,0:T(8,128)}, f32[256,256]{1,0:T(8,128)S(1)}) custom-call(s32[26]{0:T(128)S(1)} %fusion.6.places, f32[128,256]{1,0:T(8,128)S(1)} %add_add_fusion.refs_0_, f32[128,256]{1,0:T(8,128)S(1)} %collective-permute-done.66.refs_1_), custom_call_target="tpu_custom_call" | custom-call | flops 6000000000 | bytes 786432 | tf_op jit(solution)/shard_map/cholesky/pallas_call | solution.py:474
  265.9 4.5 %apply.1 = f32[4096,256]{1,0:T(8,128)} custom-call(s32[26]{0:T(128)S(1)} %fusion.6.places, f32[256,256]{1,0:T(8,128)S(1)} %get-tuple-element.87.inverse_ref, bf16[512,256]{1,0:T(8,128)(2,1)S(1)} %get-tuple-element.88.refs_0_, bf16[512,256]{1,0:T(8,128)(2,1)S(1)} %collective-permute-done.67.refs_1_, bf16[512,256]{1,0:T(8,128)(2,1)S(1)} %collective-permute-done.68.refs_2_, ...), custom_call_target="tpu_custom_call" | custom-call | flops 1610612736 | bytes 6291456 | tf_op jit(solution)/shard_map/apply/pallas_call | solution.py:512
  (179 shorter events, 103.7 us)
Async XLA Ops:
  12.6 27.0 %collective-permute-start = (bf16[800,256]{1,0:T(8,128)(2,1)S(1)}, bf16[800,256]{1,0:T(8,128)(2,1)S(1)}, u32[]{:S(2)}, u32[]{:S(2)}) collective-permute-start(bf16[800,256]{1,0:T(8,128)(2,1)S(1)} %get-tuple-element.50), channel_id=1, source_target_pairs={{0,3},{1,2},{2,1},{3,0},{4,7},{5,6},{6,5},{7,4},{8,11},{9,10},{10,... | collective-permute-start | bytes 1228808 | tf_op jit(solution)/shard_map/ppermute | solution.py:34
  24.0 15.6 %collective-permute-start.1 = (bf16[800,256]{1,0:T(8,128)(2,1)S(1)}, bf16[800,256]{1,0:T(8,128)(2,1)S(1)}, u32[]{:S(2)}, u32[]{:S(2)}) collective-permute-start(bf16[800,256]{1,0:T(8,128)(2,1)S(1)} %get-tuple-element.51), channel_id=1, source_target_pairs={{0,2},{1,3},{2,0},{3,1},{4,6},{5,7},{6,4},{7,5},{8,10},{9,11},{10,... | collective-permute-start | bytes 1228808 | tf_op jit(solution)/shard_map/ppermute | solution.py:34
  45.0 12.4 %collective-permute-start.8 = (bf16[400,256]{1,0:T(8,128)(2,1)S(1)}, bf16[400,256]{1,0:T(8,128)(2,1)S(1)}, u32[]{:S(2)}, u32[]{:S(2)}) collective-permute-start(bf16[400,256]{1,0:T(8,128)(2,1)S(1)} %get-tuple-element.94.refs_2_), channel_id=1, source_target_pairs={{0,1},{1,0},{2,3},{3,2},{4,5},{5,4},{6,7},{7,6},{8,9},{9,8},{10,11... | collective-permute-start | bytes 614408 | tf_op jit(solution)/shard_map/ppermute | solution.py:34
  46.5 15.5 %collective-permute-start.3 = (bf16[400,256]{1,0:T(8,128)(2,1)S(1)}, bf16[400,256]{1,0:T(8,128)(2,1)S(1)}, u32[]{:S(2)}, u32[]{:S(2)}) collective-permute-start(bf16[400,256]{1,0:T(8,128)(2,1)S(1)} %get-tuple-element.95.refs_1_), channel_id=1, source_target_pairs={{0,2},{1,3},{2,0},{3,1},{4,6},{5,7},{6,4},{7,5},{8,10},{9,11},{10,... | collective-permute-start | bytes 614408 | tf_op jit(solution)/shard_map/ppermute | solution.py:34
  75.6 12.4 %collective-permute-start.12 = (bf16[256,256]{1,0:T(8,128)(2,1)S(1)}, bf16[256,256]{1,0:T(8,128)(2,1)S(1)}, u32[]{:S(2)}, u32[]{:S(2)}) collective-permute-start(bf16[256,256]{1,0:T(8,128)(2,1)S(1)} %get-tuple-element.102), channel_id=1, source_target_pairs={{0,16},{4,20},{8,24},{12,28},{16,0},{20,4},{24,8},{28,12},{1,17},{... | collective-permute-start | bytes 393224 | tf_op jit(solution)/shard_map/ppermute | solution.py:34
  90.2 17.9 %collective-permute-start.19 = (bf16[512,256]{1,0:T(8,128)(2,1)S(1)}, bf16[512,256]{1,0:T(8,128)(2,1)S(1)}, u32[]{:S(2)}, u32[]{:S(2)}) collective-permute-start(bf16[512,256]{1,0:T(8,128)(2,1)S(1)} %pad_maximum_fusion.refs_0_), channel_id=1, source_target_pairs={{0,8},{4,12},{8,0},{12,4},{16,24},{20,28},{24,16},{28,20},{1,9},{5... | collective-permute-start | bytes 786440 | tf_op jit(solution)/shard_map/ppermute | solution.py:34
  91.5 17.2 %collective-permute-start.24 = (bf16[512,256]{1,0:T(8,128)(2,1)S(1)}, bf16[512,256]{1,0:T(8,128)(2,1)S(1)}, u32[]{:S(2)}, u32[]{:S(2)}) collective-permute-start(bf16[512,256]{1,0:T(8,128)(2,1)S(1)} %pad_maximum_fusion.refs_0_), channel_id=1, source_target_pairs={{0,4},{4,0},{8,12},{12,8},{16,20},{20,16},{24,28},{28,24},{1,5},{5... | collective-permute-start | bytes 786440 | tf_op jit(solution)/shard_map/ppermute | solution.py:34
  95.4 12.7 %collective-permute-start.22 = (bf16[256,256]{1,0:T(8,128)(2,1)S(1)}, bf16[256,256]{1,0:T(8,128)(2,1)S(1)}, u32[]{:S(2)}, u32[]{:S(2)}) collective-permute-start(bf16[256,256]{1,0:T(8,128)(2,1)S(1)} %get-tuple-element.101), channel_id=1, source_target_pairs={{0,16},{4,20},{8,24},{12,28},{16,0},{20,4},{24,8},{28,12},{1,17},{... | collective-permute-start | bytes 393224 | tf_op jit(solution)/shard_map/ppermute | solution.py:34
  116.1 15.3 %collective-permute-start.52 = (f32[128,256]{1,0:T(8,128)S(1)}, f32[128,256]{1,0:T(8,128)S(1)}, u32[]{:S(2)}, u32[]{:S(2)}) collective-permute-start(f32[128,256]{1,0:T(8,128)S(1)} %gram.1), channel_id=1, source_target_pairs={{0,1},{1,0},{2,3},{3,2},{4,5},{5,4},{6,7},{7,6},{8,9},{9,8},{10,11... | collective-permute-start | bytes 393224 | tf_op jit(solution)/shard_map/ppermute | solution.py:34
  117.6 15.4 %collective-permute-start.53 = (f32[128,256]{1,0:T(8,128)S(1)}, f32[128,256]{1,0:T(8,128)S(1)}, u32[]{:S(2)}, u32[]{:S(2)}) collective-permute-start(f32[128,256]{1,0:T(8,128)S(1)} %gram.1), channel_id=1, source_target_pairs={{0,2},{1,3},{2,0},{3,1},{4,6},{5,7},{6,4},{7,5},{8,10},{9,11},{10,... | collective-permute-start | bytes 393224 | tf_op jit(solution)/shard_map/ppermute | solution.py:34
  118.2 15.4 %collective-permute-start.54 = (f32[128,256]{1,0:T(8,128)S(1)}, f32[128,256]{1,0:T(8,128)S(1)}, u32[]{:S(2)}, u32[]{:S(2)}) collective-permute-start(f32[128,256]{1,0:T(8,128)S(1)} %gram.1), channel_id=1, source_target_pairs={{0,3},{1,2},{2,1},{3,0},{4,7},{5,6},{6,5},{7,4},{8,11},{9,10},{10,... | collective-permute-start | bytes 393224 | tf_op jit(solution)/shard_map/ppermute | solution.py:34
  122.0 11.6 %collective-permute-start.34 = (bf16[400,256]{1,0:T(8,128)(2,1)S(1)}, bf16[400,256]{1,0:T(8,128)(2,1)S(1)}, u32[]{:S(2)}, u32[]{:S(2)}) collective-permute-start(bf16[400,256]{1,0:T(8,128)(2,1)S(1)} %get-tuple-element.68), channel_id=1, source_target_pairs={{0,2},{1,3},{2,0},{3,1},{4,6},{5,7},{6,4},{7,5},{8,10},{9,11},{10,... | collective-permute-start | bytes 614408 | tf_op jit(solution)/shard_map/ppermute | solution.py:34
  126.0 19.4 %collective-permute-start.36 = (bf16[400,256]{1,0:T(8,128)(2,1)S(1)}, bf16[400,256]{1,0:T(8,128)(2,1)S(1)}, u32[]{:S(2)}, u32[]{:S(2)}) collective-permute-start(bf16[400,256]{1,0:T(8,128)(2,1)S(1)} %get-tuple-element.69), channel_id=1, source_target_pairs={{0,2},{1,3},{2,0},{3,1},{4,6},{5,7},{6,4},{7,5},{8,10},{9,11},{10,... | collective-permute-start | bytes 614408 | tf_op jit(solution)/shard_map/ppermute | solution.py:34
  131.4 16.8 %collective-permute-start.30 = (bf16[400,256]{1,0:T(8,128)(2,1)S(1)}, bf16[400,256]{1,0:T(8,128)(2,1)S(1)}, u32[]{:S(2)}, u32[]{:S(2)}) collective-permute-start(bf16[400,256]{1,0:T(8,128)(2,1)S(1)} %get-tuple-element.63), channel_id=1, source_target_pairs={{0,1},{1,0},{2,3},{3,2},{4,5},{5,4},{6,7},{7,6},{8,9},{9,8},{10,11... | collective-permute-start | bytes 614408 | tf_op jit(solution)/shard_map/ppermute | solution.py:34
  133.6 19.4 %collective-permute-start.55 = (f32[128,256]{1,0:T(8,128)S(1)}, f32[128,256]{1,0:T(8,128)S(1)}, u32[]{:S(2)}, u32[]{:S(2)}) collective-permute-start(f32[128,256]{1,0:T(8,128)S(1)} %add_add_fusion.1.refs_0_), channel_id=1, source_target_pairs={{0,4},{4,0},{8,12},{12,8},{16,20},{20,16},{24,28},{28,24},{1,5},{5... | collective-permute-start | bytes 393224 | tf_op jit(solution)/shard_map/ppermute | solution.py:34
  133.7 12.3 %collective-permute-start.35 = (bf16[400,256]{1,0:T(8,128)(2,1)S(1)}, bf16[400,256]{1,0:T(8,128)(2,1)S(1)}, u32[]{:S(2)}, u32[]{:S(2)}) collective-permute-start(bf16[400,256]{1,0:T(8,128)(2,1)S(1)} %add_convert_fusion.2), channel_id=1, source_target_pairs={{0,1},{1,0},{2,3},{3,2},{4,5},{5,4},{6,7},{7,6},{8,9},{9,8},{10,11... | collective-permute-start | bytes 614408 | tf_op jit(solution)/shard_map/ppermute | solution.py:34
  146.1 20.3 %collective-permute-start.41 = (bf16[400,256]{1,0:T(8,128)(2,1)S(1)}, bf16[400,256]{1,0:T(8,128)(2,1)S(1)}, u32[]{:S(2)}, u32[]{:S(2)}) collective-permute-start(bf16[400,256]{1,0:T(8,128)(2,1)S(1)} %multiply_convert_fusion.refs_2_), channel_id=1, source_target_pairs={{0,1},{1,0},{2,3},{3,2},{4,5},{5,4},{6,7},{7,6},{8,9},{9,8},{10,11... | collective-permute-start | bytes 614408 | tf_op jit(solution)/shard_map/ppermute | solution.py:34
  147.7 12.2 %collective-permute-start.37 = (bf16[400,256]{1,0:T(8,128)(2,1)S(1)}, bf16[400,256]{1,0:T(8,128)(2,1)S(1)}, u32[]{:S(2)}, u32[]{:S(2)}) collective-permute-start(bf16[400,256]{1,0:T(8,128)(2,1)S(1)} %multiply_convert_fusion.refs_2_), channel_id=1, source_target_pairs={{0,2},{1,3},{2,0},{3,1},{4,6},{5,7},{6,4},{7,5},{8,10},{9,11},{10,... | collective-permute-start | bytes 614408 | tf_op jit(solution)/shard_map/ppermute | solution.py:34
  159.2 11.8 %collective-permute-start.33 = (bf16[400,256]{1,0:T(8,128)(2,1)S(1)}, bf16[400,256]{1,0:T(8,128)(2,1)S(1)}, u32[]{:S(2)}, u32[]{:S(2)}) collective-permute-start(bf16[400,256]{1,0:T(8,128)(2,1)S(1)} %multiply_convert_fusion.1.refs_1_), channel_id=1, source_target_pairs={{0,2},{1,3},{2,0},{3,1},{4,6},{5,7},{6,4},{7,5},{8,10},{9,11},{10,... | collective-permute-start | bytes 614408 | tf_op jit(solution)/shard_map/ppermute | solution.py:34
  185.0 11.9 %collective-permute-start.48 = (bf16[512,256]{1,0:T(8,128)(2,1)S(1)}, bf16[512,256]{1,0:T(8,128)(2,1)S(1)}, u32[]{:S(2)}, u32[]{:S(2)}) collective-permute-start(bf16[512,256]{1,0:T(8,128)(2,1)S(1)} %get-tuple-element.75), channel_id=1, source_target_pairs={{0,4},{4,0},{8,12},{12,8},{16,20},{20,16},{24,28},{28,24},{1,5},{5... | collective-permute-start | bytes 786440 | tf_op jit(solution)/shard_map/ppermute | solution.py:34
  193.9 11.6 %collective-permute-start.45 = (bf16[256,256]{1,0:T(8,128)(2,1)S(1)}, bf16[256,256]{1,0:T(8,128)(2,1)S(1)}, u32[]{:S(2)}, u32[]{:S(2)}) collective-permute-start(bf16[256,256]{1,0:T(8,128)(2,1)S(1)} %get-tuple-element.99), channel_id=1, source_target_pairs={{0,16},{4,20},{8,24},{12,28},{16,0},{20,4},{24,8},{28,12},{1,17},{... | collective-permute-start | bytes 393224 | tf_op jit(solution)/shard_map/ppermute | solution.py:34
  195.3 13.0 %collective-permute-start.47 = (bf16[256,256]{1,0:T(8,128)(2,1)S(1)}, bf16[256,256]{1,0:T(8,128)(2,1)S(1)}, u32[]{:S(2)}, u32[]{:S(2)}) collective-permute-start(bf16[256,256]{1,0:T(8,128)(2,1)S(1)} %get-tuple-element.98), channel_id=1, source_target_pairs={{0,16},{4,20},{8,24},{12,28},{16,0},{20,4},{24,8},{28,12},{1,17},{... | collective-permute-start | bytes 393224 | tf_op jit(solution)/shard_map/ppermute | solution.py:34
  197.0 11.5 %collective-permute-start.49 = (bf16[256,256]{1,0:T(8,128)(2,1)S(1)}, bf16[256,256]{1,0:T(8,128)(2,1)S(1)}, u32[]{:S(2)}, u32[]{:S(2)}) collective-permute-start(bf16[256,256]{1,0:T(8,128)(2,1)S(1)} %get-tuple-element.105), channel_id=1, source_target_pairs={{0,8},{4,12},{8,0},{12,4},{16,24},{20,28},{24,16},{28,20},{1,9},{5... | collective-permute-start | bytes 393224 | tf_op jit(solution)/shard_map/ppermute | solution.py:34
  197.4 12.5 %collective-permute-start.50 = (bf16[256,256]{1,0:T(8,128)(2,1)S(1)}, bf16[256,256]{1,0:T(8,128)(2,1)S(1)}, u32[]{:S(2)}, u32[]{:S(2)}) collective-permute-start(bf16[256,256]{1,0:T(8,128)(2,1)S(1)} %get-tuple-element.104), channel_id=1, source_target_pairs={{0,8},{4,12},{8,0},{12,4},{16,24},{20,28},{24,16},{28,20},{1,9},{5... | collective-permute-start | bytes 393224 | tf_op jit(solution)/shard_map/ppermute | solution.py:34
  234.0 11.4 %collective-permute-start.67 = (bf16[512,256]{1,0:T(8,128)(2,1)S(1)}, bf16[512,256]{1,0:T(8,128)(2,1)S(1)}, u32[]{:S(2)}, u32[]{:S(2)}) collective-permute-start(bf16[512,256]{1,0:T(8,128)(2,1)S(1)} %get-tuple-element.88.refs_0_), channel_id=1, source_target_pairs={{0,8},{4,12},{8,0},{12,4},{16,24},{20,28},{24,16},{28,20},{1,9},{5... | collective-permute-start | bytes 786440 | tf_op jit(solution)/shard_map/ppermute | solution.py:34
  234.0 19.2 %collective-permute-start.68 = (bf16[512,256]{1,0:T(8,128)(2,1)S(1)}, bf16[512,256]{1,0:T(8,128)(2,1)S(1)}, u32[]{:S(2)}, u32[]{:S(2)}) collective-permute-start(bf16[512,256]{1,0:T(8,128)(2,1)S(1)} %get-tuple-element.88.refs_0_), channel_id=1, source_target_pairs={{0,16},{4,20},{8,24},{12,28},{16,0},{20,4},{24,8},{28,12},{1,17},{... | collective-permute-start | bytes 786440 | tf_op jit(solution)/shard_map/ppermute | solution.py:34
  237.0 16.2 %collective-permute-start.69 = (bf16[512,256]{1,0:T(8,128)(2,1)S(1)}, bf16[512,256]{1,0:T(8,128)(2,1)S(1)}, u32[]{:S(2)}, u32[]{:S(2)}) collective-permute-start(bf16[512,256]{1,0:T(8,128)(2,1)S(1)} %get-tuple-element.88.refs_0_), channel_id=1, source_target_pairs={{0,24},{4,28},{8,16},{12,20},{16,8},{20,12},{24,0},{28,4},{1,25},{... | collective-permute-start | bytes 786440 | tf_op jit(solution)/shard_map/ppermute | solution.py:34
  238.4 15.3 %collective-permute-start.66 = (f32[128,256]{1,0:T(8,128)S(1)}, f32[128,256]{1,0:T(8,128)S(1)}, u32[]{:S(2)}, u32[]{:S(2)}) collective-permute-start(f32[128,256]{1,0:T(8,128)S(1)} %add_add_fusion.refs_0_), channel_id=1, source_target_pairs={{0,4},{4,0},{8,12},{12,8},{16,20},{20,16},{24,28},{28,24},{1,5},{5... | collective-permute-start | bytes 393224 | tf_op jit(solution)/shard_map/ppermute | solution.py:34
  238.5 27.4 %collective-permute-start.70 = (bf16[512,256]{1,0:T(8,128)(2,1)S(1)}, bf16[512,256]{1,0:T(8,128)(2,1)S(1)}, u32[]{:S(2)}, u32[]{:S(2)}) collective-permute-start(bf16[512,256]{1,0:T(8,128)(2,1)S(1)} %get-tuple-element.88.refs_0_), channel_id=1, source_target_pairs={{0,4},{4,0},{8,12},{12,8},{16,20},{20,16},{24,28},{28,24},{1,5},{5... | collective-permute-start | bytes 786440 | tf_op jit(solution)/shard_map/ppermute | solution.py:34
  245.4 20.5 %collective-permute-start.71 = (bf16[512,256]{1,0:T(8,128)(2,1)S(1)}, bf16[512,256]{1,0:T(8,128)(2,1)S(1)}, u32[]{:S(2)}, u32[]{:S(2)}) collective-permute-start(bf16[512,256]{1,0:T(8,128)(2,1)S(1)} %collective-permute-done.67.refs_1_), channel_id=1, source_target_pairs={{0,4},{4,0},{8,12},{12,8},{16,20},{20,16},{24,28},{28,24},{1,5},{5... | collective-permute-start | bytes 786440 | tf_op jit(solution)/shard_map/ppermute | solution.py:34
  253.2 12.7 %collective-permute-start.72 = (bf16[512,256]{1,0:T(8,128)(2,1)S(1)}, bf16[512,256]{1,0:T(8,128)(2,1)S(1)}, u32[]{:S(2)}, u32[]{:S(2)}) collective-permute-start(bf16[512,256]{1,0:T(8,128)(2,1)S(1)} %collective-permute-done.68.refs_2_), channel_id=1, source_target_pairs={{0,4},{4,0},{8,12},{12,8},{16,20},{20,16},{24,28},{28,24},{1,5},{5... | collective-permute-start | bytes 786440 | tf_op jit(solution)/shard_map/ppermute | solution.py:34
  253.2 12.7 %collective-permute-start.73 = (bf16[512,256]{1,0:T(8,128)(2,1)S(1)}, bf16[512,256]{1,0:T(8,128)(2,1)S(1)}, u32[]{:S(2)}, u32[]{:S(2)}) collective-permute-start(bf16[512,256]{1,0:T(8,128)(2,1)S(1)} %collective-permute-done.69.refs_3_), channel_id=1, source_target_pairs={{0,4},{4,0},{8,12},{12,8},{16,20},{20,16},{24,28},{28,24},{1,5},{5... | collective-permute-start | bytes 786440 | tf_op jit(solution)/shard_map/ppermute | solution.py:34
  (44 other events, 308.4 us)

commit v6 on v5

--- a/solution.py
+++ b/solution.py
@@ -105,31 +105,45 @@
     return [jnp.concatenate(blocks[at], 0) for at in sorted(blocks)]
 
 
-def score_kernel(first, width, spots, places, filtered_ref, *refs):
+def score_kernel(first, width, spots, count, spans, places, *refs):
+    filtered_refs, refs = refs[:count], refs[count:]
     *basis_refs, top_ref, low_ref = refs
     rows = top_ref.shape[0]
-    total = None
-    for at, block in enumerate(whole_blocks(spots, basis_refs)):
-        columns = pl.ds(pl.multiple_of(places[first + at] * width, width), width)
-        term = jnp.dot(filtered_ref[:, columns], block, preferred_element_type=F32)
-        total = term if total is None else total + term
-    top_ref[...] = total[:rows].astype(top_ref.dtype)
-    low_ref[...] = total[rows:].astype(low_ref.dtype)
-
-
-def score(places, first, filtered, basis, out_types):
-    rows, pixels = filtered.shape
+    blocks = whole_blocks(spots, basis_refs)
+    totals = []
+    for which, begin, size in spans:
+        total = None
+        for at, block in enumerate(blocks):
+            columns = pl.ds(pl.multiple_of(places[first + at] * width, width), width)
+            left = filtered_refs[which][begin : begin + size, columns]
+            term = jnp.dot(left, block, preferred_element_type=F32)
+            total = term if total is None else total + term
+        totals.append(total)
+    if len(totals) == 1:
+        totals = [totals[0][:rows], totals[0][rows:]]
+    top_ref[...] = totals[0].astype(top_ref.dtype)
+    low_ref[...] = totals[1].astype(low_ref.dtype)
+
+
+def score(places, first, filtered, chosen, basis, out_types):
+    rows, pixels = filtered[0].shape
+    half = rows // 2
+    used = sorted({at for at, _ in chosen})
+    if len(used) == 1:
+        spans = [(0, 0, rows)]
+    else:
+        spans = [(used.index(at), which * half, half) for at, which in chosen]
     spots, blocks = [piece[:2] for piece in basis], [piece[2] for piece in basis]
     columns = blocks[0].shape[1]
     width = pixels // (1 + max(at for at, _ in spots))
     return pl.pallas_call(
-        functools.partial(score_kernel, first, width, spots),
-        grid_spec=prefetched(1 + len(basis), 2),
-        out_shape=[jax.ShapeDtypeStruct((rows // 2, columns), kind) for kind in out_types],
+        functools.partial(score_kernel, first, width, spots, len(used), spans),
+        grid_spec=prefetched(len(used) + len(basis), 2),
+        out_shape=[jax.ShapeDtypeStruct((half, columns), kind) for kind in out_types],
         compiler_params=vmem(16 * 2**20),
         cost_estimate=cost(2 * rows * pixels * columns, 2 * rows * columns),
         name="score",
-    )(places, filtered, *blocks)
+    )(places, *[filtered[at] for at in used], *blocks)
 
 
 def sum_blocks(filtered, scaled):
@@ -148,29 +162,23 @@
     return total
 
 
-def stack_pieces(stacked_ref, pieces):
-    rows = pieces[0].shape[0]
-    for at, ref in enumerate(pieces):
-        stacked_ref[at * rows : (at + 1) * rows, :] = ref[...]
-
-
-def block_sum(filtered_refs, stacked_ref, columns):
-    rows = filtered_refs[0].shape[0]
-    return sum_blocks(
-        [ref[:, columns] for ref in filtered_refs],
-        [stacked_ref[at * rows : (at + 1) * rows, :] for at in range(len(filtered_refs))],
-    )
-
-
-def early_sum_kernel(count, first, width, places, *refs):
-    filtered_refs, piece_refs = refs[:count], refs[count : 3 * count]
-    before, out_ref, stacked_ref = refs[3 * count : -2], refs[-2], refs[-1]
-    stack_pieces(stacked_ref, piece_refs)
+def entry_sum(entries, filtered_refs, piece_refs, columns):
+    rows = piece_refs[0].shape[0]
+    blocks = [
+        filtered_refs[at][half * rows : (half + 1) * rows, columns] for at, half in entries
+    ]
+    return sum_blocks(blocks, [ref[...] for ref in piece_refs])
+
+
+def early_sum_kernel(count, entries, first, width, places, *refs):
+    *refs, out_ref = refs
+    filtered_refs, refs = refs[:count], refs[count:]
+    piece_refs, before = refs[: len(entries)], refs[len(entries) :]
 
     def block(at, carry):
         columns = pl.ds(pl.multiple_of(places[first + at] * width, width), width)
         here = pl.ds(pl.multiple_of(at * width, width), width)
-        total = block_sum(filtered_refs, stacked_ref, columns)
+        total = entry_sum(entries, filtered_refs, piece_refs, columns)
         for ref in before:
             total = total + ref[here, :]
         out_ref[here, :] = total
@@ -179,41 +187,36 @@
     lax.fori_loop(0, out_ref.shape[0] // width, block, 0)
 
 
-def sum_grid(count, extra, outs, rows, columns):
-    return pltpu.PrefetchScalarGridSpec(
-        num_scalar_prefetch=1,
-        grid=(),
-        in_specs=[in_vmem()] * (3 * count + extra),
-        out_specs=[in_vmem()] * outs,
-        scratch_shapes=[pltpu.VMEM((count * rows, columns), BF16)],
-    )
-
-
-def early_sum(places, first, filtered, scaled, width, before):
-    count = len(filtered)
-    rows, pixels = filtered[0].shape
-    columns = scaled[0][0].shape[1]
+def take_entries(filtered, scaled, chosen):
+    used = sorted({at for at, _ in chosen})
+    entries = [(used.index(at), half) for at, half in chosen]
+    return entries, [filtered[at] for at in used], [scaled[at][half] for at, half in chosen]
+
+
+def early_sum(places, first, filtered, scaled, chosen, width, before):
+    entries, blocks, pieces = take_entries(filtered, scaled, chosen)
+    pixels = blocks[0].shape[1]
+    rows, columns = pieces[0].shape
     return pl.pallas_call(
-        functools.partial(early_sum_kernel, count, first, width),
-        grid_spec=sum_grid(count, len(before), 1, rows, columns),
+        functools.partial(early_sum_kernel, len(blocks), entries, first, width),
+        grid_spec=prefetched(len(blocks) + len(pieces) + len(before), 1),
         out_shape=[jax.ShapeDtypeStruct((pixels, columns), F32)],
         compiler_params=vmem(12 * 2**20),
-        cost_estimate=cost(2 * count * rows * pixels * columns, 4 * pixels * columns),
+        cost_estimate=cost(2 * len(pieces) * rows * pixels * columns, 4 * pixels * columns),
         name="early_sum",
-    )(places, *filtered, *sum(scaled, []), *before)[0]
-
-
-def late_sum_kernel(count, first, at_early, places, *refs):
-    filtered_refs, piece_refs = refs[:count], refs[count : 3 * count]
-    early_ref = refs[3 * count]
-    send_ref, keep_ref, stacked_ref = refs[-3:]
+    )(places, *blocks, *pieces, *before)[0]
+
+
+def late_sum_kernel(count, entries, first, at_early, places, *refs):
+    filtered_refs, piece_refs = refs[:count], refs[count : count + len(entries)]
+    early_ref = refs[count + len(entries)]
+    send_ref, keep_ref = refs[-2:]
     width = send_ref.shape[0]
-    stack_pieces(stacked_ref, piece_refs)
 
     def block(at, carry):
         columns = pl.ds(pl.multiple_of(places[first + at] * width, width), width)
         here = pl.ds(pl.multiple_of((at_early + at) * width, width), width)
-        total = early_ref[here, :] + block_sum(filtered_refs, stacked_ref, columns)
+        total = early_ref[here, :] + entry_sum(entries, filtered_refs, piece_refs, columns)
 
         @pl.when(at == 0)
         def _():
@@ -228,21 +231,20 @@
     lax.fori_loop(0, 2, block, 0)
 
 
-def late_sum(places, first, at_early, filtered, scaled, early, width, after):
-    count = len(filtered)
-    rows = filtered[0].shape[0]
-    columns = scaled[0][0].shape[1]
+def late_sum(places, first, at_early, filtered, scaled, chosen, early, width, after):
+    entries, blocks, pieces = take_entries(filtered, scaled, chosen)
+    rows, columns = pieces[0].shape
     return pl.pallas_call(
-        functools.partial(late_sum_kernel, count, first, at_early),
-        grid_spec=sum_grid(count, 1 + len(after), 2, rows, columns),
+        functools.partial(late_sum_kernel, len(blocks), entries, first, at_early),
+        grid_spec=prefetched(len(blocks) + len(pieces) + 1 + len(after), 2),
         out_shape=[
             jax.ShapeDtypeStruct((width, columns), BF16),
             jax.ShapeDtypeStruct((width, columns), F32),
         ],
         compiler_params=vmem(12 * 2**20),
-        cost_estimate=cost(4 * count * rows * width * columns, 6 * width * columns),
+        cost_estimate=cost(4 * len(pieces) * rows * width * columns, 6 * width * columns),
         name="late_sum",
-    )(places, *filtered, *sum(scaled, []), early, *after)
+    )(places, *blocks, *pieces, early, *after)
 
 
 def tree_sum(terms):
@@ -318,49 +320,6 @@
         cost_estimate=cost(14 * rows * columns * columns, 8 * rows * columns),
         name="normalize",
     )(places, *parts, inverse)
-
-
-def scatter_kernel(first, places, keep_ref, got_ref, *piece_refs):
-    rows = piece_refs[0].shape[0]
-    for at, ref in enumerate(piece_refs):
-        here = pl.ds(pl.multiple_of(places[first + at] * rows, rows), rows)
-        ref[...] = keep_ref[here, :] + got_ref[here, :]
-
-
-def scatter_rows(places, first, keep, got, count):
-    rows, columns = keep.shape
-    return pl.pallas_call(
-        functools.partial(scatter_kernel, first),
-        grid_spec=prefetched(2, count),
-        out_shape=[jax.ShapeDtypeStruct((rows // count, columns), F32)] * count,
-        compiler_params=vmem(4 * 2**20),
-        cost_estimate=cost(rows * columns, 12 * rows * columns),
-        name="scatter",
-    )(places, keep, got)
-
-
-def gather_kernel(first, count, places, *refs):
-    piece_refs, (block_ref, out_ref, block_out_ref) = refs[:count], refs[count:]
-    rows = piece_refs[0].shape[0]
-    for at, ref in enumerate(piece_refs):
-        out_ref[pl.ds(pl.multiple_of(places[first + at] * rows, rows), rows), :] = ref[...]
-    block_out_ref[...] = block_ref[...]
-
-
-def gather_rows(places, first, pieces, block):
-    count = len(pieces)
-    rows, columns = pieces[0].shape
-    return pl.pallas_call(
-        functools.partial(gather_kernel, first, count),
-        grid_spec=prefetched(count + 1, 2),
-        out_shape=[
-            jax.ShapeDtypeStruct((rows * count, columns), F32),
-            jax.ShapeDtypeStruct(block.shape, block.dtype),
-        ],
-        compiler_params=vmem(4 * 2**20),
-        cost_estimate=cost(rows * columns, 8 * count * rows * columns),
-        name="gather",
-    )(places, *pieces, block)
 
 
 def square_places(size):
@@ -533,15 +492,13 @@
     rows, gathered = 0, pix
     pairs = gathered + img
     cores = pairs + img
-    levels = cores + 2
-    at = jnp.arange(levels + depth, dtype=jnp.int32)
+    at = jnp.arange(cores + 2, dtype=jnp.int32)
     block = at - gathered
     pair = at - pairs
     table = jnp.where(at < gathered, me ^ at, (core ^ (block // depth)) * depth + (level ^ (block % depth)))
     table = jnp.where(at < pairs, table, (core ^ 1 ^ (pair % 2)) * depth + (level ^ (pair // 2)))
     table = jnp.where(at < cores, table, core ^ (at - cores))
-    table = jnp.where(at < levels, table, level ^ (at - levels))
-    return table, rows, gathered, pairs, cores, levels
+    return table, rows, gathered, pairs, cores
 
 
 def level_order(depth):
@@ -607,24 +564,29 @@
 
 
 def score_and_scatter(places, gathered_at, filtered, basis, pix):
-    def scores(shift, *kinds):
-        return score(places, gathered_at, filtered[shift], basis, kinds)
+    def scores(chosen, *kinds):
+        return score(places, gathered_at, filtered, chosen, basis, kinds)
 
     def swap(value, shift):
         return xor_swap(value, "pix", shift)
 
+    def both(shift):
+        return [(shift, 0), (shift, 1)]
+
     if pix != 4:
-        arrived = [[swap(half, s) for half in scores(s, BF16, BF16)] for s in range(pix - 1, 0, -1)]
-        return scores(0, F32, F32), arrived
-    far = scores(3, BF16, BF16)
+        arrived = [
+            [swap(part, s) for part in scores(both(s), BF16, BF16)]
+            for s in range(pix - 1, 0, -1)
+        ]
+        return scores(both(0), F32, F32), arrived
+    far = scores(both(3), BF16, BF16)
     by_x, by_y = swap(far[0], 1), swap(far[1], 2)
-    x_top, x_low = scores(1, BF16, F32)
-    from_x = [swap(x_top, 1), None]
-    y_top, y_low = scores(2, F32, BF16)
-    from_y = [None, swap(y_low, 2)]
-    own = scores(0, F32, F32)
+    x_top, y_low = scores([(1, 0), (2, 1)], BF16, BF16)
+    from_x, from_y = [swap(x_top, 1), None], [None, swap(y_low, 2)]
+    x_low, y_top = scores([(1, 1), (2, 0)], F32, F32)
+    from_x[1] = swap(add_round(x_low, by_y), 1)
     from_y[0] = swap(add_round(y_top, by_x), 2)
-    from_x[1] = swap(add_round(x_low, by_y), 1)
+    own = scores(both(0), F32, F32)
     return own, [from_x, from_y]
 
 
@@ -636,11 +598,12 @@
     width = pixels // img
     me = lax.axis_index("pix")
     place = lax.axis_index("img")
-    places, rows_at, gathered_at, pairs_at, cores_at, levels_at = place_table(
+    places, rows_at, gathered_at, pairs_at, cores_at = place_table(
         me, place & 1, place >> 1, pix, depth
     )
-    weight_share = lax.dynamic_slice_in_dim(weights, me * chunk, chunk, 0)
-    places = places + (weight_share[0] > 2.0).astype(jnp.int32)
+    begin = (me * chunk).astype(jnp.uint32)
+    places = places + (begin > jnp.uint32(images_here)).astype(jnp.int32)
+    weight_share = lax.dynamic_slice(weights, (begin,), (chunk,))
     weight_share = row_halves(weight_share[:, None])
 
     shifts = list(range(pix - 1, -1, -1))
@@ -674,18 +637,23 @@
             share.append((here * total).astype(BF16))
         scaled = spread(share, pix)
 
-        early = early_sum(places, pairs_at, filtered[:1], scaled[:1], width, [])
-        split = pix // 2
-        if split > 1:
-            early = early_sum(places, pairs_at, filtered[1:split], scaled[1:split], width, [early])
+        rows_of = [(at, half) for at in range(pix) for half in (0, 1)]
+        early_rows = [(1, 0), (2, 1)] if pix == 4 else rows_of[2:pix]
+        late_rows = [row for row in rows_of[2:] if row not in early_rows]
+        early = early_sum(places, pairs_at, filtered, scaled, rows_of[:2], width, [])
+        if early_rows:
+            early = early_sum(
+                places, pairs_at, filtered, scaled, early_rows, width, [early]
+            )
         parts, relay, after = [], None, []
         for s in level_order(depth):
             send, keep = late_sum(
                 places,
                 pairs_at + 2 * s,
                 2 * s,
-                filtered[split:],
-                scaled[split:],
+                filtered,
+                scaled,
+                late_rows,
                 early,
                 width,
                 after[-2:-1],
@@ -713,10 +681,11 @@
         own, arrived = score_and_scatter(places, gathered_at, filtered, basis, pix)
 
     half, send, keep = normalize_and_gram(places, cores_at, sum(parts, []), inverse, 1.0 / RANGE)
-    pieces = scatter_rows(places, levels_at, keep, xor_swap(send, "img", 1), depth)
-    mine = tree_sum([pieces[0]] + [xor_swap(pieces[s], "img", 2 * s) for s in range(1, depth)])
-    pieces = [mine] + [xor_swap(mine, "img", 2 * s) for s in range(1, depth)]
-    gram, half = gather_rows(places, levels_at, pieces, half)
+    gram = keep + xor_swap(send, "img", 1)
+    step = 1
+    while step < depth:
+        gram = gram + xor_swap(gram, "img", 2 * step)
+        step *= 2
     gram = add_over_pix(gram, pix)
     other = xor_swap(gram, "img", 1)
     near = [half] + [xor_swap(half, "img", 2 * s) for s in range(1, depth)]

time: 271 us -> 267 us (0.985)
  starting transfers between devices: 70 us -> 64.2 us
    ppermute x74 -> x70, starting transfers between devices: 70 us -> 64.2 us  [xor_swap(): return lax.ppermute(value, axis, [(i, i ^ mask) for i in range(size)])]
    ppermute x74 -> x70, waiting for transfers between devices: 85 us -> 86.7 us  [xor_swap(): return lax.ppermute(value, axis, [(i, i ^ mask) for i in range(size)])]
    pallas_call x18 -> x16, Pallas kernels: 46.1 us -> 45.7 us  [the longest x4 19.2 us: early_sum(): pl.pallas_call(functools.partial(early_sum_kernel, len(blocks), entries,...]
  transfers between devices with their start and end apart: 74 -> 70, of which waited for: 28 -> 25; matrix products, arithmetic and copies ran while one was open for 0% -> 1% of each run, Pallas kernels for 33% -> 34%
where the time goes in v6:
time: 267 us; the launch traced here: 265 us
  Pallas kernels  108 us (40%)
  waiting for transfers between devices  86.7 us (32%)
  starting transfers between devices  64.2 us (24%)
  other arithmetic  3.97 us (1%)
    ppermute x70, waiting for transfers between devices, xor_swap(): return lax.ppermute(value, axis, [(i, i ^ mask) for i in range(size)])  86.7 us
    ppermute x70, starting transfers between devices, xor_swap(): return lax.ppermute(value, axis, [(i, i ^ mask) for i in range(size)])  64.2 us
    pallas_call x4, Pallas kernels, filter_and_score(): pl.pallas_call(filter_kernel, grid_spec=pltpu.PrefetchScalarGridSpec(num_...  29.7 us
    pallas_call x3, Pallas kernels, cholesky_and_inverse(): pl.pallas_call(functools.partial(cholesky_kernel, first, last, place_at),...  25 us
    pallas_call x4, Pallas kernels, early_sum(): pl.pallas_call(functools.partial(early_sum_kernel, len(blocks), entries,...  19.2 us
    pallas_call x8, Pallas kernels, late_sum(): pl.pallas_call(functools.partial(late_sum_kernel, len(blocks), entries, f...  16.9 us
    pallas_call x4, Pallas kernels, score(): pl.pallas_call(functools.partial(score_kernel, first, width, spots, len(u...  9.58 us
  transfers between devices with their start and end apart: 70, of which 25 were waited for; matrix products, arithmetic and copies ran while one was open for 1% of the time, Pallas kernels for 34%

profile of v6, /device:TPU:0, one launch (start us, length us, event | category | flops | bytes accessed | tf_op | source)
XLA Modules:
  0.0 264.8 jit_solution(6582495444438120275)
XLA Ops:
  0.7 2.4 convert_element_type.138.probe_ref
  3.3 7.4 %filter_and_score.6 = (bf16[800,4096]{1,0:T(8,128)(2,1)S(1)}, bf16[800,256]{1,0:T(8,128)(2,1)S(1)}) custom-call(s32[22]{0:T(128)S(1)} %fusion.6.places, s32[8,1,400]{2,1,0:T(1,128)S(1)} %reshape.18.class_ref, bf16[3200,4096]{1,0:T(8,128)(2,1)} %image_ref.7, bf16[64,4096]{1,0:T(8,128)(2,1)S(1)} %copy-done, bf16[4096,256]{1,0:T(8,128)(2,1)S(1)} %convert_element_type.138.probe_ref), custom_call_target="tpu_custom_call" | custom-call | flops 3355443200 | bytes 6553600 | tf_op jit(solution)/shard_map/filter_and_score/pallas_call | solution.py:69
  10.7 4.0 %collective-permute-start = (bf16[800,256]{1,0:T(8,128)(2,1)S(1)}, bf16[800,256]{1,0:T(8,128)(2,1)S(1)}, u32[]{:S(2)}, u32[]{:S(2)}) collective-permute-start(bf16[800,256]{1,0:T(8,128)(2,1)S(1)} %get-tuple-element.45), channel_id=1, source_target_pairs={{0,3},{1,2},{2,1},{3,0},{4,7},{5,6},{6,5},{7,4},{8,11},{9,10},{10,... | collective-permute-start | bytes 1228808 | tf_op jit(solution)/shard_map/ppermute | solution.py:34
  14.7 7.4 %filter_and_score.5 = (bf16[800,4096]{1,0:T(8,128)(2,1)S(1)}, bf16[800,256]{1,0:T(8,128)(2,1)S(1)}) custom-call(s32[22]{0:T(128)S(1)} %fusion.6.places, s32[8,1,400]{2,1,0:T(1,128)S(1)} %reshape.18.class_ref, bf16[3200,4096]{1,0:T(8,128)(2,1)} %image_ref.7, bf16[64,4096]{1,0:T(8,128)(2,1)S(1)} %copy-done, bf16[4096,256]{1,0:T(8,128)(2,1)S(1)} %convert_element_type.138.probe_ref), custom_call_target="tpu_custom_call" | custom-call | flops 3355443200 | bytes 6553600 | tf_op jit(solution)/shard_map/filter_and_score/pallas_call | solution.py:69
  22.7 7.4 %filter_and_score.4 = (bf16[800,4096]{1,0:T(8,128)(2,1)S(1)}, bf16[800,256]{1,0:T(8,128)(2,1)S(1)}) custom-call(s32[22]{0:T(128)S(1)} %fusion.6.places, s32[8,1,400]{2,1,0:T(1,128)S(1)} %reshape.18.class_ref, bf16[3200,4096]{1,0:T(8,128)(2,1)} %image_ref.7, bf16[64,4096]{1,0:T(8,128)(2,1)S(1)} %copy-done, bf16[4096,256]{1,0:T(8,128)(2,1)S(1)} %convert_element_type.138.probe_ref), custom_call_target="tpu_custom_call" | custom-call | flops 3355443200 | bytes 6553600 | tf_op jit(solution)/shard_map/filter_and_score/pallas_call | solution.py:69
  31.1 7.4 %filter_and_score.7 = (bf16[800,4096]{1,0:T(8,128)(2,1)S(1)}, f32[800,256]{1,0:T(8,128)S(1)}) custom-call(s32[22]{0:T(128)S(1)} %fusion.6.places, s32[8,1,400]{2,1,0:T(1,128)S(1)} %reshape.18.class_ref, bf16[3200,4096]{1,0:T(8,128)(2,1)} %image_ref.7, bf16[64,4096]{1,0:T(8,128)(2,1)S(1)} %copy-done.1, bf16[4096,256]{1,0:T(8,128)(2,1)S(1)} %convert_element_type.138.probe_ref), custom_call_target="tpu_custom_call" | custom-call | flops 3355443200 | bytes 6553600 | tf_op jit(solution)/shard_map/filter_and_score/pallas_call | solution.py:69
  45.2 3.9 %collective-permute-done.5.refs_2_ = bf16[400,256]{1,0:T(8,128)(2,1)S(1)} collective-permute-done((bf16[400,256]{1,0:T(8,128)(2,1)S(1)}, bf16[400,256]{1,0:T(8,128)(2,1)S(1)}, u32[]{:S(2)}, u32[]{:S(2)}) %collective-permute-start.5) | collective-permute-done | bytes 204832 | tf_op jit(solution)/shard_map/ppermute | solution.py:34
  51.2 4.7 %early_sum.4.refs_4_ = f32[4096,256]{1,0:T(8,128)S(1)} custom-call(s32[22]{0:T(128)S(1)} %fusion.6.places, bf16[800,4096]{1,0:T(8,128)(2,1)S(1)} %get-tuple-element.43.refs_0_, bf16[400,256]{1,0:T(8,128)(2,1)S(1)} %get-tuple-element.82.refs_1_, bf16[400,256]{1,0:T(8,128)(2,1)S(1)} %get-tuple-element.83.refs_2_), custom_call_target="tpu_custom_call" | custom-call | flops 1677721600 | bytes 4194304 | tf_op jit(solution)/shard_map/early_sum/pallas_call | solution.py:200
  55.9 4.8 %early_sum.5.refs_7_ = f32[4096,256]{1,0:T(8,128)S(1)} custom-call(s32[22]{0:T(128)S(1)} %fusion.6.places, bf16[800,4096]{1,0:T(8,128)(2,1)S(1)} %get-tuple-element.40.refs_0_, bf16[800,4096]{1,0:T(8,128)(2,1)S(1)} %get-tuple-element.41.refs_1_, bf16[400,256]{1,0:T(8,128)(2,1)S(1)} %collective-permute-done.5.refs_2_, ...), custom_call_target="tpu_custom_call" | custom-call | flops 1677721600 | bytes 4194304 | tf_op jit(solution)/shard_map/early_sum/pallas_call | solution.py:200
  74.2 2.6 collective-permute-start.12
  79.5 7.1 %collective-permute-done.12 = bf16[256,256]{1,0:T(8,128)(2,1)S(1)} collective-permute-done((bf16[256,256]{1,0:T(8,128)(2,1)S(1)}, bf16[256,256]{1,0:T(8,128)(2,1)S(1)}, u32[]{:S(2)}, u32[]{:S(2)}) %collective-permute-start.12) | collective-permute-done | bytes 131104 | tf_op jit(solution)/shard_map/ppermute | solution.py:34
  90.1 4.0 %collective-permute-start.20 = (bf16[256,256]{1,0:T(8,128)(2,1)S(1)}, bf16[256,256]{1,0:T(8,128)(2,1)S(1)}, u32[]{:S(2)}, u32[]{:S(2)}) collective-permute-start(bf16[256,256]{1,0:T(8,128)(2,1)S(1)} %get-tuple-element.88), channel_id=1, source_target_pairs={{0,16},{4,20},{8,24},{12,28},{16,0},{20,4},{24,8},{28,12},{1,17},{... | collective-permute-start | bytes 393224 | tf_op jit(solution)/shard_map/ppermute | solution.py:34
  94.1 6.6 %collective-permute-done.20.refs_3_.refs_4_.refs_2_ = bf16[256,256]{1,0:T(8,128)(2,1)S(1)} collective-permute-done((bf16[256,256]{1,0:T(8,128)(2,1)S(1)}, bf16[256,256]{1,0:T(8,128)(2,1)S(1)}, u32[]{:S(2)}, u32[]{:S(2)}) %collective-permute-start.20) | collective-permute-done | bytes 131104 | tf_op jit(solution)/shard_map/ppermute | solution.py:34
  100.7 3.1 %collective-permute-start.21 = (bf16[256,256]{1,0:T(8,128)(2,1)S(1)}, bf16[256,256]{1,0:T(8,128)(2,1)S(1)}, u32[]{:S(2)}, u32[]{:S(2)}) collective-permute-start(bf16[256,256]{1,0:T(8,128)(2,1)S(1)} %collective-permute-done.20.refs_3_.refs_4_.refs_2_), channel_id=1, source_target_pairs={{0,8},{4,12},{8,0},{12,4},{16,24},{20,28},{24,16},{28,20},{1,9},{5... | collective-permute-start | bytes 393224 | tf_op jit(solution)/shard_map/ppermute | solution.py:34
  103.8 3.0 %collective-permute-done.22.refs_5_.refs_6_.refs_4_ = bf16[256,256]{1,0:T(8,128)(2,1)S(1)} collective-permute-done((bf16[256,256]{1,0:T(8,128)(2,1)S(1)}, bf16[256,256]{1,0:T(8,128)(2,1)S(1)}, u32[]{:S(2)}, u32[]{:S(2)}) %collective-permute-start.22) | collective-permute-done | bytes 131104 | tf_op jit(solution)/shard_map/ppermute | solution.py:34
  108.9 3.2 %collective-permute-done.23.refs_6_.refs_7_.refs_5_ = bf16[256,256]{1,0:T(8,128)(2,1)S(1)} collective-permute-done((bf16[256,256]{1,0:T(8,128)(2,1)S(1)}, bf16[256,256]{1,0:T(8,128)(2,1)S(1)}, u32[]{:S(2)}, u32[]{:S(2)}) %collective-permute-start.23) | collective-permute-done | bytes 131104 | tf_op jit(solution)/shard_map/ppermute | solution.py:34
  127.6 2.4 score.4
  133.9 4.2 %collective-permute-done.30 = bf16[400,256]{1,0:T(8,128)(2,1)S(1)} collective-permute-done((bf16[400,256]{1,0:T(8,128)(2,1)S(1)}, bf16[400,256]{1,0:T(8,128)(2,1)S(1)}, u32[]{:S(2)}, u32[]{:S(2)}) %collective-permute-start.30) | collective-permute-done | bytes 204832 | tf_op jit(solution)/shard_map/ppermute | solution.py:34
  139.7 5.0 %collective-permute-done.36 = bf16[400,256]{1,0:T(8,128)(2,1)S(1)} collective-permute-done((bf16[400,256]{1,0:T(8,128)(2,1)S(1)}, bf16[400,256]{1,0:T(8,128)(2,1)S(1)}, u32[]{:S(2)}, u32[]{:S(2)}) %collective-permute-start.36) | collective-permute-done | bytes 204832 | tf_op jit(solution)/shard_map/ppermute | solution.py:34
  147.1 6.0 %cholesky.3.refs_0_ = f32[256,512]{1,0:T(8,128)S(1)} custom-call(s32[22]{0:T(128)S(1)} %fusion.6.places, f32[128,256]{1,0:T(8,128)S(1)} %add_add_fusion.1.refs_0_, f32[128,256]{1,0:T(8,128)S(1)} %collective-permute-done.55.refs_1_), custom_call_target="tpu_custom_call" | custom-call | flops 3000000000 | bytes 786432 | tf_op jit(solution)/shard_map/cholesky/pallas_call | solution.py:433
  157.2 5.0 %early_sum.6.refs_4_ = f32[4096,256]{1,0:T(8,128)S(1)} custom-call(s32[22]{0:T(128)S(1)} %fusion.6.places, bf16[800,4096]{1,0:T(8,128)(2,1)S(1)} %get-tuple-element.43.refs_0_, bf16[400,256]{1,0:T(8,128)(2,1)S(1)} %multiply_convert_fusion.refs_1_, bf16[400,256]{1,0:T(8,128)(2,1)S(1)} %multiply_convert_fusion.1.refs_2_), custom_call_target="tpu_custom_call" | custom-call | flops 1677721600 | bytes 4194304 | tf_op jit(solution)/shard_map/early_sum/pallas_call | solution.py:200
  162.1 4.7 %early_sum.7.refs_7_ = f32[4096,256]{1,0:T(8,128)S(1)} custom-call(s32[22]{0:T(128)S(1)} %fusion.6.places, bf16[800,4096]{1,0:T(8,128)(2,1)S(1)} %get-tuple-element.40.refs_0_, bf16[800,4096]{1,0:T(8,128)(2,1)S(1)} %get-tuple-element.41.refs_1_, bf16[400,256]{1,0:T(8,128)(2,1)S(1)} %collective-permute-done.38.refs_2_, ...), custom_call_target="tpu_custom_call" | custom-call | flops 1677721600 | bytes 4194304 | tf_op jit(solution)/shard_map/early_sum/pallas_call | solution.py:200
  169.1 6.8 %cholesky.4 = (f32[256,256]{1,0:T(8,128)}, f32[256,256]{1,0:T(8,128)S(1)}) custom-call(s32[22]{0:T(128)S(1)} %fusion.6.places, f32[256,512]{1,0:T(8,128)S(1)} %cholesky.3.refs_0_), custom_call_target="tpu_custom_call" | custom-call | flops 3000000000 | bytes 786432 | tf_op jit(solution)/shard_map/cholesky/pallas_call | solution.py:433
  194.9 6.3 %collective-permute-done.45.refs_0_ = bf16[256,256]{1,0:T(8,128)(2,1)S(1)} collective-permute-done((bf16[256,256]{1,0:T(8,128)(2,1)S(1)}, bf16[256,256]{1,0:T(8,128)(2,1)S(1)}, u32[]{:S(2)}, u32[]{:S(2)}) %collective-permute-start.45) | collective-permute-done | bytes 131104 | tf_op jit(solution)/shard_map/ppermute | solution.py:34
  201.3 2.7 %collective-permute-done.47.refs_1_ = bf16[256,256]{1,0:T(8,128)(2,1)S(1)} collective-permute-done((bf16[256,256]{1,0:T(8,128)(2,1)S(1)}, bf16[256,256]{1,0:T(8,128)(2,1)S(1)}, u32[]{:S(2)}, u32[]{:S(2)}) %collective-permute-start.47) | collective-permute-done | bytes 131104 | tf_op jit(solution)/shard_map/ppermute | solution.py:34
  208.6 5.5 %collective-permute-done.57 = f32[128,256]{1,0:T(8,128)S(1)} collective-permute-done((f32[128,256]{1,0:T(8,128)S(1)}, f32[128,256]{1,0:T(8,128)S(1)}, u32[]{:S(2)}, u32[]{:S(2)}) %collective-permute-start.57) | collective-permute-done | bytes 131104 | tf_op jit(solution)/shard_map/ppermute | solution.py:34
  215.5 7.2 %collective-permute-done.58 = f32[128,256]{1,0:T(8,128)S(1)} collective-permute-done((f32[128,256]{1,0:T(8,128)S(1)}, f32[128,256]{1,0:T(8,128)S(1)}, u32[]{:S(2)}, u32[]{:S(2)}) %collective-permute-start.58) | collective-permute-done | bytes 131104 | tf_op jit(solution)/shard_map/ppermute | solution.py:34
  226.2 3.0 %collective-permute-start.64 = (bf16[512,256]{1,0:T(8,128)(2,1)S(1)}, bf16[512,256]{1,0:T(8,128)(2,1)S(1)}, u32[]{:S(2)}, u32[]{:S(2)}) collective-permute-start(bf16[512,256]{1,0:T(8,128)(2,1)S(1)} %get-tuple-element.76.refs_0_), channel_id=1, source_target_pairs={{0,16},{4,20},{8,24},{12,28},{16,0},{20,4},{24,8},{28,12},{1,17},{... | collective-permute-start | bytes 786440 | tf_op jit(solution)/shard_map/ppermute | solution.py:34
  232.8 5.4 %collective-permute-done.63.refs_1_ = bf16[512,256]{1,0:T(8,128)(2,1)S(1)} collective-permute-done((bf16[512,256]{1,0:T(8,128)(2,1)S(1)}, bf16[512,256]{1,0:T(8,128)(2,1)S(1)}, u32[]{:S(2)}, u32[]{:S(2)}) %collective-permute-start.63) | collective-permute-done | bytes 262176 | tf_op jit(solution)/shard_map/ppermute | solution.py:34
  238.2 9.4 %collective-permute-done.64.refs_2_ = bf16[512,256]{1,0:T(8,128)(2,1)S(1)} collective-permute-done((bf16[512,256]{1,0:T(8,128)(2,1)S(1)}, bf16[512,256]{1,0:T(8,128)(2,1)S(1)}, u32[]{:S(2)}, u32[]{:S(2)}) %collective-permute-start.64) | collective-permute-done | bytes 262176 | tf_op jit(solution)/shard_map/ppermute | solution.py:34
  248.1 12.2 %cholesky.5 = (f32[256,256]{1,0:T(8,128)}, f32[256,256]{1,0:T(8,128)S(1)}) custom-call(s32[22]{0:T(128)S(1)} %fusion.6.places, f32[128,256]{1,0:T(8,128)S(1)} %add_add_fusion.refs_0_, f32[128,256]{1,0:T(8,128)S(1)} %collective-permute-done.62.refs_1_), custom_call_target="tpu_custom_call" | custom-call | flops 6000000000 | bytes 786432 | tf_op jit(solution)/shard_map/cholesky/pallas_call | solution.py:433
  260.3 4.5 %apply.1 = f32[4096,256]{1,0:T(8,128)} custom-call(s32[22]{0:T(128)S(1)} %fusion.6.places, f32[256,256]{1,0:T(8,128)S(1)} %get-tuple-element.75.inverse_ref, bf16[512,256]{1,0:T(8,128)(2,1)S(1)} %get-tuple-element.76.refs_0_, bf16[512,256]{1,0:T(8,128)(2,1)S(1)} %collective-permute-done.63.refs_1_, bf16[512,256]{1,0:T(8,128)(2,1)S(1)} %collective-permute-done.64.refs_2_, ...), custom_call_target="tpu_custom_call" | custom-call | flops 1610612736 | bytes 6291456 | tf_op jit(solution)/shard_map/apply/pallas_call | solution.py:471
  (172 shorter events, 94.2 us)
Async XLA Ops:
  10.7 27.9 %collective-permute-start = (bf16[800,256]{1,0:T(8,128)(2,1)S(1)}, bf16[800,256]{1,0:T(8,128)(2,1)S(1)}, u32[]{:S(2)}, u32[]{:S(2)}) collective-permute-start(bf16[800,256]{1,0:T(8,128)(2,1)S(1)} %get-tuple-element.45), channel_id=1, source_target_pairs={{0,3},{1,2},{2,1},{3,0},{4,7},{5,6},{6,5},{7,4},{8,11},{9,10},{10,... | collective-permute-start | bytes 1228808 | tf_op jit(solution)/shard_map/ppermute | solution.py:34
  22.1 16.4 %collective-permute-start.1 = (bf16[800,256]{1,0:T(8,128)(2,1)S(1)}, bf16[800,256]{1,0:T(8,128)(2,1)S(1)}, u32[]{:S(2)}, u32[]{:S(2)}) collective-permute-start(bf16[800,256]{1,0:T(8,128)(2,1)S(1)} %get-tuple-element.46), channel_id=1, source_target_pairs={{0,2},{1,3},{2,0},{3,1},{4,6},{5,7},{6,4},{7,5},{8,10},{9,11},{10,... | collective-permute-start | bytes 1228808 | tf_op jit(solution)/shard_map/ppermute | solution.py:34
  43.2 17.5 %collective-permute-start.3 = (bf16[400,256]{1,0:T(8,128)(2,1)S(1)}, bf16[400,256]{1,0:T(8,128)(2,1)S(1)}, u32[]{:S(2)}, u32[]{:S(2)}) collective-permute-start(bf16[400,256]{1,0:T(8,128)(2,1)S(1)} %get-tuple-element.83.refs_2_), channel_id=1, source_target_pairs={{0,1},{1,0},{2,3},{3,2},{4,5},{5,4},{6,7},{7,6},{8,9},{9,8},{10,11... | collective-permute-start | bytes 614408 | tf_op jit(solution)/shard_map/ppermute | solution.py:34
  44.7 16.1 %collective-permute-start.4 = (bf16[400,256]{1,0:T(8,128)(2,1)S(1)}, bf16[400,256]{1,0:T(8,128)(2,1)S(1)}, u32[]{:S(2)}, u32[]{:S(2)}) collective-permute-start(bf16[400,256]{1,0:T(8,128)(2,1)S(1)} %get-tuple-element.82.refs_1_), channel_id=1, source_target_pairs={{0,2},{1,3},{2,0},{3,1},{4,6},{5,7},{6,4},{7,5},{8,10},{9,11},{10,... | collective-permute-start | bytes 614408 | tf_op jit(solution)/shard_map/ppermute | solution.py:34
  49.1 11.6 %collective-permute-start.6 = (bf16[400,256]{1,0:T(8,128)(2,1)S(1)}, bf16[400,256]{1,0:T(8,128)(2,1)S(1)}, u32[]{:S(2)}, u32[]{:S(2)}) collective-permute-start(bf16[400,256]{1,0:T(8,128)(2,1)S(1)} %collective-permute-done.5.refs_2_), channel_id=1, source_target_pairs={{0,2},{1,3},{2,0},{3,1},{4,6},{5,7},{6,4},{7,5},{8,10},{9,11},{10,... | collective-permute-start | bytes 614408 | tf_op jit(solution)/shard_map/ppermute | solution.py:34
  74.2 12.3 %collective-permute-start.12 = (bf16[256,256]{1,0:T(8,128)(2,1)S(1)}, bf16[256,256]{1,0:T(8,128)(2,1)S(1)}, u32[]{:S(2)}, u32[]{:S(2)}) collective-permute-start(bf16[256,256]{1,0:T(8,128)(2,1)S(1)} %get-tuple-element.90), channel_id=1, source_target_pairs={{0,16},{4,20},{8,24},{12,28},{16,0},{20,4},{24,8},{28,12},{1,17},{... | collective-permute-start | bytes 393224 | tf_op jit(solution)/shard_map/ppermute | solution.py:34
  88.9 17.9 %collective-permute-start.19 = (bf16[512,256]{1,0:T(8,128)(2,1)S(1)}, bf16[512,256]{1,0:T(8,128)(2,1)S(1)}, u32[]{:S(2)}, u32[]{:S(2)}) collective-permute-start(bf16[512,256]{1,0:T(8,128)(2,1)S(1)} %pad_maximum_fusion.refs_1_.refs_2_.refs_0_), channel_id=1, source_target_pairs={{0,8},{4,12},{8,0},{12,4},{16,24},{20,28},{24,16},{28,20},{1,9},{5... | collective-permute-start | bytes 786440 | tf_op jit(solution)/shard_map/ppermute | solution.py:34
  90.1 17.2 %collective-permute-start.24 = (bf16[512,256]{1,0:T(8,128)(2,1)S(1)}, bf16[512,256]{1,0:T(8,128)(2,1)S(1)}, u32[]{:S(2)}, u32[]{:S(2)}) collective-permute-start(bf16[512,256]{1,0:T(8,128)(2,1)S(1)} %pad_maximum_fusion.refs_1_.refs_2_.refs_0_), channel_id=1, source_target_pairs={{0,4},{4,0},{8,12},{12,8},{16,20},{20,16},{24,28},{28,24},{1,5},{5... | collective-permute-start | bytes 786440 | tf_op jit(solution)/shard_map/ppermute | solution.py:34
  94.1 12.7 %collective-permute-start.22 = (bf16[256,256]{1,0:T(8,128)(2,1)S(1)}, bf16[256,256]{1,0:T(8,128)(2,1)S(1)}, u32[]{:S(2)}, u32[]{:S(2)}) collective-permute-start(bf16[256,256]{1,0:T(8,128)(2,1)S(1)} %get-tuple-element.89), channel_id=1, source_target_pairs={{0,16},{4,20},{8,24},{12,28},{16,0},{20,4},{24,8},{28,12},{1,17},{... | collective-permute-start | bytes 393224 | tf_op jit(solution)/shard_map/ppermute | solution.py:34
  114.7 15.3 %collective-permute-start.52 = (f32[128,256]{1,0:T(8,128)S(1)}, f32[128,256]{1,0:T(8,128)S(1)}, u32[]{:S(2)}, u32[]{:S(2)}) collective-permute-start(f32[128,256]{1,0:T(8,128)S(1)} %gram.1), channel_id=1, source_target_pairs={{0,1},{1,0},{2,3},{3,2},{4,5},{5,4},{6,7},{7,6},{8,9},{9,8},{10,11... | collective-permute-start | bytes 393224 | tf_op jit(solution)/shard_map/ppermute | solution.py:34
  116.3 15.3 %collective-permute-start.53 = (f32[128,256]{1,0:T(8,128)S(1)}, f32[128,256]{1,0:T(8,128)S(1)}, u32[]{:S(2)}, u32[]{:S(2)}) collective-permute-start(f32[128,256]{1,0:T(8,128)S(1)} %gram.1), channel_id=1, source_target_pairs={{0,2},{1,3},{2,0},{3,1},{4,6},{5,7},{6,4},{7,5},{8,10},{9,11},{10,... | collective-permute-start | bytes 393224 | tf_op jit(solution)/shard_map/ppermute | solution.py:34
  116.8 15.3 %collective-permute-start.54 = (f32[128,256]{1,0:T(8,128)S(1)}, f32[128,256]{1,0:T(8,128)S(1)}, u32[]{:S(2)}, u32[]{:S(2)}) collective-permute-start(f32[128,256]{1,0:T(8,128)S(1)} %gram.1), channel_id=1, source_target_pairs={{0,3},{1,2},{2,1},{3,0},{4,7},{5,6},{6,5},{7,4},{8,11},{9,10},{10,... | collective-permute-start | bytes 393224 | tf_op jit(solution)/shard_map/ppermute | solution.py:34
  120.7 11.6 %collective-permute-start.35 = (bf16[400,256]{1,0:T(8,128)(2,1)S(1)}, bf16[400,256]{1,0:T(8,128)(2,1)S(1)}, u32[]{:S(2)}, u32[]{:S(2)}) collective-permute-start(bf16[400,256]{1,0:T(8,128)(2,1)S(1)} %get-tuple-element.63), channel_id=1, source_target_pairs={{0,1},{1,0},{2,3},{3,2},{4,5},{5,4},{6,7},{7,6},{8,9},{9,8},{10,11... | collective-permute-start | bytes 614408 | tf_op jit(solution)/shard_map/ppermute | solution.py:34
  124.6 15.0 %collective-permute-start.34 = (bf16[400,256]{1,0:T(8,128)(2,1)S(1)}, bf16[400,256]{1,0:T(8,128)(2,1)S(1)}, u32[]{:S(2)}, u32[]{:S(2)}) collective-permute-start(bf16[400,256]{1,0:T(8,128)(2,1)S(1)} %get-tuple-element.61), channel_id=1, source_target_pairs={{0,1},{1,0},{2,3},{3,2},{4,5},{5,4},{6,7},{7,6},{8,9},{9,8},{10,11... | collective-permute-start | bytes 614408 | tf_op jit(solution)/shard_map/ppermute | solution.py:34
  131.6 14.7 %collective-permute-start.32 = (bf16[400,256]{1,0:T(8,128)(2,1)S(1)}, bf16[400,256]{1,0:T(8,128)(2,1)S(1)}, u32[]{:S(2)}, u32[]{:S(2)}) collective-permute-start(bf16[400,256]{1,0:T(8,128)(2,1)S(1)} %get-tuple-element.59), channel_id=1, source_target_pairs={{0,2},{1,3},{2,0},{3,1},{4,6},{5,7},{6,4},{7,5},{8,10},{9,11},{10,... | collective-permute-start | bytes 614408 | tf_op jit(solution)/shard_map/ppermute | solution.py:34
  132.2 14.9 %collective-permute-start.55 = (f32[128,256]{1,0:T(8,128)S(1)}, f32[128,256]{1,0:T(8,128)S(1)}, u32[]{:S(2)}, u32[]{:S(2)}) collective-permute-start(f32[128,256]{1,0:T(8,128)S(1)} %add_add_fusion.1.refs_0_), channel_id=1, source_target_pairs={{0,4},{4,0},{8,12},{12,8},{16,20},{20,16},{24,28},{28,24},{1,5},{5... | collective-permute-start | bytes 393224 | tf_op jit(solution)/shard_map/ppermute | solution.py:34
  132.3 12.3 %collective-permute-start.36 = (bf16[400,256]{1,0:T(8,128)(2,1)S(1)}, bf16[400,256]{1,0:T(8,128)(2,1)S(1)}, u32[]{:S(2)}, u32[]{:S(2)}) collective-permute-start(bf16[400,256]{1,0:T(8,128)(2,1)S(1)} %add_convert_fusion.2), channel_id=1, source_target_pairs={{0,2},{1,3},{2,0},{3,1},{4,6},{5,7},{6,4},{7,5},{8,10},{9,11},{10,... | collective-permute-start | bytes 614408 | tf_op jit(solution)/shard_map/ppermute | solution.py:34
  153.0 13.8 %collective-permute-start.37 = (bf16[400,256]{1,0:T(8,128)(2,1)S(1)}, bf16[400,256]{1,0:T(8,128)(2,1)S(1)}, u32[]{:S(2)}, u32[]{:S(2)}) collective-permute-start(bf16[400,256]{1,0:T(8,128)(2,1)S(1)} %multiply_convert_fusion.refs_1_), channel_id=1, source_target_pairs={{0,2},{1,3},{2,0},{3,1},{4,6},{5,7},{6,4},{7,5},{8,10},{9,11},{10,... | collective-permute-start | bytes 614408 | tf_op jit(solution)/shard_map/ppermute | solution.py:34
  154.6 12.3 %collective-permute-start.33 = (bf16[400,256]{1,0:T(8,128)(2,1)S(1)}, bf16[400,256]{1,0:T(8,128)(2,1)S(1)}, u32[]{:S(2)}, u32[]{:S(2)}) collective-permute-start(bf16[400,256]{1,0:T(8,128)(2,1)S(1)} %multiply_convert_fusion.1.refs_2_), channel_id=1, source_target_pairs={{0,1},{1,0},{2,3},{3,2},{4,5},{5,4},{6,7},{7,6},{8,9},{9,8},{10,11... | collective-permute-start | bytes 614408 | tf_op jit(solution)/shard_map/ppermute | solution.py:34
  155.1 11.8 %collective-permute-start.39 = (bf16[400,256]{1,0:T(8,128)(2,1)S(1)}, bf16[400,256]{1,0:T(8,128)(2,1)S(1)}, u32[]{:S(2)}, u32[]{:S(2)}) collective-permute-start(bf16[400,256]{1,0:T(8,128)(2,1)S(1)} %collective-permute-done.38.refs_2_), channel_id=1, source_target_pairs={{0,2},{1,3},{2,0},{3,1},{4,6},{5,7},{6,4},{7,5},{8,10},{9,11},{10,... | collective-permute-start | bytes 614408 | tf_op jit(solution)/shard_map/ppermute | solution.py:34
  180.7 11.9 %collective-permute-start.48 = (bf16[512,256]{1,0:T(8,128)(2,1)S(1)}, bf16[512,256]{1,0:T(8,128)(2,1)S(1)}, u32[]{:S(2)}, u32[]{:S(2)}) collective-permute-start(bf16[512,256]{1,0:T(8,128)(2,1)S(1)} %get-tuple-element.69), channel_id=1, source_target_pairs={{0,4},{4,0},{8,12},{12,8},{16,20},{20,16},{24,28},{28,24},{1,5},{5... | collective-permute-start | bytes 786440 | tf_op jit(solution)/shard_map/ppermute | solution.py:34
  189.7 11.6 %collective-permute-start.45 = (bf16[256,256]{1,0:T(8,128)(2,1)S(1)}, bf16[256,256]{1,0:T(8,128)(2,1)S(1)}, u32[]{:S(2)}, u32[]{:S(2)}) collective-permute-start(bf16[256,256]{1,0:T(8,128)(2,1)S(1)} %get-tuple-element.87), channel_id=1, source_target_pairs={{0,16},{4,20},{8,24},{12,28},{16,0},{20,4},{24,8},{28,12},{1,17},{... | collective-permute-start | bytes 393224 | tf_op jit(solution)/shard_map/ppermute | solution.py:34
  191.0 13.0 %collective-permute-start.47 = (bf16[256,256]{1,0:T(8,128)(2,1)S(1)}, bf16[256,256]{1,0:T(8,128)(2,1)S(1)}, u32[]{:S(2)}, u32[]{:S(2)}) collective-permute-start(bf16[256,256]{1,0:T(8,128)(2,1)S(1)} %get-tuple-element.86), channel_id=1, source_target_pairs={{0,16},{4,20},{8,24},{12,28},{16,0},{20,4},{24,8},{28,12},{1,17},{... | collective-permute-start | bytes 393224 | tf_op jit(solution)/shard_map/ppermute | solution.py:34
  193.1 12.5 %collective-permute-start.50 = (bf16[256,256]{1,0:T(8,128)(2,1)S(1)}, bf16[256,256]{1,0:T(8,128)(2,1)S(1)}, u32[]{:S(2)}, u32[]{:S(2)}) collective-permute-start(bf16[256,256]{1,0:T(8,128)(2,1)S(1)} %get-tuple-element.92), channel_id=1, source_target_pairs={{0,8},{4,12},{8,0},{12,4},{16,24},{20,28},{24,16},{28,20},{1,9},{5... | collective-permute-start | bytes 393224 | tf_op jit(solution)/shard_map/ppermute | solution.py:34
  226.2 12.0 %collective-permute-start.63 = (bf16[512,256]{1,0:T(8,128)(2,1)S(1)}, bf16[512,256]{1,0:T(8,128)(2,1)S(1)}, u32[]{:S(2)}, u32[]{:S(2)}) collective-permute-start(bf16[512,256]{1,0:T(8,128)(2,1)S(1)} %get-tuple-element.76.refs_0_), channel_id=1, source_target_pairs={{0,8},{4,12},{8,0},{12,4},{16,24},{20,28},{24,16},{28,20},{1,9},{5... | collective-permute-start | bytes 786440 | tf_op jit(solution)/shard_map/ppermute | solution.py:34
  226.2 21.4 %collective-permute-start.64 = (bf16[512,256]{1,0:T(8,128)(2,1)S(1)}, bf16[512,256]{1,0:T(8,128)(2,1)S(1)}, u32[]{:S(2)}, u32[]{:S(2)}) collective-permute-start(bf16[512,256]{1,0:T(8,128)(2,1)S(1)} %get-tuple-element.76.refs_0_), channel_id=1, source_target_pairs={{0,16},{4,20},{8,24},{12,28},{16,0},{20,4},{24,8},{28,12},{1,17},{... | collective-permute-start | bytes 786440 | tf_op jit(solution)/shard_map/ppermute | solution.py:34
  229.2 18.4 %collective-permute-start.65 = (bf16[512,256]{1,0:T(8,128)(2,1)S(1)}, bf16[512,256]{1,0:T(8,128)(2,1)S(1)}, u32[]{:S(2)}, u32[]{:S(2)}) collective-permute-start(bf16[512,256]{1,0:T(8,128)(2,1)S(1)} %get-tuple-element.76.refs_0_), channel_id=1, source_target_pairs={{0,24},{4,28},{8,16},{12,20},{16,8},{20,12},{24,0},{28,4},{1,25},{... | collective-permute-start | bytes 786440 | tf_op jit(solution)/shard_map/ppermute | solution.py:34
  232.2 15.9 %collective-permute-start.62 = (f32[128,256]{1,0:T(8,128)S(1)}, f32[128,256]{1,0:T(8,128)S(1)}, u32[]{:S(2)}, u32[]{:S(2)}) collective-permute-start(f32[128,256]{1,0:T(8,128)S(1)} %add_add_fusion.refs_0_), channel_id=1, source_target_pairs={{0,4},{4,0},{8,12},{12,8},{16,20},{20,16},{24,28},{28,24},{1,5},{5... | collective-permute-start | bytes 393224 | tf_op jit(solution)/shard_map/ppermute | solution.py:34
  232.3 28.0 %collective-permute-start.66 = (bf16[512,256]{1,0:T(8,128)(2,1)S(1)}, bf16[512,256]{1,0:T(8,128)(2,1)S(1)}, u32[]{:S(2)}, u32[]{:S(2)}) collective-permute-start(bf16[512,256]{1,0:T(8,128)(2,1)S(1)} %get-tuple-element.76.refs_0_), channel_id=1, source_target_pairs={{0,4},{4,0},{8,12},{12,8},{16,20},{20,16},{24,28},{28,24},{1,5},{5... | collective-permute-start | bytes 786440 | tf_op jit(solution)/shard_map/ppermute | solution.py:34
  238.2 22.1 %collective-permute-start.67 = (bf16[512,256]{1,0:T(8,128)(2,1)S(1)}, bf16[512,256]{1,0:T(8,128)(2,1)S(1)}, u32[]{:S(2)}, u32[]{:S(2)}) collective-permute-start(bf16[512,256]{1,0:T(8,128)(2,1)S(1)} %collective-permute-done.63.refs_1_), channel_id=1, source_target_pairs={{0,4},{4,0},{8,12},{12,8},{16,20},{20,16},{24,28},{28,24},{1,5},{5... | collective-permute-start | bytes 786440 | tf_op jit(solution)/shard_map/ppermute | solution.py:34
  247.6 12.7 %collective-permute-start.68 = (bf16[512,256]{1,0:T(8,128)(2,1)S(1)}, bf16[512,256]{1,0:T(8,128)(2,1)S(1)}, u32[]{:S(2)}, u32[]{:S(2)}) collective-permute-start(bf16[512,256]{1,0:T(8,128)(2,1)S(1)} %collective-permute-done.64.refs_2_), channel_id=1, source_target_pairs={{0,4},{4,0},{8,12},{12,8},{16,20},{20,16},{24,28},{28,24},{1,5},{5... | collective-permute-start | bytes 786440 | tf_op jit(solution)/shard_map/ppermute | solution.py:34
  247.6 12.7 %collective-permute-start.69 = (bf16[512,256]{1,0:T(8,128)(2,1)S(1)}, bf16[512,256]{1,0:T(8,128)(2,1)S(1)}, u32[]{:S(2)}, u32[]{:S(2)}) collective-permute-start(bf16[512,256]{1,0:T(8,128)(2,1)S(1)} %collective-permute-done.65.refs_3_), channel_id=1, source_target_pairs={{0,4},{4,0},{8,12},{12,8},{16,20},{20,16},{24,28},{28,24},{1,5},{5... | collective-permute-start | bytes 786440 | tf_op jit(solution)/shard_map/ppermute | solution.py:34
  (41 other events, 300.3 us)

commit v7 on v6

--- a/solution.py
+++ b/solution.py
@@ -85,7 +85,6 @@
         ],
         compiler_params=vmem(14 * 2**20),
         cost_estimate=cost(4 * chunk * pixels * columns, 2 * chunk * pixels),
-        name="filter_and_score",
     )(places, classes.reshape(rows // tile, 1, tile), images, table, probe_half)
 
 
@@ -142,7 +141,6 @@
         out_shape=[jax.ShapeDtypeStruct((half, columns), kind) for kind in out_types],
         compiler_params=vmem(16 * 2**20),
         cost_estimate=cost(2 * rows * pixels * columns, 2 * rows * columns),
-        name="score",
     )(places, *[filtered[at] for at in used], *blocks)
 
 
@@ -203,7 +201,6 @@
         out_shape=[jax.ShapeDtypeStruct((pixels, columns), F32)],
         compiler_params=vmem(12 * 2**20),
         cost_estimate=cost(2 * len(pieces) * rows * pixels * columns, 4 * pixels * columns),
-        name="early_sum",
     )(places, *blocks, *pieces, *before)[0]
 
 
@@ -243,7 +240,6 @@
         ],
         compiler_params=vmem(12 * 2**20),
         cost_estimate=cost(4 * len(pieces) * rows * width * columns, 6 * width * columns),
-        name="late_sum",
     )(places, *blocks, *pieces, early, *after)
 
 
@@ -277,7 +273,6 @@
         out_shape=[jax.ShapeDtypeStruct((columns // 2, columns), F32)],
         compiler_params=vmem(12 * 2**20),
         cost_estimate=cost(2 * rows * columns * columns, 2 * rows * columns),
-        name="gram",
     )(places, *blocks)[0]
 
 
@@ -318,7 +313,6 @@
         ],
         compiler_params=vmem(12 * 2**20),
         cost_estimate=cost(14 * rows * columns * columns, 8 * rows * columns),
-        name="normalize",
     )(places, *parts, inverse)
 
 
@@ -442,7 +436,6 @@
             out_shape=[square, square] if final else [work],
             compiler_params=vmem(12 * 2**20),
             cost_estimate=cost(6e9 // calls, 12 * size * size),
-            name="cholesky",
         )(places, *state)
     return state
 
@@ -460,7 +453,7 @@
     block = stacked_ref[pl.ds(pl.multiple_of(pl.program_id(0) * span, span), span), :]
     out_ref[...] = sum(
         lax.dot_general(block, part, (((1,), (1,)), ((), ())), preferred_element_type=F32)
-        for part in reversed(split_in_three(inverse_ref[...]))
+        for part in reversed(split_in_three(inverse_ref[...])[:2])
     )
 
 
@@ -480,7 +473,6 @@
         out_shape=jax.ShapeDtypeStruct((pixels, columns), F32),
         compiler_params=vmem(16 * 2**20),
         cost_estimate=cost(6 * pixels * columns * columns, 6 * pixels * columns),
-        name="apply",
     )(places, inverse, *basis)
 
 
@@ -671,7 +663,7 @@
             gram = half_gram(places, cores_at, basis)
             gram = add_over_pix(gram, pix)
             other = xor_swap(gram, "img", 1)
-            _, inverse = cholesky_and_inverse(places, cores_at, [gram, other], 2)
+            _, inverse = cholesky_and_inverse(places, cores_at, [gram, other], 1)
             break
 
         total = [sum(part[at].astype(F32) for part in parts) for at in (0, 1)]

time: 267 us -> 272 us (1.019)
  waiting for transfers between devices: 86.7 us -> 91.1 us
    ppermute x70, waiting for transfers between devices: 86.7 us -> 91.1 us  [xor_swap(): return lax.ppermute(value, axis, [(i, i ^ mask) for i in range(size)])]
    pallas_call x3 -> x2, Pallas kernels: 25 us -> 24.4 us  [cholesky_and_inverse(): pl.pallas_call(functools.partial(cholesky_kernel, first, last, place_at),...]
  transfers between devices with their start and end apart: 70 -> 70, of which waited for: 25 -> 27; matrix products, arithmetic and copies ran while one was open for 1% -> 1% of each run, Pallas kernels for 34% -> 33%
where the time goes in v7:
time: 272 us; the launch traced here: 271 us
  Pallas kernels  107 us (39%)
  waiting for transfers between devices  91.1 us (33%)
  starting transfers between devices  66.6 us (24%)
  other arithmetic  3.98 us (1%)
    ppermute x70, waiting for transfers between devices, xor_swap(): return lax.ppermute(value, axis, [(i, i ^ mask) for i in range(size)])  91.1 us
    ppermute x70, starting transfers between devices, xor_swap(): return lax.ppermute(value, axis, [(i, i ^ mask) for i in range(size)])  66.6 us
    pallas_call x4, Pallas kernels, filter_and_score(): pl.pallas_call(filter_kernel, grid_spec=pltpu.PrefetchScalarGridSpec(num_...  29.7 us
    pallas_call x2, Pallas kernels, cholesky_and_inverse(): pl.pallas_call(functools.partial(cholesky_kernel, first, last, place_at),...  24.4 us
    pallas_call x4, Pallas kernels, early_sum(): pl.pallas_call(functools.partial(early_sum_kernel, len(blocks), entries,...  19 us
    pallas_call x8, Pallas kernels, late_sum(): pl.pallas_call(functools.partial(late_sum_kernel, len(blocks), entries, f...  17.1 us
    pallas_call x4, Pallas kernels, score(): pl.pallas_call(functools.partial(score_kernel, first, width, spots, len(u...  9.58 us
  transfers between devices with their start and end apart: 70, of which 27 were waited for; matrix products, arithmetic and copies ran while one was open for 1% of the time, Pallas kernels for 33%

profile of v7, /device:TPU:0, one launch (start us, length us, event | category | flops | bytes accessed | tf_op | source)
XLA Modules:
  0.0 270.6 jit_solution(1294788669079502241)
XLA Ops:
  0.7 2.4 convert_element_type.138.probe_ref
  3.3 7.4 %shard_map.70 = (bf16[800,4096]{1,0:T(8,128)(2,1)S(1)}, bf16[800,256]{1,0:T(8,128)(2,1)S(1)}) custom-call(s32[22]{0:T(128)S(1)} %fusion.6.places, s32[8,1,400]{2,1,0:T(1,128)S(1)} %reshape.18.class_ref, bf16[3200,4096]{1,0:T(8,128)(2,1)} %image_ref.7, bf16[64,4096]{1,0:T(8,128)(2,1)S(1)} %copy-done, bf16[4096,256]{1,0:T(8,128)(2,1)S(1)} %convert_element_type.138.probe_ref), custom_call_target="tpu_custom_call" | custom-call | flops 3355443200 | bytes 6553600 | tf_op jit(solution)/shard_map/pallas_call | solution.py:69
  10.7 4.0 %collective-permute-start = (bf16[800,256]{1,0:T(8,128)(2,1)S(1)}, bf16[800,256]{1,0:T(8,128)(2,1)S(1)}, u32[]{:S(2)}, u32[]{:S(2)}) collective-permute-start(bf16[800,256]{1,0:T(8,128)(2,1)S(1)} %get-tuple-element.45), channel_id=1, source_target_pairs={{0,3},{1,2},{2,1},{3,0},{4,7},{5,6},{6,5},{7,4},{8,11},{9,10},{10,... | collective-permute-start | bytes 1228808 | tf_op jit(solution)/shard_map/ppermute | solution.py:34
  14.7 7.4 %shard_map.69 = (bf16[800,4096]{1,0:T(8,128)(2,1)S(1)}, bf16[800,256]{1,0:T(8,128)(2,1)S(1)}) custom-call(s32[22]{0:T(128)S(1)} %fusion.6.places, s32[8,1,400]{2,1,0:T(1,128)S(1)} %reshape.18.class_ref, bf16[3200,4096]{1,0:T(8,128)(2,1)} %image_ref.7, bf16[64,4096]{1,0:T(8,128)(2,1)S(1)} %copy-done, bf16[4096,256]{1,0:T(8,128)(2,1)S(1)} %convert_element_type.138.probe_ref), custom_call_target="tpu_custom_call" | custom-call | flops 3355443200 | bytes 6553600 | tf_op jit(solution)/shard_map/pallas_call | solution.py:69
  22.7 7.4 %shard_map.68 = (bf16[800,4096]{1,0:T(8,128)(2,1)S(1)}, bf16[800,256]{1,0:T(8,128)(2,1)S(1)}) custom-call(s32[22]{0:T(128)S(1)} %fusion.6.places, s32[8,1,400]{2,1,0:T(1,128)S(1)} %reshape.18.class_ref, bf16[3200,4096]{1,0:T(8,128)(2,1)} %image_ref.7, bf16[64,4096]{1,0:T(8,128)(2,1)S(1)} %copy-done, bf16[4096,256]{1,0:T(8,128)(2,1)S(1)} %convert_element_type.138.probe_ref), custom_call_target="tpu_custom_call" | custom-call | flops 3355443200 | bytes 6553600 | tf_op jit(solution)/shard_map/pallas_call | solution.py:69
  31.1 7.4 %shard_map.71 = (bf16[800,4096]{1,0:T(8,128)(2,1)S(1)}, f32[800,256]{1,0:T(8,128)S(1)}) custom-call(s32[22]{0:T(128)S(1)} %fusion.6.places, s32[8,1,400]{2,1,0:T(1,128)S(1)} %reshape.18.class_ref, bf16[3200,4096]{1,0:T(8,128)(2,1)} %image_ref.7, bf16[64,4096]{1,0:T(8,128)(2,1)S(1)} %copy-done.1, bf16[4096,256]{1,0:T(8,128)(2,1)S(1)} %convert_element_type.138.probe_ref), custom_call_target="tpu_custom_call" | custom-call | flops 3355443200 | bytes 6553600 | tf_op jit(solution)/shard_map/pallas_call | solution.py:69
  45.2 3.9 %collective-permute-done.5.refs_2_ = bf16[400,256]{1,0:T(8,128)(2,1)S(1)} collective-permute-done((bf16[400,256]{1,0:T(8,128)(2,1)S(1)}, bf16[400,256]{1,0:T(8,128)(2,1)S(1)}, u32[]{:S(2)}, u32[]{:S(2)}) %collective-permute-start.5) | collective-permute-done | bytes 204832 | tf_op jit(solution)/shard_map/ppermute | solution.py:34
  51.2 4.7 %shard_map.72.refs_4_ = f32[4096,256]{1,0:T(8,128)S(1)} custom-call(s32[22]{0:T(128)S(1)} %fusion.6.places, bf16[800,4096]{1,0:T(8,128)(2,1)S(1)} %get-tuple-element.43.refs_0_, bf16[400,256]{1,0:T(8,128)(2,1)S(1)} %get-tuple-element.82.refs_1_, bf16[400,256]{1,0:T(8,128)(2,1)S(1)} %get-tuple-element.83.refs_2_), custom_call_target="tpu_custom_call" | custom-call | flops 1677721600 | bytes 4194304 | tf_op jit(solution)/shard_map/pallas_call | solution.py:198
  55.9 4.8 %shard_map.73.refs_7_ = f32[4096,256]{1,0:T(8,128)S(1)} custom-call(s32[22]{0:T(128)S(1)} %fusion.6.places, bf16[800,4096]{1,0:T(8,128)(2,1)S(1)} %get-tuple-element.40.refs_0_, bf16[800,4096]{1,0:T(8,128)(2,1)S(1)} %get-tuple-element.41.refs_1_, bf16[400,256]{1,0:T(8,128)(2,1)S(1)} %collective-permute-done.5.refs_2_, ...), custom_call_target="tpu_custom_call" | custom-call | flops 1677721600 | bytes 4194304 | tf_op jit(solution)/shard_map/pallas_call | solution.py:198
  74.2 2.6 collective-permute-start.12
  79.4 7.1 %collective-permute-done.12 = bf16[256,256]{1,0:T(8,128)(2,1)S(1)} collective-permute-done((bf16[256,256]{1,0:T(8,128)(2,1)S(1)}, bf16[256,256]{1,0:T(8,128)(2,1)S(1)}, u32[]{:S(2)}, u32[]{:S(2)}) %collective-permute-start.12) | collective-permute-done | bytes 131104 | tf_op jit(solution)/shard_map/ppermute | solution.py:34
  90.1 4.0 %collective-permute-start.20 = (bf16[256,256]{1,0:T(8,128)(2,1)S(1)}, bf16[256,256]{1,0:T(8,128)(2,1)S(1)}, u32[]{:S(2)}, u32[]{:S(2)}) collective-permute-start(bf16[256,256]{1,0:T(8,128)(2,1)S(1)} %get-tuple-element.88), channel_id=1, source_target_pairs={{0,16},{4,20},{8,24},{12,28},{16,0},{20,4},{24,8},{28,12},{1,17},{... | collective-permute-start | bytes 393224 | tf_op jit(solution)/shard_map/ppermute | solution.py:34
  94.0 6.6 %collective-permute-done.20.refs_3_.refs_4_.refs_2_ = bf16[256,256]{1,0:T(8,128)(2,1)S(1)} collective-permute-done((bf16[256,256]{1,0:T(8,128)(2,1)S(1)}, bf16[256,256]{1,0:T(8,128)(2,1)S(1)}, u32[]{:S(2)}, u32[]{:S(2)}) %collective-permute-start.20) | collective-permute-done | bytes 131104 | tf_op jit(solution)/shard_map/ppermute | solution.py:34
  100.6 3.1 %collective-permute-start.21 = (bf16[256,256]{1,0:T(8,128)(2,1)S(1)}, bf16[256,256]{1,0:T(8,128)(2,1)S(1)}, u32[]{:S(2)}, u32[]{:S(2)}) collective-permute-start(bf16[256,256]{1,0:T(8,128)(2,1)S(1)} %collective-permute-done.20.refs_3_.refs_4_.refs_2_), channel_id=1, source_target_pairs={{0,8},{4,12},{8,0},{12,4},{16,24},{20,28},{24,16},{28,20},{1,9},{5... | collective-permute-start | bytes 393224 | tf_op jit(solution)/shard_map/ppermute | solution.py:34
  103.7 3.0 %collective-permute-done.22.refs_5_.refs_6_.refs_4_ = bf16[256,256]{1,0:T(8,128)(2,1)S(1)} collective-permute-done((bf16[256,256]{1,0:T(8,128)(2,1)S(1)}, bf16[256,256]{1,0:T(8,128)(2,1)S(1)}, u32[]{:S(2)}, u32[]{:S(2)}) %collective-permute-start.22) | collective-permute-done | bytes 131104 | tf_op jit(solution)/shard_map/ppermute | solution.py:34
  108.8 3.2 %collective-permute-done.23.refs_6_.refs_7_.refs_5_ = bf16[256,256]{1,0:T(8,128)(2,1)S(1)} collective-permute-done((bf16[256,256]{1,0:T(8,128)(2,1)S(1)}, bf16[256,256]{1,0:T(8,128)(2,1)S(1)}, u32[]{:S(2)}, u32[]{:S(2)}) %collective-permute-start.23) | collective-permute-done | bytes 131104 | tf_op jit(solution)/shard_map/ppermute | solution.py:34
  131.6 4.2 %collective-permute-done.30 = bf16[400,256]{1,0:T(8,128)(2,1)S(1)} collective-permute-done((bf16[400,256]{1,0:T(8,128)(2,1)S(1)}, bf16[400,256]{1,0:T(8,128)(2,1)S(1)}, u32[]{:S(2)}, u32[]{:S(2)}) %collective-permute-start.30) | collective-permute-done | bytes 204832 | tf_op jit(solution)/shard_map/ppermute | solution.py:34
  138.0 4.6 %collective-permute-done.36 = bf16[400,256]{1,0:T(8,128)(2,1)S(1)} collective-permute-done((bf16[400,256]{1,0:T(8,128)(2,1)S(1)}, bf16[400,256]{1,0:T(8,128)(2,1)S(1)}, u32[]{:S(2)}, u32[]{:S(2)}) %collective-permute-start.36) | collective-permute-done | bytes 204832 | tf_op jit(solution)/shard_map/ppermute | solution.py:34
  153.0 2.5 collective-permute-done.40.refs_3_
  155.5 2.5 collective-permute-start.41
  158.0 4.7 %shard_map.82.refs_4_ = f32[4096,256]{1,0:T(8,128)S(1)} custom-call(s32[22]{0:T(128)S(1)} %fusion.6.places, bf16[800,4096]{1,0:T(8,128)(2,1)S(1)} %get-tuple-element.43.refs_0_, bf16[400,256]{1,0:T(8,128)(2,1)S(1)} %multiply_convert_fusion.refs_1_, bf16[400,256]{1,0:T(8,128)(2,1)S(1)} %multiply_convert_fusion.1.refs_2_), custom_call_target="tpu_custom_call" | custom-call | flops 1677721600 | bytes 4194304 | tf_op jit(solution)/shard_map/pallas_call | solution.py:198
  162.7 4.7 %shard_map.83.refs_7_ = f32[4096,256]{1,0:T(8,128)S(1)} custom-call(s32[22]{0:T(128)S(1)} %fusion.6.places, bf16[800,4096]{1,0:T(8,128)(2,1)S(1)} %get-tuple-element.40.refs_0_, bf16[800,4096]{1,0:T(8,128)(2,1)S(1)} %get-tuple-element.41.refs_1_, bf16[400,256]{1,0:T(8,128)(2,1)S(1)} %collective-permute-done.38.refs_2_, ...), custom_call_target="tpu_custom_call" | custom-call | flops 1677721600 | bytes 4194304 | tf_op jit(solution)/shard_map/pallas_call | solution.py:198
  169.9 12.2 %shard_map.89 = (f32[256,256]{1,0:T(8,128)}, f32[256,256]{1,0:T(8,128)S(1)}) custom-call(s32[22]{0:T(128)S(1)} %fusion.6.places, f32[128,256]{1,0:T(8,128)S(1)} %add_add_fusion.1.refs_0_, f32[128,256]{1,0:T(8,128)S(1)} %collective-permute-done.55.refs_1_), custom_call_target="tpu_custom_call" | custom-call | flops 6000000000 | bytes 786432 | tf_op jit(solution)/shard_map/pallas_call | solution.py:427
  201.1 6.3 %collective-permute-done.45.refs_0_ = bf16[256,256]{1,0:T(8,128)(2,1)S(1)} collective-permute-done((bf16[256,256]{1,0:T(8,128)(2,1)S(1)}, bf16[256,256]{1,0:T(8,128)(2,1)S(1)}, u32[]{:S(2)}, u32[]{:S(2)}) %collective-permute-start.45) | collective-permute-done | bytes 131104 | tf_op jit(solution)/shard_map/ppermute | solution.py:34
  207.5 2.7 %collective-permute-done.47.refs_1_ = bf16[256,256]{1,0:T(8,128)(2,1)S(1)} collective-permute-done((bf16[256,256]{1,0:T(8,128)(2,1)S(1)}, bf16[256,256]{1,0:T(8,128)(2,1)S(1)}, u32[]{:S(2)}, u32[]{:S(2)}) %collective-permute-start.47) | collective-permute-done | bytes 131104 | tf_op jit(solution)/shard_map/ppermute | solution.py:34
  214.8 5.5 %collective-permute-done.57 = f32[128,256]{1,0:T(8,128)S(1)} collective-permute-done((f32[128,256]{1,0:T(8,128)S(1)}, f32[128,256]{1,0:T(8,128)S(1)}, u32[]{:S(2)}, u32[]{:S(2)}) %collective-permute-start.57) | collective-permute-done | bytes 131104 | tf_op jit(solution)/shard_map/ppermute | solution.py:34
  221.7 7.2 %collective-permute-done.58 = f32[128,256]{1,0:T(8,128)S(1)} collective-permute-done((f32[128,256]{1,0:T(8,128)S(1)}, f32[128,256]{1,0:T(8,128)S(1)}, u32[]{:S(2)}, u32[]{:S(2)}) %collective-permute-start.58) | collective-permute-done | bytes 131104 | tf_op jit(solution)/shard_map/ppermute | solution.py:34
  232.4 3.0 %collective-permute-start.64 = (bf16[512,256]{1,0:T(8,128)(2,1)S(1)}, bf16[512,256]{1,0:T(8,128)(2,1)S(1)}, u32[]{:S(2)}, u32[]{:S(2)}) collective-permute-start(bf16[512,256]{1,0:T(8,128)(2,1)S(1)} %get-tuple-element.76.refs_0_), channel_id=1, source_target_pairs={{0,16},{4,20},{8,24},{12,28},{16,0},{20,4},{24,8},{28,12},{1,17},{... | collective-permute-start | bytes 786440 | tf_op jit(solution)/shard_map/ppermute | solution.py:34
  238.3 6.1 %collective-permute-done.63.refs_1_ = bf16[512,256]{1,0:T(8,128)(2,1)S(1)} collective-permute-done((bf16[512,256]{1,0:T(8,128)(2,1)S(1)}, bf16[512,256]{1,0:T(8,128)(2,1)S(1)}, u32[]{:S(2)}, u32[]{:S(2)}) %collective-permute-start.63) | collective-permute-done | bytes 262176 | tf_op jit(solution)/shard_map/ppermute | solution.py:34
  244.4 9.4 %collective-permute-done.64.refs_2_ = bf16[512,256]{1,0:T(8,128)(2,1)S(1)} collective-permute-done((bf16[512,256]{1,0:T(8,128)(2,1)S(1)}, bf16[512,256]{1,0:T(8,128)(2,1)S(1)}, u32[]{:S(2)}, u32[]{:S(2)}) %collective-permute-start.64) | collective-permute-done | bytes 262176 | tf_op jit(solution)/shard_map/ppermute | solution.py:34
  254.3 12.2 %shard_map.91 = (f32[256,256]{1,0:T(8,128)}, f32[256,256]{1,0:T(8,128)S(1)}) custom-call(s32[22]{0:T(128)S(1)} %fusion.6.places, f32[128,256]{1,0:T(8,128)S(1)} %add_add_fusion.refs_0_, f32[128,256]{1,0:T(8,128)S(1)} %collective-permute-done.62.refs_1_), custom_call_target="tpu_custom_call" | custom-call | flops 6000000000 | bytes 786432 | tf_op jit(solution)/shard_map/pallas_call | solution.py:427
  266.5 4.1 %shard_map.92 = f32[4096,256]{1,0:T(8,128)} custom-call(s32[22]{0:T(128)S(1)} %fusion.6.places, f32[256,256]{1,0:T(8,128)S(1)} %get-tuple-element.75.inverse_ref, bf16[512,256]{1,0:T(8,128)(2,1)S(1)} %get-tuple-element.76.refs_0_, bf16[512,256]{1,0:T(8,128)(2,1)S(1)} %collective-permute-done.63.refs_1_, ...), custom_call_target="tpu_custom_call" | custom-call | flops 1610612736 | bytes 6291456 | tf_op jit(solution)/shard_map/pallas_call | solution.py:464
  (171 shorter events, 98.4 us)
Async XLA Ops:
  10.7 27.9 %collective-permute-start = (bf16[800,256]{1,0:T(8,128)(2,1)S(1)}, bf16[800,256]{1,0:T(8,128)(2,1)S(1)}, u32[]{:S(2)}, u32[]{:S(2)}) collective-permute-start(bf16[800,256]{1,0:T(8,128)(2,1)S(1)} %get-tuple-element.45), channel_id=1, source_target_pairs={{0,3},{1,2},{2,1},{3,0},{4,7},{5,6},{6,5},{7,4},{8,11},{9,10},{10,... | collective-permute-start | bytes 1228808 | tf_op jit(solution)/shard_map/ppermute | solution.py:34
  22.1 16.4 %collective-permute-start.1 = (bf16[800,256]{1,0:T(8,128)(2,1)S(1)}, bf16[800,256]{1,0:T(8,128)(2,1)S(1)}, u32[]{:S(2)}, u32[]{:S(2)}) collective-permute-start(bf16[800,256]{1,0:T(8,128)(2,1)S(1)} %get-tuple-element.46), channel_id=1, source_target_pairs={{0,2},{1,3},{2,0},{3,1},{4,6},{5,7},{6,4},{7,5},{8,10},{9,11},{10,... | collective-permute-start | bytes 1228808 | tf_op jit(solution)/shard_map/ppermute | solution.py:34
  43.2 17.5 %collective-permute-start.3 = (bf16[400,256]{1,0:T(8,128)(2,1)S(1)}, bf16[400,256]{1,0:T(8,128)(2,1)S(1)}, u32[]{:S(2)}, u32[]{:S(2)}) collective-permute-start(bf16[400,256]{1,0:T(8,128)(2,1)S(1)} %get-tuple-element.83.refs_2_), channel_id=1, source_target_pairs={{0,1},{1,0},{2,3},{3,2},{4,5},{5,4},{6,7},{7,6},{8,9},{9,8},{10,11... | collective-permute-start | bytes 614408 | tf_op jit(solution)/shard_map/ppermute | solution.py:34
  44.7 16.0 %collective-permute-start.4 = (bf16[400,256]{1,0:T(8,128)(2,1)S(1)}, bf16[400,256]{1,0:T(8,128)(2,1)S(1)}, u32[]{:S(2)}, u32[]{:S(2)}) collective-permute-start(bf16[400,256]{1,0:T(8,128)(2,1)S(1)} %get-tuple-element.82.refs_1_), channel_id=1, source_target_pairs={{0,2},{1,3},{2,0},{3,1},{4,6},{5,7},{6,4},{7,5},{8,10},{9,11},{10,... | collective-permute-start | bytes 614408 | tf_op jit(solution)/shard_map/ppermute | solution.py:34
  49.1 11.6 %collective-permute-start.6 = (bf16[400,256]{1,0:T(8,128)(2,1)S(1)}, bf16[400,256]{1,0:T(8,128)(2,1)S(1)}, u32[]{:S(2)}, u32[]{:S(2)}) collective-permute-start(bf16[400,256]{1,0:T(8,128)(2,1)S(1)} %collective-permute-done.5.refs_2_), channel_id=1, source_target_pairs={{0,2},{1,3},{2,0},{3,1},{4,6},{5,7},{6,4},{7,5},{8,10},{9,11},{10,... | collective-permute-start | bytes 614408 | tf_op jit(solution)/shard_map/ppermute | solution.py:34
  74.2 12.4 %collective-permute-start.12 = (bf16[256,256]{1,0:T(8,128)(2,1)S(1)}, bf16[256,256]{1,0:T(8,128)(2,1)S(1)}, u32[]{:S(2)}, u32[]{:S(2)}) collective-permute-start(bf16[256,256]{1,0:T(8,128)(2,1)S(1)} %get-tuple-element.90), channel_id=1, source_target_pairs={{0,16},{4,20},{8,24},{12,28},{16,0},{20,4},{24,8},{28,12},{1,17},{... | collective-permute-start | bytes 393224 | tf_op jit(solution)/shard_map/ppermute | solution.py:34
  88.8 17.9 %collective-permute-start.19 = (bf16[512,256]{1,0:T(8,128)(2,1)S(1)}, bf16[512,256]{1,0:T(8,128)(2,1)S(1)}, u32[]{:S(2)}, u32[]{:S(2)}) collective-permute-start(bf16[512,256]{1,0:T(8,128)(2,1)S(1)} %pad_maximum_fusion.refs_1_.refs_2_.refs_0_), channel_id=1, source_target_pairs={{0,8},{4,12},{8,0},{12,4},{16,24},{20,28},{24,16},{28,20},{1,9},{5... | collective-permute-start | bytes 786440 | tf_op jit(solution)/shard_map/ppermute | solution.py:34
  90.1 17.2 %collective-permute-start.24 = (bf16[512,256]{1,0:T(8,128)(2,1)S(1)}, bf16[512,256]{1,0:T(8,128)(2,1)S(1)}, u32[]{:S(2)}, u32[]{:S(2)}) collective-permute-start(bf16[512,256]{1,0:T(8,128)(2,1)S(1)} %pad_maximum_fusion.refs_1_.refs_2_.refs_0_), channel_id=1, source_target_pairs={{0,4},{4,0},{8,12},{12,8},{16,20},{20,16},{24,28},{28,24},{1,5},{5... | collective-permute-start | bytes 786440 | tf_op jit(solution)/shard_map/ppermute | solution.py:34
  94.0 12.7 %collective-permute-start.22 = (bf16[256,256]{1,0:T(8,128)(2,1)S(1)}, bf16[256,256]{1,0:T(8,128)(2,1)S(1)}, u32[]{:S(2)}, u32[]{:S(2)}) collective-permute-start(bf16[256,256]{1,0:T(8,128)(2,1)S(1)} %get-tuple-element.89), channel_id=1, source_target_pairs={{0,16},{4,20},{8,24},{12,28},{16,0},{20,4},{24,8},{28,12},{1,17},{... | collective-permute-start | bytes 393224 | tf_op jit(solution)/shard_map/ppermute | solution.py:34
  114.7 35.6 %collective-permute-start.52 = (f32[128,256]{1,0:T(8,128)S(1)}, f32[128,256]{1,0:T(8,128)S(1)}, u32[]{:S(2)}, u32[]{:S(2)}) collective-permute-start(f32[128,256]{1,0:T(8,128)S(1)} %shard_map.88), channel_id=1, source_target_pairs={{0,1},{1,0},{2,3},{3,2},{4,5},{5,4},{6,7},{7,6},{8,9},{9,8},{10,11... | collective-permute-start | bytes 393224 | tf_op jit(solution)/shard_map/ppermute | solution.py:34
  116.2 34.0 %collective-permute-start.53 = (f32[128,256]{1,0:T(8,128)S(1)}, f32[128,256]{1,0:T(8,128)S(1)}, u32[]{:S(2)}, u32[]{:S(2)}) collective-permute-start(f32[128,256]{1,0:T(8,128)S(1)} %shard_map.88), channel_id=1, source_target_pairs={{0,2},{1,3},{2,0},{3,1},{4,6},{5,7},{6,4},{7,5},{8,10},{9,11},{10,... | collective-permute-start | bytes 393224 | tf_op jit(solution)/shard_map/ppermute | solution.py:34
  116.7 33.5 %collective-permute-start.54 = (f32[128,256]{1,0:T(8,128)S(1)}, f32[128,256]{1,0:T(8,128)S(1)}, u32[]{:S(2)}, u32[]{:S(2)}) collective-permute-start(f32[128,256]{1,0:T(8,128)S(1)} %shard_map.88), channel_id=1, source_target_pairs={{0,3},{1,2},{2,1},{3,0},{4,7},{5,6},{6,5},{7,4},{8,11},{9,10},{10,... | collective-permute-start | bytes 393224 | tf_op jit(solution)/shard_map/ppermute | solution.py:34
  124.6 12.8 %collective-permute-start.34 = (bf16[400,256]{1,0:T(8,128)(2,1)S(1)}, bf16[400,256]{1,0:T(8,128)(2,1)S(1)}, u32[]{:S(2)}, u32[]{:S(2)}) collective-permute-start(bf16[400,256]{1,0:T(8,128)(2,1)S(1)} %get-tuple-element.61), channel_id=1, source_target_pairs={{0,1},{1,0},{2,3},{3,2},{4,5},{5,4},{6,7},{7,6},{8,9},{9,8},{10,11... | collective-permute-start | bytes 614408 | tf_op jit(solution)/shard_map/ppermute | solution.py:34
  150.3 19.6 %collective-permute-start.55 = (f32[128,256]{1,0:T(8,128)S(1)}, f32[128,256]{1,0:T(8,128)S(1)}, u32[]{:S(2)}, u32[]{:S(2)}) collective-permute-start(f32[128,256]{1,0:T(8,128)S(1)} %add_add_fusion.1.refs_0_), channel_id=1, source_target_pairs={{0,4},{4,0},{8,12},{12,8},{16,20},{20,16},{24,28},{28,24},{1,5},{5... | collective-permute-start | bytes 393224 | tf_op jit(solution)/shard_map/ppermute | solution.py:34
  150.3 17.1 %collective-permute-start.37 = (bf16[400,256]{1,0:T(8,128)(2,1)S(1)}, bf16[400,256]{1,0:T(8,128)(2,1)S(1)}, u32[]{:S(2)}, u32[]{:S(2)}) collective-permute-start(bf16[400,256]{1,0:T(8,128)(2,1)S(1)} %multiply_convert_fusion.refs_1_), channel_id=1, source_target_pairs={{0,2},{1,3},{2,0},{3,1},{4,6},{5,7},{6,4},{7,5},{8,10},{9,11},{10,... | collective-permute-start | bytes 614408 | tf_op jit(solution)/shard_map/ppermute | solution.py:34
  150.9 16.5 %collective-permute-start.33 = (bf16[400,256]{1,0:T(8,128)(2,1)S(1)}, bf16[400,256]{1,0:T(8,128)(2,1)S(1)}, u32[]{:S(2)}, u32[]{:S(2)}) collective-permute-start(bf16[400,256]{1,0:T(8,128)(2,1)S(1)} %multiply_convert_fusion.1.refs_2_), channel_id=1, source_target_pairs={{0,1},{1,0},{2,3},{3,2},{4,5},{5,4},{6,7},{7,6},{8,9},{9,8},{10,11... | collective-permute-start | bytes 614408 | tf_op jit(solution)/shard_map/ppermute | solution.py:34
  152.4 15.0 %collective-permute-start.39 = (bf16[400,256]{1,0:T(8,128)(2,1)S(1)}, bf16[400,256]{1,0:T(8,128)(2,1)S(1)}, u32[]{:S(2)}, u32[]{:S(2)}) collective-permute-start(bf16[400,256]{1,0:T(8,128)(2,1)S(1)} %collective-permute-done.38.refs_2_), channel_id=1, source_target_pairs={{0,2},{1,3},{2,0},{3,1},{4,6},{5,7},{6,4},{7,5},{8,10},{9,11},{10,... | collective-permute-start | bytes 614408 | tf_op jit(solution)/shard_map/ppermute | solution.py:34
  155.5 12.0 %collective-permute-start.41 = (bf16[400,256]{1,0:T(8,128)(2,1)S(1)}, bf16[400,256]{1,0:T(8,128)(2,1)S(1)}, u32[]{:S(2)}, u32[]{:S(2)}) collective-permute-start(bf16[400,256]{1,0:T(8,128)(2,1)S(1)} %collective-permute-done.40.refs_3_), channel_id=1, source_target_pairs={{0,1},{1,0},{2,3},{3,2},{4,5},{5,4},{6,7},{7,6},{8,9},{9,8},{10,11... | collective-permute-start | bytes 614408 | tf_op jit(solution)/shard_map/ppermute | solution.py:34
  169.8 14.9 %collective-permute-start.43 = (bf16[512,256]{1,0:T(8,128)(2,1)S(1)}, bf16[512,256]{1,0:T(8,128)(2,1)S(1)}, u32[]{:S(2)}, u32[]{:S(2)}) collective-permute-start(bf16[512,256]{1,0:T(8,128)(2,1)S(1)} %get-tuple-element.67), channel_id=1, source_target_pairs={{0,4},{4,0},{8,12},{12,8},{16,20},{20,16},{24,28},{28,24},{1,5},{5... | collective-permute-start | bytes 786440 | tf_op jit(solution)/shard_map/ppermute | solution.py:34
  186.9 11.9 %collective-permute-start.48 = (bf16[512,256]{1,0:T(8,128)(2,1)S(1)}, bf16[512,256]{1,0:T(8,128)(2,1)S(1)}, u32[]{:S(2)}, u32[]{:S(2)}) collective-permute-start(bf16[512,256]{1,0:T(8,128)(2,1)S(1)} %get-tuple-element.69), channel_id=1, source_target_pairs={{0,4},{4,0},{8,12},{12,8},{16,20},{20,16},{24,28},{28,24},{1,5},{5... | collective-permute-start | bytes 786440 | tf_op jit(solution)/shard_map/ppermute | solution.py:34
  195.9 11.6 %collective-permute-start.45 = (bf16[256,256]{1,0:T(8,128)(2,1)S(1)}, bf16[256,256]{1,0:T(8,128)(2,1)S(1)}, u32[]{:S(2)}, u32[]{:S(2)}) collective-permute-start(bf16[256,256]{1,0:T(8,128)(2,1)S(1)} %get-tuple-element.87), channel_id=1, source_target_pairs={{0,16},{4,20},{8,24},{12,28},{16,0},{20,4},{24,8},{28,12},{1,17},{... | collective-permute-start | bytes 393224 | tf_op jit(solution)/shard_map/ppermute | solution.py:34
  197.2 13.0 %collective-permute-start.47 = (bf16[256,256]{1,0:T(8,128)(2,1)S(1)}, bf16[256,256]{1,0:T(8,128)(2,1)S(1)}, u32[]{:S(2)}, u32[]{:S(2)}) collective-permute-start(bf16[256,256]{1,0:T(8,128)(2,1)S(1)} %get-tuple-element.86), channel_id=1, source_target_pairs={{0,16},{4,20},{8,24},{12,28},{16,0},{20,4},{24,8},{28,12},{1,17},{... | collective-permute-start | bytes 393224 | tf_op jit(solution)/shard_map/ppermute | solution.py:34
  198.9 11.5 %collective-permute-start.49 = (bf16[256,256]{1,0:T(8,128)(2,1)S(1)}, bf16[256,256]{1,0:T(8,128)(2,1)S(1)}, u32[]{:S(2)}, u32[]{:S(2)}) collective-permute-start(bf16[256,256]{1,0:T(8,128)(2,1)S(1)} %get-tuple-element.93), channel_id=1, source_target_pairs={{0,8},{4,12},{8,0},{12,4},{16,24},{20,28},{24,16},{28,20},{1,9},{5... | collective-permute-start | bytes 393224 | tf_op jit(solution)/shard_map/ppermute | solution.py:34
  199.3 12.5 %collective-permute-start.50 = (bf16[256,256]{1,0:T(8,128)(2,1)S(1)}, bf16[256,256]{1,0:T(8,128)(2,1)S(1)}, u32[]{:S(2)}, u32[]{:S(2)}) collective-permute-start(bf16[256,256]{1,0:T(8,128)(2,1)S(1)} %get-tuple-element.92), channel_id=1, source_target_pairs={{0,8},{4,12},{8,0},{12,4},{16,24},{20,28},{24,16},{28,20},{1,9},{5... | collective-permute-start | bytes 393224 | tf_op jit(solution)/shard_map/ppermute | solution.py:34
  232.4 12.0 %collective-permute-start.63 = (bf16[512,256]{1,0:T(8,128)(2,1)S(1)}, bf16[512,256]{1,0:T(8,128)(2,1)S(1)}, u32[]{:S(2)}, u32[]{:S(2)}) collective-permute-start(bf16[512,256]{1,0:T(8,128)(2,1)S(1)} %get-tuple-element.76.refs_0_), channel_id=1, source_target_pairs={{0,8},{4,12},{8,0},{12,4},{16,24},{20,28},{24,16},{28,20},{1,9},{5... | collective-permute-start | bytes 786440 | tf_op jit(solution)/shard_map/ppermute | solution.py:34
  232.4 21.4 %collective-permute-start.64 = (bf16[512,256]{1,0:T(8,128)(2,1)S(1)}, bf16[512,256]{1,0:T(8,128)(2,1)S(1)}, u32[]{:S(2)}, u32[]{:S(2)}) collective-permute-start(bf16[512,256]{1,0:T(8,128)(2,1)S(1)} %get-tuple-element.76.refs_0_), channel_id=1, source_target_pairs={{0,16},{4,20},{8,24},{12,28},{16,0},{20,4},{24,8},{28,12},{1,17},{... | collective-permute-start | bytes 786440 | tf_op jit(solution)/shard_map/ppermute | solution.py:34
  235.4 18.4 %collective-permute-start.65 = (bf16[512,256]{1,0:T(8,128)(2,1)S(1)}, bf16[512,256]{1,0:T(8,128)(2,1)S(1)}, u32[]{:S(2)}, u32[]{:S(2)}) collective-permute-start(bf16[512,256]{1,0:T(8,128)(2,1)S(1)} %get-tuple-element.76.refs_0_), channel_id=1, source_target_pairs={{0,24},{4,28},{8,16},{12,20},{16,8},{20,12},{24,0},{28,4},{1,25},{... | collective-permute-start | bytes 786440 | tf_op jit(solution)/shard_map/ppermute | solution.py:34
  237.8 16.5 %collective-permute-start.62 = (f32[128,256]{1,0:T(8,128)S(1)}, f32[128,256]{1,0:T(8,128)S(1)}, u32[]{:S(2)}, u32[]{:S(2)}) collective-permute-start(f32[128,256]{1,0:T(8,128)S(1)} %add_add_fusion.refs_0_), channel_id=1, source_target_pairs={{0,4},{4,0},{8,12},{12,8},{16,20},{20,16},{24,28},{28,24},{1,5},{5... | collective-permute-start | bytes 393224 | tf_op jit(solution)/shard_map/ppermute | solution.py:34
  237.8 28.7 %collective-permute-start.66 = (bf16[512,256]{1,0:T(8,128)(2,1)S(1)}, bf16[512,256]{1,0:T(8,128)(2,1)S(1)}, u32[]{:S(2)}, u32[]{:S(2)}) collective-permute-start(bf16[512,256]{1,0:T(8,128)(2,1)S(1)} %get-tuple-element.76.refs_0_), channel_id=1, source_target_pairs={{0,4},{4,0},{8,12},{12,8},{16,20},{20,16},{24,28},{28,24},{1,5},{5... | collective-permute-start | bytes 786440 | tf_op jit(solution)/shard_map/ppermute | solution.py:34
  244.4 22.1 %collective-permute-start.67 = (bf16[512,256]{1,0:T(8,128)(2,1)S(1)}, bf16[512,256]{1,0:T(8,128)(2,1)S(1)}, u32[]{:S(2)}, u32[]{:S(2)}) collective-permute-start(bf16[512,256]{1,0:T(8,128)(2,1)S(1)} %collective-permute-done.63.refs_1_), channel_id=1, source_target_pairs={{0,4},{4,0},{8,12},{12,8},{16,20},{20,16},{24,28},{28,24},{1,5},{5... | collective-permute-start | bytes 786440 | tf_op jit(solution)/shard_map/ppermute | solution.py:34
  253.8 12.7 %collective-permute-start.68 = (bf16[512,256]{1,0:T(8,128)(2,1)S(1)}, bf16[512,256]{1,0:T(8,128)(2,1)S(1)}, u32[]{:S(2)}, u32[]{:S(2)}) collective-permute-start(bf16[512,256]{1,0:T(8,128)(2,1)S(1)} %collective-permute-done.64.refs_2_), channel_id=1, source_target_pairs={{0,4},{4,0},{8,12},{12,8},{16,20},{20,16},{24,28},{28,24},{1,5},{5... | collective-permute-start | bytes 786440 | tf_op jit(solution)/shard_map/ppermute | solution.py:34
  253.8 12.7 %collective-permute-start.69 = (bf16[512,256]{1,0:T(8,128)(2,1)S(1)}, bf16[512,256]{1,0:T(8,128)(2,1)S(1)}, u32[]{:S(2)}, u32[]{:S(2)}) collective-permute-start(bf16[512,256]{1,0:T(8,128)(2,1)S(1)} %collective-permute-done.65.refs_3_), channel_id=1, source_target_pairs={{0,4},{4,0},{8,12},{12,8},{16,20},{20,16},{24,28},{28,24},{1,5},{5... | collective-permute-start | bytes 786440 | tf_op jit(solution)/shard_map/ppermute | solution.py:34
  (41 other events, 282.1 us)
